TPU v7x, 32 devices: a whole 2x2x4 slice. The times are simulated.
32 devices in a mesh: req: 8 (over z, y), ctx: 4 (over x, core).
Axes of the slice: x: 2, y: 2, z: 4, core: 2. Of those that a mesh axis runs over, the one named last changes fastest.
Arguments:
- history: bfloat16 [24576, 1024], P(('req', 'ctx')), may hold values from -6 to 6
- block_owner: int32 [1536, 1], P(('req', 'ctx')), may hold values from 0 to 7; in each aligned block of 48 rows (0 to 47, 48 to 95, ...) at most 12 rows name the same one
- candidates: bfloat16 [4096, 1024], P(('req', 'ctx')), may hold values from -6 to 6
- w_kv: bfloat16 [1024, 2048], replicated, may hold values from -0.1875 to 0.1875
- w_qu: bfloat16 [1024, 2048], replicated, may hold values from -0.1875 to 0.1875
- w_out: bfloat16 [1024, 1024], replicated, may hold values from -0.1875 to 0.1875
Outputs:
- scored: bfloat16 [4096, 1024], P(('req', 'ctx'))
Inputs may be any that keep to these rules, and one draw needn't show every extreme that they name: `block_owner`: each packed block belongs to one request; among the 48 blocks of one device at most 12 belong to the same request, and that most is reached on some device; every request owns at least one block.
All inputs are finite; a program needn't handle non-finite values.
Results may differ from a plain program's by a relative error of at most 0.0052.
Values may be sent and summed in bfloat16 or wider, within the bound.
No kernel may reach another device: no remote copies, remote signals or barrier semaphores. Data moves between devices by JAX's collectives and lax.ppermute only.
A program may use at most 128 MiB of HBM per device.

v0:
```python
import functools

import jax
import jax.numpy as jnp
from jax import lax
from jax.experimental import pallas as pl
from jax.experimental.pallas import tpu as pltpu
from jax.sharding import PartitionSpec as P


HEAD = 128
TILE = 256
BF16 = jnp.bfloat16
F32 = jnp.float32


def silu(v):
    h = 0.5 * v
    return h + h * jnp.tanh(h)


def swap(value, axis, mask):
    count = lax.axis_size(axis)
    return lax.ppermute(value, axis, [(i, i ^ mask) for i in range(count)])


def scalar_grid(grid, in_specs, out_specs, scratch_shapes=()):
    return pltpu.PrefetchScalarGridSpec(
        num_scalar_prefetch=1,
        grid=grid,
        in_specs=in_specs,
        out_specs=out_specs,
        scratch_shapes=scratch_shapes,
    )


def cost(flops, moved, transcendentals=0):
    return pl.CostEstimate(
        flops=int(flops), bytes_accessed=int(moved), transcendentals=int(transcendentals)
    )


def query_kernel(_, cand_ref, w_ref, owner_ref, *outs):
    rows = cand_ref.shape[0]
    made = silu(jnp.dot(cand_ref[...], w_ref[...], preferred_element_type=F32)).astype(BF16)
    for k, out in enumerate(outs):

        @pl.when(pl.program_id(0) == k)
        def _(out=out):
            out[:rows, :] = made
            out[rows:, :] = owner_ref[...]


def project_queries(me, candidates, w_qu, owner_rows, parts):
    rows, width = candidates.shape
    cols = width // parts
    extra = owner_rows.shape[0]
    return pl.pallas_call(
        query_kernel,
        grid_spec=scalar_grid(
            (parts,),
            [
                pl.BlockSpec((rows, width), lambda k, m: (0, 0)),
                pl.BlockSpec((width, cols), lambda k, m: (0, k ^ m[0])),
                pl.BlockSpec((extra, cols), lambda k, m: (0, 0)),
            ],
            [pl.BlockSpec((rows + extra, cols), lambda k, m: (0, 0))] * parts,
        ),
        out_shape=[jax.ShapeDtypeStruct((rows + extra, cols), BF16)] * parts,
        cost_estimate=cost(2 * rows * width * width, 2 * width * width + 4 * rows * width),
        name="queries",
    )(me, candidates, w_qu, owner_rows)


def gate_kernel(_, cand_ref, w_ref, out_ref):
    out_ref[0] = silu(jnp.dot(cand_ref[...], w_ref[...], preferred_element_type=F32))


def project_gate(me, candidates, w_qu, parts):
    rows, width = candidates.shape
    cols = width // parts
    return pl.pallas_call(
        gate_kernel,
        grid_spec=scalar_grid(
            (parts,),
            [
                pl.BlockSpec((rows, width), lambda k, m: (0, 0)),
                pl.BlockSpec((width, cols), lambda k, m: (0, parts + (k ^ m[0]))),
            ],
            pl.BlockSpec((1, rows, cols), lambda k, m: (k, 0, 0)),
        ),
        out_shape=jax.ShapeDtypeStruct((parts, rows, cols), F32),
        cost_estimate=cost(2 * rows * width * width, 2 * width * width + 6 * rows * width),
        name="gate",
    )(me, candidates, w_qu)


def keys_values_kernel(_, hist_ref, wk_ref, wv_ref, *outs):
    rows = hist_ref.shape[0]
    step = min(rows, 256)
    for k, out in enumerate(outs):

        @pl.when(pl.program_id(0) == k)
        def _(out=out):
            for at in range(0, rows, step):
                part = hist_ref[at : at + step, :]
                keys = silu(jnp.dot(part, wk_ref[...], preferred_element_type=F32))
                out[at : at + step, :HEAD] = keys.astype(BF16)
                values = jnp.dot(part, wv_ref[...], preferred_element_type=F32)
                out[at : at + step, HEAD:] = values.astype(BF16)


def project_keys_values(me, history, w_kv, each, which, ks):
    rows, width = history.shape
    first, count = ks[0], len(ks)
    heads = width // HEAD
    return pl.pallas_call(
        keys_values_kernel,
        grid_spec=scalar_grid(
            (count,),
            [
                pl.BlockSpec((rows, width), lambda k, m: (0, 0)),
                pl.BlockSpec(
                    (width, HEAD), lambda k, m: (0, ((k + first) ^ m[0]) * each + which)
                ),
                pl.BlockSpec(
                    (width, HEAD), lambda k, m: (0, heads + ((k + first) ^ m[0]) * each + which)
                ),
            ],
            [pl.BlockSpec((rows, 2 * HEAD), lambda k, m: (0, 0))] * count,
        ),
        out_shape=[jax.ShapeDtypeStruct((rows, 2 * HEAD), BF16)] * count,
        cost_estimate=cost(
            4 * rows * width * HEAD * count,
            2 * rows * width + 4 * width * HEAD * count + 4 * rows * HEAD * count,
        ),
    )(me, history, w_kv, w_kv)


def attend_kernel(source, sink, events, room, pos_ref, count_ref, code_ref, *refs):
    codes = len(source)
    n_q = 1 + max(a for a, _ in source)
    n_out = 1 + max(a for a, _ in sink)
    n_kv = len(refs) - n_q - n_out - 3
    kvs, queries = refs[:n_kv], refs[n_kv : n_kv + n_q]
    outs = refs[n_kv + n_q : n_kv + n_q + n_out]
    packed, asked, total = refs[n_kv + n_q + n_out :]
    blocks = kvs[0].shape[0] // events
    cands = asked.shape[0] // codes
    half = 0.5 * HEAD ** (-0.5)
    packed[...] = jnp.zeros_like(packed)
    for s, kv in enumerate(kvs):

        def place(b, carry, s=s, kv=kv):
            at = pl.multiple_of(pos_ref[s * blocks + b] * events, events)
            packed[pl.ds(at, events), :] = kv[pl.ds(pl.multiple_of(b * events, events), events), :]
            return carry

        lax.fori_loop(0, blocks, place, 0, unroll=8)
    for j, (array, at) in enumerate(source):
        asked[j * cands : (j + 1) * cands, :] = queries[array][at : at + cands, :]

    def one_code(j, carry):
        code = code_ref[j]
        base = pl.multiple_of(code * room, TILE)
        rows = pl.ds(pl.multiple_of(j * cands, cands), cands)
        tiles = lax.div(count_ref[code] * events + (TILE - 1), TILE)
        for number in range(room // TILE + 1):

            @pl.when(tiles == number)
            def _(number=number):
                if number == 0:
                    total[rows, :] = jnp.zeros((cands, HEAD), BF16)
                    return
                sums = None
                for t in range(number):
                    at = pl.ds(base + t * TILE, TILE)
                    scores = lax.dot_general(
                        asked[rows, :],
                        packed[at, :HEAD],
                        (((1,), (1,)), ((), ())),
                        preferred_element_type=F32,
                    )
                    h = scores * half
                    weights = (h + h * jnp.tanh(h)).astype(BF16)
                    part = jnp.dot(weights, packed[at, HEAD:], preferred_element_type=F32)
                    sums = part if sums is None else sums + part
                total[rows, :] = sums.astype(BF16)

        return carry

    lax.fori_loop(0, codes, one_code, 0)
    for j, (array, at) in enumerate(sink):
        outs[array][at : at + cands, :] = total[j * cands : (j + 1) * cands, :]


def attend(pos, counts, kvs, arrays, where, groups, cands, events, room):
    codes = [c for group in groups for c in group]
    sink = [(g, j * cands) for g, group in enumerate(groups) for j in range(len(group))]
    used = sorted({where[c][0] for c in codes})
    source = [(used.index(where[c][0]), where[c][1]) for c in codes]
    queries = [arrays[a] for a in used]
    rows = sum(kv.shape[0] for kv in kvs)
    n_req = counts.shape[0]
    share = len(codes) / n_req
    vmem = pl.BlockSpec(memory_space=pltpu.VMEM)
    smem = pl.BlockSpec(memory_space=pltpu.SMEM)
    return pl.pallas_call(
        functools.partial(attend_kernel, source, sink, events, room),
        in_specs=[smem] * 3 + [vmem] * (len(kvs) + len(queries)),
        out_specs=[vmem] * len(groups),
        out_shape=[jax.ShapeDtypeStruct((len(g) * cands, HEAD), BF16) for g in groups],
        scratch_shapes=[
            pltpu.VMEM((n_req * room, 2 * HEAD), BF16),
            pltpu.VMEM((len(codes) * cands, HEAD), BF16),
            pltpu.VMEM((len(codes) * cands, HEAD), BF16),
        ],
        cost_estimate=cost(
            8 * rows * cands * HEAD * share,
            4 * rows * HEAD + 4 * len(codes) * cands * HEAD,
            rows * cands * share,
        ),
    )(pos, counts, jnp.array(codes, dtype=jnp.int32), *kvs, *queries)


def finish_kernel(count, _, cand_ref, gate_ref, w_ref, *refs):
    parts, out_ref, stat, total = refs[:count], refs[count], refs[count + 1], refs[count + 2]
    k = pl.program_id(0)
    width = cand_ref.shape[1]

    @pl.when(k == 0)
    def _():
        mean = sum(jnp.sum(p[...].astype(F32), axis=1, keepdims=True) for p in parts) / width
        square = sum(
            jnp.sum(jnp.square(p[...].astype(F32) - mean), axis=1, keepdims=True) for p in parts
        )
        scale = lax.rsqrt(square / width + 1e-05)
        for j, p in enumerate(parts):
            stat[j] = (p[...].astype(F32) - mean) * scale
        total[...] = cand_ref[...].astype(F32)

    mixed = (stat[k] * gate_ref[0]).astype(BF16)
    total[...] += jnp.dot(mixed, w_ref[...], preferred_element_type=F32)

    @pl.when(k == count - 1)
    def _():
        out_ref[...] = total[...].astype(BF16)


def finish(me, candidates, gate, w_out, parts):
    rows, width = candidates.shape
    count = len(parts)
    cols = width // count
    return pl.pallas_call(
        functools.partial(finish_kernel, count),
        grid_spec=scalar_grid(
            (count,),
            [
                pl.BlockSpec((rows, width), lambda k, m: (0, 0)),
                pl.BlockSpec((1, rows, cols), lambda k, m: (k, 0, 0)),
                pl.BlockSpec((cols, width), lambda k, m: (k ^ m[0], 0)),
            ]
            + [pl.BlockSpec((rows, cols), lambda k, m: (0, 0))] * count,
            pl.BlockSpec((rows, width), lambda k, m: (0, 0)),
            [pltpu.VMEM((count, rows, cols), F32), pltpu.VMEM((rows, width), F32)],
        ),
        out_shape=jax.ShapeDtypeStruct((rows, width), BF16),
        cost_estimate=cost(2 * rows * width * width, 2 * width * width + 10 * rows * width),
        name="finish",
    )(me, candidates, gate, w_out, *parts)


def stages(count, inner_first):
    outer = []
    bit = count // 2
    while bit >= 2:
        outer.append(2 * bit - 2)
        bit //= 2
    inner = [1] if count > 1 else []
    held, plan = [0], []

    def step(mask, codes):
        plan.append((mask, tuple(codes)))
        held.extend(c ^ mask for c in codes)

    if inner_first:
        for mask in inner + outer:
            step(mask, list(held))
        return plan
    for mask in outer[:-1]:
        step(mask, list(held))
    early = list(held)
    if outer:
        if inner:
            plan.append((1, tuple(early)))
        step(outer[-1], early)
    late = [c for c in held if c not in early] or early
    if inner:
        plan.append((1, tuple(late)))
    return plan


def joined(pieces):
    return pieces[0] if len(pieces) == 1 else jnp.concatenate(pieces, axis=0)


def gather_queries(own, count, inner_first):
    cands = own.shape[0]
    arrays, where = [own], {0: (0, 0)}
    for mask, codes in stages(count, inner_first):
        pieces = [arrays[where[c][0]][where[c][1] : where[c][1] + cands] for c in codes]
        arrays.append(swap(joined(pieces), "req", mask))
        for j, c in enumerate(codes):
            where[c ^ mask] = (len(arrays) - 1, j * cands)
    return arrays, where


def scatter_sums(groups, arrays, count, cands):
    whole = {tuple(g): a for g, a in zip(groups, arrays)}
    held = {}
    for group, array in zip(groups, arrays):
        for j, c in enumerate(group):
            held[c] = array[j * cands : (j + 1) * cands]
    plan = stages(count, False)
    for number in reversed(range(len(plan))):
        mask, codes = plan[number]
        away = tuple(c ^ mask for c in codes)
        sent = whole[away] if away in whole else joined([held[c] for c in away])
        got = swap(sent, "req", mask)
        whole = {g: a for g, a in whole.items() if not set(g) & set(codes)}
        for j, c in enumerate(codes):
            part = held[c].astype(F32) + got[j * cands : (j + 1) * cands].astype(F32)
            held[c] = part.astype(BF16)
    return held[0]


def on_device(history, block_owner, candidates, w_kv, w_qu, w_out):
    n_req, n_ctx = lax.axis_size("req"), lax.axis_size("ctx")
    rows, width = history.shape
    blocks = block_owner.shape[0]
    events = rows // blocks
    mine = candidates.shape[0]
    cands = mine * n_ctx
    each = width // HEAD // n_ctx
    cols = each * HEAD
    room = -(-n_ctx * (2 * blocks // n_req) * events // TILE) * TILE
    me_ctx = lax.axis_index("ctx").astype(jnp.int32).reshape(1)
    me_req = lax.axis_index("req").astype(jnp.int32)

    owner_rows = jnp.pad(
        block_owner.reshape(1, blocks).astype(BF16), ((0, 15), (0, cols - blocks))
    )
    made = project_queries(me_ctx, candidates, w_qu, owner_rows, n_ctx)
    arrived = [made[0]] + [swap(made[k], "ctx", k) for k in range(1, n_ctx)]

    far = range(n_ctx // 2, n_ctx)
    near = range(0, n_ctx // 2)
    kvs = []
    for h in range(each):
        sent = project_keys_values(me_ctx, history, w_kv, each, h, list(far))
        got_far = [swap(s, "ctx", k) for s, k in zip(sent, far)]
        kept = project_keys_values(me_ctx, history, w_kv, each, h, list(near))
        got_near = [kept[0]] + [swap(kept[k], "ctx", k) for k in near if k > 0]
        kvs.append(got_near + got_far)

    owners = jnp.concatenate([a[mine, :blocks] for a in arrived]).astype(jnp.int32)
    code = owners ^ me_req
    total_blocks = n_ctx * blocks
    order = jnp.arange(total_blocks, dtype=jnp.int32)
    same = code[:, None] == code[None, :]
    rank = jnp.sum((same & (order[None, :] < order[:, None])).astype(jnp.int32), axis=1)
    pos = code * (room // events) + rank
    counts = jnp.sum(
        (code[None, :] == jnp.arange(n_req, dtype=jnp.int32)[:, None]).astype(jnp.int32), axis=1
    )

    gate = project_gate(me_ctx, candidates, w_qu, n_ctx)

    plan = stages(n_req, False)
    groups = [[c ^ mask for c in codes] for mask, codes in plan] + [[0]]
    summed = []
    for h in range(each):
        own = jnp.concatenate([a[:mine, h * HEAD : (h + 1) * HEAD] for a in arrived], axis=0)
        arrays, where = gather_queries(own, n_req, h % 2 == 1)
        last = len(plan) - 1
        if h == 0:
            calls = [[i for i in range(len(groups)) if i != last], [last]]
        else:
            calls = [[i for i in range(len(plan)) if plan[i][0] == 1]]
            calls.append([i for i in range(len(groups)) if i not in calls[0]])
        sums = {}
        for call in calls:
            if call:
                made = attend(
                    pos, counts, kvs[h], arrays, where, [groups[i] for i in call],
                    cands, events, room,
                )
                sums.update(zip(call, made))
        summed.append(scatter_sums(groups, [sums[i] for i in range(len(groups))], n_req, cands))

    full = jnp.concatenate(summed, axis=1)
    parts = [full[:mine]] + [
        swap(full[k * mine : (k + 1) * mine], "ctx", k) for k in range(1, n_ctx)
    ]
    return finish(me_ctx, candidates, gate, w_out, parts)


def solution(mesh):
    placed = (
        P(("req", "ctx"), None),
        P(("req", "ctx"), None),
        P(("req", "ctx"), None),
        P(),
        P(),
        P(),
    )
    return jax.shard_map(
        on_device, mesh=mesh, in_specs=placed, out_specs=P(("req", "ctx"), None), check_vma=False
    )
```

profile of v0, /device:TPU:0, one launch (start us, length us, event | category | flops | bytes accessed | tf_op | source)
XLA Modules:
  0.0 120.6 jit_solution(5946624277744810995)
XLA Ops:
  1.3 3.7 %queries.1 = (bf16[144,256]{1,0:T(8,128)(2,1)}, bf16[144,256]{1,0:T(8,128)(2,1)}, bf16[144,256]{1,0:T(8,128)(2,1)}, bf16[144,256]{1,0:T(8,128)(2,1)}) custom-call(s32[1]{0:T(128)} %bitcast._, bf16[128,1024]{1,0:T(8,128)(2,1)} %cand_ref.5, bf16[1024,2048]{1,0:T(8,128)(2,1)} %w_ref.4, bf16[16,256]{1,0:T(8,128)(2,1)} %pad.4.owner_ref), custom_call_target="tpu_custom_call" | custom-call | flops 268435456 | bytes 2621440 | tf_op jit(solution)/shard_map/queries/pallas_call | solution.py:58
  5.5 2.5 %collective-permute-start.1 = (bf16[144,256]{1,0:T(8,128)(2,1)}, bf16[144,256]{1,0:T(8,128)(2,1)S(1)}, u32[]{:S(2)}, u32[]{:S(2)}) collective-permute-start(bf16[144,256]{1,0:T(8,128)(2,1)} %get-tuple-element.28), channel_id=1, source_target_pairs={{0,2},{1,3},{2,0},{3,1},{4,6},{5,7},{6,4},{7,5},{8,10},{9,11},{10,... | collective-permute-start | bytes 221192 | tf_op jit(solution)/shard_map/ppermute | solution.py:24
  8.1 4.5 %shard_map.100 = (bf16[768,256]{1,0:T(8,128)(2,1)}, bf16[768,256]{1,0:T(8,128)(2,1)}) custom-call(s32[1]{0:T(128)} %bitcast._, bf16[768,1024]{1,0:T(8,128)(2,1)} %hist_ref.7, bf16[1024,2048]{1,0:T(8,128)(2,1)} %wv_ref.7, bf16[1024,2048]{1,0:T(8,128)(2,1)} %wv_ref.7), custom_call_target="tpu_custom_call" | custom-call | flops 805306368 | bytes 3407872 | tf_op jit(solution)/shard_map/pallas_call | solution.py:117
  12.7 4.5 %shard_map.101 = (bf16[768,256]{1,0:T(8,128)(2,1)}, bf16[768,256]{1,0:T(8,128)(2,1)}) custom-call(s32[1]{0:T(128)} %bitcast._, bf16[768,1024]{1,0:T(8,128)(2,1)} %hist_ref.7, bf16[1024,2048]{1,0:T(8,128)(2,1)} %wv_ref.7, bf16[1024,2048]{1,0:T(8,128)(2,1)} %wv_ref.7), custom_call_target="tpu_custom_call" | custom-call | flops 805306368 | bytes 3407872 | tf_op jit(solution)/shard_map/pallas_call | solution.py:117
  17.2 1.9 %collective-permute-start.4 = (bf16[768,256]{1,0:T(8,128)(2,1)}, bf16[768,256]{1,0:T(8,128)(2,1)S(1)}, u32[]{:S(2)}, u32[]{:S(2)}) collective-permute-start(bf16[768,256]{1,0:T(8,128)(2,1)} %get-tuple-element.32), channel_id=1, source_target_pairs={{0,2},{1,3},{2,0},{3,1},{4,6},{5,7},{6,4},{7,5},{8,10},{9,11},{10,... | collective-permute-start | bytes 1179656 | tf_op jit(solution)/shard_map/ppermute | solution.py:24
  19.1 4.5 %shard_map.104 = (bf16[768,256]{1,0:T(8,128)(2,1)}, bf16[768,256]{1,0:T(8,128)(2,1)}) custom-call(s32[1]{0:T(128)} %bitcast._, bf16[768,1024]{1,0:T(8,128)(2,1)} %hist_ref.7, bf16[1024,2048]{1,0:T(8,128)(2,1)} %wv_ref.7, bf16[1024,2048]{1,0:T(8,128)(2,1)} %wv_ref.7), custom_call_target="tpu_custom_call" | custom-call | flops 805306368 | bytes 3407872 | tf_op jit(solution)/shard_map/pallas_call | solution.py:117
  23.7 4.5 %shard_map.105 = (bf16[768,256]{1,0:T(8,128)(2,1)}, bf16[768,256]{1,0:T(8,128)(2,1)}) custom-call(s32[1]{0:T(128)} %bitcast._, bf16[768,1024]{1,0:T(8,128)(2,1)} %hist_ref.7, bf16[1024,2048]{1,0:T(8,128)(2,1)} %wv_ref.7, bf16[1024,2048]{1,0:T(8,128)(2,1)} %wv_ref.7), custom_call_target="tpu_custom_call" | custom-call | flops 805306368 | bytes 3407872 | tf_op jit(solution)/shard_map/pallas_call | solution.py:117
  28.3 3.7 %collective-permute-start.6 = (bf16[512,128]{1,0:T(8,128)(2,1)S(1)}, bf16[512,128]{1,0:T(8,128)(2,1)S(1)}, u32[]{:S(2)}, u32[]{:S(2)}) collective-permute-start(bf16[512,128]{1,0:T(8,128)(2,1)S(1)} %pad_maximum_fusion.2.refs_4_), channel_id=1, source_target_pairs={{0,24},{4,28},{8,16},{12,20},{16,8},{20,12},{24,0},{28,4},{1,25},{... | collective-permute-start | bytes 393224 | tf_op jit(solution)/shard_map/ppermute | solution.py:24
  32.0 1.6 %collective-permute-start.17 = (bf16[512,128]{1,0:T(8,128)(2,1)S(1)}, bf16[512,128]{1,0:T(8,128)(2,1)S(1)}, u32[]{:S(2)}, u32[]{:S(2)}) collective-permute-start(bf16[512,128]{1,0:T(8,128)(2,1)S(1)} %pad_maximum_fusion.3.refs_4_), channel_id=1, source_target_pairs={{0,4},{4,0},{8,12},{12,8},{16,20},{20,16},{24,28},{28,24},{1,5},{5... | collective-permute-start | bytes 393224 | tf_op jit(solution)/shard_map/ppermute | solution.py:24
  33.6 2.8 %collective-permute-done.6.refs_5_ = bf16[512,128]{1,0:T(8,128)(2,1)S(1)} collective-permute-done((bf16[512,128]{1,0:T(8,128)(2,1)S(1)}, bf16[512,128]{1,0:T(8,128)(2,1)S(1)}, u32[]{:S(2)}, u32[]{:S(2)}) %collective-permute-start.6) | collective-permute-done | bytes 131104 | tf_op jit(solution)/shard_map/ppermute | solution.py:24
  36.4 2.5 %collective-permute-start.8 = (bf16[1024,128]{1,0:T(8,128)(2,1)S(1)}, bf16[1024,128]{1,0:T(8,128)(2,1)S(1)}, u32[]{:S(2)}, u32[]{:S(2)}) collective-permute-start(bf16[1024,128]{1,0:T(8,128)(2,1)S(1)} %constant_dynamic-update-slice_fusion), channel_id=1, source_target_pairs={{0,8},{4,12},{8,0},{12,4},{16,24},{20,28},{24,16},{28,20},{1,9},{5... | collective-permute-start | bytes 786440 | tf_op jit(solution)/shard_map/ppermute | solution.py:24
  38.9 2.5 %collective-permute-start.18 = (bf16[1024,128]{1,0:T(8,128)(2,1)S(1)}, bf16[1024,128]{1,0:T(8,128)(2,1)S(1)}, u32[]{:S(2)}, u32[]{:S(2)}) collective-permute-start(bf16[1024,128]{1,0:T(8,128)(2,1)S(1)} %get-tuple-element.56), channel_id=1, source_target_pairs={{0,24},{4,28},{8,16},{12,20},{16,8},{20,12},{24,0},{28,4},{1,25},{... | collective-permute-start | bytes 786440 | tf_op jit(solution)/shard_map/ppermute | solution.py:24
  41.5 4.1 %collective-permute-done.8.refs_7_ = bf16[1024,128]{1,0:T(8,128)(2,1)S(1)} collective-permute-done((bf16[1024,128]{1,0:T(8,128)(2,1)S(1)}, bf16[1024,128]{1,0:T(8,128)(2,1)S(1)}, u32[]{:S(2)}, u32[]{:S(2)}) %collective-permute-start.8) | collective-permute-done | bytes 262176 | tf_op jit(solution)/shard_map/ppermute | solution.py:24
  45.6 1.5 %collective-permute-start.9 = (bf16[1024,128]{1,0:T(8,128)(2,1)S(1)}, bf16[1024,128]{1,0:T(8,128)(2,1)S(1)}, u32[]{:S(2)}, u32[]{:S(2)}) collective-permute-start(bf16[1024,128]{1,0:T(8,128)(2,1)S(1)} %collective-permute-done.8.refs_7_), channel_id=1, source_target_pairs={{0,4},{4,0},{8,12},{12,8},{16,20},{20,16},{24,28},{28,24},{1,5},{5... | collective-permute-start | bytes 786440 | tf_op jit(solution)/shard_map/ppermute | solution.py:24
  47.2 5.7 %collective-permute-done.18.refs_5_ = bf16[1024,128]{1,0:T(8,128)(2,1)S(1)} collective-permute-done((bf16[1024,128]{1,0:T(8,128)(2,1)S(1)}, bf16[1024,128]{1,0:T(8,128)(2,1)S(1)}, u32[]{:S(2)}, u32[]{:S(2)}) %collective-permute-start.18) | collective-permute-done | bytes 262176 | tf_op jit(solution)/shard_map/ppermute | solution.py:24
  53.4 1.5 %collective-permute-start.15 = (bf16[768,256]{1,0:T(8,128)(2,1)}, bf16[768,256]{1,0:T(8,128)(2,1)}, u32[]{:S(2)}, u32[]{:S(2)}) collective-permute-start(bf16[768,256]{1,0:T(8,128)(2,1)} %get-tuple-element.40), channel_id=1, source_target_pairs={{0,2},{1,3},{2,0},{3,1},{4,6},{5,7},{6,4},{7,5},{8,10},{9,11},{10,... | collective-permute-start | bytes 1179656 | tf_op jit(solution)/shard_map/ppermute | solution.py:24
  55.2 1.5 %collective-permute-start.7 = (bf16[1024,128]{1,0:T(8,128)(2,1)S(1)}, bf16[1024,128]{1,0:T(8,128)(2,1)S(1)}, u32[]{:S(2)}, u32[]{:S(2)}) collective-permute-start(bf16[1024,128]{1,0:T(8,128)(2,1)S(1)} %constant_dynamic-update-slice_fusion), channel_id=1, source_target_pairs={{0,4},{4,0},{8,12},{12,8},{16,20},{20,16},{24,28},{28,24},{1,5},{5... | collective-permute-start | bytes 786440 | tf_op jit(solution)/shard_map/ppermute | solution.py:24
  58.0 4.1 %shard_map.103 = bf16[1024,128]{1,0:T(8,128)(2,1)} custom-call(s32[192]{0:T(256)} %multiply_add_fusion.pos_ref, s32[8]{0:T(128)} %convert_reduce_fusion.1.count_ref, s32[2]{0:T(128)} %constant.24.clone.code_ref, bf16[768,256]{1,0:T(8,128)(2,1)} %get-tuple-element.30.refs_0_, bf16[768,256]{1,0:T(8,128)(2,1)} %copy-done, bf16[768,256]{1,0:T(8,128)(2,1)} %copy-done.1, ...), custom_call_target="tpu_custom_call" | custom-call | flops 402653184 | bytes 2097152 | tf_op jit(solution)/shard_map/pallas_call | solution.py:208
  62.1 1.7 %collective-permute-done.7.refs_6_ = bf16[1024,128]{1,0:T(8,128)(2,1)S(1)} collective-permute-done((bf16[1024,128]{1,0:T(8,128)(2,1)S(1)}, bf16[1024,128]{1,0:T(8,128)(2,1)S(1)}, u32[]{:S(2)}, u32[]{:S(2)}) %collective-permute-start.7) | collective-permute-done | bytes 262176 | tf_op jit(solution)/shard_map/ppermute | solution.py:24
  63.8 1.5 %collective-permute-start.10 = (bf16[1024,128]{1,0:T(8,128)(2,1)}, bf16[1024,128]{1,0:T(8,128)(2,1)S(1)}, u32[]{:S(2)}, u32[]{:S(2)}) collective-permute-start(bf16[1024,128]{1,0:T(8,128)(2,1)} %shard_map.103), channel_id=1, source_target_pairs={{0,4},{4,0},{8,12},{12,8},{16,20},{20,16},{24,28},{28,24},{1,5},{5... | collective-permute-start | bytes 786440 | tf_op jit(solution)/shard_map/ppermute | solution.py:24
  65.3 7.5 %shard_map.102 = (bf16[512,128]{1,0:T(8,128)(2,1)}, bf16[1024,128]{1,0:T(8,128)(2,1)}, bf16[1024,128]{1,0:T(8,128)(2,1)}, bf16[512,128]{1,0:T(8,128)(2,1)}) custom-call(s32[192]{0:T(256)} %multiply_add_fusion.pos_ref, s32[8]{0:T(128)} %convert_reduce_fusion.1.count_ref, s32[6]{0:T(128)} %constant.23.clone.code_ref, ...), custom_call_target="tpu_custom_call" | custom-call | flops 1207959552 | bytes 3145728 | tf_op jit(solution)/shard_map/pallas_call | solution.py:208
  73.6 5.7 %shard_map.107 = (bf16[1024,128]{1,0:T(8,128)(2,1)}, bf16[1024,128]{1,0:T(8,128)(2,1)}) custom-call(s32[192]{0:T(256)} %multiply_add_fusion.pos_ref, s32[8]{0:T(128)} %convert_reduce_fusion.1.count_ref, s32[4]{0:T(128)} %constant.25.clone.code_ref, bf16[768,256]{1,0:T(8,128)(2,1)} %get-tuple-element.38.refs_0_, ...), custom_call_target="tpu_custom_call" | custom-call | flops 805306368 | bytes 2621440 | tf_op jit(solution)/shard_map/pallas_call | solution.py:208
  81.4 6.0 %shard_map.106 = (bf16[512,128]{1,0:T(8,128)(2,1)}, bf16[1024,128]{1,0:T(8,128)(2,1)}, bf16[512,128]{1,0:T(8,128)(2,1)}) custom-call(s32[192]{0:T(256)} %multiply_add_fusion.pos_ref, s32[8]{0:T(128)} %convert_reduce_fusion.1.count_ref, s32[4]{0:T(128)} %constant.26.clone.code_ref, bf16[768,256]{1,0:T(8,128)(2,1)} %get-tuple-element.38.refs_0_, ...), custom_call_target="tpu_custom_call" | custom-call | flops 805306368 | bytes 2621440 | tf_op jit(solution)/shard_map/pallas_call | solution.py:208
  87.4 1.5 %collective-permute-start.11 = (bf16[1024,128]{1,0:T(8,128)(2,1)S(1)}, bf16[1024,128]{1,0:T(8,128)(2,1)S(1)}, u32[]{:S(2)}, u32[]{:S(2)}) collective-permute-start(bf16[1024,128]{1,0:T(8,128)(2,1)S(1)} %pad_maximum_fusion), channel_id=1, source_target_pairs={{0,8},{4,12},{8,0},{12,4},{16,24},{20,28},{24,16},{28,20},{1,9},{5... | collective-permute-start | bytes 786440 | tf_op jit(solution)/shard_map/ppermute | solution.py:24
  90.0 1.5 %collective-permute-start.21 = (bf16[1024,128]{1,0:T(8,128)(2,1)S(1)}, bf16[1024,128]{1,0:T(8,128)(2,1)S(1)}, u32[]{:S(2)}, u32[]{:S(2)}) collective-permute-start(bf16[1024,128]{1,0:T(8,128)(2,1)S(1)} %pad_maximum_fusion.1), channel_id=1, source_target_pairs={{0,8},{4,12},{8,0},{12,4},{16,24},{20,28},{24,16},{28,20},{1,9},{5... | collective-permute-start | bytes 786440 | tf_op jit(solution)/shard_map/ppermute | solution.py:24
  91.6 5.1 %collective-permute-done.11 = bf16[1024,128]{1,0:T(8,128)(2,1)S(1)} collective-permute-done((bf16[1024,128]{1,0:T(8,128)(2,1)S(1)}, bf16[1024,128]{1,0:T(8,128)(2,1)S(1)}, u32[]{:S(2)}, u32[]{:S(2)}) %collective-permute-start.11) | collective-permute-done | bytes 262176 | tf_op jit(solution)/shard_map/ppermute | solution.py:24
  96.7 2.5 %collective-permute-start.13 = (bf16[512,128]{1,0:T(8,128)(2,1)S(1)}, bf16[512,128]{1,0:T(8,128)(2,1)S(1)}, u32[]{:S(2)}, u32[]{:S(2)}) collective-permute-start(bf16[512,128]{1,0:T(8,128)(2,1)S(1)} %add_convert_fusion.8), channel_id=1, source_target_pairs={{0,24},{4,28},{8,16},{12,20},{16,8},{20,12},{24,0},{28,4},{1,25},{... | collective-permute-start | bytes 393224 | tf_op jit(solution)/shard_map/ppermute | solution.py:24
  99.3 2.0 %collective-permute-done.21 = bf16[1024,128]{1,0:T(8,128)(2,1)S(1)} collective-permute-done((bf16[1024,128]{1,0:T(8,128)(2,1)S(1)}, bf16[1024,128]{1,0:T(8,128)(2,1)S(1)}, u32[]{:S(2)}, u32[]{:S(2)}) %collective-permute-start.21) | collective-permute-done | bytes 262176 | tf_op jit(solution)/shard_map/ppermute | solution.py:24
  102.2 2.0 %collective-permute-start.23 = (bf16[512,128]{1,0:T(8,128)(2,1)S(1)}, bf16[512,128]{1,0:T(8,128)(2,1)S(1)}, u32[]{:S(2)}, u32[]{:S(2)}) collective-permute-start(bf16[512,128]{1,0:T(8,128)(2,1)S(1)} %add_convert_fusion.1), channel_id=1, source_target_pairs={{0,24},{4,28},{8,16},{12,20},{16,8},{20,12},{24,0},{28,4},{1,25},{... | collective-permute-start | bytes 393224 | tf_op jit(solution)/shard_map/ppermute | solution.py:24
  104.8 4.4 %collective-permute-done.23 = bf16[512,128]{1,0:T(8,128)(2,1)S(1)} collective-permute-done((bf16[512,128]{1,0:T(8,128)(2,1)S(1)}, bf16[512,128]{1,0:T(8,128)(2,1)S(1)}, u32[]{:S(2)}, u32[]{:S(2)}) %collective-permute-start.23) | collective-permute-done | bytes 131104 | tf_op jit(solution)/shard_map/ppermute | solution.py:24
  111.8 4.0 %gate.1.gate_ref = f32[4,128,256]{2,1,0:T(8,128)} custom-call(s32[1]{0:T(128)} %bitcast._, bf16[128,1024]{1,0:T(8,128)(2,1)} %cand_ref.5, bf16[1024,2048]{1,0:T(8,128)(2,1)} %w_ref.4), custom_call_target="tpu_custom_call" | custom-call | flops 268435456 | bytes 2883584 | tf_op jit(solution)/shard_map/gate/pallas_call | solution.py:82
  116.4 4.2 %finish.1 = bf16[128,1024]{1,0:T(8,128)(2,1)} custom-call(s32[1]{0:T(128)} %bitcast._, bf16[128,1024]{1,0:T(8,128)(2,1)} %cand_ref.5, f32[4,128,256]{2,1,0:T(8,128)} %gate.1.gate_ref, bf16[1024,1024]{1,0:T(8,128)(2,1)} %w_ref.5, bf16[128,256]{1,0:T(8,128)(2,1)} %get-tuple-element.52.refs_0_, bf16[128,256]{1,0:T(8,128)(2,1)} %copy-done.13, ...), custom_call_target="tpu_custom_call" | custom-call | flops 268435456 | bytes 3407872 | tf_op jit(solution)/shard_map/finish/pallas_call | solution.py:254
  (99 shorter events, 13.0 us)
Async XLA Ops:
  5.0 23.1 %collective-permute-start = (bf16[144,256]{1,0:T(8,128)(2,1)}, bf16[144,256]{1,0:T(8,128)(2,1)S(1)}, u32[]{:S(2)}, u32[]{:S(2)}) collective-permute-start(bf16[144,256]{1,0:T(8,128)(2,1)} %get-tuple-element.27), channel_id=1, source_target_pairs={{0,1},{1,0},{2,3},{3,2},{4,5},{5,4},{6,7},{7,6},{8,9},{9,8},{10,11... | collective-permute-start | bytes 221192 | tf_op jit(solution)/shard_map/ppermute | solution.py:24
  5.5 22.7 %collective-permute-start.1 = (bf16[144,256]{1,0:T(8,128)(2,1)}, bf16[144,256]{1,0:T(8,128)(2,1)S(1)}, u32[]{:S(2)}, u32[]{:S(2)}) collective-permute-start(bf16[144,256]{1,0:T(8,128)(2,1)} %get-tuple-element.28), channel_id=1, source_target_pairs={{0,2},{1,3},{2,0},{3,1},{4,6},{5,7},{6,4},{7,5},{8,10},{9,11},{10,... | collective-permute-start | bytes 221192 | tf_op jit(solution)/shard_map/ppermute | solution.py:24
  8.0 20.2 %collective-permute-start.2 = (bf16[144,256]{1,0:T(8,128)(2,1)}, bf16[144,256]{1,0:T(8,128)(2,1)S(1)}, u32[]{:S(2)}, u32[]{:S(2)}) collective-permute-start(bf16[144,256]{1,0:T(8,128)(2,1)} %get-tuple-element.29), channel_id=1, source_target_pairs={{0,3},{1,2},{2,1},{3,0},{4,7},{5,6},{6,5},{7,4},{8,11},{9,10},{10,... | collective-permute-start | bytes 221192 | tf_op jit(solution)/shard_map/ppermute | solution.py:24
  12.6 40.7 %collective-permute-start.3 = (bf16[768,256]{1,0:T(8,128)(2,1)}, bf16[768,256]{1,0:T(8,128)(2,1)S(1)}, u32[]{:S(2)}, u32[]{:S(2)}) collective-permute-start(bf16[768,256]{1,0:T(8,128)(2,1)} %get-tuple-element.31), channel_id=1, source_target_pairs={{0,1},{1,0},{2,3},{3,2},{4,5},{5,4},{6,7},{7,6},{8,9},{9,8},{10,11... | collective-permute-start | bytes 1179656 | tf_op jit(solution)/shard_map/ppermute | solution.py:24
  17.2 36.2 %collective-permute-start.4 = (bf16[768,256]{1,0:T(8,128)(2,1)}, bf16[768,256]{1,0:T(8,128)(2,1)S(1)}, u32[]{:S(2)}, u32[]{:S(2)}) collective-permute-start(bf16[768,256]{1,0:T(8,128)(2,1)} %get-tuple-element.32), channel_id=1, source_target_pairs={{0,2},{1,3},{2,0},{3,1},{4,6},{5,7},{6,4},{7,5},{8,10},{9,11},{10,... | collective-permute-start | bytes 1179656 | tf_op jit(solution)/shard_map/ppermute | solution.py:24
  28.1 26.8 %collective-permute-start.5 = (bf16[768,256]{1,0:T(8,128)(2,1)}, bf16[768,256]{1,0:T(8,128)(2,1)S(1)}, u32[]{:S(2)}, u32[]{:S(2)}) collective-permute-start(bf16[768,256]{1,0:T(8,128)(2,1)} %get-tuple-element.33), channel_id=1, source_target_pairs={{0,3},{1,2},{2,1},{3,0},{4,7},{5,6},{6,5},{7,4},{8,11},{9,10},{10,... | collective-permute-start | bytes 1179656 | tf_op jit(solution)/shard_map/ppermute | solution.py:24
  28.3 37.0 %copy-start.10 = (bf16[512,128]{1,0:T(8,128)(2,1)}, bf16[512,128]{1,0:T(8,128)(2,1)S(1)}, u32[]{:S(2)}) copy-start(bf16[512,128]{1,0:T(8,128)(2,1)S(1)} %pad_maximum_fusion.2.refs_4_) | copy-start | bytes 393220
  28.3 8.1 %collective-permute-start.6 = (bf16[512,128]{1,0:T(8,128)(2,1)S(1)}, bf16[512,128]{1,0:T(8,128)(2,1)S(1)}, u32[]{:S(2)}, u32[]{:S(2)}) collective-permute-start(bf16[512,128]{1,0:T(8,128)(2,1)S(1)} %pad_maximum_fusion.2.refs_4_), channel_id=1, source_target_pairs={{0,24},{4,28},{8,16},{12,20},{16,8},{20,12},{24,0},{28,4},{1,25},{... | collective-permute-start | bytes 393224 | tf_op jit(solution)/shard_map/ppermute | solution.py:24
  32.0 47.3 %copy-start.9 = (bf16[512,128]{1,0:T(8,128)(2,1)}, bf16[512,128]{1,0:T(8,128)(2,1)S(1)}, u32[]{:S(2)}) copy-start(bf16[512,128]{1,0:T(8,128)(2,1)S(1)} %pad_maximum_fusion.3.refs_4_) | copy-start | bytes 393220
  32.0 6.9 %collective-permute-start.17 = (bf16[512,128]{1,0:T(8,128)(2,1)S(1)}, bf16[512,128]{1,0:T(8,128)(2,1)S(1)}, u32[]{:S(2)}, u32[]{:S(2)}) collective-permute-start(bf16[512,128]{1,0:T(8,128)(2,1)S(1)} %pad_maximum_fusion.3.refs_4_), channel_id=1, source_target_pairs={{0,4},{4,0},{8,12},{12,8},{16,20},{20,16},{24,28},{28,24},{1,5},{5... | collective-permute-start | bytes 393224 | tf_op jit(solution)/shard_map/ppermute | solution.py:24
  36.4 28.9 %copy-start.11 = (bf16[512,128]{1,0:T(8,128)(2,1)}, bf16[512,128]{1,0:T(8,128)(2,1)S(1)}, u32[]{:S(2)}) copy-start(bf16[512,128]{1,0:T(8,128)(2,1)S(1)} %collective-permute-done.6.refs_5_) | copy-start | bytes 393220
  36.4 9.2 %collective-permute-start.8 = (bf16[1024,128]{1,0:T(8,128)(2,1)S(1)}, bf16[1024,128]{1,0:T(8,128)(2,1)S(1)}, u32[]{:S(2)}, u32[]{:S(2)}) collective-permute-start(bf16[1024,128]{1,0:T(8,128)(2,1)S(1)} %constant_dynamic-update-slice_fusion), channel_id=1, source_target_pairs={{0,8},{4,12},{8,0},{12,4},{16,24},{20,28},{24,16},{28,20},{1,9},{5... | collective-permute-start | bytes 786440 | tf_op jit(solution)/shard_map/ppermute | solution.py:24
  38.9 34.7 %copy-start.6 = (bf16[512,128]{1,0:T(8,128)(2,1)}, bf16[512,128]{1,0:T(8,128)(2,1)S(1)}, u32[]{:S(2)}) copy-start(bf16[512,128]{1,0:T(8,128)(2,1)S(1)} %collective-permute-done.17.refs_4_) | copy-start | bytes 393220
  38.9 14.0 %collective-permute-start.18 = (bf16[1024,128]{1,0:T(8,128)(2,1)S(1)}, bf16[1024,128]{1,0:T(8,128)(2,1)S(1)}, u32[]{:S(2)}, u32[]{:S(2)}) collective-permute-start(bf16[1024,128]{1,0:T(8,128)(2,1)S(1)} %get-tuple-element.56), channel_id=1, source_target_pairs={{0,24},{4,28},{8,16},{12,20},{16,8},{20,12},{24,0},{28,4},{1,25},{... | collective-permute-start | bytes 786440 | tf_op jit(solution)/shard_map/ppermute | solution.py:24
  45.6 9.6 %collective-permute-start.9 = (bf16[1024,128]{1,0:T(8,128)(2,1)S(1)}, bf16[1024,128]{1,0:T(8,128)(2,1)S(1)}, u32[]{:S(2)}, u32[]{:S(2)}) collective-permute-start(bf16[1024,128]{1,0:T(8,128)(2,1)S(1)} %collective-permute-done.8.refs_7_), channel_id=1, source_target_pairs={{0,4},{4,0},{8,12},{12,8},{16,20},{20,16},{24,28},{28,24},{1,5},{5... | collective-permute-start | bytes 786440 | tf_op jit(solution)/shard_map/ppermute | solution.py:24
  53.0 20.6 %collective-permute-start.19 = (bf16[2048,128]{1,0:T(8,128)(2,1)S(1)}, bf16[2048,128]{1,0:T(8,128)(2,1)}, u32[]{:S(2)}, u32[]{:S(2)}) collective-permute-start(bf16[2048,128]{1,0:T(8,128)(2,1)S(1)} %constant_dynamic-update-slice_fusion.10), channel_id=1, source_target_pairs={{0,8},{4,12},{8,0},{12,4},{16,24},{20,28},{24,16},{28,20},{1,9},{5... | collective-permute-start | bytes 1572872 | tf_op jit(solution)/shard_map/ppermute | solution.py:24
  53.3 19.5 %collective-permute-start.14 = (bf16[768,256]{1,0:T(8,128)(2,1)}, bf16[768,256]{1,0:T(8,128)(2,1)}, u32[]{:S(2)}, u32[]{:S(2)}) collective-permute-start(bf16[768,256]{1,0:T(8,128)(2,1)} %get-tuple-element.39), channel_id=1, source_target_pairs={{0,1},{1,0},{2,3},{3,2},{4,5},{5,4},{6,7},{7,6},{8,9},{9,8},{10,11... | collective-permute-start | bytes 1179656 | tf_op jit(solution)/shard_map/ppermute | solution.py:24
  53.4 20.2 %collective-permute-start.15 = (bf16[768,256]{1,0:T(8,128)(2,1)}, bf16[768,256]{1,0:T(8,128)(2,1)}, u32[]{:S(2)}, u32[]{:S(2)}) collective-permute-start(bf16[768,256]{1,0:T(8,128)(2,1)} %get-tuple-element.40), channel_id=1, source_target_pairs={{0,2},{1,3},{2,0},{3,1},{4,6},{5,7},{6,4},{7,5},{8,10},{9,11},{10,... | collective-permute-start | bytes 1179656 | tf_op jit(solution)/shard_map/ppermute | solution.py:24
  54.9 18.7 %collective-permute-start.16 = (bf16[768,256]{1,0:T(8,128)(2,1)}, bf16[768,256]{1,0:T(8,128)(2,1)}, u32[]{:S(2)}, u32[]{:S(2)}) collective-permute-start(bf16[768,256]{1,0:T(8,128)(2,1)} %get-tuple-element.41), channel_id=1, source_target_pairs={{0,3},{1,2},{2,1},{3,0},{4,7},{5,6},{6,5},{7,4},{8,11},{9,10},{10,... | collective-permute-start | bytes 1179656 | tf_op jit(solution)/shard_map/ppermute | solution.py:24
  55.2 8.6 %collective-permute-start.7 = (bf16[1024,128]{1,0:T(8,128)(2,1)S(1)}, bf16[1024,128]{1,0:T(8,128)(2,1)S(1)}, u32[]{:S(2)}, u32[]{:S(2)}) collective-permute-start(bf16[1024,128]{1,0:T(8,128)(2,1)S(1)} %constant_dynamic-update-slice_fusion), channel_id=1, source_target_pairs={{0,4},{4,0},{8,12},{12,8},{16,20},{20,16},{24,28},{28,24},{1,5},{5... | collective-permute-start | bytes 786440 | tf_op jit(solution)/shard_map/ppermute | solution.py:24
  63.8 23.5 %collective-permute-start.10 = (bf16[1024,128]{1,0:T(8,128)(2,1)}, bf16[1024,128]{1,0:T(8,128)(2,1)S(1)}, u32[]{:S(2)}, u32[]{:S(2)}) collective-permute-start(bf16[1024,128]{1,0:T(8,128)(2,1)} %shard_map.103), channel_id=1, source_target_pairs={{0,4},{4,0},{8,12},{12,8},{16,20},{20,16},{24,28},{28,24},{1,5},{5... | collective-permute-start | bytes 786440 | tf_op jit(solution)/shard_map/ppermute | solution.py:24
  72.8 18.8 %collective-permute-start.12 = (bf16[1024,128]{1,0:T(8,128)(2,1)}, bf16[1024,128]{1,0:T(8,128)(2,1)S(1)}, u32[]{:S(2)}, u32[]{:S(2)}) collective-permute-start(bf16[1024,128]{1,0:T(8,128)(2,1)} %get-tuple-element.36), channel_id=1, source_target_pairs={{0,4},{4,0},{8,12},{12,8},{16,20},{20,16},{24,28},{28,24},{1,5},{5... | collective-permute-start | bytes 786440 | tf_op jit(solution)/shard_map/ppermute | solution.py:24
  73.6 31.0 %copy-start.7 = (bf16[512,128]{1,0:T(8,128)(2,1)S(1)}, bf16[512,128]{1,0:T(8,128)(2,1)}, u32[]{:S(2)}) copy-start(bf16[512,128]{1,0:T(8,128)(2,1)} %get-tuple-element.34) | copy-start | bytes 393220
  79.3 9.6 %collective-permute-start.20 = (bf16[1024,128]{1,0:T(8,128)(2,1)}, bf16[1024,128]{1,0:T(8,128)(2,1)S(1)}, u32[]{:S(2)}, u32[]{:S(2)}) collective-permute-start(bf16[1024,128]{1,0:T(8,128)(2,1)} %get-tuple-element.44), channel_id=1, source_target_pairs={{0,4},{4,0},{8,12},{12,8},{16,20},{20,16},{24,28},{28,24},{1,5},{5... | collective-permute-start | bytes 786440 | tf_op jit(solution)/shard_map/ppermute | solution.py:24
  80.6 18.7 %collective-permute-start.22 = (bf16[1024,128]{1,0:T(8,128)(2,1)}, bf16[1024,128]{1,0:T(8,128)(2,1)S(1)}, u32[]{:S(2)}, u32[]{:S(2)}) collective-permute-start(bf16[1024,128]{1,0:T(8,128)(2,1)} %get-tuple-element.45), channel_id=1, source_target_pairs={{0,4},{4,0},{8,12},{12,8},{16,20},{20,16},{24,28},{28,24},{1,5},{5... | collective-permute-start | bytes 786440 | tf_op jit(solution)/shard_map/ppermute | solution.py:24
  87.4 9.2 %collective-permute-start.11 = (bf16[1024,128]{1,0:T(8,128)(2,1)S(1)}, bf16[1024,128]{1,0:T(8,128)(2,1)S(1)}, u32[]{:S(2)}, u32[]{:S(2)}) collective-permute-start(bf16[1024,128]{1,0:T(8,128)(2,1)S(1)} %pad_maximum_fusion), channel_id=1, source_target_pairs={{0,8},{4,12},{8,0},{12,4},{16,24},{20,28},{24,16},{28,20},{1,9},{5... | collective-permute-start | bytes 786440 | tf_op jit(solution)/shard_map/ppermute | solution.py:24
  90.0 11.2 %collective-permute-start.21 = (bf16[1024,128]{1,0:T(8,128)(2,1)S(1)}, bf16[1024,128]{1,0:T(8,128)(2,1)S(1)}, u32[]{:S(2)}, u32[]{:S(2)}) collective-permute-start(bf16[1024,128]{1,0:T(8,128)(2,1)S(1)} %pad_maximum_fusion.1), channel_id=1, source_target_pairs={{0,8},{4,12},{8,0},{12,4},{16,24},{20,28},{24,16},{28,20},{1,9},{5... | collective-permute-start | bytes 786440 | tf_op jit(solution)/shard_map/ppermute | solution.py:24
  96.7 7.9 %collective-permute-start.13 = (bf16[512,128]{1,0:T(8,128)(2,1)S(1)}, bf16[512,128]{1,0:T(8,128)(2,1)S(1)}, u32[]{:S(2)}, u32[]{:S(2)}) collective-permute-start(bf16[512,128]{1,0:T(8,128)(2,1)S(1)} %add_convert_fusion.8), channel_id=1, source_target_pairs={{0,24},{4,28},{8,16},{12,20},{16,8},{20,12},{24,0},{28,4},{1,25},{... | collective-permute-start | bytes 393224 | tf_op jit(solution)/shard_map/ppermute | solution.py:24
  102.2 6.9 %collective-permute-start.23 = (bf16[512,128]{1,0:T(8,128)(2,1)S(1)}, bf16[512,128]{1,0:T(8,128)(2,1)S(1)}, u32[]{:S(2)}, u32[]{:S(2)}) collective-permute-start(bf16[512,128]{1,0:T(8,128)(2,1)S(1)} %add_convert_fusion.1), channel_id=1, source_target_pairs={{0,24},{4,28},{8,16},{12,20},{16,8},{20,12},{24,0},{28,4},{1,25},{... | collective-permute-start | bytes 393224 | tf_op jit(solution)/shard_map/ppermute | solution.py:24
  109.9 5.9 %collective-permute-start.24 = (bf16[128,256]{1,0:T(8,128)(2,1)S(1)}, bf16[128,256]{1,0:T(8,128)(2,1)S(1)}, u32[]{:S(2)}, u32[]{:S(2)}) collective-permute-start(bf16[128,256]{1,0:T(8,128)(2,1)S(1)} %get-tuple-element.53), channel_id=1, source_target_pairs={{0,1},{1,0},{2,3},{3,2},{4,5},{5,4},{6,7},{7,6},{8,9},{9,8},{10,11... | collective-permute-start | bytes 196616 | tf_op jit(solution)/shard_map/ppermute | solution.py:24
  109.9 5.9 %collective-permute-start.25 = (bf16[128,256]{1,0:T(8,128)(2,1)S(1)}, bf16[128,256]{1,0:T(8,128)(2,1)S(1)}, u32[]{:S(2)}, u32[]{:S(2)}) collective-permute-start(bf16[128,256]{1,0:T(8,128)(2,1)S(1)} %get-tuple-element.54), channel_id=1, source_target_pairs={{0,2},{1,3},{2,0},{3,1},{4,6},{5,7},{6,4},{7,5},{8,10},{9,11},{10,... | collective-permute-start | bytes 196616 | tf_op jit(solution)/shard_map/ppermute | solution.py:24
  111.4 4.4 %collective-permute-start.26 = (bf16[128,256]{1,0:T(8,128)(2,1)S(1)}, bf16[128,256]{1,0:T(8,128)(2,1)S(1)}, u32[]{:S(2)}, u32[]{:S(2)}) collective-permute-start(bf16[128,256]{1,0:T(8,128)(2,1)S(1)} %get-tuple-element.51), channel_id=1, source_target_pairs={{0,3},{1,2},{2,1},{3,0},{4,7},{5,6},{6,5},{7,4},{8,11},{9,10},{10,... | collective-permute-start | bytes 196616 | tf_op jit(solution)/shard_map/ppermute | solution.py:24
  (14 other events, 117.8 us)
where the time goes:
time: 121 us
  Pallas kernels  53.1 us (44%)
  starting transfers between devices  34.2 us (28%)
  waiting for transfers between devices  26.3 us (22%)
  other arithmetic  5.19 us (4%)
  local copies, waits for them, and re-layouts  1.52 us (1%)
    ppermute x27, starting transfers between devices, swap(): return lax.ppermute(value, axis, [(i, i ^ mask) for i in range(count)])  34.2 us
    ppermute x27, waiting for transfers between devices, swap(): return lax.ppermute(value, axis, [(i, i ^ mask) for i in range(count)])  26.3 us
    pallas_call x4, Pallas kernels, attend(): pl.pallas_call(functools.partial(attend_kernel, source, sink, events, roo...  23.2 us
    pallas_call x4, Pallas kernels, project_keys_values(): pl.pallas_call(keys_values_kernel, grid_spec=scalar_grid((count,), [pl.Bl...  17.9 us
    pallas_call x1, Pallas kernels, finish(): pl.pallas_call(functools.partial(finish_kernel, count), grid_spec=scalar_...  4.17 us
    pallas_call x1, Pallas kernels, project_gate(): pl.pallas_call(gate_kernel, grid_spec=scalar_grid((parts,), [pl.BlockSpec...  4 us
    pallas_call x1, Pallas kernels, project_queries(): pl.pallas_call(query_kernel, grid_spec=scalar_grid((parts,), [pl.BlockSpe...  3.74 us
  transfers between devices with their start and end apart: 27, of which 8 were waited for; matrix products, arithmetic and copies ran while one was open for 3% of the time, Pallas kernels for 37%

commit v1 on v0

--- a/solution.py
+++ b/solution.py
@@ -40,36 +40,40 @@
     )
 
 
-def query_kernel(_, cand_ref, w_ref, owner_ref, *outs):
+def query_kernel(me_ref, cand_ref, w_ref, owner_ref, *refs):
+    outs, made = refs[:-1], refs[-1]
     rows = cand_ref.shape[0]
-    made = silu(jnp.dot(cand_ref[...], w_ref[...], preferred_element_type=F32)).astype(BF16)
+    cols = outs[0].shape[1]
+    blocks = owner_ref.shape[0]
+    projected = jnp.dot(cand_ref[...], w_ref[...], preferred_element_type=F32)
+    made[...] = silu(projected).astype(BF16)
+    owners = jnp.broadcast_to(owner_ref[...].astype(F32), (blocks, cols)).astype(BF16)
     for k, out in enumerate(outs):
-
-        @pl.when(pl.program_id(0) == k)
-        def _(out=out):
-            out[:rows, :] = made
-            out[rows:, :] = owner_ref[...]
-
-
-def project_queries(me, candidates, w_qu, owner_rows, parts):
+        at = pl.multiple_of((k ^ me_ref[0]) * cols, cols)
+        out[:rows, :] = made[:, pl.ds(at, cols)]
+        out[rows:, :] = owners
+
+
+def project_queries(me, candidates, w_qu, block_owner, parts):
     rows, width = candidates.shape
     cols = width // parts
-    extra = owner_rows.shape[0]
+    blocks = block_owner.shape[0]
     return pl.pallas_call(
         query_kernel,
         grid_spec=scalar_grid(
-            (parts,),
+            (1,),
             [
-                pl.BlockSpec((rows, width), lambda k, m: (0, 0)),
-                pl.BlockSpec((width, cols), lambda k, m: (0, k ^ m[0])),
-                pl.BlockSpec((extra, cols), lambda k, m: (0, 0)),
+                pl.BlockSpec((rows, width), lambda i, m: (0, 0)),
+                pl.BlockSpec((width, width), lambda i, m: (0, 0)),
+                pl.BlockSpec((blocks, 1), lambda i, m: (0, 0)),
             ],
-            [pl.BlockSpec((rows + extra, cols), lambda k, m: (0, 0))] * parts,
+            [pl.BlockSpec((rows + blocks, cols), lambda i, m: (0, 0))] * parts,
+            [pltpu.VMEM((rows, width), BF16)],
         ),
-        out_shape=[jax.ShapeDtypeStruct((rows + extra, cols), BF16)] * parts,
+        out_shape=[jax.ShapeDtypeStruct((rows + blocks, cols), BF16)] * parts,
         cost_estimate=cost(2 * rows * width * width, 2 * width * width + 4 * rows * width),
         name="queries",
-    )(me, candidates, w_qu, owner_rows)
+    )(me, candidates, w_qu, block_owner)
 
 
 def gate_kernel(_, cand_ref, w_ref, out_ref):
@@ -95,46 +99,42 @@
     )(me, candidates, w_qu)
 
 
-def keys_values_kernel(_, hist_ref, wk_ref, wv_ref, *outs):
-    rows = hist_ref.shape[0]
-    step = min(rows, 256)
-    for k, out in enumerate(outs):
-
-        @pl.when(pl.program_id(0) == k)
-        def _(out=out):
-            for at in range(0, rows, step):
-                part = hist_ref[at : at + step, :]
-                keys = silu(jnp.dot(part, wk_ref[...], preferred_element_type=F32))
-                out[at : at + step, :HEAD] = keys.astype(BF16)
-                values = jnp.dot(part, wv_ref[...], preferred_element_type=F32)
-                out[at : at + step, HEAD:] = values.astype(BF16)
-
-
-def project_keys_values(me, history, w_kv, each, which, ks):
+def keys_values_kernel(count, each, _, hist_ref, *refs):
+    weights, outs = refs[: 2 * count], refs[2 * count :]
+    for k in range(count):
+        keys = silu(jnp.dot(hist_ref[...], weights[2 * k][...], preferred_element_type=F32))
+        values = jnp.dot(hist_ref[...], weights[2 * k + 1][...], preferred_element_type=F32)
+        for h in range(each):
+            out = outs[k * each + h]
+            out[:, :HEAD] = keys[:, h * HEAD : (h + 1) * HEAD].astype(BF16)
+            out[:, HEAD:] = values[:, h * HEAD : (h + 1) * HEAD].astype(BF16)
+
+
+def project_keys_values(me, history, w_kv, parts, ks):
     rows, width = history.shape
-    first, count = ks[0], len(ks)
-    heads = width // HEAD
-    return pl.pallas_call(
-        keys_values_kernel,
+    cols = width // parts
+    each = cols // HEAD
+    count = len(ks)
+    step = rows // 2
+
+    def weight(k, side):
+        return pl.BlockSpec((width, cols), lambda r, m: (0, side * parts + (k ^ m[0])))
+
+    made = pl.pallas_call(
+        functools.partial(keys_values_kernel, count, each),
         grid_spec=scalar_grid(
-            (count,),
-            [
-                pl.BlockSpec((rows, width), lambda k, m: (0, 0)),
-                pl.BlockSpec(
-                    (width, HEAD), lambda k, m: (0, ((k + first) ^ m[0]) * each + which)
-                ),
-                pl.BlockSpec(
-                    (width, HEAD), lambda k, m: (0, heads + ((k + first) ^ m[0]) * each + which)
-                ),
-            ],
-            [pl.BlockSpec((rows, 2 * HEAD), lambda k, m: (0, 0))] * count,
+            (rows // step,),
+            [pl.BlockSpec((step, width), lambda r, m: (r, 0))]
+            + [weight(k, side) for k in ks for side in range(2)],
+            [pl.BlockSpec((step, 2 * HEAD), lambda r, m: (r, 0))] * (count * each),
         ),
-        out_shape=[jax.ShapeDtypeStruct((rows, 2 * HEAD), BF16)] * count,
+        out_shape=[jax.ShapeDtypeStruct((rows, 2 * HEAD), BF16)] * (count * each),
         cost_estimate=cost(
-            4 * rows * width * HEAD * count,
-            2 * rows * width + 4 * width * HEAD * count + 4 * rows * HEAD * count,
+            4 * rows * width * cols * count,
+            2 * rows * width + 4 * width * cols * count + 4 * rows * cols * count,
         ),
-    )(me, history, w_kv, w_kv)
+    )(me, history, *[w_kv] * (2 * count))
+    return [made[k * each : (k + 1) * each] for k in range(count)]
 
 
 def attend_kernel(source, sink, events, room, pos_ref, count_ref, code_ref, *refs):
@@ -148,7 +148,13 @@
     blocks = kvs[0].shape[0] // events
     cands = asked.shape[0] // codes
     half = 0.5 * HEAD ** (-0.5)
-    packed[...] = jnp.zeros_like(packed)
+
+    def code_tiles(j):
+        return lax.div(count_ref[code_ref[j]] * events + (TILE - 1), TILE)
+
+    for j in range(codes):
+        at = code_ref[j] * room + (lax.max(code_tiles(j), 1) - 1) * TILE
+        packed[pl.ds(pl.multiple_of(at, TILE), TILE), :] = jnp.zeros((TILE, 2 * HEAD), BF16)
     for s, kv in enumerate(kvs):
 
         def place(b, carry, s=s, kv=kv):
@@ -164,7 +170,7 @@
         code = code_ref[j]
         base = pl.multiple_of(code * room, TILE)
         rows = pl.ds(pl.multiple_of(j * cands, cands), cands)
-        tiles = lax.div(count_ref[code] * events + (TILE - 1), TILE)
+        tiles = code_tiles(j)
         for number in range(room // TILE + 1):
 
             @pl.when(tiles == number)
@@ -223,47 +229,30 @@
     )(pos, counts, jnp.array(codes, dtype=jnp.int32), *kvs, *queries)
 
 
-def finish_kernel(count, _, cand_ref, gate_ref, w_ref, *refs):
-    parts, out_ref, stat, total = refs[:count], refs[count], refs[count + 1], refs[count + 2]
-    k = pl.program_id(0)
+def finish_kernel(me_ref, cand_ref, gate_ref, w_ref, *refs):
+    parts, out_ref = refs[:-1], refs[-1]
     width = cand_ref.shape[1]
-
-    @pl.when(k == 0)
-    def _():
-        mean = sum(jnp.sum(p[...].astype(F32), axis=1, keepdims=True) for p in parts) / width
-        square = sum(
-            jnp.sum(jnp.square(p[...].astype(F32) - mean), axis=1, keepdims=True) for p in parts
-        )
-        scale = lax.rsqrt(square / width + 1e-05)
-        for j, p in enumerate(parts):
-            stat[j] = (p[...].astype(F32) - mean) * scale
-        total[...] = cand_ref[...].astype(F32)
-
-    mixed = (stat[k] * gate_ref[0]).astype(BF16)
-    total[...] += jnp.dot(mixed, w_ref[...], preferred_element_type=F32)
-
-    @pl.when(k == count - 1)
-    def _():
-        out_ref[...] = total[...].astype(BF16)
+    cols = parts[0].shape[1]
+    values = [p[...].astype(F32) for p in parts]
+    mean = sum(jnp.sum(v, axis=1, keepdims=True) for v in values) / width
+    values = [v - mean for v in values]
+    square = sum(jnp.sum(v * v, axis=1, keepdims=True) for v in values)
+    scale = lax.rsqrt(square / width + 1e-05)
+    total = cand_ref[...].astype(F32)
+    for k, v in enumerate(values):
+        mixed = (v * scale * gate_ref[k]).astype(BF16)
+        rows = pl.ds(pl.multiple_of((k ^ me_ref[0]) * cols, cols), cols)
+        total += jnp.dot(mixed, w_ref[rows, :], preferred_element_type=F32)
+    out_ref[...] = total.astype(BF16)
 
 
 def finish(me, candidates, gate, w_out, parts):
     rows, width = candidates.shape
-    count = len(parts)
-    cols = width // count
+    vmem = pl.BlockSpec(memory_space=pltpu.VMEM)
     return pl.pallas_call(
-        functools.partial(finish_kernel, count),
-        grid_spec=scalar_grid(
-            (count,),
-            [
-                pl.BlockSpec((rows, width), lambda k, m: (0, 0)),
-                pl.BlockSpec((1, rows, cols), lambda k, m: (k, 0, 0)),
-                pl.BlockSpec((cols, width), lambda k, m: (k ^ m[0], 0)),
-            ]
-            + [pl.BlockSpec((rows, cols), lambda k, m: (0, 0))] * count,
-            pl.BlockSpec((rows, width), lambda k, m: (0, 0)),
-            [pltpu.VMEM((count, rows, cols), F32), pltpu.VMEM((rows, width), F32)],
-        ),
+        finish_kernel,
+        in_specs=[pl.BlockSpec(memory_space=pltpu.SMEM)] + [vmem] * (3 + len(parts)),
+        out_specs=vmem,
         out_shape=jax.ShapeDtypeStruct((rows, width), BF16),
         cost_estimate=cost(2 * rows * width * width, 2 * width * width + 10 * rows * width),
         name="finish",
@@ -342,28 +331,27 @@
     mine = candidates.shape[0]
     cands = mine * n_ctx
     each = width // HEAD // n_ctx
-    cols = each * HEAD
     room = -(-n_ctx * (2 * blocks // n_req) * events // TILE) * TILE
     me_ctx = lax.axis_index("ctx").astype(jnp.int32).reshape(1)
     me_req = lax.axis_index("req").astype(jnp.int32)
 
-    owner_rows = jnp.pad(
-        block_owner.reshape(1, blocks).astype(BF16), ((0, 15), (0, cols - blocks))
-    )
-    made = project_queries(me_ctx, candidates, w_qu, owner_rows, n_ctx)
+    made = project_queries(me_ctx, candidates, w_qu, block_owner, n_ctx)
     arrived = [made[0]] + [swap(made[k], "ctx", k) for k in range(1, n_ctx)]
 
-    far = range(n_ctx // 2, n_ctx)
-    near = range(0, n_ctx // 2)
+    far = list(range(n_ctx // 2, n_ctx))
+    near = list(range(0, n_ctx // 2))
+    made_far = project_keys_values(me_ctx, history, w_kv, n_ctx, far)
+    made_near = project_keys_values(me_ctx, history, w_kv, n_ctx, near)
     kvs = []
     for h in range(each):
-        sent = project_keys_values(me_ctx, history, w_kv, each, h, list(far))
-        got_far = [swap(s, "ctx", k) for s, k in zip(sent, far)]
-        kept = project_keys_values(me_ctx, history, w_kv, each, h, list(near))
-        got_near = [kept[0]] + [swap(kept[k], "ctx", k) for k in near if k > 0]
-        kvs.append(got_near + got_far)
-
-    owners = jnp.concatenate([a[mine, :blocks] for a in arrived]).astype(jnp.int32)
+        kvs.append(
+            [
+                heads[h] if k == 0 else swap(heads[h], "ctx", k)
+                for k, heads in zip(near + far, made_near + made_far)
+            ]
+        )
+
+    owners = jnp.concatenate([a[mine:, 0] for a in arrived]).astype(jnp.int32)
     code = owners ^ me_req
     total_blocks = n_ctx * blocks
     order = jnp.arange(total_blocks, dtype=jnp.int32)

time: 121 us -> 110 us (0.909)
  Pallas kernels: 53.1 us -> 41.5 us
  local copies, waits for them, and re-layouts: 1.52 us -> 2.86 us
    pallas_call x6 -> x4, Pallas kernels: 25.8 us -> 15.2 us  [the longest x2 9.12 us: project_keys_values(): pl.pallas_call(functools.partial(keys_values_kernel, count, each), grid_s...]
    unnamed x43 -> x44, local copies, waits for them, and re-layouts: 0.86 us -> 2.37 us
  transfers between devices with their start and end apart: 27 -> 27, of which waited for: 8 -> 8; matrix products, arithmetic and copies ran while one was open for 3% -> 4% of each run, Pallas kernels for 37% -> 32%
where the time goes in v1:
time: 110 us
  Pallas kernels  41.5 us (38%)
  starting transfers between devices  34.6 us (31%)
  waiting for transfers between devices  26 us (24%)
  other arithmetic  4.53 us (4%)
  local copies, waits for them, and re-layouts  2.86 us (3%)
    ppermute x27, starting transfers between devices, swap(): return lax.ppermute(value, axis, [(i, i ^ mask) for i in range(count)])  34.6 us
    ppermute x27, waiting for transfers between devices, swap(): return lax.ppermute(value, axis, [(i, i ^ mask) for i in range(count)])  26 us
    pallas_call x4, Pallas kernels, attend(): pl.pallas_call(functools.partial(attend_kernel, source, sink, events, roo...  22.4 us
    pallas_call x2, Pallas kernels, project_keys_values(): pl.pallas_call(functools.partial(keys_values_kernel, count, each), grid_s...  9.12 us
    pallas_call x1, Pallas kernels, project_gate(): pl.pallas_call(gate_kernel, grid_spec=scalar_grid((parts,), [pl.BlockSpec...  3.98 us
    pallas_call x1, Pallas kernels, finish(): pl.pallas_call(finish_kernel, in_specs=[pl.BlockSpec(memory_space=pltpu.S...  3.23 us
    pallas_call x1, Pallas kernels, project_queries(): pl.pallas_call(query_kernel, grid_spec=scalar_grid((1,), [pl.BlockSpec((r...  2.81 us
    unnamed x44, local copies, waits for them, and re-layouts  2.37 us
  transfers between devices with their start and end apart: 27, of which 8 were waited for; matrix products, arithmetic and copies ran while one was open for 4% of the time, Pallas kernels for 32%

profile of v1, /device:TPU:0, one launch (start us, length us, event | category | flops | bytes accessed | tf_op | source)
XLA Modules:
  0.0 109.8 jit_solution(6152207731457615182)
XLA Ops:
  1.3 2.8 %queries.1 = (bf16[176,256]{1,0:T(8,128)(2,1)}, bf16[176,256]{1,0:T(8,128)(2,1)}, bf16[176,256]{1,0:T(8,128)(2,1)}, bf16[176,256]{1,0:T(8,128)(2,1)}) custom-call(s32[1]{0:T(128)} %bitcast._.me_ref, bf16[128,1024]{1,0:T(8,128)(2,1)} %cand_ref.5, bf16[1024,2048]{1,0:T(8,128)(2,1)} %w_ref.4, s32[48,1]{1,0:T(8,128)} %copy.13.owner_ref), custom_call_target="tpu_custom_call" | custom-call | flops 268435456 | bytes 2621440 | tf_op jit(solution)/shard_map/queries/pallas_call | solution.py:61
  4.7 2.5 %collective-permute-start.1 = (bf16[176,256]{1,0:T(8,128)(2,1)}, bf16[176,256]{1,0:T(8,128)(2,1)S(1)}, u32[]{:S(2)}, u32[]{:S(2)}) collective-permute-start(bf16[176,256]{1,0:T(8,128)(2,1)} %get-tuple-element.28), channel_id=1, source_target_pairs={{0,2},{1,3},{2,0},{3,1},{4,6},{5,7},{6,4},{7,5},{8,10},{9,11},{10,... | collective-permute-start | bytes 270344 | tf_op jit(solution)/shard_map/ppermute | solution.py:24
  7.2 4.6 %shard_map.100 = (bf16[768,256]{1,0:T(8,128)(2,1)}, bf16[768,256]{1,0:T(8,128)(2,1)}, bf16[768,256]{1,0:T(8,128)(2,1)}, bf16[768,256]{1,0:T(8,128)(2,1)}) custom-call(s32[1]{0:T(128)} %bitcast._.me_ref, bf16[768,1024]{1,0:T(8,128)(2,1)} %hist_ref.3, bf16[1024,2048]{1,0:T(8,128)(2,1)} %refs_3_.3, bf16[1024,2048]{1,0:T(8,128)(2,1)} %refs_3_.3, ...), custom_call_target="tpu_custom_call" | custom-call | flops 1610612736 | bytes 5242880 | tf_op jit(solution)/shard_map/pallas_call | solution.py:123
  12.0 4.6 %shard_map.101 = (bf16[768,256]{1,0:T(8,128)(2,1)}, bf16[768,256]{1,0:T(8,128)(2,1)}, bf16[768,256]{1,0:T(8,128)(2,1)}, bf16[768,256]{1,0:T(8,128)(2,1)}) custom-call(s32[1]{0:T(128)} %bitcast._.me_ref, bf16[768,1024]{1,0:T(8,128)(2,1)} %hist_ref.3, bf16[1024,2048]{1,0:T(8,128)(2,1)} %refs_3_.3, bf16[1024,2048]{1,0:T(8,128)(2,1)} %refs_3_.3, ...), custom_call_target="tpu_custom_call" | custom-call | flops 1610612736 | bytes 5242880 | tf_op jit(solution)/shard_map/pallas_call | solution.py:123
  16.6 1.9 %collective-permute-start.4 = (bf16[768,256]{1,0:T(8,128)(2,1)}, bf16[768,256]{1,0:T(8,128)(2,1)S(1)}, u32[]{:S(2)}, u32[]{:S(2)}) collective-permute-start(bf16[768,256]{1,0:T(8,128)(2,1)} %get-tuple-element.32), channel_id=1, source_target_pairs={{0,2},{1,3},{2,0},{3,1},{4,6},{5,7},{6,4},{7,5},{8,10},{9,11},{10,... | collective-permute-start | bytes 1179656 | tf_op jit(solution)/shard_map/ppermute | solution.py:24
  18.8 3.7 %collective-permute-start.6 = (bf16[512,128]{1,0:T(8,128)(2,1)S(1)}, bf16[512,128]{1,0:T(8,128)(2,1)S(1)}, u32[]{:S(2)}, u32[]{:S(2)}) collective-permute-start(bf16[512,128]{1,0:T(8,128)(2,1)S(1)} %pad_maximum_fusion.2.refs_4_), channel_id=1, source_target_pairs={{0,24},{4,28},{8,16},{12,20},{16,8},{20,12},{24,0},{28,4},{1,25},{... | collective-permute-start | bytes 393224 | tf_op jit(solution)/shard_map/ppermute | solution.py:24
  22.6 1.6 %collective-permute-start.17 = (bf16[512,128]{1,0:T(8,128)(2,1)S(1)}, bf16[512,128]{1,0:T(8,128)(2,1)S(1)}, u32[]{:S(2)}, u32[]{:S(2)}) collective-permute-start(bf16[512,128]{1,0:T(8,128)(2,1)S(1)} %pad_maximum_fusion.3.refs_4_), channel_id=1, source_target_pairs={{0,4},{4,0},{8,12},{12,8},{16,20},{20,16},{24,28},{28,24},{1,5},{5... | collective-permute-start | bytes 393224 | tf_op jit(solution)/shard_map/ppermute | solution.py:24
  24.3 2.6 %collective-permute-done.6.refs_5_ = bf16[512,128]{1,0:T(8,128)(2,1)S(1)} collective-permute-done((bf16[512,128]{1,0:T(8,128)(2,1)S(1)}, bf16[512,128]{1,0:T(8,128)(2,1)S(1)}, u32[]{:S(2)}, u32[]{:S(2)}) %collective-permute-start.6) | collective-permute-done | bytes 131104 | tf_op jit(solution)/shard_map/ppermute | solution.py:24
  26.9 2.5 %collective-permute-start.8 = (bf16[1024,128]{1,0:T(8,128)(2,1)S(1)}, bf16[1024,128]{1,0:T(8,128)(2,1)S(1)}, u32[]{:S(2)}, u32[]{:S(2)}) collective-permute-start(bf16[1024,128]{1,0:T(8,128)(2,1)S(1)} %constant_dynamic-update-slice_fusion), channel_id=1, source_target_pairs={{0,8},{4,12},{8,0},{12,4},{16,24},{20,28},{24,16},{28,20},{1,9},{5... | collective-permute-start | bytes 786440 | tf_op jit(solution)/shard_map/ppermute | solution.py:24
  29.5 2.5 %collective-permute-start.18 = (bf16[1024,128]{1,0:T(8,128)(2,1)S(1)}, bf16[1024,128]{1,0:T(8,128)(2,1)S(1)}, u32[]{:S(2)}, u32[]{:S(2)}) collective-permute-start(bf16[1024,128]{1,0:T(8,128)(2,1)S(1)} %get-tuple-element.56), channel_id=1, source_target_pairs={{0,24},{4,28},{8,16},{12,20},{16,8},{20,12},{24,0},{28,4},{1,25},{... | collective-permute-start | bytes 786440 | tf_op jit(solution)/shard_map/ppermute | solution.py:24
  32.2 3.9 %collective-permute-done.8.refs_7_ = bf16[1024,128]{1,0:T(8,128)(2,1)S(1)} collective-permute-done((bf16[1024,128]{1,0:T(8,128)(2,1)S(1)}, bf16[1024,128]{1,0:T(8,128)(2,1)S(1)}, u32[]{:S(2)}, u32[]{:S(2)}) %collective-permute-start.8) | collective-permute-done | bytes 262176 | tf_op jit(solution)/shard_map/ppermute | solution.py:24
  36.1 1.5 %collective-permute-start.9 = (bf16[1024,128]{1,0:T(8,128)(2,1)S(1)}, bf16[1024,128]{1,0:T(8,128)(2,1)S(1)}, u32[]{:S(2)}, u32[]{:S(2)}) collective-permute-start(bf16[1024,128]{1,0:T(8,128)(2,1)S(1)} %collective-permute-done.8.refs_7_), channel_id=1, source_target_pairs={{0,4},{4,0},{8,12},{12,8},{16,20},{20,16},{24,28},{28,24},{1,5},{5... | collective-permute-start | bytes 786440 | tf_op jit(solution)/shard_map/ppermute | solution.py:24
  37.7 5.7 %collective-permute-done.18.refs_5_ = bf16[1024,128]{1,0:T(8,128)(2,1)S(1)} collective-permute-done((bf16[1024,128]{1,0:T(8,128)(2,1)S(1)}, bf16[1024,128]{1,0:T(8,128)(2,1)S(1)}, u32[]{:S(2)}, u32[]{:S(2)}) %collective-permute-start.18) | collective-permute-done | bytes 262176 | tf_op jit(solution)/shard_map/ppermute | solution.py:24
  43.8 1.6 %collective-permute-start.15 = (bf16[768,256]{1,0:T(8,128)(2,1)}, bf16[768,256]{1,0:T(8,128)(2,1)}, u32[]{:S(2)}, u32[]{:S(2)}) collective-permute-start(bf16[768,256]{1,0:T(8,128)(2,1)} %get-tuple-element.40), channel_id=1, source_target_pairs={{0,2},{1,3},{2,0},{3,1},{4,6},{5,7},{6,4},{7,5},{8,10},{9,11},{10,... | collective-permute-start | bytes 1179656 | tf_op jit(solution)/shard_map/ppermute | solution.py:24
  45.7 1.5 %collective-permute-start.7 = (bf16[1024,128]{1,0:T(8,128)(2,1)S(1)}, bf16[1024,128]{1,0:T(8,128)(2,1)}, u32[]{:S(2)}, u32[]{:S(2)}) collective-permute-start(bf16[1024,128]{1,0:T(8,128)(2,1)S(1)} %constant_dynamic-update-slice_fusion), channel_id=1, source_target_pairs={{0,4},{4,0},{8,12},{12,8},{16,20},{20,16},{24,28},{28,24},{1,5},{5... | collective-permute-start | bytes 786440 | tf_op jit(solution)/shard_map/ppermute | solution.py:24
  48.5 3.9 %shard_map.103 = bf16[1024,128]{1,0:T(8,128)(2,1)} custom-call(s32[192]{0:T(256)} %multiply_add_fusion.pos_ref, s32[8]{0:T(128)} %convert_reduce_fusion.1.count_ref, s32[2]{0:T(128)} %constant.22.clone.code_ref, bf16[768,256]{1,0:T(8,128)(2,1)} %get-tuple-element.30.refs_0_, bf16[768,256]{1,0:T(8,128)(2,1)} %copy-done, bf16[768,256]{1,0:T(8,128)(2,1)} %copy-done.1, ...), custom_call_target="tpu_custom_call" | custom-call | flops 402653184 | bytes 2097152 | tf_op jit(solution)/shard_map/pallas_call | solution.py:214
  52.4 2.0 %collective-permute-done.7.refs_6_ = bf16[1024,128]{1,0:T(8,128)(2,1)} collective-permute-done((bf16[1024,128]{1,0:T(8,128)(2,1)S(1)}, bf16[1024,128]{1,0:T(8,128)(2,1)}, u32[]{:S(2)}, u32[]{:S(2)}) %collective-permute-start.7) | collective-permute-done | bytes 262176 | tf_op jit(solution)/shard_map/ppermute | solution.py:24
  54.4 1.5 %collective-permute-start.10 = (bf16[1024,128]{1,0:T(8,128)(2,1)}, bf16[1024,128]{1,0:T(8,128)(2,1)S(1)}, u32[]{:S(2)}, u32[]{:S(2)}) collective-permute-start(bf16[1024,128]{1,0:T(8,128)(2,1)} %shard_map.103), channel_id=1, source_target_pairs={{0,4},{4,0},{8,12},{12,8},{16,20},{20,16},{24,28},{28,24},{1,5},{5... | collective-permute-start | bytes 786440 | tf_op jit(solution)/shard_map/ppermute | solution.py:24
  55.9 7.1 %shard_map.102 = (bf16[512,128]{1,0:T(8,128)(2,1)}, bf16[1024,128]{1,0:T(8,128)(2,1)}, bf16[1024,128]{1,0:T(8,128)(2,1)}, bf16[512,128]{1,0:T(8,128)(2,1)}) custom-call(s32[192]{0:T(256)} %multiply_add_fusion.pos_ref, s32[8]{0:T(128)} %convert_reduce_fusion.1.count_ref, s32[6]{0:T(128)} %constant.21.clone.code_ref, ...), custom_call_target="tpu_custom_call" | custom-call | flops 1207959552 | bytes 3145728 | tf_op jit(solution)/shard_map/pallas_call | solution.py:214
  63.8 5.5 %shard_map.105 = (bf16[1024,128]{1,0:T(8,128)(2,1)}, bf16[1024,128]{1,0:T(8,128)(2,1)}) custom-call(s32[192]{0:T(256)} %multiply_add_fusion.pos_ref, s32[8]{0:T(128)} %convert_reduce_fusion.1.count_ref, s32[4]{0:T(128)} %constant.23.clone.code_ref, bf16[768,256]{1,0:T(8,128)(2,1)} %get-tuple-element.38.refs_0_, bf16[768,256]{1,0:T(8,128)(2,1)} %copy-done.17, ...), custom_call_target="tpu_custom_call" | custom-call | flops 805306368 | bytes 2621440 | tf_op jit(solution)/shard_map/pallas_call | solution.py:214
  69.3 1.4 %collective-permute-start.20 = (bf16[1024,128]{1,0:T(8,128)(2,1)}, bf16[1024,128]{1,0:T(8,128)(2,1)S(1)}, u32[]{:S(2)}, u32[]{:S(2)}) collective-permute-start(bf16[1024,128]{1,0:T(8,128)(2,1)} %get-tuple-element.44), channel_id=1, source_target_pairs={{0,4},{4,0},{8,12},{12,8},{16,20},{20,16},{24,28},{28,24},{1,5},{5... | collective-permute-start | bytes 786440 | tf_op jit(solution)/shard_map/ppermute | solution.py:24
  71.4 5.8 %shard_map.104 = (bf16[512,128]{1,0:T(8,128)(2,1)}, bf16[1024,128]{1,0:T(8,128)(2,1)}, bf16[512,128]{1,0:T(8,128)(2,1)}) custom-call(s32[192]{0:T(256)} %multiply_add_fusion.pos_ref, s32[8]{0:T(128)} %convert_reduce_fusion.1.count_ref, s32[4]{0:T(128)} %constant.24.clone.code_ref, bf16[768,256]{1,0:T(8,128)(2,1)} %get-tuple-element.38.refs_0_, ...), custom_call_target="tpu_custom_call" | custom-call | flops 805306368 | bytes 2621440 | tf_op jit(solution)/shard_map/pallas_call | solution.py:214
  77.3 1.8 %collective-permute-start.11 = (bf16[1024,128]{1,0:T(8,128)(2,1)S(1)}, bf16[1024,128]{1,0:T(8,128)(2,1)S(1)}, u32[]{:S(2)}, u32[]{:S(2)}) collective-permute-start(bf16[1024,128]{1,0:T(8,128)(2,1)S(1)} %pad_maximum_fusion), channel_id=1, source_target_pairs={{0,8},{4,12},{8,0},{12,4},{16,24},{20,28},{24,16},{28,20},{1,9},{5... | collective-permute-start | bytes 786440 | tf_op jit(solution)/shard_map/ppermute | solution.py:24
  80.2 1.7 %collective-permute-start.21 = (bf16[1024,128]{1,0:T(8,128)(2,1)S(1)}, bf16[1024,128]{1,0:T(8,128)(2,1)S(1)}, u32[]{:S(2)}, u32[]{:S(2)}) collective-permute-start(bf16[1024,128]{1,0:T(8,128)(2,1)S(1)} %pad_maximum_fusion.1), channel_id=1, source_target_pairs={{0,8},{4,12},{8,0},{12,4},{16,24},{20,28},{24,16},{28,20},{1,9},{5... | collective-permute-start | bytes 786440 | tf_op jit(solution)/shard_map/ppermute | solution.py:24
  81.9 4.6 %collective-permute-done.11 = bf16[1024,128]{1,0:T(8,128)(2,1)S(1)} collective-permute-done((bf16[1024,128]{1,0:T(8,128)(2,1)S(1)}, bf16[1024,128]{1,0:T(8,128)(2,1)S(1)}, u32[]{:S(2)}, u32[]{:S(2)}) %collective-permute-start.11) | collective-permute-done | bytes 262176 | tf_op jit(solution)/shard_map/ppermute | solution.py:24
  86.6 2.5 %collective-permute-start.13 = (bf16[512,128]{1,0:T(8,128)(2,1)S(1)}, bf16[512,128]{1,0:T(8,128)(2,1)S(1)}, u32[]{:S(2)}, u32[]{:S(2)}) collective-permute-start(bf16[512,128]{1,0:T(8,128)(2,1)S(1)} %add_convert_fusion.8), channel_id=1, source_target_pairs={{0,24},{4,28},{8,16},{12,20},{16,8},{20,12},{24,0},{28,4},{1,25},{... | collective-permute-start | bytes 393224 | tf_op jit(solution)/shard_map/ppermute | solution.py:24
  89.1 2.3 %collective-permute-done.21 = bf16[1024,128]{1,0:T(8,128)(2,1)S(1)} collective-permute-done((bf16[1024,128]{1,0:T(8,128)(2,1)S(1)}, bf16[1024,128]{1,0:T(8,128)(2,1)S(1)}, u32[]{:S(2)}, u32[]{:S(2)}) %collective-permute-start.21) | collective-permute-done | bytes 262176 | tf_op jit(solution)/shard_map/ppermute | solution.py:24
  92.4 2.0 %collective-permute-start.23 = (bf16[512,128]{1,0:T(8,128)(2,1)S(1)}, bf16[512,128]{1,0:T(8,128)(2,1)S(1)}, u32[]{:S(2)}, u32[]{:S(2)}) collective-permute-start(bf16[512,128]{1,0:T(8,128)(2,1)S(1)} %add_convert_fusion.1), channel_id=1, source_target_pairs={{0,24},{4,28},{8,16},{12,20},{16,8},{20,12},{24,0},{28,4},{1,25},{... | collective-permute-start | bytes 393224 | tf_op jit(solution)/shard_map/ppermute | solution.py:24
  94.9 4.4 %collective-permute-done.23 = bf16[512,128]{1,0:T(8,128)(2,1)S(1)} collective-permute-done((bf16[512,128]{1,0:T(8,128)(2,1)S(1)}, bf16[512,128]{1,0:T(8,128)(2,1)S(1)}, u32[]{:S(2)}, u32[]{:S(2)}) %collective-permute-start.23) | collective-permute-done | bytes 131104 | tf_op jit(solution)/shard_map/ppermute | solution.py:24
  100.1 1.5 %collective-permute-start.25 = (bf16[128,256]{1,0:T(8,128)(2,1)S(1)}, bf16[128,256]{1,0:T(8,128)(2,1)S(1)}, u32[]{:S(2)}, u32[]{:S(2)}) collective-permute-start(bf16[128,256]{1,0:T(8,128)(2,1)S(1)} %get-tuple-element.54), channel_id=1, source_target_pairs={{0,2},{1,3},{2,0},{3,1},{4,6},{5,7},{6,4},{7,5},{8,10},{9,11},{10,... | collective-permute-start | bytes 196616 | tf_op jit(solution)/shard_map/ppermute | solution.py:24
  101.9 4.0 %gate.1.gate_ref = f32[4,128,256]{2,1,0:T(8,128)} custom-call(s32[1]{0:T(128)} %bitcast._.me_ref, bf16[128,1024]{1,0:T(8,128)(2,1)} %cand_ref.5, bf16[1024,2048]{1,0:T(8,128)(2,1)} %w_ref.4), custom_call_target="tpu_custom_call" | custom-call | flops 268435456 | bytes 2883584 | tf_op jit(solution)/shard_map/gate/pallas_call | solution.py:86
  106.6 3.2 %finish.1 = bf16[128,1024]{1,0:T(8,128)(2,1)} custom-call(s32[1]{0:T(128)} %bitcast._.me_ref, bf16[128,1024]{1,0:T(8,128)(2,1)} %cand_ref.5, f32[4,128,256]{2,1,0:T(8,128)} %gate.1.gate_ref, bf16[1024,1024]{1,0:T(8,128)(2,1)} %w_ref.5, bf16[128,256]{1,0:T(8,128)(2,1)} %get-tuple-element.52.refs_0_, bf16[128,256]{1,0:T(8,128)(2,1)} %copy-done.14, ...), custom_call_target="tpu_custom_call" | custom-call | flops 268435456 | bytes 3407872 | tf_op jit(solution)/shard_map/finish/pallas_call | solution.py:252
  (96 shorter events, 10.8 us)
Async XLA Ops:
  4.2 14.4 %collective-permute-start = (bf16[176,256]{1,0:T(8,128)(2,1)}, bf16[176,256]{1,0:T(8,128)(2,1)S(1)}, u32[]{:S(2)}, u32[]{:S(2)}) collective-permute-start(bf16[176,256]{1,0:T(8,128)(2,1)} %get-tuple-element.27), channel_id=1, source_target_pairs={{0,1},{1,0},{2,3},{3,2},{4,5},{5,4},{6,7},{7,6},{8,9},{9,8},{10,11... | collective-permute-start | bytes 270344 | tf_op jit(solution)/shard_map/ppermute | solution.py:24
  4.7 14.1 %collective-permute-start.1 = (bf16[176,256]{1,0:T(8,128)(2,1)}, bf16[176,256]{1,0:T(8,128)(2,1)S(1)}, u32[]{:S(2)}, u32[]{:S(2)}) collective-permute-start(bf16[176,256]{1,0:T(8,128)(2,1)} %get-tuple-element.28), channel_id=1, source_target_pairs={{0,2},{1,3},{2,0},{3,1},{4,6},{5,7},{6,4},{7,5},{8,10},{9,11},{10,... | collective-permute-start | bytes 270344 | tf_op jit(solution)/shard_map/ppermute | solution.py:24
  7.1 11.6 %collective-permute-start.2 = (bf16[176,256]{1,0:T(8,128)(2,1)}, bf16[176,256]{1,0:T(8,128)(2,1)S(1)}, u32[]{:S(2)}, u32[]{:S(2)}) collective-permute-start(bf16[176,256]{1,0:T(8,128)(2,1)} %get-tuple-element.29), channel_id=1, source_target_pairs={{0,3},{1,2},{2,1},{3,0},{4,7},{5,6},{6,5},{7,4},{8,11},{9,10},{10,... | collective-permute-start | bytes 270344 | tf_op jit(solution)/shard_map/ppermute | solution.py:24
  11.8 31.9 %collective-permute-start.3 = (bf16[768,256]{1,0:T(8,128)(2,1)}, bf16[768,256]{1,0:T(8,128)(2,1)S(1)}, u32[]{:S(2)}, u32[]{:S(2)}) collective-permute-start(bf16[768,256]{1,0:T(8,128)(2,1)} %get-tuple-element.31), channel_id=1, source_target_pairs={{0,1},{1,0},{2,3},{3,2},{4,5},{5,4},{6,7},{7,6},{8,9},{9,8},{10,11... | collective-permute-start | bytes 1179656 | tf_op jit(solution)/shard_map/ppermute | solution.py:24
  16.6 27.2 %collective-permute-start.4 = (bf16[768,256]{1,0:T(8,128)(2,1)}, bf16[768,256]{1,0:T(8,128)(2,1)S(1)}, u32[]{:S(2)}, u32[]{:S(2)}) collective-permute-start(bf16[768,256]{1,0:T(8,128)(2,1)} %get-tuple-element.32), channel_id=1, source_target_pairs={{0,2},{1,3},{2,0},{3,1},{4,6},{5,7},{6,4},{7,5},{8,10},{9,11},{10,... | collective-permute-start | bytes 1179656 | tf_op jit(solution)/shard_map/ppermute | solution.py:24
  18.6 26.8 %collective-permute-start.5 = (bf16[768,256]{1,0:T(8,128)(2,1)}, bf16[768,256]{1,0:T(8,128)(2,1)S(1)}, u32[]{:S(2)}, u32[]{:S(2)}) collective-permute-start(bf16[768,256]{1,0:T(8,128)(2,1)} %get-tuple-element.33), channel_id=1, source_target_pairs={{0,3},{1,2},{2,1},{3,0},{4,7},{5,6},{6,5},{7,4},{8,11},{9,10},{10,... | collective-permute-start | bytes 1179656 | tf_op jit(solution)/shard_map/ppermute | solution.py:24
  18.8 37.0 %copy-start.10 = (bf16[512,128]{1,0:T(8,128)(2,1)}, bf16[512,128]{1,0:T(8,128)(2,1)S(1)}, u32[]{:S(2)}) copy-start(bf16[512,128]{1,0:T(8,128)(2,1)S(1)} %pad_maximum_fusion.2.refs_4_) | copy-start | bytes 393220
  18.8 8.1 %collective-permute-start.6 = (bf16[512,128]{1,0:T(8,128)(2,1)S(1)}, bf16[512,128]{1,0:T(8,128)(2,1)S(1)}, u32[]{:S(2)}, u32[]{:S(2)}) collective-permute-start(bf16[512,128]{1,0:T(8,128)(2,1)S(1)} %pad_maximum_fusion.2.refs_4_), channel_id=1, source_target_pairs={{0,24},{4,28},{8,16},{12,20},{16,8},{20,12},{24,0},{28,4},{1,25},{... | collective-permute-start | bytes 393224 | tf_op jit(solution)/shard_map/ppermute | solution.py:24
  22.6 46.8 %copy-start.9 = (bf16[512,128]{1,0:T(8,128)(2,1)}, bf16[512,128]{1,0:T(8,128)(2,1)S(1)}, u32[]{:S(2)}) copy-start(bf16[512,128]{1,0:T(8,128)(2,1)S(1)} %pad_maximum_fusion.3.refs_4_) | copy-start | bytes 393220
  22.6 6.8 %collective-permute-start.17 = (bf16[512,128]{1,0:T(8,128)(2,1)S(1)}, bf16[512,128]{1,0:T(8,128)(2,1)S(1)}, u32[]{:S(2)}, u32[]{:S(2)}) collective-permute-start(bf16[512,128]{1,0:T(8,128)(2,1)S(1)} %pad_maximum_fusion.3.refs_4_), channel_id=1, source_target_pairs={{0,4},{4,0},{8,12},{12,8},{16,20},{20,16},{24,28},{28,24},{1,5},{5... | collective-permute-start | bytes 393224 | tf_op jit(solution)/shard_map/ppermute | solution.py:24
  26.9 29.0 %copy-start.11 = (bf16[512,128]{1,0:T(8,128)(2,1)}, bf16[512,128]{1,0:T(8,128)(2,1)S(1)}, u32[]{:S(2)}) copy-start(bf16[512,128]{1,0:T(8,128)(2,1)S(1)} %collective-permute-done.6.refs_5_) | copy-start | bytes 393220
  26.9 9.2 %collective-permute-start.8 = (bf16[1024,128]{1,0:T(8,128)(2,1)S(1)}, bf16[1024,128]{1,0:T(8,128)(2,1)S(1)}, u32[]{:S(2)}, u32[]{:S(2)}) collective-permute-start(bf16[1024,128]{1,0:T(8,128)(2,1)S(1)} %constant_dynamic-update-slice_fusion), channel_id=1, source_target_pairs={{0,8},{4,12},{8,0},{12,4},{16,24},{20,28},{24,16},{28,20},{1,9},{5... | collective-permute-start | bytes 786440 | tf_op jit(solution)/shard_map/ppermute | solution.py:24
  29.4 34.2 %copy-start.6 = (bf16[512,128]{1,0:T(8,128)(2,1)}, bf16[512,128]{1,0:T(8,128)(2,1)S(1)}, u32[]{:S(2)}) copy-start(bf16[512,128]{1,0:T(8,128)(2,1)S(1)} %collective-permute-done.17.refs_4_) | copy-start | bytes 393220
  29.5 13.9 %collective-permute-start.18 = (bf16[1024,128]{1,0:T(8,128)(2,1)S(1)}, bf16[1024,128]{1,0:T(8,128)(2,1)S(1)}, u32[]{:S(2)}, u32[]{:S(2)}) collective-permute-start(bf16[1024,128]{1,0:T(8,128)(2,1)S(1)} %get-tuple-element.56), channel_id=1, source_target_pairs={{0,24},{4,28},{8,16},{12,20},{16,8},{20,12},{24,0},{28,4},{1,25},{... | collective-permute-start | bytes 786440 | tf_op jit(solution)/shard_map/ppermute | solution.py:24
  36.1 9.6 %collective-permute-start.9 = (bf16[1024,128]{1,0:T(8,128)(2,1)S(1)}, bf16[1024,128]{1,0:T(8,128)(2,1)S(1)}, u32[]{:S(2)}, u32[]{:S(2)}) collective-permute-start(bf16[1024,128]{1,0:T(8,128)(2,1)S(1)} %collective-permute-done.8.refs_7_), channel_id=1, source_target_pairs={{0,4},{4,0},{8,12},{12,8},{16,20},{20,16},{24,28},{28,24},{1,5},{5... | collective-permute-start | bytes 786440 | tf_op jit(solution)/shard_map/ppermute | solution.py:24
  43.4 20.2 %collective-permute-start.19 = (bf16[2048,128]{1,0:T(8,128)(2,1)S(1)}, bf16[2048,128]{1,0:T(8,128)(2,1)}, u32[]{:S(2)}, u32[]{:S(2)}) collective-permute-start(bf16[2048,128]{1,0:T(8,128)(2,1)S(1)} %constant_dynamic-update-slice_fusion.10), channel_id=1, source_target_pairs={{0,8},{4,12},{8,0},{12,4},{16,24},{20,28},{24,16},{28,20},{1,9},{5... | collective-permute-start | bytes 1572872 | tf_op jit(solution)/shard_map/ppermute | solution.py:24
  43.7 19.3 %collective-permute-start.14 = (bf16[768,256]{1,0:T(8,128)(2,1)}, bf16[768,256]{1,0:T(8,128)(2,1)S(1)}, u32[]{:S(2)}, u32[]{:S(2)}) collective-permute-start(bf16[768,256]{1,0:T(8,128)(2,1)} %get-tuple-element.39), channel_id=1, source_target_pairs={{0,1},{1,0},{2,3},{3,2},{4,5},{5,4},{6,7},{7,6},{8,9},{9,8},{10,11... | collective-permute-start | bytes 1179656 | tf_op jit(solution)/shard_map/ppermute | solution.py:24
  43.8 19.8 %collective-permute-start.15 = (bf16[768,256]{1,0:T(8,128)(2,1)}, bf16[768,256]{1,0:T(8,128)(2,1)}, u32[]{:S(2)}, u32[]{:S(2)}) collective-permute-start(bf16[768,256]{1,0:T(8,128)(2,1)} %get-tuple-element.40), channel_id=1, source_target_pairs={{0,2},{1,3},{2,0},{3,1},{4,6},{5,7},{6,4},{7,5},{8,10},{9,11},{10,... | collective-permute-start | bytes 1179656 | tf_op jit(solution)/shard_map/ppermute | solution.py:24
  45.4 18.2 %collective-permute-start.16 = (bf16[768,256]{1,0:T(8,128)(2,1)}, bf16[768,256]{1,0:T(8,128)(2,1)}, u32[]{:S(2)}, u32[]{:S(2)}) collective-permute-start(bf16[768,256]{1,0:T(8,128)(2,1)} %get-tuple-element.41), channel_id=1, source_target_pairs={{0,3},{1,2},{2,1},{3,0},{4,7},{5,6},{6,5},{7,4},{8,11},{9,10},{10,... | collective-permute-start | bytes 1179656 | tf_op jit(solution)/shard_map/ppermute | solution.py:24
  45.7 8.7 %collective-permute-start.7 = (bf16[1024,128]{1,0:T(8,128)(2,1)S(1)}, bf16[1024,128]{1,0:T(8,128)(2,1)}, u32[]{:S(2)}, u32[]{:S(2)}) collective-permute-start(bf16[1024,128]{1,0:T(8,128)(2,1)S(1)} %constant_dynamic-update-slice_fusion), channel_id=1, source_target_pairs={{0,4},{4,0},{8,12},{12,8},{16,20},{20,16},{24,28},{28,24},{1,5},{5... | collective-permute-start | bytes 786440 | tf_op jit(solution)/shard_map/ppermute | solution.py:24
  54.4 22.8 %collective-permute-start.10 = (bf16[1024,128]{1,0:T(8,128)(2,1)}, bf16[1024,128]{1,0:T(8,128)(2,1)S(1)}, u32[]{:S(2)}, u32[]{:S(2)}) collective-permute-start(bf16[1024,128]{1,0:T(8,128)(2,1)} %shard_map.103), channel_id=1, source_target_pairs={{0,4},{4,0},{8,12},{12,8},{16,20},{20,16},{24,28},{28,24},{1,5},{5... | collective-permute-start | bytes 786440 | tf_op jit(solution)/shard_map/ppermute | solution.py:24
  63.0 18.9 %collective-permute-start.12 = (bf16[1024,128]{1,0:T(8,128)(2,1)}, bf16[1024,128]{1,0:T(8,128)(2,1)S(1)}, u32[]{:S(2)}, u32[]{:S(2)}) collective-permute-start(bf16[1024,128]{1,0:T(8,128)(2,1)} %get-tuple-element.36), channel_id=1, source_target_pairs={{0,4},{4,0},{8,12},{12,8},{16,20},{20,16},{24,28},{28,24},{1,5},{5... | collective-permute-start | bytes 786440 | tf_op jit(solution)/shard_map/ppermute | solution.py:24
  63.8 31.0 %copy-start.7 = (bf16[512,128]{1,0:T(8,128)(2,1)S(1)}, bf16[512,128]{1,0:T(8,128)(2,1)}, u32[]{:S(2)}) copy-start(bf16[512,128]{1,0:T(8,128)(2,1)} %get-tuple-element.34) | copy-start | bytes 393220
  69.3 9.8 %collective-permute-start.20 = (bf16[1024,128]{1,0:T(8,128)(2,1)}, bf16[1024,128]{1,0:T(8,128)(2,1)S(1)}, u32[]{:S(2)}, u32[]{:S(2)}) collective-permute-start(bf16[1024,128]{1,0:T(8,128)(2,1)} %get-tuple-element.44), channel_id=1, source_target_pairs={{0,4},{4,0},{8,12},{12,8},{16,20},{20,16},{24,28},{28,24},{1,5},{5... | collective-permute-start | bytes 786440 | tf_op jit(solution)/shard_map/ppermute | solution.py:24
  70.7 18.4 %collective-permute-start.22 = (bf16[1024,128]{1,0:T(8,128)(2,1)}, bf16[1024,128]{1,0:T(8,128)(2,1)S(1)}, u32[]{:S(2)}, u32[]{:S(2)}) collective-permute-start(bf16[1024,128]{1,0:T(8,128)(2,1)} %get-tuple-element.45), channel_id=1, source_target_pairs={{0,4},{4,0},{8,12},{12,8},{16,20},{20,16},{24,28},{28,24},{1,5},{5... | collective-permute-start | bytes 786440 | tf_op jit(solution)/shard_map/ppermute | solution.py:24
  77.3 9.2 %collective-permute-start.11 = (bf16[1024,128]{1,0:T(8,128)(2,1)S(1)}, bf16[1024,128]{1,0:T(8,128)(2,1)S(1)}, u32[]{:S(2)}, u32[]{:S(2)}) collective-permute-start(bf16[1024,128]{1,0:T(8,128)(2,1)S(1)} %pad_maximum_fusion), channel_id=1, source_target_pairs={{0,8},{4,12},{8,0},{12,4},{16,24},{20,28},{24,16},{28,20},{1,9},{5... | collective-permute-start | bytes 786440 | tf_op jit(solution)/shard_map/ppermute | solution.py:24
  80.2 11.2 %collective-permute-start.21 = (bf16[1024,128]{1,0:T(8,128)(2,1)S(1)}, bf16[1024,128]{1,0:T(8,128)(2,1)S(1)}, u32[]{:S(2)}, u32[]{:S(2)}) collective-permute-start(bf16[1024,128]{1,0:T(8,128)(2,1)S(1)} %pad_maximum_fusion.1), channel_id=1, source_target_pairs={{0,8},{4,12},{8,0},{12,4},{16,24},{20,28},{24,16},{28,20},{1,9},{5... | collective-permute-start | bytes 786440 | tf_op jit(solution)/shard_map/ppermute | solution.py:24
  86.6 8.2 %collective-permute-start.13 = (bf16[512,128]{1,0:T(8,128)(2,1)S(1)}, bf16[512,128]{1,0:T(8,128)(2,1)S(1)}, u32[]{:S(2)}, u32[]{:S(2)}) collective-permute-start(bf16[512,128]{1,0:T(8,128)(2,1)S(1)} %add_convert_fusion.8), channel_id=1, source_target_pairs={{0,24},{4,28},{8,16},{12,20},{16,8},{20,12},{24,0},{28,4},{1,25},{... | collective-permute-start | bytes 393224 | tf_op jit(solution)/shard_map/ppermute | solution.py:24
  92.4 6.9 %collective-permute-start.23 = (bf16[512,128]{1,0:T(8,128)(2,1)S(1)}, bf16[512,128]{1,0:T(8,128)(2,1)S(1)}, u32[]{:S(2)}, u32[]{:S(2)}) collective-permute-start(bf16[512,128]{1,0:T(8,128)(2,1)S(1)} %add_convert_fusion.1), channel_id=1, source_target_pairs={{0,24},{4,28},{8,16},{12,20},{16,8},{20,12},{24,0},{28,4},{1,25},{... | collective-permute-start | bytes 393224 | tf_op jit(solution)/shard_map/ppermute | solution.py:24
  100.1 5.8 %collective-permute-start.24 = (bf16[128,256]{1,0:T(8,128)(2,1)S(1)}, bf16[128,256]{1,0:T(8,128)(2,1)S(1)}, u32[]{:S(2)}, u32[]{:S(2)}) collective-permute-start(bf16[128,256]{1,0:T(8,128)(2,1)S(1)} %get-tuple-element.53), channel_id=1, source_target_pairs={{0,1},{1,0},{2,3},{3,2},{4,5},{5,4},{6,7},{7,6},{8,9},{9,8},{10,11... | collective-permute-start | bytes 196616 | tf_op jit(solution)/shard_map/ppermute | solution.py:24
  100.1 5.8 %collective-permute-start.25 = (bf16[128,256]{1,0:T(8,128)(2,1)S(1)}, bf16[128,256]{1,0:T(8,128)(2,1)S(1)}, u32[]{:S(2)}, u32[]{:S(2)}) collective-permute-start(bf16[128,256]{1,0:T(8,128)(2,1)S(1)} %get-tuple-element.54), channel_id=1, source_target_pairs={{0,2},{1,3},{2,0},{3,1},{4,6},{5,7},{6,4},{7,5},{8,10},{9,11},{10,... | collective-permute-start | bytes 196616 | tf_op jit(solution)/shard_map/ppermute | solution.py:24
  101.5 4.4 %collective-permute-start.26 = (bf16[128,256]{1,0:T(8,128)(2,1)S(1)}, bf16[128,256]{1,0:T(8,128)(2,1)S(1)}, u32[]{:S(2)}, u32[]{:S(2)}) collective-permute-start(bf16[128,256]{1,0:T(8,128)(2,1)S(1)} %get-tuple-element.51), channel_id=1, source_target_pairs={{0,3},{1,2},{2,1},{3,0},{4,7},{5,6},{6,5},{7,4},{8,11},{9,10},{10,... | collective-permute-start | bytes 196616 | tf_op jit(solution)/shard_map/ppermute | solution.py:24
  (14 other events, 116.2 us)

commit v2 on v1

--- a/solution.py
+++ b/solution.py
@@ -32,6 +32,16 @@
         out_specs=out_specs,
         scratch_shapes=scratch_shapes,
     )
+
+
+def room_for(*arrays, extra=0):
+    total = extra
+    for shape, kind in arrays:
+        size = jnp.dtype(kind).itemsize
+        for dim in shape:
+            size *= dim
+        total += size
+    return pltpu.CompilerParams(vmem_limit_bytes=int(total * 1.25) + (2 << 20))
 
 
 def cost(flops, moved, transcendentals=0):
@@ -71,6 +81,9 @@
             [pltpu.VMEM((rows, width), BF16)],
         ),
         out_shape=[jax.ShapeDtypeStruct((rows + blocks, cols), BF16)] * parts,
+        compiler_params=room_for(
+            ((2, width, width), BF16), ((8, rows + blocks, width), BF16), ((rows, width), F32)
+        ),
         cost_estimate=cost(2 * rows * width * width, 2 * width * width + 4 * rows * width),
         name="queries",
     )(me, candidates, w_qu, block_owner)
@@ -94,6 +107,9 @@
             pl.BlockSpec((1, rows, cols), lambda k, m: (k, 0, 0)),
         ),
         out_shape=jax.ShapeDtypeStruct((parts, rows, cols), F32),
+        compiler_params=room_for(
+            ((2, width, cols), BF16), ((2, rows, width), BF16), ((4, rows, cols), F32)
+        ),
         cost_estimate=cost(2 * rows * width * width, 2 * width * width + 6 * rows * width),
         name="gate",
     )(me, candidates, w_qu)
@@ -132,6 +148,12 @@
         cost_estimate=cost(
             4 * rows * width * cols * count,
             2 * rows * width + 4 * width * cols * count + 4 * rows * cols * count,
+        ),
+        compiler_params=room_for(
+            ((2, step, width), BF16),
+            ((4 * count, width, cols), BF16),
+            ((4 * count, step, cols), BF16),
+            ((2, step, cols), F32),
         ),
     )(me, history, *[w_kv] * (2 * count))
     return [made[k * each : (k + 1) * each] for k in range(count)]
@@ -178,19 +200,16 @@
                 if number == 0:
                     total[rows, :] = jnp.zeros((cands, HEAD), BF16)
                     return
-                sums = None
-                for t in range(number):
-                    at = pl.ds(base + t * TILE, TILE)
-                    scores = lax.dot_general(
-                        asked[rows, :],
-                        packed[at, :HEAD],
-                        (((1,), (1,)), ((), ())),
-                        preferred_element_type=F32,
-                    )
-                    h = scores * half
-                    weights = (h + h * jnp.tanh(h)).astype(BF16)
-                    part = jnp.dot(weights, packed[at, HEAD:], preferred_element_type=F32)
-                    sums = part if sums is None else sums + part
+                at = pl.ds(base, number * TILE)
+                scores = lax.dot_general(
+                    asked[rows, :],
+                    packed[at, :HEAD],
+                    (((1,), (1,)), ((), ())),
+                    preferred_element_type=F32,
+                )
+                h = scores * half
+                weights = (h + h * jnp.tanh(h)).astype(BF16)
+                sums = jnp.dot(weights, packed[at, HEAD:], preferred_element_type=F32)
                 total[rows, :] = sums.astype(BF16)
 
         return carry
@@ -221,6 +240,11 @@
             pltpu.VMEM((len(codes) * cands, HEAD), BF16),
             pltpu.VMEM((len(codes) * cands, HEAD), BF16),
         ],
+        compiler_params=room_for(
+            ((n_req * room + rows, 2 * HEAD), BF16),
+            ((5 * len(codes) * cands, HEAD), BF16),
+            ((2, cands, room), F32),
+        ),
         cost_estimate=cost(
             8 * rows * cands * HEAD * share,
             4 * rows * HEAD + 4 * len(codes) * cands * HEAD,
@@ -254,6 +278,7 @@
         in_specs=[pl.BlockSpec(memory_space=pltpu.SMEM)] + [vmem] * (3 + len(parts)),
         out_specs=vmem,
         out_shape=jax.ShapeDtypeStruct((rows, width), BF16),
+        compiler_params=room_for(((width, width), BF16), ((8, rows, width), F32)),
         cost_estimate=cost(2 * rows * width * width, 2 * width * width + 10 * rows * width),
         name="finish",
     )(me, candidates, gate, w_out, *parts)

time: 110 us -> 108 us (0.982); the launches traced: 110 us -> 106 us
  Pallas kernels: 41.5 us -> 22.6 us
  local copies, waits for them, and re-layouts: 2.86 us -> 15.2 us
  waiting for transfers between devices: 26 us -> 29.3 us
  other arithmetic: 4.53 us -> 1.65 us
  starting transfers between devices: 34.6 us -> 37.4 us
    unnamed x44 -> x28, local copies, waits for them, and re-layouts: 2.37 us -> 11.3 us
    pallas_call x4, Pallas kernels: 22.4 us -> 13.7 us  [attend(): pl.pallas_call(functools.partial(attend_kernel, source, sink, events, roo...]
    pallas_call x2, Pallas kernels: 9.12 us -> 5.74 us  [project_keys_values(): pl.pallas_call(functools.partial(keys_values_kernel, count, each), grid_s...]
    ppermute x27, waiting for transfers between devices: 26 us -> 29.3 us  [swap(): return lax.ppermute(value, axis, [(i, i ^ mask) for i in range(count)])]
    ppermute x27, starting transfers between devices: 34.6 us -> 37.4 us  [swap(): return lax.ppermute(value, axis, [(i, i ^ mask) for i in range(count)])]
    pallas_call x1, Pallas kernels: 3.98 us -> 1.35 us  [project_gate(): pl.pallas_call(gate_kernel, grid_spec=scalar_grid((parts,), [pl.BlockSpec...]
    pallas_call x1, Pallas kernels: 2.81 us -> 0.51 us  [project_queries(): pl.pallas_call(query_kernel, grid_spec=scalar_grid((1,), [pl.BlockSpec((r...]
    slice x4, local copies, waits for them, and re-layouts: 0.44 us -> 2.56 us  [on_device(): owners = jnp.concatenate([a[mine:, 0] for a in arrived]).astype(jnp.int32)]
  transfers between devices with their start and end apart: 27 -> 27, of which waited for: 8 -> 12; matrix products, arithmetic and copies ran while one was open for 4% -> 10% of each run, Pallas kernels for 32% -> 20%
where the time goes in v2:
time: 108 us; the launch traced here: 106 us
  starting transfers between devices  37.4 us (35%)
  waiting for transfers between devices  29.3 us (27%)
  Pallas kernels  22.6 us (21%)
  local copies, waits for them, and re-layouts  15.2 us (14%)
  other arithmetic  1.65 us (2%)
    ppermute x27, starting transfers between devices, swap(): return lax.ppermute(value, axis, [(i, i ^ mask) for i in range(count)])  37.4 us
    ppermute x27, waiting for transfers between devices, swap(): return lax.ppermute(value, axis, [(i, i ^ mask) for i in range(count)])  29.3 us
    pallas_call x4, Pallas kernels, attend(): pl.pallas_call(functools.partial(attend_kernel, source, sink, events, roo...  13.7 us
    unnamed x28, local copies, waits for them, and re-layouts  11.3 us
    pallas_call x2, Pallas kernels, project_keys_values(): pl.pallas_call(functools.partial(keys_values_kernel, count, each), grid_s...  5.74 us
    slice x4, local copies, waits for them, and re-layouts, on_device(): owners = jnp.concatenate([a[mine:, 0] for a in arrived]).astype(jnp.int32)  2.56 us
  transfers between devices with their start and end apart: 27, of which 12 were waited for; matrix products, arithmetic and copies ran while one was open for 10% of the time, Pallas kernels for 20%

profile of v2, /device:TPU:0, one launch (start us, length us, event | category | flops | bytes accessed | tf_op | source)
XLA Modules:
  0.0 106.4 jit_solution(5160966941952647506)
XLA Ops:
  0.7 2.3 %copy-done.1 = bf16[1024,2048]{1,0:T(8,128)(2,1)S(1)} copy-done((bf16[1024,2048]{1,0:T(8,128)(2,1)S(1)}, bf16[1024,2048]{1,0:T(8,128)(2,1)}, u32[]{:S(2)}) %copy-start.1) | copy-done | bytes 4194328
  5.3 2.6 %collective-permute-start.1 = (bf16[176,256]{1,0:T(8,128)(2,1)S(1)}, bf16[176,256]{1,0:T(8,128)(2,1)}, u32[]{:S(2)}, u32[]{:S(2)}) collective-permute-start(bf16[176,256]{1,0:T(8,128)(2,1)S(1)} %get-tuple-element.28), channel_id=1, source_target_pairs={{0,2},{1,3},{2,0},{3,1},{4,6},{5,7},{6,4},{7,5},{8,10},{9,11},{10,... | collective-permute-start | bytes 270344 | tf_op jit(solution)/shard_map/ppermute | solution.py:24
  9.3 3.0 %shard_map.100 = (bf16[768,256]{1,0:T(8,128)(2,1)S(1)}, bf16[768,256]{1,0:T(8,128)(2,1)S(1)}, bf16[768,256]{1,0:T(8,128)(2,1)}, bf16[768,256]{1,0:T(8,128)(2,1)S(1)}) custom-call(s32[1]{0:T(128)} %bitcast._.me_ref, bf16[768,1024]{1,0:T(8,128)(2,1)S(1)} %copy-done.3, bf16[1024,2048]{1,0:T(8,128)(2,1)S(1)} %copy-done, bf16[1024,2048]{1,0:T(8,128)(2,1)S(1)} %copy-done, ...), custom_call_target="tpu_custom_call" | custom-call | flops 1610612736 | bytes 5242880 | tf_op jit(solution)/shard_map/pallas_call | solution.py:139
  12.5 2.7 %shard_map.101 = (bf16[768,256]{1,0:T(8,128)(2,1)}, bf16[768,256]{1,0:T(8,128)(2,1)S(1)}, bf16[768,256]{1,0:T(8,128)(2,1)S(1)}, bf16[768,256]{1,0:T(8,128)(2,1)S(1)}) custom-call(s32[1]{0:T(128)} %bitcast._.me_ref, bf16[768,1024]{1,0:T(8,128)(2,1)S(1)} %copy-done.3, bf16[1024,2048]{1,0:T(8,128)(2,1)S(1)} %copy-done, bf16[1024,2048]{1,0:T(8,128)(2,1)S(1)} %copy-done, ...), custom_call_target="tpu_custom_call" | custom-call | flops 1610612736 | bytes 5242880 | tf_op jit(solution)/shard_map/pallas_call | solution.py:139
  15.2 1.9 %collective-permute-start.4 = (bf16[768,256]{1,0:T(8,128)(2,1)}, bf16[768,256]{1,0:T(8,128)(2,1)S(1)}, u32[]{:S(2)}, u32[]{:S(2)}) collective-permute-start(bf16[768,256]{1,0:T(8,128)(2,1)} %get-tuple-element.32), channel_id=1, source_target_pairs={{0,2},{1,3},{2,0},{3,1},{4,6},{5,7},{6,4},{7,5},{8,10},{9,11},{10,... | collective-permute-start | bytes 1179656 | tf_op jit(solution)/shard_map/ppermute | solution.py:24
  23.1 3.7 %collective-permute-start.6 = (bf16[512,128]{1,0:T(8,128)(2,1)S(1)}, bf16[512,128]{1,0:T(8,128)(2,1)S(1)}, u32[]{:S(2)}, u32[]{:S(2)}) collective-permute-start(bf16[512,128]{1,0:T(8,128)(2,1)S(1)} %pad_maximum_fusion.2.refs_4_), channel_id=1, source_target_pairs={{0,24},{4,28},{8,16},{12,20},{16,8},{20,12},{24,0},{28,4},{1,25},{... | collective-permute-start | bytes 393224 | tf_op jit(solution)/shard_map/ppermute | solution.py:24
  26.8 1.6 %collective-permute-start.17 = (bf16[512,128]{1,0:T(8,128)(2,1)S(1)}, bf16[512,128]{1,0:T(8,128)(2,1)S(1)}, u32[]{:S(2)}, u32[]{:S(2)}) collective-permute-start(bf16[512,128]{1,0:T(8,128)(2,1)S(1)} %pad_maximum_fusion.3.refs_4_), channel_id=1, source_target_pairs={{0,4},{4,0},{8,12},{12,8},{16,20},{20,16},{24,28},{28,24},{1,5},{5... | collective-permute-start | bytes 393224 | tf_op jit(solution)/shard_map/ppermute | solution.py:24
  29.2 2.0 %collective-permute-done.6.refs_5_ = bf16[512,128]{1,0:T(8,128)(2,1)S(1)} collective-permute-done((bf16[512,128]{1,0:T(8,128)(2,1)S(1)}, bf16[512,128]{1,0:T(8,128)(2,1)S(1)}, u32[]{:S(2)}, u32[]{:S(2)}) %collective-permute-start.6) | collective-permute-done | bytes 131104 | tf_op jit(solution)/shard_map/ppermute | solution.py:24
  31.8 2.4 %collective-permute-start.8 = (bf16[1024,128]{1,0:T(8,128)(2,1)}, bf16[1024,128]{1,0:T(8,128)(2,1)S(1)}, u32[]{:S(2)}, u32[]{:S(2)}) collective-permute-start(bf16[1024,128]{1,0:T(8,128)(2,1)} %constant_dynamic-update-slice_fusion), channel_id=1, source_target_pairs={{0,8},{4,12},{8,0},{12,4},{16,24},{20,28},{24,16},{28,20},{1,9},{5... | collective-permute-start | bytes 786440 | tf_op jit(solution)/shard_map/ppermute | solution.py:24
  34.9 2.5 %collective-permute-start.18 = (bf16[1024,128]{1,0:T(8,128)(2,1)}, bf16[1024,128]{1,0:T(8,128)(2,1)S(1)}, u32[]{:S(2)}, u32[]{:S(2)}) collective-permute-start(bf16[1024,128]{1,0:T(8,128)(2,1)} %get-tuple-element.56), channel_id=1, source_target_pairs={{0,24},{4,28},{8,16},{12,20},{16,8},{20,12},{24,0},{28,4},{1,25},{... | collective-permute-start | bytes 786440 | tf_op jit(solution)/shard_map/ppermute | solution.py:24
  39.0 2.2 %collective-permute-done.8.refs_7_ = bf16[1024,128]{1,0:T(8,128)(2,1)S(1)} collective-permute-done((bf16[1024,128]{1,0:T(8,128)(2,1)}, bf16[1024,128]{1,0:T(8,128)(2,1)S(1)}, u32[]{:S(2)}, u32[]{:S(2)}) %collective-permute-start.8) | collective-permute-done | bytes 262176 | tf_op jit(solution)/shard_map/ppermute | solution.py:24
  41.2 1.5 %collective-permute-start.9 = (bf16[1024,128]{1,0:T(8,128)(2,1)S(1)}, bf16[1024,128]{1,0:T(8,128)(2,1)S(1)}, u32[]{:S(2)}, u32[]{:S(2)}) collective-permute-start(bf16[1024,128]{1,0:T(8,128)(2,1)S(1)} %collective-permute-done.8.refs_7_), channel_id=1, source_target_pairs={{0,4},{4,0},{8,12},{12,8},{16,20},{20,16},{24,28},{28,24},{1,5},{5... | collective-permute-start | bytes 786440 | tf_op jit(solution)/shard_map/ppermute | solution.py:24
  42.8 5.6 %collective-permute-done.18.refs_5_ = bf16[1024,128]{1,0:T(8,128)(2,1)S(1)} collective-permute-done((bf16[1024,128]{1,0:T(8,128)(2,1)}, bf16[1024,128]{1,0:T(8,128)(2,1)S(1)}, u32[]{:S(2)}, u32[]{:S(2)}) %collective-permute-start.18) | collective-permute-done | bytes 262176 | tf_op jit(solution)/shard_map/ppermute | solution.py:24
  49.5 1.6 %collective-permute-start.15 = (bf16[768,256]{1,0:T(8,128)(2,1)S(1)}, bf16[768,256]{1,0:T(8,128)(2,1)S(1)}, u32[]{:S(2)}, u32[]{:S(2)}) collective-permute-start(bf16[768,256]{1,0:T(8,128)(2,1)S(1)} %get-tuple-element.40), channel_id=1, source_target_pairs={{0,2},{1,3},{2,0},{3,1},{4,6},{5,7},{6,4},{7,5},{8,10},{9,11},{10,... | collective-permute-start | bytes 1179656 | tf_op jit(solution)/shard_map/ppermute | solution.py:24
  51.3 1.5 %collective-permute-start.7 = (bf16[1024,128]{1,0:T(8,128)(2,1)}, bf16[1024,128]{1,0:T(8,128)(2,1)S(1)}, u32[]{:S(2)}, u32[]{:S(2)}) collective-permute-start(bf16[1024,128]{1,0:T(8,128)(2,1)} %constant_dynamic-update-slice_fusion), channel_id=1, source_target_pairs={{0,4},{4,0},{8,12},{12,8},{16,20},{20,16},{24,28},{28,24},{1,5},{5... | collective-permute-start | bytes 786440 | tf_op jit(solution)/shard_map/ppermute | solution.py:24
  53.0 2.2 %shard_map.103 = bf16[1024,128]{1,0:T(8,128)(2,1)S(1)} custom-call(s32[192]{0:T(256)S(1)} %multiply_add_fusion.pos_ref, s32[8]{0:T(128)S(1)} %convert_reduce_fusion.1.count_ref, s32[2]{0:T(128)S(1)} %copy-done.7, bf16[768,256]{1,0:T(8,128)(2,1)S(1)} %get-tuple-element.30.refs_0_, bf16[768,256]{1,0:T(8,128)(2,1)S(1)} %collective-permute-done.3.refs_1_, ...), custom_call_target="tpu_custom_call" | custom-call | flops 402653184 | bytes 2097152 | tf_op jit(solution)/shard_map/pallas_call | solution.py:233
  55.2 4.9 %collective-permute-done.7.refs_6_ = bf16[1024,128]{1,0:T(8,128)(2,1)S(1)} collective-permute-done((bf16[1024,128]{1,0:T(8,128)(2,1)}, bf16[1024,128]{1,0:T(8,128)(2,1)S(1)}, u32[]{:S(2)}, u32[]{:S(2)}) %collective-permute-start.7) | collective-permute-done | bytes 262176 | tf_op jit(solution)/shard_map/ppermute | solution.py:24
  60.1 1.5 %collective-permute-start.10 = (bf16[1024,128]{1,0:T(8,128)(2,1)S(1)}, bf16[1024,128]{1,0:T(8,128)(2,1)S(1)}, u32[]{:S(2)}, u32[]{:S(2)}) collective-permute-start(bf16[1024,128]{1,0:T(8,128)(2,1)S(1)} %shard_map.103), channel_id=1, source_target_pairs={{0,4},{4,0},{8,12},{12,8},{16,20},{20,16},{24,28},{28,24},{1,5},{5... | collective-permute-start | bytes 786440 | tf_op jit(solution)/shard_map/ppermute | solution.py:24
  61.6 4.7 %shard_map.102 = (bf16[512,128]{1,0:T(8,128)(2,1)S(1)}, bf16[1024,128]{1,0:T(8,128)(2,1)S(1)}, bf16[1024,128]{1,0:T(8,128)(2,1)S(1)}, bf16[512,128]{1,0:T(8,128)(2,1)S(1)}) custom-call(s32[192]{0:T(256)S(1)} %multiply_add_fusion.pos_ref, s32[8]{0:T(128)S(1)} %convert_reduce_fusion.1.count_ref, s32[6]{0:T(128)S(1)} %copy-done.10, ...), custom_call_target="tpu_custom_call" | custom-call | flops 1207959552 | bytes 3145728 | tf_op jit(solution)/shard_map/pallas_call | solution.py:233
  66.9 1.9 %collective-permute-done.16.refs_3_ = bf16[768,256]{1,0:T(8,128)(2,1)S(1)} collective-permute-done((bf16[768,256]{1,0:T(8,128)(2,1)S(1)}, bf16[768,256]{1,0:T(8,128)(2,1)S(1)}, u32[]{:S(2)}, u32[]{:S(2)}) %collective-permute-start.16) | collective-permute-done | bytes 393248 | tf_op jit(solution)/shard_map/ppermute | solution.py:24
  68.9 3.4 %shard_map.105 = (bf16[1024,128]{1,0:T(8,128)(2,1)S(1)}, bf16[1024,128]{1,0:T(8,128)(2,1)S(1)}) custom-call(s32[192]{0:T(256)S(1)} %multiply_add_fusion.pos_ref, s32[8]{0:T(128)S(1)} %convert_reduce_fusion.1.count_ref, s32[4]{0:T(128)S(1)} %copy-done.9, bf16[768,256]{1,0:T(8,128)(2,1)S(1)} %get-tuple-element.38.refs_0_, ...), custom_call_target="tpu_custom_call" | custom-call | flops 805306368 | bytes 2621440 | tf_op jit(solution)/shard_map/pallas_call | solution.py:233
  72.2 1.6 %collective-permute-start.20 = (bf16[1024,128]{1,0:T(8,128)(2,1)S(1)}, bf16[1024,128]{1,0:T(8,128)(2,1)S(1)}, u32[]{:S(2)}, u32[]{:S(2)}) collective-permute-start(bf16[1024,128]{1,0:T(8,128)(2,1)S(1)} %get-tuple-element.44), channel_id=1, source_target_pairs={{0,4},{4,0},{8,12},{12,8},{16,20},{20,16},{24,28},{28,24},{1,5},{5... | collective-permute-start | bytes 786440 | tf_op jit(solution)/shard_map/ppermute | solution.py:24
  74.3 3.5 %shard_map.104 = (bf16[512,128]{1,0:T(8,128)(2,1)S(1)}, bf16[1024,128]{1,0:T(8,128)(2,1)S(1)}, bf16[512,128]{1,0:T(8,128)(2,1)S(1)}) custom-call(s32[192]{0:T(256)S(1)} %multiply_add_fusion.pos_ref, s32[8]{0:T(128)S(1)} %convert_reduce_fusion.1.count_ref, s32[4]{0:T(128)S(1)} %copy-done.8, bf16[768,256]{1,0:T(8,128)(2,1)S(1)} %get-tuple-element.38.refs_0_, ...), custom_call_target="tpu_custom_call" | custom-call | flops 805306368 | bytes 2621440 | tf_op jit(solution)/shard_map/pallas_call | solution.py:233
  77.9 2.1 %collective-permute-start.11 = (bf16[1024,128]{1,0:T(8,128)(2,1)S(1)}, bf16[1024,128]{1,0:T(8,128)(2,1)S(1)}, u32[]{:S(2)}, u32[]{:S(2)}) collective-permute-start(bf16[1024,128]{1,0:T(8,128)(2,1)S(1)} %pad_maximum_fusion), channel_id=1, source_target_pairs={{0,8},{4,12},{8,0},{12,4},{16,24},{20,28},{24,16},{28,20},{1,9},{5... | collective-permute-start | bytes 786440 | tf_op jit(solution)/shard_map/ppermute | solution.py:24
  80.0 1.4 %collective-permute-done.20 = bf16[1024,128]{1,0:T(8,128)(2,1)S(1)} collective-permute-done((bf16[1024,128]{1,0:T(8,128)(2,1)S(1)}, bf16[1024,128]{1,0:T(8,128)(2,1)S(1)}, u32[]{:S(2)}, u32[]{:S(2)}) %collective-permute-start.20) | collective-permute-done | bytes 262176 | tf_op jit(solution)/shard_map/ppermute | solution.py:24
  81.6 2.2 %collective-permute-start.21 = (bf16[1024,128]{1,0:T(8,128)(2,1)S(1)}, bf16[1024,128]{1,0:T(8,128)(2,1)S(1)}, u32[]{:S(2)}, u32[]{:S(2)}) collective-permute-start(bf16[1024,128]{1,0:T(8,128)(2,1)S(1)} %pad_maximum_fusion.1), channel_id=1, source_target_pairs={{0,8},{4,12},{8,0},{12,4},{16,24},{20,28},{24,16},{28,20},{1,9},{5... | collective-permute-start | bytes 786440 | tf_op jit(solution)/shard_map/ppermute | solution.py:24
  83.8 3.4 %collective-permute-done.11 = bf16[1024,128]{1,0:T(8,128)(2,1)S(1)} collective-permute-done((bf16[1024,128]{1,0:T(8,128)(2,1)S(1)}, bf16[1024,128]{1,0:T(8,128)(2,1)S(1)}, u32[]{:S(2)}, u32[]{:S(2)}) %collective-permute-start.11) | collective-permute-done | bytes 262176 | tf_op jit(solution)/shard_map/ppermute | solution.py:24
  87.3 3.1 %collective-permute-start.13 = (bf16[512,128]{1,0:T(8,128)(2,1)S(1)}, bf16[512,128]{1,0:T(8,128)(2,1)S(1)}, u32[]{:S(2)}, u32[]{:S(2)}) collective-permute-start(bf16[512,128]{1,0:T(8,128)(2,1)S(1)} %add_convert_fusion.8), channel_id=1, source_target_pairs={{0,24},{4,28},{8,16},{12,20},{16,8},{20,12},{24,0},{28,4},{1,25},{... | collective-permute-start | bytes 393224 | tf_op jit(solution)/shard_map/ppermute | solution.py:24
  90.4 1.9 %collective-permute-done.21 = bf16[1024,128]{1,0:T(8,128)(2,1)S(1)} collective-permute-done((bf16[1024,128]{1,0:T(8,128)(2,1)S(1)}, bf16[1024,128]{1,0:T(8,128)(2,1)S(1)}, u32[]{:S(2)}, u32[]{:S(2)}) %collective-permute-start.21) | collective-permute-done | bytes 262176 | tf_op jit(solution)/shard_map/ppermute | solution.py:24
  92.4 3.4 %collective-permute-start.23 = (bf16[512,128]{1,0:T(8,128)(2,1)S(1)}, bf16[512,128]{1,0:T(8,128)(2,1)S(1)}, u32[]{:S(2)}, u32[]{:S(2)}) collective-permute-start(bf16[512,128]{1,0:T(8,128)(2,1)S(1)} %add_convert_fusion.1), channel_id=1, source_target_pairs={{0,24},{4,28},{8,16},{12,20},{16,8},{20,12},{24,0},{28,4},{1,25},{... | collective-permute-start | bytes 393224 | tf_op jit(solution)/shard_map/ppermute | solution.py:24
  96.7 2.6 %collective-permute-done.23 = bf16[512,128]{1,0:T(8,128)(2,1)S(1)} collective-permute-done((bf16[512,128]{1,0:T(8,128)(2,1)S(1)}, bf16[512,128]{1,0:T(8,128)(2,1)S(1)}, u32[]{:S(2)}, u32[]{:S(2)}) %collective-permute-start.23) | collective-permute-done | bytes 131104 | tf_op jit(solution)/shard_map/ppermute | solution.py:24
  99.4 1.6 %collective-permute-start.25 = (bf16[128,256]{1,0:T(8,128)(2,1)S(1)}, bf16[128,256]{1,0:T(8,128)(2,1)S(1)}, u32[]{:S(2)}, u32[]{:S(2)}) collective-permute-start(bf16[128,256]{1,0:T(8,128)(2,1)S(1)} %get-tuple-element.54), channel_id=1, source_target_pairs={{0,2},{1,3},{2,0},{3,1},{4,6},{5,7},{6,4},{7,5},{8,10},{9,11},{10,... | collective-permute-start | bytes 196616 | tf_op jit(solution)/shard_map/ppermute | solution.py:24
  (80 shorter events, 23.6 us)
Async XLA Ops:
  4.7 13.2 %collective-permute-start = (bf16[176,256]{1,0:T(8,128)(2,1)S(1)}, bf16[176,256]{1,0:T(8,128)(2,1)}, u32[]{:S(2)}, u32[]{:S(2)}) collective-permute-start(bf16[176,256]{1,0:T(8,128)(2,1)S(1)} %get-tuple-element.27), channel_id=1, source_target_pairs={{0,1},{1,0},{2,3},{3,2},{4,5},{5,4},{6,7},{7,6},{8,9},{9,8},{10,11... | collective-permute-start | bytes 270344 | tf_op jit(solution)/shard_map/ppermute | solution.py:24
  5.3 14.1 %collective-permute-start.1 = (bf16[176,256]{1,0:T(8,128)(2,1)S(1)}, bf16[176,256]{1,0:T(8,128)(2,1)}, u32[]{:S(2)}, u32[]{:S(2)}) collective-permute-start(bf16[176,256]{1,0:T(8,128)(2,1)S(1)} %get-tuple-element.28), channel_id=1, source_target_pairs={{0,2},{1,3},{2,0},{3,1},{4,6},{5,7},{6,4},{7,5},{8,10},{9,11},{10,... | collective-permute-start | bytes 270344 | tf_op jit(solution)/shard_map/ppermute | solution.py:24
  7.8 13.0 %collective-permute-start.2 = (bf16[176,256]{1,0:T(8,128)(2,1)S(1)}, bf16[176,256]{1,0:T(8,128)(2,1)}, u32[]{:S(2)}, u32[]{:S(2)}) collective-permute-start(bf16[176,256]{1,0:T(8,128)(2,1)S(1)} %get-tuple-element.29), channel_id=1, source_target_pairs={{0,3},{1,2},{2,1},{3,0},{4,7},{5,6},{6,5},{7,4},{8,11},{9,10},{10,... | collective-permute-start | bytes 270344 | tf_op jit(solution)/shard_map/ppermute | solution.py:24
  12.3 40.7 %copy-start.7 = (s32[2]{0:T(128)S(1)}, s32[2]{0:T(128)}, u32[]{:S(2)}) copy-start(s32[2]{0:T(128)} %constant.22.clone.code_ref) | copy-start | bytes 28
  12.3 37.1 %collective-permute-start.3 = (bf16[768,256]{1,0:T(8,128)(2,1)}, bf16[768,256]{1,0:T(8,128)(2,1)S(1)}, u32[]{:S(2)}, u32[]{:S(2)}) collective-permute-start(bf16[768,256]{1,0:T(8,128)(2,1)} %get-tuple-element.31), channel_id=1, source_target_pairs={{0,1},{1,0},{2,3},{3,2},{4,5},{5,4},{6,7},{7,6},{8,9},{9,8},{10,11... | collective-permute-start | bytes 1179656 | tf_op jit(solution)/shard_map/ppermute | solution.py:24
  15.2 46.5 %copy-start.10 = (s32[6]{0:T(128)S(1)}, s32[6]{0:T(128)}, u32[]{:S(2)}) copy-start(s32[6]{0:T(128)} %constant.21.clone.code_ref) | copy-start | bytes 76
  15.2 34.3 %collective-permute-start.4 = (bf16[768,256]{1,0:T(8,128)(2,1)}, bf16[768,256]{1,0:T(8,128)(2,1)S(1)}, u32[]{:S(2)}, u32[]{:S(2)}) collective-permute-start(bf16[768,256]{1,0:T(8,128)(2,1)} %get-tuple-element.32), channel_id=1, source_target_pairs={{0,2},{1,3},{2,0},{3,1},{4,6},{5,7},{6,4},{7,5},{8,10},{9,11},{10,... | collective-permute-start | bytes 1179656 | tf_op jit(solution)/shard_map/ppermute | solution.py:24
  17.9 33.1 %collective-permute-start.5 = (bf16[768,256]{1,0:T(8,128)(2,1)S(1)}, bf16[768,256]{1,0:T(8,128)(2,1)S(1)}, u32[]{:S(2)}, u32[]{:S(2)}) collective-permute-start(bf16[768,256]{1,0:T(8,128)(2,1)S(1)} %get-tuple-element.33), channel_id=1, source_target_pairs={{0,3},{1,2},{2,1},{3,0},{4,7},{5,6},{6,5},{7,4},{8,11},{9,10},{10,... | collective-permute-start | bytes 1179656 | tf_op jit(solution)/shard_map/ppermute | solution.py:24
  22.3 46.6 %copy-start.9 = (s32[4]{0:T(128)S(1)}, s32[4]{0:T(128)}, u32[]{:S(2)}) copy-start(s32[4]{0:T(128)} %constant.23.clone.code_ref) | copy-start | bytes 52
  23.1 8.1 %collective-permute-start.6 = (bf16[512,128]{1,0:T(8,128)(2,1)S(1)}, bf16[512,128]{1,0:T(8,128)(2,1)S(1)}, u32[]{:S(2)}, u32[]{:S(2)}) collective-permute-start(bf16[512,128]{1,0:T(8,128)(2,1)S(1)} %pad_maximum_fusion.2.refs_4_), channel_id=1, source_target_pairs={{0,24},{4,28},{8,16},{12,20},{16,8},{20,12},{24,0},{28,4},{1,25},{... | collective-permute-start | bytes 393224 | tf_op jit(solution)/shard_map/ppermute | solution.py:24
  26.8 7.5 %collective-permute-start.17 = (bf16[512,128]{1,0:T(8,128)(2,1)S(1)}, bf16[512,128]{1,0:T(8,128)(2,1)S(1)}, u32[]{:S(2)}, u32[]{:S(2)}) collective-permute-start(bf16[512,128]{1,0:T(8,128)(2,1)S(1)} %pad_maximum_fusion.3.refs_4_), channel_id=1, source_target_pairs={{0,4},{4,0},{8,12},{12,8},{16,20},{20,16},{24,28},{28,24},{1,5},{5... | collective-permute-start | bytes 393224 | tf_op jit(solution)/shard_map/ppermute | solution.py:24
  31.8 9.4 %collective-permute-start.8 = (bf16[1024,128]{1,0:T(8,128)(2,1)}, bf16[1024,128]{1,0:T(8,128)(2,1)S(1)}, u32[]{:S(2)}, u32[]{:S(2)}) collective-permute-start(bf16[1024,128]{1,0:T(8,128)(2,1)} %constant_dynamic-update-slice_fusion), channel_id=1, source_target_pairs={{0,8},{4,12},{8,0},{12,4},{16,24},{20,28},{24,16},{28,20},{1,9},{5... | collective-permute-start | bytes 786440 | tf_op jit(solution)/shard_map/ppermute | solution.py:24
  34.9 13.5 %collective-permute-start.18 = (bf16[1024,128]{1,0:T(8,128)(2,1)}, bf16[1024,128]{1,0:T(8,128)(2,1)S(1)}, u32[]{:S(2)}, u32[]{:S(2)}) collective-permute-start(bf16[1024,128]{1,0:T(8,128)(2,1)} %get-tuple-element.56), channel_id=1, source_target_pairs={{0,24},{4,28},{8,16},{12,20},{16,8},{20,12},{24,0},{28,4},{1,25},{... | collective-permute-start | bytes 786440 | tf_op jit(solution)/shard_map/ppermute | solution.py:24
  41.2 10.1 %collective-permute-start.9 = (bf16[1024,128]{1,0:T(8,128)(2,1)S(1)}, bf16[1024,128]{1,0:T(8,128)(2,1)S(1)}, u32[]{:S(2)}, u32[]{:S(2)}) collective-permute-start(bf16[1024,128]{1,0:T(8,128)(2,1)S(1)} %collective-permute-done.8.refs_7_), channel_id=1, source_target_pairs={{0,4},{4,0},{8,12},{12,8},{16,20},{20,16},{24,28},{28,24},{1,5},{5... | collective-permute-start | bytes 786440 | tf_op jit(solution)/shard_map/ppermute | solution.py:24
  49.2 19.7 %collective-permute-start.19 = (bf16[2048,128]{1,0:T(8,128)(2,1)}, bf16[2048,128]{1,0:T(8,128)(2,1)S(1)}, u32[]{:S(2)}, u32[]{:S(2)}) collective-permute-start(bf16[2048,128]{1,0:T(8,128)(2,1)} %constant_dynamic-update-slice_fusion.10), channel_id=1, source_target_pairs={{0,8},{4,12},{8,0},{12,4},{16,24},{20,28},{24,16},{28,20},{1,9},{5... | collective-permute-start | bytes 1572872 | tf_op jit(solution)/shard_map/ppermute | solution.py:24
  49.4 17.0 %collective-permute-start.14 = (bf16[768,256]{1,0:T(8,128)(2,1)S(1)}, bf16[768,256]{1,0:T(8,128)(2,1)S(1)}, u32[]{:S(2)}, u32[]{:S(2)}) collective-permute-start(bf16[768,256]{1,0:T(8,128)(2,1)S(1)} %get-tuple-element.39), channel_id=1, source_target_pairs={{0,1},{1,0},{2,3},{3,2},{4,5},{5,4},{6,7},{7,6},{8,9},{9,8},{10,11... | collective-permute-start | bytes 1179656 | tf_op jit(solution)/shard_map/ppermute | solution.py:24
  49.5 17.4 %collective-permute-start.15 = (bf16[768,256]{1,0:T(8,128)(2,1)S(1)}, bf16[768,256]{1,0:T(8,128)(2,1)S(1)}, u32[]{:S(2)}, u32[]{:S(2)}) collective-permute-start(bf16[768,256]{1,0:T(8,128)(2,1)S(1)} %get-tuple-element.40), channel_id=1, source_target_pairs={{0,2},{1,3},{2,0},{3,1},{4,6},{5,7},{6,4},{7,5},{8,10},{9,11},{10,... | collective-permute-start | bytes 1179656 | tf_op jit(solution)/shard_map/ppermute | solution.py:24
  51.1 17.8 %collective-permute-start.16 = (bf16[768,256]{1,0:T(8,128)(2,1)S(1)}, bf16[768,256]{1,0:T(8,128)(2,1)S(1)}, u32[]{:S(2)}, u32[]{:S(2)}) collective-permute-start(bf16[768,256]{1,0:T(8,128)(2,1)S(1)} %get-tuple-element.41), channel_id=1, source_target_pairs={{0,3},{1,2},{2,1},{3,0},{4,7},{5,6},{6,5},{7,4},{8,11},{9,10},{10,... | collective-permute-start | bytes 1179656 | tf_op jit(solution)/shard_map/ppermute | solution.py:24
  51.3 8.8 %collective-permute-start.7 = (bf16[1024,128]{1,0:T(8,128)(2,1)}, bf16[1024,128]{1,0:T(8,128)(2,1)S(1)}, u32[]{:S(2)}, u32[]{:S(2)}) collective-permute-start(bf16[1024,128]{1,0:T(8,128)(2,1)} %constant_dynamic-update-slice_fusion), channel_id=1, source_target_pairs={{0,4},{4,0},{8,12},{12,8},{16,20},{20,16},{24,28},{28,24},{1,5},{5... | collective-permute-start | bytes 786440 | tf_op jit(solution)/shard_map/ppermute | solution.py:24
  60.1 17.7 %collective-permute-start.10 = (bf16[1024,128]{1,0:T(8,128)(2,1)S(1)}, bf16[1024,128]{1,0:T(8,128)(2,1)S(1)}, u32[]{:S(2)}, u32[]{:S(2)}) collective-permute-start(bf16[1024,128]{1,0:T(8,128)(2,1)S(1)} %shard_map.103), channel_id=1, source_target_pairs={{0,4},{4,0},{8,12},{12,8},{16,20},{20,16},{24,28},{28,24},{1,5},{5... | collective-permute-start | bytes 786440 | tf_op jit(solution)/shard_map/ppermute | solution.py:24
  66.3 17.5 %collective-permute-start.12 = (bf16[1024,128]{1,0:T(8,128)(2,1)S(1)}, bf16[1024,128]{1,0:T(8,128)(2,1)S(1)}, u32[]{:S(2)}, u32[]{:S(2)}) collective-permute-start(bf16[1024,128]{1,0:T(8,128)(2,1)S(1)} %get-tuple-element.36), channel_id=1, source_target_pairs={{0,4},{4,0},{8,12},{12,8},{16,20},{20,16},{24,28},{28,24},{1,5},{5... | collective-permute-start | bytes 786440 | tf_op jit(solution)/shard_map/ppermute | solution.py:24
  72.2 9.2 %collective-permute-start.20 = (bf16[1024,128]{1,0:T(8,128)(2,1)S(1)}, bf16[1024,128]{1,0:T(8,128)(2,1)S(1)}, u32[]{:S(2)}, u32[]{:S(2)}) collective-permute-start(bf16[1024,128]{1,0:T(8,128)(2,1)S(1)} %get-tuple-element.44), channel_id=1, source_target_pairs={{0,4},{4,0},{8,12},{12,8},{16,20},{20,16},{24,28},{28,24},{1,5},{5... | collective-permute-start | bytes 786440 | tf_op jit(solution)/shard_map/ppermute | solution.py:24
  73.8 27.5 %copy-start.2 = (bf16[1024,2048]{1,0:T(8,128)(2,1)S(1)}, bf16[1024,2048]{1,0:T(8,128)(2,1)}, u32[]{:S(2)}) copy-start(bf16[1024,2048]{1,0:T(8,128)(2,1)} %w_ref.4) | copy-start | bytes 12582916
  73.8 27.5 %copy-start.5 = (bf16[128,1024]{1,0:T(8,128)(2,1)S(1)}, bf16[128,1024]{1,0:T(8,128)(2,1)}, u32[]{:S(2)}) copy-start(bf16[128,1024]{1,0:T(8,128)(2,1)} %cand_ref.5) | copy-start | bytes 786436
  73.8 16.6 %collective-permute-start.22 = (bf16[1024,128]{1,0:T(8,128)(2,1)S(1)}, bf16[1024,128]{1,0:T(8,128)(2,1)S(1)}, u32[]{:S(2)}, u32[]{:S(2)}) collective-permute-start(bf16[1024,128]{1,0:T(8,128)(2,1)S(1)} %get-tuple-element.45), channel_id=1, source_target_pairs={{0,4},{4,0},{8,12},{12,8},{16,20},{20,16},{24,28},{28,24},{1,5},{5... | collective-permute-start | bytes 786440 | tf_op jit(solution)/shard_map/ppermute | solution.py:24
  77.9 9.2 %collective-permute-start.11 = (bf16[1024,128]{1,0:T(8,128)(2,1)S(1)}, bf16[1024,128]{1,0:T(8,128)(2,1)S(1)}, u32[]{:S(2)}, u32[]{:S(2)}) collective-permute-start(bf16[1024,128]{1,0:T(8,128)(2,1)S(1)} %pad_maximum_fusion), channel_id=1, source_target_pairs={{0,8},{4,12},{8,0},{12,4},{16,24},{20,28},{24,16},{28,20},{1,9},{5... | collective-permute-start | bytes 786440 | tf_op jit(solution)/shard_map/ppermute | solution.py:24
  81.6 10.8 %collective-permute-start.21 = (bf16[1024,128]{1,0:T(8,128)(2,1)S(1)}, bf16[1024,128]{1,0:T(8,128)(2,1)S(1)}, u32[]{:S(2)}, u32[]{:S(2)}) collective-permute-start(bf16[1024,128]{1,0:T(8,128)(2,1)S(1)} %pad_maximum_fusion.1), channel_id=1, source_target_pairs={{0,8},{4,12},{8,0},{12,4},{16,24},{20,28},{24,16},{28,20},{1,9},{5... | collective-permute-start | bytes 786440 | tf_op jit(solution)/shard_map/ppermute | solution.py:24
  87.3 9.3 %collective-permute-start.13 = (bf16[512,128]{1,0:T(8,128)(2,1)S(1)}, bf16[512,128]{1,0:T(8,128)(2,1)S(1)}, u32[]{:S(2)}, u32[]{:S(2)}) collective-permute-start(bf16[512,128]{1,0:T(8,128)(2,1)S(1)} %add_convert_fusion.8), channel_id=1, source_target_pairs={{0,24},{4,28},{8,16},{12,20},{16,8},{20,12},{24,0},{28,4},{1,25},{... | collective-permute-start | bytes 393224 | tf_op jit(solution)/shard_map/ppermute | solution.py:24
  92.4 6.8 %collective-permute-start.23 = (bf16[512,128]{1,0:T(8,128)(2,1)S(1)}, bf16[512,128]{1,0:T(8,128)(2,1)S(1)}, u32[]{:S(2)}, u32[]{:S(2)}) collective-permute-start(bf16[512,128]{1,0:T(8,128)(2,1)S(1)} %add_convert_fusion.1), channel_id=1, source_target_pairs={{0,24},{4,28},{8,16},{12,20},{16,8},{20,12},{24,0},{28,4},{1,25},{... | collective-permute-start | bytes 393224 | tf_op jit(solution)/shard_map/ppermute | solution.py:24
  99.4 3.3 %collective-permute-start.24 = (bf16[128,256]{1,0:T(8,128)(2,1)S(1)}, bf16[128,256]{1,0:T(8,128)(2,1)S(1)}, u32[]{:S(2)}, u32[]{:S(2)}) collective-permute-start(bf16[128,256]{1,0:T(8,128)(2,1)S(1)} %get-tuple-element.53), channel_id=1, source_target_pairs={{0,1},{1,0},{2,3},{3,2},{4,5},{5,4},{6,7},{7,6},{8,9},{9,8},{10,11... | collective-permute-start | bytes 196616 | tf_op jit(solution)/shard_map/ppermute | solution.py:24
  99.4 4.5 %collective-permute-start.25 = (bf16[128,256]{1,0:T(8,128)(2,1)S(1)}, bf16[128,256]{1,0:T(8,128)(2,1)S(1)}, u32[]{:S(2)}, u32[]{:S(2)}) collective-permute-start(bf16[128,256]{1,0:T(8,128)(2,1)S(1)} %get-tuple-element.54), channel_id=1, source_target_pairs={{0,2},{1,3},{2,0},{3,1},{4,6},{5,7},{6,4},{7,5},{8,10},{9,11},{10,... | collective-permute-start | bytes 196616 | tf_op jit(solution)/shard_map/ppermute | solution.py:24
  101.0 4.1 %collective-permute-start.26 = (bf16[128,256]{1,0:T(8,128)(2,1)S(1)}, bf16[128,256]{1,0:T(8,128)(2,1)S(1)}, u32[]{:S(2)}, u32[]{:S(2)}) collective-permute-start(bf16[128,256]{1,0:T(8,128)(2,1)S(1)} %get-tuple-element.51), channel_id=1, source_target_pairs={{0,3},{1,2},{2,1},{3,0},{4,7},{5,6},{6,5},{7,4},{8,11},{9,10},{10,... | collective-permute-start | bytes 196616 | tf_op jit(solution)/shard_map/ppermute | solution.py:24
  (6 other events, 54.7 us)

commit v3 on v2

--- a/solution.py
+++ b/solution.py
@@ -10,6 +10,7 @@
 
 HEAD = 128
 TILE = 256
+MOST_DIRECT = 4
 BF16 = jnp.bfloat16
 F32 = jnp.float32
 
@@ -54,20 +55,23 @@
     outs, made = refs[:-1], refs[-1]
     rows = cand_ref.shape[0]
     cols = outs[0].shape[1]
-    blocks = owner_ref.shape[0]
+    blocks = owner_ref.shape[1]
+    extra = outs[0].shape[0] - rows
     projected = jnp.dot(cand_ref[...], w_ref[...], preferred_element_type=F32)
     made[...] = silu(projected).astype(BF16)
-    owners = jnp.broadcast_to(owner_ref[...].astype(F32), (blocks, cols)).astype(BF16)
+    owners = jnp.broadcast_to(owner_ref[...].astype(F32), (extra, blocks)).astype(BF16)
     for k, out in enumerate(outs):
         at = pl.multiple_of((k ^ me_ref[0]) * cols, cols)
         out[:rows, :] = made[:, pl.ds(at, cols)]
-        out[rows:, :] = owners
+        out[rows:, :] = jnp.zeros((extra, cols), BF16)
+        out[rows:, :blocks] = owners
 
 
 def project_queries(me, candidates, w_qu, block_owner, parts):
     rows, width = candidates.shape
     cols = width // parts
     blocks = block_owner.shape[0]
+    extra = 16
     return pl.pallas_call(
         query_kernel,
         grid_spec=scalar_grid(
@@ -75,18 +79,18 @@
             [
                 pl.BlockSpec((rows, width), lambda i, m: (0, 0)),
                 pl.BlockSpec((width, width), lambda i, m: (0, 0)),
-                pl.BlockSpec((blocks, 1), lambda i, m: (0, 0)),
+                pl.BlockSpec((1, blocks), lambda i, m: (0, 0)),
             ],
-            [pl.BlockSpec((rows + blocks, cols), lambda i, m: (0, 0))] * parts,
+            [pl.BlockSpec((rows + extra, cols), lambda i, m: (0, 0))] * parts,
             [pltpu.VMEM((rows, width), BF16)],
         ),
-        out_shape=[jax.ShapeDtypeStruct((rows + blocks, cols), BF16)] * parts,
+        out_shape=[jax.ShapeDtypeStruct((rows + extra, cols), BF16)] * parts,
         compiler_params=room_for(
-            ((2, width, width), BF16), ((8, rows + blocks, width), BF16), ((rows, width), F32)
+            ((2, width, width), BF16), ((8, rows + extra, width), BF16), ((rows, width), F32)
         ),
         cost_estimate=cost(2 * rows * width * width, 2 * width * width + 4 * rows * width),
         name="queries",
-    )(me, candidates, w_qu, block_owner)
+    )(me, candidates, w_qu, block_owner.reshape(1, blocks))
 
 
 def gate_kernel(_, cand_ref, w_ref, out_ref):
@@ -255,9 +259,13 @@
 
 def finish_kernel(me_ref, cand_ref, gate_ref, w_ref, *refs):
     parts, out_ref = refs[:-1], refs[-1]
+    count, _, cols = gate_ref.shape
     width = cand_ref.shape[1]
-    cols = parts[0].shape[1]
-    values = [p[...].astype(F32) for p in parts]
+    each = len(parts) // count
+    values = [
+        jnp.concatenate([p[...].astype(F32) for p in parts[k * each : (k + 1) * each]], axis=1)
+        for k in range(count)
+    ]
     mean = sum(jnp.sum(v, axis=1, keepdims=True) for v in values) / width
     values = [v - mean for v in values]
     square = sum(jnp.sum(v * v, axis=1, keepdims=True) for v in values)
@@ -318,10 +326,35 @@
     return pieces[0] if len(pieces) == 1 else jnp.concatenate(pieces, axis=0)
 
 
-def gather_queries(own, count, inner_first):
+def direct(count):
+    return 2 <= count // 2 <= MOST_DIRECT
+
+
+def gather_plan(count, head):
+    if head % 2 == 1:
+        return stages(count, True)
+    if not direct(count):
+        return stages(count, False)
+    even = list(range(0, count, 2))
+    cut = len(even) // 2
+    plan = [(mask, (0,)) for mask in reversed(even[1:])]
+    return plan + [(1, tuple(even[:cut])), (1, tuple(even[cut:]))]
+
+
+def scatter_plan(count, head):
+    plan = stages(count, False)
+    if head % 2 == 1 or not direct(count):
+        return plan
+    even = list(range(0, count, 2))
+    cut = len(even) // 2
+    plan = [step for step in plan if step[0] != 1]
+    return plan + [(1, tuple(even[cut:])), (1, tuple(even[:cut]))]
+
+
+def gather_queries(own, plan):
     cands = own.shape[0]
     arrays, where = [own], {0: (0, 0)}
-    for mask, codes in stages(count, inner_first):
+    for mask, codes in plan:
         pieces = [arrays[where[c][0]][where[c][1] : where[c][1] + cands] for c in codes]
         arrays.append(swap(joined(pieces), "req", mask))
         for j, c in enumerate(codes):
@@ -329,22 +362,20 @@
     return arrays, where
 
 
-def scatter_sums(groups, arrays, count, cands):
+def scatter_sums(plan, groups, arrays, cands):
     whole = {tuple(g): a for g, a in zip(groups, arrays)}
     held = {}
     for group, array in zip(groups, arrays):
         for j, c in enumerate(group):
             held[c] = array[j * cands : (j + 1) * cands]
-    plan = stages(count, False)
     for number in reversed(range(len(plan))):
         mask, codes = plan[number]
         away = tuple(c ^ mask for c in codes)
-        sent = whole[away] if away in whole else joined([held[c] for c in away])
+        sent = whole[away] if away in whole else joined([held[c].astype(BF16) for c in away])
         got = swap(sent, "req", mask)
         whole = {g: a for g, a in whole.items() if not set(g) & set(codes)}
         for j, c in enumerate(codes):
-            part = held[c].astype(F32) + got[j * cands : (j + 1) * cands].astype(F32)
-            held[c] = part.astype(BF16)
+            held[c] = held[c].astype(F32) + got[j * cands : (j + 1) * cands].astype(F32)
     return held[0]
 
 
@@ -376,7 +407,7 @@
             ]
         )
 
-    owners = jnp.concatenate([a[mine:, 0] for a in arrived]).astype(jnp.int32)
+    owners = jnp.concatenate([a[mine, :blocks] for a in arrived]).astype(jnp.int32)
     code = owners ^ me_req
     total_blocks = n_ctx * blocks
     order = jnp.arange(total_blocks, dtype=jnp.int32)
@@ -389,33 +420,38 @@
 
     gate = project_gate(me_ctx, candidates, w_qu, n_ctx)
 
-    plan = stages(n_req, False)
-    groups = [[c ^ mask for c in codes] for mask, codes in plan] + [[0]]
-    summed = []
+    parts = [[None] * each for _ in range(n_ctx)]
     for h in range(each):
         own = jnp.concatenate([a[:mine, h * HEAD : (h + 1) * HEAD] for a in arrived], axis=0)
-        arrays, where = gather_queries(own, n_req, h % 2 == 1)
-        last = len(plan) - 1
-        if h == 0:
-            calls = [[i for i in range(len(groups)) if i != last], [last]]
-        else:
-            calls = [[i for i in range(len(plan)) if plan[i][0] == 1]]
-            calls.append([i for i in range(len(groups)) if i not in calls[0]])
+        arrays, where = gather_queries(own, gather_plan(n_req, h))
+        plan = scatter_plan(n_req, h)
+        groups = [[c ^ mask for c in codes] for mask, codes in plan] + [[0]]
         sums = {}
-        for call in calls:
-            if call:
-                made = attend(
-                    pos, counts, kvs[h], arrays, where, [groups[i] for i in call],
-                    cands, events, room,
-                )
-                sums.update(zip(call, made))
-        summed.append(scatter_sums(groups, [sums[i] for i in range(len(groups))], n_req, cands))
-
-    full = jnp.concatenate(summed, axis=1)
-    parts = [full[:mine]] + [
-        swap(full[k * mine : (k + 1) * mine], "ctx", k) for k in range(1, n_ctx)
-    ]
-    return finish(me_ctx, candidates, gate, w_out, parts)
+        for call in calls_of(n_req, h):
+            made = attend(
+                pos, counts, kvs[h], arrays, where, [groups[i] for i in call],
+                cands, events, room,
+            )
+            sums.update(zip(call, made))
+        total = scatter_sums(plan, groups, [sums[i] for i in range(len(groups))], cands)
+        parts[0][h] = total[:mine]
+        for k in range(1, n_ctx):
+            piece = total[k * mine : (k + 1) * mine].astype(BF16)
+            parts[k][h] = swap(piece, "ctx", k)
+    return finish(me_ctx, candidates, gate, w_out, [p for row in parts for p in row])
+
+
+def calls_of(count, head):
+    plan = scatter_plan(count, head)
+    everything = list(range(len(plan) + 1))
+    inner = [i for i in range(len(plan)) if plan[i][0] == 1]
+    if len(inner) < 2:
+        return [everything]
+    if head % 2 == 0:
+        late = inner[0] if direct(count) else inner[-1]
+        return [[i for i in everything if i != late], [late]]
+    last = inner[-1]
+    return [[i for i in everything if i not in (last, last - 1)], [last], [last - 1]]
 
 
 def solution(mesh):

time: 108 us -> 120 us (1.11); the launches traced: 106 us -> 120 us
  waiting for transfers between devices: 29.3 us -> 47.1 us
  starting transfers between devices: 37.4 us -> 32.2 us
    ppermute x27 -> x31, waiting for transfers between devices: 29.3 us -> 47.1 us  [swap(): return lax.ppermute(value, axis, [(i, i ^ mask) for i in range(count)])]
    ppermute x27 -> x31, starting transfers between devices: 37.4 us -> 32.2 us  [swap(): return lax.ppermute(value, axis, [(i, i ^ mask) for i in range(count)])]
    slice x4, local copies, waits for them, and re-layouts: 2.56 us -> 0.03 us  [the longest x2 0.02 us: on_device(): piece = total[k * mine:(k + 1) * mine].astype(BF16)]
    squeeze x0 -> x4, local copies, waits for them, and re-layouts: none -> 2.02 us  [on_device(): a[mine, :blocks]]
    pallas_call x4 -> x5, Pallas kernels: 13.7 us -> 14.8 us  [attend(): pl.pallas_call(functools.partial(attend_kernel, source, sink, events, roo...]
    unnamed x28 -> x33, local copies, waits for them, and re-layouts: 11.3 us -> 11.2 us
  transfers between devices with their start and end apart: 27 -> 31, of which waited for: 12 -> 12; matrix products, arithmetic and copies ran while one was open for 10% -> 9% of each run, Pallas kernels for 20% -> 18%
where the time goes in v3:
time: 120 us
  waiting for transfers between devices  47.1 us (39%)
  starting transfers between devices  32.2 us (27%)
  Pallas kernels  23.8 us (20%)
  local copies, waits for them, and re-layouts  14 us (12%)
  other arithmetic  2.39 us (2%)
    ppermute x31, waiting for transfers between devices, swap(): return lax.ppermute(value, axis, [(i, i ^ mask) for i in range(count)])  47.1 us
    ppermute x31, starting transfers between devices, swap(): return lax.ppermute(value, axis, [(i, i ^ mask) for i in range(count)])  32.2 us
    pallas_call x5, Pallas kernels, attend(): pl.pallas_call(functools.partial(attend_kernel, source, sink, events, roo...  14.8 us
    unnamed x33, local copies, waits for them, and re-layouts  11.2 us
    pallas_call x2, Pallas kernels, project_keys_values(): pl.pallas_call(functools.partial(keys_values_kernel, count, each), grid_s...  5.14 us
  transfers between devices with their start and end apart: 31, of which 12 were waited for; matrix products, arithmetic and copies ran while one was open for 9% of the time, Pallas kernels for 18%

profile of v3, /device:TPU:0, one launch (start us, length us, event | category | flops | bytes accessed | tf_op | source)
XLA Modules:
  0.0 119.8 jit_solution(16910748952342598670)
XLA Ops:
  0.0 2.3 %copy-done.1 = bf16[1024,2048]{1,0:T(8,128)(2,1)S(1)} copy-done((bf16[1024,2048]{1,0:T(8,128)(2,1)S(1)}, bf16[1024,2048]{1,0:T(8,128)(2,1)}, u32[]{:S(2)}) %copy-start.1) | copy-done | bytes 4194328
  5.8 2.5 %collective-permute-start.1 = (bf16[144,256]{1,0:T(8,128)(2,1)}, bf16[144,256]{1,0:T(8,128)(2,1)}, u32[]{:S(2)}, u32[]{:S(2)}) collective-permute-start(bf16[144,256]{1,0:T(8,128)(2,1)} %get-tuple-element.26), channel_id=1, source_target_pairs={{0,2},{1,3},{2,0},{3,1},{4,6},{5,7},{6,4},{7,5},{8,10},{9,11},{10,... | collective-permute-start | bytes 221192 | tf_op jit(solution)/shard_map/ppermute | solution.py:25
  8.4 1.4 %copy-done.3 = bf16[768,1024]{1,0:T(8,128)(2,1)S(1)} copy-done((bf16[768,1024]{1,0:T(8,128)(2,1)S(1)}, bf16[768,1024]{1,0:T(8,128)(2,1)}, u32[]{:S(2)}) %copy-start.3) | copy-done | bytes 1572888
  9.8 2.4 %shard_map.109 = (bf16[768,256]{1,0:T(8,128)(2,1)S(1)}, bf16[768,256]{1,0:T(8,128)(2,1)S(1)}, bf16[768,256]{1,0:T(8,128)(2,1)S(1)}, bf16[768,256]{1,0:T(8,128)(2,1)S(1)}) custom-call(s32[1]{0:T(128)} %bitcast._.me_ref, bf16[768,1024]{1,0:T(8,128)(2,1)S(1)} %copy-done.3, bf16[1024,2048]{1,0:T(8,128)(2,1)S(1)} %copy-done, bf16[1024,2048]{1,0:T(8,128)(2,1)S(1)} %copy-done, ...), custom_call_target="tpu_custom_call" | custom-call | flops 1610612736 | bytes 5242880 | tf_op jit(solution)/shard_map/pallas_call | solution.py:143
  12.4 2.8 %shard_map.110 = (bf16[768,256]{1,0:T(8,128)(2,1)}, bf16[768,256]{1,0:T(8,128)(2,1)S(1)}, bf16[768,256]{1,0:T(8,128)(2,1)S(1)}, bf16[768,256]{1,0:T(8,128)(2,1)S(1)}) custom-call(s32[1]{0:T(128)} %bitcast._.me_ref, bf16[768,1024]{1,0:T(8,128)(2,1)S(1)} %copy-done.3, bf16[1024,2048]{1,0:T(8,128)(2,1)S(1)} %copy-done, bf16[1024,2048]{1,0:T(8,128)(2,1)S(1)} %copy-done, ...), custom_call_target="tpu_custom_call" | custom-call | flops 1610612736 | bytes 5242880 | tf_op jit(solution)/shard_map/pallas_call | solution.py:143
  15.1 1.9 %collective-permute-start.4 = (bf16[768,256]{1,0:T(8,128)(2,1)}, bf16[768,256]{1,0:T(8,128)(2,1)S(1)}, u32[]{:S(2)}, u32[]{:S(2)}) collective-permute-start(bf16[768,256]{1,0:T(8,128)(2,1)} %get-tuple-element.30), channel_id=1, source_target_pairs={{0,2},{1,3},{2,0},{3,1},{4,6},{5,7},{6,4},{7,5},{8,10},{9,11},{10,... | collective-permute-start | bytes 1179656 | tf_op jit(solution)/shard_map/ppermute | solution.py:25
  17.7 1.4 %constant_dynamic-update-slice_fusion.14 = (bf16[2048,128]{1,0:T(8,128)(2,1)}, bf16[1024,128]{1,0:T(8,128)(2,1)}, bf16[1024,128]{1,0:T(8,128)(2,1)}, bf16[128,128]{1,0:T(8,128)(2,1)S(1)}, bf16[128,128]{1,0:T(8,128)(2,1)S(1)}) fusion(bf16[2048,128]{1,0:T(8,128)(2,1)} %get-tuple-element.74, bf16[144,256]{1,0:T(8,128)(2,1)} %collective-permute-done, ...), kind=kLoop, calls=%fused_computation.30 | loop fusion | bytes 229376
  19.1 1.4 %constant_dynamic-update-slice_fusion.13 = (bf16[2048,128]{1,0:T(8,128)(2,1)}, bf16[1024,128]{1,0:T(8,128)(2,1)}, bf16[1024,128]{1,0:T(8,128)(2,1)}, bf16[128,128]{1,0:T(8,128)(2,1)S(1)}, bf16[128,128]{1,0:T(8,128)(2,1)S(1)}) fusion(bf16[2048,128]{1,0:T(8,128)(2,1)} %get-tuple-element.69, bf16[144,256]{1,0:T(8,128)(2,1)} %collective-permute-done.1, ...), kind=kLoop, calls=%fused_computation.29 | loop fusion | bytes 229376
  20.6 1.4 %constant_dynamic-update-slice_fusion.12 = (bf16[2048,128]{1,0:T(8,128)(2,1)}, bf16[1024,128]{1,0:T(8,128)(2,1)}, bf16[1024,128]{1,0:T(8,128)(2,1)}, bf16[128,128]{1,0:T(8,128)(2,1)S(1)}, bf16[128,128]{1,0:T(8,128)(2,1)S(1)}) fusion(bf16[2048,128]{1,0:T(8,128)(2,1)} %get-tuple-element.64, bf16[144,256]{1,0:T(8,128)(2,1)} %collective-permute-done.2, ...), kind=kLoop, calls=%fused_computation.28 | loop fusion | bytes 229376
  22.7 3.7 %collective-permute-start.6 = (bf16[512,128]{1,0:T(8,128)(2,1)S(1)}, bf16[512,128]{1,0:T(8,128)(2,1)S(1)}, u32[]{:S(2)}, u32[]{:S(2)}) collective-permute-start(bf16[512,128]{1,0:T(8,128)(2,1)S(1)} %pad_maximum_fusion.3.refs_4_), channel_id=1, source_target_pairs={{0,24},{4,28},{8,16},{12,20},{16,8},{20,12},{24,0},{28,4},{1,25},{... | collective-permute-start | bytes 393224 | tf_op jit(solution)/shard_map/ppermute | solution.py:25
  31.1 6.5 %collective-permute-done.7.refs_6_ = bf16[512,128]{1,0:T(8,128)(2,1)S(1)} collective-permute-done((bf16[512,128]{1,0:T(8,128)(2,1)S(1)}, bf16[512,128]{1,0:T(8,128)(2,1)S(1)}, u32[]{:S(2)}, u32[]{:S(2)}) %collective-permute-start.7) | collective-permute-done | bytes 131104 | tf_op jit(solution)/shard_map/ppermute | solution.py:25
  37.6 1.5 %collective-permute-start.18 = (bf16[512,128]{1,0:T(8,128)(2,1)S(1)}, bf16[512,128]{1,0:T(8,128)(2,1)S(1)}, u32[]{:S(2)}, u32[]{:S(2)}) collective-permute-start(bf16[512,128]{1,0:T(8,128)(2,1)S(1)} %pad_maximum_fusion.4.refs_4_), channel_id=1, source_target_pairs={{0,4},{4,0},{8,12},{12,8},{16,20},{20,16},{24,28},{28,24},{1,5},{5... | collective-permute-start | bytes 393224 | tf_op jit(solution)/shard_map/ppermute | solution.py:25
  40.4 3.6 %collective-permute-done.18.refs_5_ = bf16[512,128]{1,0:T(8,128)(2,1)S(1)} collective-permute-done((bf16[512,128]{1,0:T(8,128)(2,1)S(1)}, bf16[512,128]{1,0:T(8,128)(2,1)S(1)}, u32[]{:S(2)}, u32[]{:S(2)}) %collective-permute-start.18) | collective-permute-done | bytes 131104 | tf_op jit(solution)/shard_map/ppermute | solution.py:25
  44.0 1.5 %collective-permute-start.9 = (bf16[1024,128]{1,0:T(8,128)(2,1)}, bf16[1024,128]{1,0:T(8,128)(2,1)S(1)}, u32[]{:S(2)}, u32[]{:S(2)}) collective-permute-start(bf16[1024,128]{1,0:T(8,128)(2,1)} %constant_dynamic-update-slice_fusion), channel_id=1, source_target_pairs={{0,4},{4,0},{8,12},{12,8},{16,20},{20,16},{24,28},{28,24},{1,5},{5... | collective-permute-start | bytes 786440 | tf_op jit(solution)/shard_map/ppermute | solution.py:25
  46.3 2.5 %collective-permute-start.19 = (bf16[1024,128]{1,0:T(8,128)(2,1)}, bf16[1024,128]{1,0:T(8,128)(2,1)S(1)}, u32[]{:S(2)}, u32[]{:S(2)}) collective-permute-start(bf16[1024,128]{1,0:T(8,128)(2,1)} %get-tuple-element.58), channel_id=1, source_target_pairs={{0,24},{4,28},{8,16},{12,20},{16,8},{20,12},{24,0},{28,4},{1,25},{... | collective-permute-start | bytes 786440 | tf_op jit(solution)/shard_map/ppermute | solution.py:25
  49.6 2.2 %shard_map.112 = bf16[1024,128]{1,0:T(8,128)(2,1)S(1)} custom-call(s32[192]{0:T(256)S(1)} %multiply_add_fusion.pos_ref, s32[8]{0:T(128)S(1)} %convert_reduce_fusion.1.count_ref, s32[2]{0:T(128)S(1)} %copy-done.8, bf16[768,256]{1,0:T(8,128)(2,1)S(1)} %get-tuple-element.28.refs_0_, bf16[768,256]{1,0:T(8,128)(2,1)S(1)} %collective-permute-done.3.refs_1_, ...), custom_call_target="tpu_custom_call" | custom-call | flops 402653184 | bytes 2097152 | tf_op jit(solution)/shard_map/pallas_call | solution.py:237
  51.8 1.7 %collective-permute-start.12 = (bf16[1024,128]{1,0:T(8,128)(2,1)S(1)}, bf16[1024,128]{1,0:T(8,128)(2,1)S(1)}, u32[]{:S(2)}, u32[]{:S(2)}) collective-permute-start(bf16[1024,128]{1,0:T(8,128)(2,1)S(1)} %shard_map.112), channel_id=1, source_target_pairs={{0,4},{4,0},{8,12},{12,8},{16,20},{20,16},{24,28},{28,24},{1,5},{5... | collective-permute-start | bytes 786440 | tf_op jit(solution)/shard_map/ppermute | solution.py:25
  53.5 1.7 %collective-permute-done.9.refs_8_ = bf16[1024,128]{1,0:T(8,128)(2,1)S(1)} collective-permute-done((bf16[1024,128]{1,0:T(8,128)(2,1)}, bf16[1024,128]{1,0:T(8,128)(2,1)S(1)}, u32[]{:S(2)}, u32[]{:S(2)}) %collective-permute-start.9) | collective-permute-done | bytes 262176 | tf_op jit(solution)/shard_map/ppermute | solution.py:25
  55.2 4.7 %shard_map.111 = (bf16[512,128]{1,0:T(8,128)(2,1)S(1)}, bf16[1024,128]{1,0:T(8,128)(2,1)S(1)}, bf16[1024,128]{1,0:T(8,128)(2,1)S(1)}, bf16[512,128]{1,0:T(8,128)(2,1)S(1)}) custom-call(s32[192]{0:T(256)S(1)} %multiply_add_fusion.pos_ref, s32[8]{0:T(128)S(1)} %convert_reduce_fusion.1.count_ref, s32[6]{0:T(128)S(1)} %copy-done.12, ...), custom_call_target="tpu_custom_call" | custom-call | flops 1207959552 | bytes 3145728 | tf_op jit(solution)/shard_map/pallas_call | solution.py:237
  63.2 3.1 %collective-permute-done.10 = bf16[1024,128]{1,0:T(8,128)(2,1)S(1)} collective-permute-done((bf16[1024,128]{1,0:T(8,128)(2,1)S(1)}, bf16[1024,128]{1,0:T(8,128)(2,1)S(1)}, u32[]{:S(2)}, u32[]{:S(2)}) %collective-permute-start.10) | collective-permute-done | bytes 262176 | tf_op jit(solution)/shard_map/ppermute | solution.py:25
  66.5 6.7 %collective-permute-done.16.refs_2_ = bf16[768,256]{1,0:T(8,128)(2,1)S(1)} collective-permute-done((bf16[768,256]{1,0:T(8,128)(2,1)S(1)}, bf16[768,256]{1,0:T(8,128)(2,1)S(1)}, u32[]{:S(2)}, u32[]{:S(2)}) %collective-permute-start.16) | collective-permute-done | bytes 393248 | tf_op jit(solution)/shard_map/ppermute | solution.py:25
  73.2 7.5 %collective-permute-done.17.refs_3_ = bf16[768,256]{1,0:T(8,128)(2,1)S(1)} collective-permute-done((bf16[768,256]{1,0:T(8,128)(2,1)S(1)}, bf16[768,256]{1,0:T(8,128)(2,1)S(1)}, u32[]{:S(2)}, u32[]{:S(2)}) %collective-permute-start.17) | collective-permute-done | bytes 393248 | tf_op jit(solution)/shard_map/ppermute | solution.py:25
  80.7 3.6 %shard_map.113 = (bf16[512,128]{1,0:T(8,128)(2,1)S(1)}, bf16[1024,128]{1,0:T(8,128)(2,1)S(1)}, bf16[512,128]{1,0:T(8,128)(2,1)S(1)}) custom-call(s32[192]{0:T(256)S(1)} %multiply_add_fusion.pos_ref, s32[8]{0:T(128)S(1)} %convert_reduce_fusion.1.count_ref, s32[4]{0:T(128)S(1)} %copy-done.11, bf16[768,256]{1,0:T(8,128)(2,1)S(1)} %get-tuple-element.36.refs_0_, ...), custom_call_target="tpu_custom_call" | custom-call | flops 805306368 | bytes 2621440 | tf_op jit(solution)/shard_map/pallas_call | solution.py:237
  85.2 2.2 %shard_map.115 = bf16[1024,128]{1,0:T(8,128)(2,1)S(1)} custom-call(s32[192]{0:T(256)S(1)} %multiply_add_fusion.pos_ref, s32[8]{0:T(128)S(1)} %convert_reduce_fusion.1.count_ref, s32[2]{0:T(128)S(1)} %copy-done.10, bf16[768,256]{1,0:T(8,128)(2,1)S(1)} %get-tuple-element.36.refs_0_, bf16[768,256]{1,0:T(8,128)(2,1)S(1)} %collective-permute-done.15.refs_1_, ...), custom_call_target="tpu_custom_call" | custom-call | flops 402653184 | bytes 2097152 | tf_op jit(solution)/shard_map/pallas_call | solution.py:237
  88.6 2.2 %shard_map.114 = bf16[1024,128]{1,0:T(8,128)(2,1)S(1)} custom-call(s32[192]{0:T(256)S(1)} %multiply_add_fusion.pos_ref, s32[8]{0:T(128)S(1)} %convert_reduce_fusion.1.count_ref, s32[2]{0:T(128)S(1)} %copy-done.9, bf16[768,256]{1,0:T(8,128)(2,1)S(1)} %get-tuple-element.36.refs_0_, bf16[768,256]{1,0:T(8,128)(2,1)S(1)} %collective-permute-done.15.refs_1_, ...), custom_call_target="tpu_custom_call" | custom-call | flops 402653184 | bytes 2097152 | tf_op jit(solution)/shard_map/pallas_call | solution.py:237
  90.8 2.8 %collective-permute-start.14 = (bf16[512,128]{1,0:T(8,128)(2,1)S(1)}, bf16[512,128]{1,0:T(8,128)(2,1)S(1)}, u32[]{:S(2)}, u32[]{:S(2)}) collective-permute-start(bf16[512,128]{1,0:T(8,128)(2,1)S(1)} %add_convert_fusion.3), channel_id=1, source_target_pairs={{0,24},{4,28},{8,16},{12,20},{16,8},{20,12},{24,0},{28,4},{1,25},{... | collective-permute-start | bytes 393224 | tf_op jit(solution)/shard_map/ppermute | solution.py:25
  93.6 5.2 %collective-permute-done.21 = bf16[1024,128]{1,0:T(8,128)(2,1)S(1)} collective-permute-done((bf16[1024,128]{1,0:T(8,128)(2,1)S(1)}, bf16[1024,128]{1,0:T(8,128)(2,1)S(1)}, u32[]{:S(2)}, u32[]{:S(2)}) %collective-permute-start.21) | collective-permute-done | bytes 262176 | tf_op jit(solution)/shard_map/ppermute | solution.py:25
  99.1 7.8 %collective-permute-done.22 = bf16[1024,128]{1,0:T(8,128)(2,1)S(1)} collective-permute-done((bf16[1024,128]{1,0:T(8,128)(2,1)S(1)}, bf16[1024,128]{1,0:T(8,128)(2,1)S(1)}, u32[]{:S(2)}, u32[]{:S(2)}) %collective-permute-start.22) | collective-permute-done | bytes 262176 | tf_op jit(solution)/shard_map/ppermute | solution.py:25
  107.0 2.7 %collective-permute-start.24 = (bf16[512,128]{1,0:T(8,128)(2,1)S(1)}, bf16[512,128]{1,0:T(8,128)(2,1)S(1)}, u32[]{:S(2)}, u32[]{:S(2)}) collective-permute-start(bf16[512,128]{1,0:T(8,128)(2,1)S(1)} %add_convert_fusion), channel_id=1, source_target_pairs={{0,24},{4,28},{8,16},{12,20},{16,8},{20,12},{24,0},{28,4},{1,25},{... | collective-permute-start | bytes 393224 | tf_op jit(solution)/shard_map/ppermute | solution.py:25
  111.6 2.3 %collective-permute-done.24 = bf16[512,128]{1,0:T(8,128)(2,1)S(1)} collective-permute-done((bf16[512,128]{1,0:T(8,128)(2,1)S(1)}, bf16[512,128]{1,0:T(8,128)(2,1)S(1)}, u32[]{:S(2)}, u32[]{:S(2)}) %collective-permute-start.24) | collective-permute-done | bytes 131104 | tf_op jit(solution)/shard_map/ppermute | solution.py:25
  116.0 1.4 %gate.1.gate_ref = f32[4,128,256]{2,1,0:T(8,128)S(1)} custom-call(s32[1]{0:T(128)} %bitcast._.me_ref, bf16[128,1024]{1,0:T(8,128)(2,1)S(1)} %copy-done.5, bf16[1024,2048]{1,0:T(8,128)(2,1)S(1)} %copy-done.2), custom_call_target="tpu_custom_call" | custom-call | flops 268435456 | bytes 2883584 | tf_op jit(solution)/shard_map/gate/pallas_call | solution.py:103
  118.4 1.3 %finish.1 = bf16[128,1024]{1,0:T(8,128)(2,1)} custom-call(s32[1]{0:T(128)} %bitcast._.me_ref, bf16[128,1024]{1,0:T(8,128)(2,1)S(1)} %copy-done.5, f32[4,128,256]{2,1,0:T(8,128)S(1)} %gate.1.gate_ref, bf16[1024,1024]{1,0:T(8,128)(2,1)S(1)} %copy-done.6, f32[128,128]{1,0:T(8,128)S(1)} %slice.165.refs_0_, f32[128,128]{1,0:T(8,128)S(1)} %slice.177.refs_1_, ...), custom_call_target="tpu_custom_call" | custom-call | flops 268435456 | bytes 3407872 | tf_op jit(solution)/shard_map/finish/pallas_call | solution.py:284
  (98 shorter events, 23.5 us)
Async XLA Ops:
  5.3 12.4 %collective-permute-start = (bf16[144,256]{1,0:T(8,128)(2,1)}, bf16[144,256]{1,0:T(8,128)(2,1)}, u32[]{:S(2)}, u32[]{:S(2)}) collective-permute-start(bf16[144,256]{1,0:T(8,128)(2,1)} %get-tuple-element.25), channel_id=1, source_target_pairs={{0,1},{1,0},{2,3},{3,2},{4,5},{5,4},{6,7},{7,6},{8,9},{9,8},{10,11... | collective-permute-start | bytes 221192 | tf_op jit(solution)/shard_map/ppermute | solution.py:25
  5.8 13.3 %collective-permute-start.1 = (bf16[144,256]{1,0:T(8,128)(2,1)}, bf16[144,256]{1,0:T(8,128)(2,1)}, u32[]{:S(2)}, u32[]{:S(2)}) collective-permute-start(bf16[144,256]{1,0:T(8,128)(2,1)} %get-tuple-element.26), channel_id=1, source_target_pairs={{0,2},{1,3},{2,0},{3,1},{4,6},{5,7},{6,4},{7,5},{8,10},{9,11},{10,... | collective-permute-start | bytes 221192 | tf_op jit(solution)/shard_map/ppermute | solution.py:25
  8.3 12.3 %collective-permute-start.2 = (bf16[144,256]{1,0:T(8,128)(2,1)}, bf16[144,256]{1,0:T(8,128)(2,1)}, u32[]{:S(2)}, u32[]{:S(2)}) collective-permute-start(bf16[144,256]{1,0:T(8,128)(2,1)} %get-tuple-element.27), channel_id=1, source_target_pairs={{0,3},{1,2},{2,1},{3,0},{4,7},{5,6},{6,5},{7,4},{8,11},{9,10},{10,... | collective-permute-start | bytes 221192 | tf_op jit(solution)/shard_map/ppermute | solution.py:25
  12.2 34.1 %collective-permute-start.3 = (bf16[768,256]{1,0:T(8,128)(2,1)S(1)}, bf16[768,256]{1,0:T(8,128)(2,1)S(1)}, u32[]{:S(2)}, u32[]{:S(2)}) collective-permute-start(bf16[768,256]{1,0:T(8,128)(2,1)S(1)} %get-tuple-element.29), channel_id=1, source_target_pairs={{0,1},{1,0},{2,3},{3,2},{4,5},{5,4},{6,7},{7,6},{8,9},{9,8},{10,11... | collective-permute-start | bytes 1179656 | tf_op jit(solution)/shard_map/ppermute | solution.py:25
  15.1 40.1 %copy-start.12 = (s32[6]{0:T(128)S(1)}, s32[6]{0:T(128)}, u32[]{:S(2)}) copy-start(s32[6]{0:T(128)} %constant.23.clone.code_ref) | copy-start | bytes 76
  15.1 33.7 %collective-permute-start.4 = (bf16[768,256]{1,0:T(8,128)(2,1)}, bf16[768,256]{1,0:T(8,128)(2,1)S(1)}, u32[]{:S(2)}, u32[]{:S(2)}) collective-permute-start(bf16[768,256]{1,0:T(8,128)(2,1)} %get-tuple-element.30), channel_id=1, source_target_pairs={{0,2},{1,3},{2,0},{3,1},{4,6},{5,7},{6,4},{7,5},{8,10},{9,11},{10,... | collective-permute-start | bytes 1179656 | tf_op jit(solution)/shard_map/ppermute | solution.py:25
  22.7 8.3 %collective-permute-start.6 = (bf16[512,128]{1,0:T(8,128)(2,1)S(1)}, bf16[512,128]{1,0:T(8,128)(2,1)S(1)}, u32[]{:S(2)}, u32[]{:S(2)}) collective-permute-start(bf16[512,128]{1,0:T(8,128)(2,1)S(1)} %pad_maximum_fusion.3.refs_4_), channel_id=1, source_target_pairs={{0,24},{4,28},{8,16},{12,20},{16,8},{20,12},{24,0},{28,4},{1,25},{... | collective-permute-start | bytes 393224 | tf_op jit(solution)/shard_map/ppermute | solution.py:25
  26.4 11.2 %collective-permute-start.7 = (bf16[512,128]{1,0:T(8,128)(2,1)S(1)}, bf16[512,128]{1,0:T(8,128)(2,1)S(1)}, u32[]{:S(2)}, u32[]{:S(2)}) collective-permute-start(bf16[512,128]{1,0:T(8,128)(2,1)S(1)} %pad_maximum_fusion.3.refs_4_), channel_id=1, source_target_pairs={{0,16},{4,20},{8,24},{12,28},{16,0},{20,4},{24,8},{28,12},{1,17},{... | collective-permute-start | bytes 393224 | tf_op jit(solution)/shard_map/ppermute | solution.py:25
  26.4 12.7 %collective-permute-start.8 = (bf16[512,128]{1,0:T(8,128)(2,1)S(1)}, bf16[512,128]{1,0:T(8,128)(2,1)S(1)}, u32[]{:S(2)}, u32[]{:S(2)}) collective-permute-start(bf16[512,128]{1,0:T(8,128)(2,1)S(1)} %pad_maximum_fusion.3.refs_4_), channel_id=1, source_target_pairs={{0,8},{4,12},{8,0},{12,4},{16,24},{20,28},{24,16},{28,20},{1,9},{5... | collective-permute-start | bytes 393224 | tf_op jit(solution)/shard_map/ppermute | solution.py:25
  31.1 17.7 %collective-permute-start.5 = (bf16[768,256]{1,0:T(8,128)(2,1)S(1)}, bf16[768,256]{1,0:T(8,128)(2,1)S(1)}, u32[]{:S(2)}, u32[]{:S(2)}) collective-permute-start(bf16[768,256]{1,0:T(8,128)(2,1)S(1)} %get-tuple-element.31), channel_id=1, source_target_pairs={{0,3},{1,2},{2,1},{3,0},{4,7},{5,6},{6,5},{7,4},{8,11},{9,10},{10,... | collective-permute-start | bytes 1179656 | tf_op jit(solution)/shard_map/ppermute | solution.py:25
  37.6 6.4 %collective-permute-start.18 = (bf16[512,128]{1,0:T(8,128)(2,1)S(1)}, bf16[512,128]{1,0:T(8,128)(2,1)S(1)}, u32[]{:S(2)}, u32[]{:S(2)}) collective-permute-start(bf16[512,128]{1,0:T(8,128)(2,1)S(1)} %pad_maximum_fusion.4.refs_4_), channel_id=1, source_target_pairs={{0,4},{4,0},{8,12},{12,8},{16,20},{20,16},{24,28},{28,24},{1,5},{5... | collective-permute-start | bytes 393224 | tf_op jit(solution)/shard_map/ppermute | solution.py:25
  39.1 10.4 %collective-permute-start.11 = (bf16[1024,128]{1,0:T(8,128)(2,1)S(1)}, bf16[1024,128]{1,0:T(8,128)(2,1)S(1)}, u32[]{:S(2)}, u32[]{:S(2)}) collective-permute-start(bf16[1024,128]{1,0:T(8,128)(2,1)S(1)} %pad_maximum_fusion), channel_id=1, source_target_pairs={{0,4},{4,0},{8,12},{12,8},{16,20},{20,16},{24,28},{28,24},{1,5},{5... | collective-permute-start | bytes 786440 | tf_op jit(solution)/shard_map/ppermute | solution.py:25
  44.0 11.2 %collective-permute-start.9 = (bf16[1024,128]{1,0:T(8,128)(2,1)}, bf16[1024,128]{1,0:T(8,128)(2,1)S(1)}, u32[]{:S(2)}, u32[]{:S(2)}) collective-permute-start(bf16[1024,128]{1,0:T(8,128)(2,1)} %constant_dynamic-update-slice_fusion), channel_id=1, source_target_pairs={{0,4},{4,0},{8,12},{12,8},{16,20},{20,16},{24,28},{28,24},{1,5},{5... | collective-permute-start | bytes 786440 | tf_op jit(solution)/shard_map/ppermute | solution.py:25
  46.3 15.4 %collective-permute-start.19 = (bf16[1024,128]{1,0:T(8,128)(2,1)}, bf16[1024,128]{1,0:T(8,128)(2,1)S(1)}, u32[]{:S(2)}, u32[]{:S(2)}) collective-permute-start(bf16[1024,128]{1,0:T(8,128)(2,1)} %get-tuple-element.58), channel_id=1, source_target_pairs={{0,24},{4,28},{8,16},{12,20},{16,8},{20,12},{24,0},{28,4},{1,25},{... | collective-permute-start | bytes 786440 | tf_op jit(solution)/shard_map/ppermute | solution.py:25
  51.8 11.4 %collective-permute-start.12 = (bf16[1024,128]{1,0:T(8,128)(2,1)S(1)}, bf16[1024,128]{1,0:T(8,128)(2,1)S(1)}, u32[]{:S(2)}, u32[]{:S(2)}) collective-permute-start(bf16[1024,128]{1,0:T(8,128)(2,1)S(1)} %shard_map.112), channel_id=1, source_target_pairs={{0,4},{4,0},{8,12},{12,8},{16,20},{20,16},{24,28},{28,24},{1,5},{5... | collective-permute-start | bytes 786440 | tf_op jit(solution)/shard_map/ppermute | solution.py:25
  59.9 6.4 %collective-permute-start.10 = (bf16[1024,128]{1,0:T(8,128)(2,1)S(1)}, bf16[1024,128]{1,0:T(8,128)(2,1)S(1)}, u32[]{:S(2)}, u32[]{:S(2)}) collective-permute-start(bf16[1024,128]{1,0:T(8,128)(2,1)S(1)} %get-tuple-element.33), channel_id=1, source_target_pairs={{0,4},{4,0},{8,12},{12,8},{16,20},{20,16},{24,28},{28,24},{1,5},{5... | collective-permute-start | bytes 786440 | tf_op jit(solution)/shard_map/ppermute | solution.py:25
  61.2 5.3 %collective-permute-start.15 = (bf16[768,256]{1,0:T(8,128)(2,1)S(1)}, bf16[768,256]{1,0:T(8,128)(2,1)S(1)}, u32[]{:S(2)}, u32[]{:S(2)}) collective-permute-start(bf16[768,256]{1,0:T(8,128)(2,1)S(1)} %get-tuple-element.37), channel_id=1, source_target_pairs={{0,1},{1,0},{2,3},{3,2},{4,5},{5,4},{6,7},{7,6},{8,9},{9,8},{10,11... | collective-permute-start | bytes 1179656 | tf_op jit(solution)/shard_map/ppermute | solution.py:25
  61.2 12.0 %collective-permute-start.16 = (bf16[768,256]{1,0:T(8,128)(2,1)S(1)}, bf16[768,256]{1,0:T(8,128)(2,1)S(1)}, u32[]{:S(2)}, u32[]{:S(2)}) collective-permute-start(bf16[768,256]{1,0:T(8,128)(2,1)S(1)} %get-tuple-element.38), channel_id=1, source_target_pairs={{0,2},{1,3},{2,0},{3,1},{4,6},{5,7},{6,4},{7,5},{8,10},{9,11},{10,... | collective-permute-start | bytes 1179656 | tf_op jit(solution)/shard_map/ppermute | solution.py:25
  61.8 18.9 %collective-permute-start.17 = (bf16[768,256]{1,0:T(8,128)(2,1)S(1)}, bf16[768,256]{1,0:T(8,128)(2,1)S(1)}, u32[]{:S(2)}, u32[]{:S(2)}) collective-permute-start(bf16[768,256]{1,0:T(8,128)(2,1)S(1)} %get-tuple-element.39), channel_id=1, source_target_pairs={{0,3},{1,2},{2,1},{3,0},{4,7},{5,6},{6,5},{7,4},{8,11},{9,10},{10,... | collective-permute-start | bytes 1179656 | tf_op jit(solution)/shard_map/ppermute | solution.py:25
  63.1 22.1 %collective-permute-start.20 = (bf16[2048,128]{1,0:T(8,128)(2,1)S(1)}, bf16[2048,128]{1,0:T(8,128)(2,1)S(1)}, u32[]{:S(2)}, u32[]{:S(2)}) collective-permute-start(bf16[2048,128]{1,0:T(8,128)(2,1)S(1)} %constant_dynamic-update-slice_fusion.10), channel_id=1, source_target_pairs={{0,8},{4,12},{8,0},{12,4},{16,24},{20,28},{24,16},{28,20},{1,9},{5... | collective-permute-start | bytes 1572872 | tf_op jit(solution)/shard_map/ppermute | solution.py:25
  66.4 24.3 %collective-permute-start.13 = (bf16[1024,128]{1,0:T(8,128)(2,1)S(1)}, bf16[1024,128]{1,0:T(8,128)(2,1)S(1)}, u32[]{:S(2)}, u32[]{:S(2)}) collective-permute-start(bf16[1024,128]{1,0:T(8,128)(2,1)S(1)} %pad_maximum_fusion.1), channel_id=1, source_target_pairs={{0,8},{4,12},{8,0},{12,4},{16,24},{20,28},{24,16},{28,20},{1,9},{5... | collective-permute-start | bytes 786440 | tf_op jit(solution)/shard_map/ppermute | solution.py:25
  84.4 14.8 %collective-permute-start.23 = (bf16[1024,128]{1,0:T(8,128)(2,1)S(1)}, bf16[1024,128]{1,0:T(8,128)(2,1)S(1)}, u32[]{:S(2)}, u32[]{:S(2)}) collective-permute-start(bf16[1024,128]{1,0:T(8,128)(2,1)S(1)} %get-tuple-element.41), channel_id=1, source_target_pairs={{0,4},{4,0},{8,12},{12,8},{16,20},{20,16},{24,28},{28,24},{1,5},{5... | collective-permute-start | bytes 786440 | tf_op jit(solution)/shard_map/ppermute | solution.py:25
  87.4 11.4 %collective-permute-start.21 = (bf16[1024,128]{1,0:T(8,128)(2,1)S(1)}, bf16[1024,128]{1,0:T(8,128)(2,1)S(1)}, u32[]{:S(2)}, u32[]{:S(2)}) collective-permute-start(bf16[1024,128]{1,0:T(8,128)(2,1)S(1)} %shard_map.115), channel_id=1, source_target_pairs={{0,4},{4,0},{8,12},{12,8},{16,20},{20,16},{24,28},{28,24},{1,5},{5... | collective-permute-start | bytes 786440 | tf_op jit(solution)/shard_map/ppermute | solution.py:25
  90.8 8.2 %collective-permute-start.14 = (bf16[512,128]{1,0:T(8,128)(2,1)S(1)}, bf16[512,128]{1,0:T(8,128)(2,1)S(1)}, u32[]{:S(2)}, u32[]{:S(2)}) collective-permute-start(bf16[512,128]{1,0:T(8,128)(2,1)S(1)} %add_convert_fusion.3), channel_id=1, source_target_pairs={{0,24},{4,28},{8,16},{12,20},{16,8},{20,12},{24,0},{28,4},{1,25},{... | collective-permute-start | bytes 393224 | tf_op jit(solution)/shard_map/ppermute | solution.py:25
  99.0 8.0 %collective-permute-start.22 = (bf16[1024,128]{1,0:T(8,128)(2,1)S(1)}, bf16[1024,128]{1,0:T(8,128)(2,1)S(1)}, u32[]{:S(2)}, u32[]{:S(2)}) collective-permute-start(bf16[1024,128]{1,0:T(8,128)(2,1)S(1)} %pad_maximum_fusion.2), channel_id=1, source_target_pairs={{0,8},{4,12},{8,0},{12,4},{16,24},{20,28},{24,16},{28,20},{1,9},{5... | collective-permute-start | bytes 786440 | tf_op jit(solution)/shard_map/ppermute | solution.py:25
  107.0 6.9 %collective-permute-start.24 = (bf16[512,128]{1,0:T(8,128)(2,1)S(1)}, bf16[512,128]{1,0:T(8,128)(2,1)S(1)}, u32[]{:S(2)}, u32[]{:S(2)}) collective-permute-start(bf16[512,128]{1,0:T(8,128)(2,1)S(1)} %add_convert_fusion), channel_id=1, source_target_pairs={{0,24},{4,28},{8,16},{12,20},{16,8},{20,12},{24,0},{28,4},{1,25},{... | collective-permute-start | bytes 393224 | tf_op jit(solution)/shard_map/ppermute | solution.py:25
  109.7 5.0 %collective-permute-start.25 = (bf16[128,128]{1,0:T(8,128)(2,1)S(1)}, bf16[128,128]{1,0:T(8,128)(2,1)S(1)}, u32[]{:S(2)}, u32[]{:S(2)}) collective-permute-start(bf16[128,128]{1,0:T(8,128)(2,1)S(1)} %get-tuple-element.56), channel_id=1, source_target_pairs={{0,1},{1,0},{2,3},{3,2},{4,5},{5,4},{6,7},{7,6},{8,9},{9,8},{10,11... | collective-permute-start | bytes 98312 | tf_op jit(solution)/shard_map/ppermute | solution.py:25
  109.8 7.6 %collective-permute-start.27 = (bf16[128,128]{1,0:T(8,128)(2,1)S(1)}, bf16[128,128]{1,0:T(8,128)(2,1)S(1)}, u32[]{:S(2)}, u32[]{:S(2)}) collective-permute-start(bf16[128,128]{1,0:T(8,128)(2,1)S(1)} %get-tuple-element.55), channel_id=1, source_target_pairs={{0,2},{1,3},{2,0},{3,1},{4,6},{5,7},{6,4},{7,5},{8,10},{9,11},{10,... | collective-permute-start | bytes 98312 | tf_op jit(solution)/shard_map/ppermute | solution.py:25
  110.4 7.0 %collective-permute-start.29 = (bf16[128,128]{1,0:T(8,128)(2,1)S(1)}, bf16[128,128]{1,0:T(8,128)(2,1)S(1)}, u32[]{:S(2)}, u32[]{:S(2)}) collective-permute-start(bf16[128,128]{1,0:T(8,128)(2,1)S(1)} %get-tuple-element.54), channel_id=1, source_target_pairs={{0,3},{1,2},{2,1},{3,0},{4,7},{5,6},{6,5},{7,4},{8,11},{9,10},{10,... | collective-permute-start | bytes 98312 | tf_op jit(solution)/shard_map/ppermute | solution.py:25
  114.1 3.4 %collective-permute-start.26 = (bf16[128,128]{1,0:T(8,128)(2,1)S(1)}, bf16[128,128]{1,0:T(8,128)(2,1)S(1)}, u32[]{:S(2)}, u32[]{:S(2)}) collective-permute-start(bf16[128,128]{1,0:T(8,128)(2,1)S(1)} %get-tuple-element.53), channel_id=1, source_target_pairs={{0,1},{1,0},{2,3},{3,2},{4,5},{5,4},{6,7},{7,6},{8,9},{9,8},{10,11... | collective-permute-start | bytes 98312 | tf_op jit(solution)/shard_map/ppermute | solution.py:25
  114.1 4.3 %collective-permute-start.28 = (bf16[128,128]{1,0:T(8,128)(2,1)S(1)}, bf16[128,128]{1,0:T(8,128)(2,1)S(1)}, u32[]{:S(2)}, u32[]{:S(2)}) collective-permute-start(bf16[128,128]{1,0:T(8,128)(2,1)S(1)} %get-tuple-element.52), channel_id=1, source_target_pairs={{0,2},{1,3},{2,0},{3,1},{4,6},{5,7},{6,4},{7,5},{8,10},{9,11},{10,... | collective-permute-start | bytes 98312 | tf_op jit(solution)/shard_map/ppermute | solution.py:25
  114.7 3.7 %collective-permute-start.30 = (bf16[128,128]{1,0:T(8,128)(2,1)S(1)}, bf16[128,128]{1,0:T(8,128)(2,1)S(1)}, u32[]{:S(2)}, u32[]{:S(2)}) collective-permute-start(bf16[128,128]{1,0:T(8,128)(2,1)S(1)} %get-tuple-element.51), channel_id=1, source_target_pairs={{0,3},{1,2},{2,1},{3,0},{4,7},{5,6},{6,5},{7,4},{8,11},{9,10},{10,... | collective-permute-start | bytes 98312 | tf_op jit(solution)/shard_map/ppermute | solution.py:25
  (13 other events, 244.2 us)

commit v4 on v3

--- a/solution.py
+++ b/solution.py
@@ -10,7 +10,6 @@
 
 HEAD = 128
 TILE = 256
-MOST_DIRECT = 4
 BF16 = jnp.bfloat16
 F32 = jnp.float32
 
@@ -51,20 +50,32 @@
     )
 
 
-def query_kernel(me_ref, cand_ref, w_ref, owner_ref, *refs):
-    outs, made = refs[:-1], refs[-1]
-    rows = cand_ref.shape[0]
+def query_kernel(me_ref, cand_hbm, w_hbm, owner_ref, *refs):
+    outs, (cand, weight, made, sems) = refs[:-4], refs[-4:]
+    rows = cand.shape[0]
+    parts = len(outs)
     cols = outs[0].shape[1]
     blocks = owner_ref.shape[1]
     extra = outs[0].shape[0] - rows
-    projected = jnp.dot(cand_ref[...], w_ref[...], preferred_element_type=F32)
-    made[...] = silu(projected).astype(BF16)
+    fetch = [pltpu.make_async_copy(cand_hbm, cand, sems.at[parts])]
+    for k in range(parts):
+        at = pl.ds(k * cols, cols)
+        fetch.append(pltpu.make_async_copy(w_hbm.at[:, at], weight.at[:, at], sems.at[k]))
+    for copy in fetch:
+        copy.start()
     owners = jnp.broadcast_to(owner_ref[...].astype(F32), (extra, blocks)).astype(BF16)
+    for out in outs:
+        out[rows:, :] = jnp.zeros((extra, cols), BF16)
+        out[rows:, :blocks] = owners
+    fetch[0].wait()
+    for k in range(parts):
+        fetch[k + 1].wait()
+        at = slice(k * cols, (k + 1) * cols)
+        projected = jnp.dot(cand[...], weight[:, at], preferred_element_type=F32)
+        made[:, at] = silu(projected).astype(BF16)
     for k, out in enumerate(outs):
         at = pl.multiple_of((k ^ me_ref[0]) * cols, cols)
         out[:rows, :] = made[:, pl.ds(at, cols)]
-        out[rows:, :] = jnp.zeros((extra, cols), BF16)
-        out[rows:, :blocks] = owners
 
 
 def project_queries(me, candidates, w_qu, block_owner, parts):
@@ -72,25 +83,52 @@
     cols = width // parts
     blocks = block_owner.shape[0]
     extra = 16
+    vmem = pl.BlockSpec(memory_space=pltpu.VMEM)
+    hbm = pl.BlockSpec(memory_space=pltpu.HBM)
     return pl.pallas_call(
         query_kernel,
-        grid_spec=scalar_grid(
-            (1,),
-            [
-                pl.BlockSpec((rows, width), lambda i, m: (0, 0)),
-                pl.BlockSpec((width, width), lambda i, m: (0, 0)),
-                pl.BlockSpec((1, blocks), lambda i, m: (0, 0)),
-            ],
-            [pl.BlockSpec((rows + extra, cols), lambda i, m: (0, 0))] * parts,
-            [pltpu.VMEM((rows, width), BF16)],
-        ),
+        in_specs=[pl.BlockSpec(memory_space=pltpu.SMEM), hbm, hbm, vmem],
+        out_specs=[vmem] * parts,
         out_shape=[jax.ShapeDtypeStruct((rows + extra, cols), BF16)] * parts,
+        scratch_shapes=[
+            pltpu.VMEM((rows, width), BF16),
+            pltpu.VMEM((width, width), BF16),
+            pltpu.VMEM((rows, width), BF16),
+            pltpu.SemaphoreType.DMA((parts + 1,)),
+        ],
         compiler_params=room_for(
-            ((2, width, width), BF16), ((8, rows + extra, width), BF16), ((rows, width), F32)
+            ((width, width), BF16), ((4, rows + extra, width), BF16), ((rows, width), F32)
         ),
         cost_estimate=cost(2 * rows * width * width, 2 * width * width + 4 * rows * width),
         name="queries",
     )(me, candidates, w_qu, block_owner.reshape(1, blocks))
+
+
+def assemble_kernel(count, *refs):
+    arrived, outs, owner_ref = refs[:count], refs[count:-1], refs[-1]
+    blocks = owner_ref.shape[1]
+    rows = outs[0].shape[0] // count
+    for k, ref in enumerate(arrived):
+        for h, out in enumerate(outs):
+            out[k * rows : (k + 1) * rows, :] = ref[:rows, h * HEAD : (h + 1) * HEAD]
+        below = ref[rows : rows + 16, :HEAD].astype(F32)
+        owner_ref[k : k + 1, :] = below[:1, :blocks].astype(jnp.int32)
+
+
+def assemble(arrived, rows, each, blocks):
+    count = len(arrived)
+    vmem = pl.BlockSpec(memory_space=pltpu.VMEM)
+    made = pl.pallas_call(
+        functools.partial(assemble_kernel, count),
+        in_specs=[vmem] * count,
+        out_specs=[vmem] * (each + 1),
+        out_shape=[jax.ShapeDtypeStruct((count * rows, HEAD), BF16)] * each
+        + [jax.ShapeDtypeStruct((count, blocks), jnp.int32)],
+        compiler_params=room_for(((4, count * rows, each * HEAD), BF16)),
+        cost_estimate=cost(0, 4 * count * rows * each * HEAD),
+        name="assemble",
+    )(*arrived)
+    return made[:each], made[each]
 
 
 def gate_kernel(_, cand_ref, w_ref, out_ref):
@@ -326,29 +364,12 @@
     return pieces[0] if len(pieces) == 1 else jnp.concatenate(pieces, axis=0)
 
 
-def direct(count):
-    return 2 <= count // 2 <= MOST_DIRECT
-
-
 def gather_plan(count, head):
-    if head % 2 == 1:
-        return stages(count, True)
-    if not direct(count):
-        return stages(count, False)
-    even = list(range(0, count, 2))
-    cut = len(even) // 2
-    plan = [(mask, (0,)) for mask in reversed(even[1:])]
-    return plan + [(1, tuple(even[:cut])), (1, tuple(even[cut:]))]
-
-
-def scatter_plan(count, head):
-    plan = stages(count, False)
-    if head % 2 == 1 or not direct(count):
-        return plan
-    even = list(range(0, count, 2))
-    cut = len(even) // 2
-    plan = [step for step in plan if step[0] != 1]
-    return plan + [(1, tuple(even[cut:])), (1, tuple(even[:cut]))]
+    return stages(count, head % 2 == 1)
+
+
+def scatter_plan(count):
+    return stages(count, False)
 
 
 def gather_queries(own, plan):
@@ -407,7 +428,8 @@
             ]
         )
 
-    owners = jnp.concatenate([a[mine, :blocks] for a in arrived]).astype(jnp.int32)
+    asked, owners = assemble(arrived, mine, each, blocks)
+    owners = owners.reshape(-1)
     code = owners ^ me_req
     total_blocks = n_ctx * blocks
     order = jnp.arange(total_blocks, dtype=jnp.int32)
@@ -422,9 +444,8 @@
 
     parts = [[None] * each for _ in range(n_ctx)]
     for h in range(each):
-        own = jnp.concatenate([a[:mine, h * HEAD : (h + 1) * HEAD] for a in arrived], axis=0)
-        arrays, where = gather_queries(own, gather_plan(n_req, h))
-        plan = scatter_plan(n_req, h)
+        arrays, where = gather_queries(asked[h], gather_plan(n_req, h))
+        plan = scatter_plan(n_req)
         groups = [[c ^ mask for c in codes] for mask, codes in plan] + [[0]]
         sums = {}
         for call in calls_of(n_req, h):
@@ -442,16 +463,14 @@
 
 
 def calls_of(count, head):
-    plan = scatter_plan(count, head)
+    plan = scatter_plan(count)
     everything = list(range(len(plan) + 1))
     inner = [i for i in range(len(plan)) if plan[i][0] == 1]
     if len(inner) < 2:
         return [everything]
-    if head % 2 == 0:
-        late = inner[0] if direct(count) else inner[-1]
-        return [[i for i in everything if i != late], [late]]
     last = inner[-1]
-    return [[i for i in everything if i not in (last, last - 1)], [last], [last - 1]]
+    rest = [i for i in everything if i != last]
+    return [rest, [last]] if head % 2 == 0 else [[last], rest]
 
 
 def solution(mesh):

time: 120 us -> 99.8 us (0.83)
  waiting for transfers between devices: 47.1 us -> 35.6 us
  local copies, waits for them, and re-layouts: 14 us -> 7.75 us
  starting transfers between devices: 32.2 us -> 29.9 us
    ppermute x31 -> x30, waiting for transfers between devices: 47.1 us -> 35.6 us  [swap(): return lax.ppermute(value, axis, [(i, i ^ mask) for i in range(count)])]
    unnamed x33 -> x23, local copies, waits for them, and re-layouts: 11.2 us -> 6.97 us
    ppermute x31 -> x30, starting transfers between devices: 32.2 us -> 29.9 us  [swap(): return lax.ppermute(value, axis, [(i, i ^ mask) for i in range(count)])]
    squeeze x4 -> x0, local copies, waits for them, and re-layouts: 2.02 us -> none  [on_device(): a[mine, :blocks]]
    concatenate x2 -> x0, other arithmetic: 1.54 us -> none  [on_device(): jnp.concatenate([a[:mine, h * HEAD:(h + 1) * HEAD] for a in arrived], axi...]
    pallas_call x5 -> x4, Pallas kernels: 14.8 us -> 14.1 us  [attend(): pl.pallas_call(functools.partial(attend_kernel, source, sink, events, roo...]
  transfers between devices with their start and end apart: 31 -> 30, of which waited for: 12 -> 11; matrix products, arithmetic and copies ran while one was open for 9% -> 3% of each run, Pallas kernels for 18% -> 22%
where the time goes in v4:
time: 99.8 us; the launch traced here: 99.6 us
  waiting for transfers between devices  35.6 us (36%)
  starting transfers between devices  29.9 us (30%)
  Pallas kernels  24.6 us (25%)
  local copies, waits for them, and re-layouts  7.75 us (8%)
  other arithmetic  1.51 us (2%)
    ppermute x30, waiting for transfers between devices, swap(): return lax.ppermute(value, axis, [(i, i ^ mask) for i in range(count)])  35.6 us
    ppermute x30, starting transfers between devices, swap(): return lax.ppermute(value, axis, [(i, i ^ mask) for i in range(count)])  29.9 us
    pallas_call x4, Pallas kernels, attend(): pl.pallas_call(functools.partial(attend_kernel, source, sink, events, roo...  14.1 us
    unnamed x23, local copies, waits for them, and re-layouts  6.97 us
    pallas_call x2, Pallas kernels, project_keys_values(): pl.pallas_call(functools.partial(keys_values_kernel, count, each), grid_s...  6.01 us
  transfers between devices with their start and end apart: 30, of which 11 were waited for; matrix products, arithmetic and copies ran while one was open for 3% of the time, Pallas kernels for 22%

profile of v4, /device:TPU:0, one launch (start us, length us, event | category | flops | bytes accessed | tf_op | source)
XLA Modules:
  0.0 99.6 jit_solution(17425440480348396683)
XLA Ops:
  0.0 2.3 %copy-done.1 = bf16[1024,2048]{1,0:T(8,128)(2,1)S(1)} copy-done((bf16[1024,2048]{1,0:T(8,128)(2,1)S(1)}, bf16[1024,2048]{1,0:T(8,128)(2,1)}, u32[]{:S(2)}) %copy-start.1) | copy-done | bytes 4194328
  4.1 1.7 %queries.1 = (bf16[144,256]{1,0:T(8,128)(2,1)S(1)}, bf16[144,256]{1,0:T(8,128)(2,1)S(1)}, bf16[144,256]{1,0:T(8,128)(2,1)S(1)}, bf16[144,256]{1,0:T(8,128)(2,1)S(1)}) custom-call(s32[1]{0:T(128)} %bitcast._.me_ref, bf16[128,1024]{1,0:T(8,128)(2,1)S(1)} %copy-done.4, bf16[1024,2048]{1,0:T(8,128)(2,1)S(1)} %copy-done.1, s32[1,48]{1,0:T(1,128)S(1)} %bitcast.2), custom_call_target="tpu_custom_call" | custom-call | flops 268435456 | bytes 2621440 | tf_op jit(solution)/shard_map/queries/pallas_call | solution.py:88
  6.4 2.6 %collective-permute-start.1 = (bf16[144,256]{1,0:T(8,128)(2,1)S(1)}, bf16[144,256]{1,0:T(8,128)(2,1)S(1)}, u32[]{:S(2)}, u32[]{:S(2)}) collective-permute-start(bf16[144,256]{1,0:T(8,128)(2,1)S(1)} %get-tuple-element.30), channel_id=1, source_target_pairs={{0,2},{1,3},{2,0},{3,1},{4,6},{5,7},{6,4},{7,5},{8,10},{9,11},{10,... | collective-permute-start | bytes 221192 | tf_op jit(solution)/shard_map/ppermute | solution.py:24
  9.0 1.4 %copy-done.3 = bf16[768,1024]{1,0:T(8,128)(2,1)S(1)} copy-done((bf16[768,1024]{1,0:T(8,128)(2,1)S(1)}, bf16[768,1024]{1,0:T(8,128)(2,1)}, u32[]{:S(2)}) %copy-start.3) | copy-done | bytes 1572888
  10.4 3.0 %shard_map.100 = (bf16[768,256]{1,0:T(8,128)(2,1)S(1)}, bf16[768,256]{1,0:T(8,128)(2,1)S(1)}, bf16[768,256]{1,0:T(8,128)(2,1)}, bf16[768,256]{1,0:T(8,128)(2,1)S(1)}) custom-call(s32[1]{0:T(128)} %bitcast._.me_ref, bf16[768,1024]{1,0:T(8,128)(2,1)S(1)} %copy-done.3, bf16[1024,2048]{1,0:T(8,128)(2,1)S(1)} %copy-done, bf16[1024,2048]{1,0:T(8,128)(2,1)S(1)} %copy-done, ...), custom_call_target="tpu_custom_call" | custom-call | flops 1610612736 | bytes 5242880 | tf_op jit(solution)/shard_map/pallas_call | solution.py:181
  13.6 4.1 %collective-permute-start.6 = (bf16[512,128]{1,0:T(8,128)(2,1)S(1)}, bf16[512,128]{1,0:T(8,128)(2,1)S(1)}, u32[]{:S(2)}, u32[]{:S(2)}) collective-permute-start(bf16[512,128]{1,0:T(8,128)(2,1)S(1)} %get-tuple-element.37.refs_4_), channel_id=1, source_target_pairs={{0,24},{4,28},{8,16},{12,20},{16,8},{20,12},{24,0},{28,4},{1,25},{... | collective-permute-start | bytes 393224 | tf_op jit(solution)/shard_map/ppermute | solution.py:24
  17.8 3.0 %shard_map.101 = (bf16[768,256]{1,0:T(8,128)(2,1)}, bf16[768,256]{1,0:T(8,128)(2,1)S(1)}, bf16[768,256]{1,0:T(8,128)(2,1)}, bf16[768,256]{1,0:T(8,128)(2,1)S(1)}) custom-call(s32[1]{0:T(128)} %bitcast._.me_ref, bf16[768,1024]{1,0:T(8,128)(2,1)S(1)} %copy-done.3, bf16[1024,2048]{1,0:T(8,128)(2,1)S(1)} %copy-done, bf16[1024,2048]{1,0:T(8,128)(2,1)S(1)} %copy-done, ...), custom_call_target="tpu_custom_call" | custom-call | flops 1610612736 | bytes 5242880 | tf_op jit(solution)/shard_map/pallas_call | solution.py:181
  21.5 1.5 %collective-permute-start.4 = (bf16[768,256]{1,0:T(8,128)(2,1)}, bf16[768,256]{1,0:T(8,128)(2,1)S(1)}, u32[]{:S(2)}, u32[]{:S(2)}) collective-permute-start(bf16[768,256]{1,0:T(8,128)(2,1)} %get-tuple-element.35), channel_id=1, source_target_pairs={{0,2},{1,3},{2,0},{3,1},{4,6},{5,7},{6,4},{7,5},{8,10},{9,11},{10,... | collective-permute-start | bytes 1179656 | tf_op jit(solution)/shard_map/ppermute | solution.py:24
  23.0 1.5 %collective-permute-start.17 = (bf16[512,128]{1,0:T(8,128)(2,1)S(1)}, bf16[512,128]{1,0:T(8,128)(2,1)S(1)}, u32[]{:S(2)}, u32[]{:S(2)}) collective-permute-start(bf16[512,128]{1,0:T(8,128)(2,1)S(1)} %get-tuple-element.46.refs_4_), channel_id=1, source_target_pairs={{0,4},{4,0},{8,12},{12,8},{16,20},{20,16},{24,28},{28,24},{1,5},{5... | collective-permute-start | bytes 393224 | tf_op jit(solution)/shard_map/ppermute | solution.py:24
  25.9 3.2 %collective-permute-done.17.refs_5_ = bf16[512,128]{1,0:T(8,128)(2,1)S(1)} collective-permute-done((bf16[512,128]{1,0:T(8,128)(2,1)S(1)}, bf16[512,128]{1,0:T(8,128)(2,1)S(1)}, u32[]{:S(2)}, u32[]{:S(2)}) %collective-permute-start.17) | collective-permute-done | bytes 131104 | tf_op jit(solution)/shard_map/ppermute | solution.py:24
  29.9 10.4 %collective-permute-done.8.refs_7_ = bf16[1024,128]{1,0:T(8,128)(2,1)} collective-permute-done((bf16[1024,128]{1,0:T(8,128)(2,1)}, bf16[1024,128]{1,0:T(8,128)(2,1)}, u32[]{:S(2)}, u32[]{:S(2)}) %collective-permute-start.8) | collective-permute-done | bytes 262176 | tf_op jit(solution)/shard_map/ppermute | solution.py:24
  40.7 1.6 %collective-permute-start.15 = (bf16[768,256]{1,0:T(8,128)(2,1)}, bf16[768,256]{1,0:T(8,128)(2,1)S(1)}, u32[]{:S(2)}, u32[]{:S(2)}) collective-permute-start(bf16[768,256]{1,0:T(8,128)(2,1)} %copy-done.9), channel_id=1, source_target_pairs={{0,2},{1,3},{2,0},{3,1},{4,6},{5,7},{6,4},{7,5},{8,10},{9,11},{10,... | collective-permute-start | bytes 1179656 | tf_op jit(solution)/shard_map/ppermute | solution.py:24
  42.6 2.0 %collective-permute-start.7 = (bf16[1024,128]{1,0:T(8,128)(2,1)}, bf16[1024,128]{1,0:T(8,128)(2,1)S(1)}, u32[]{:S(2)}, u32[]{:S(2)}) collective-permute-start(bf16[1024,128]{1,0:T(8,128)(2,1)} %constant_dynamic-update-slice_fusion), channel_id=1, source_target_pairs={{0,4},{4,0},{8,12},{12,8},{16,20},{20,16},{24,28},{28,24},{1,5},{5... | collective-permute-start | bytes 786440 | tf_op jit(solution)/shard_map/ppermute | solution.py:24
  44.6 3.3 %collective-permute-done.9.refs_4_ = bf16[1024,128]{1,0:T(8,128)(2,1)S(1)} collective-permute-done((bf16[1024,128]{1,0:T(8,128)(2,1)}, bf16[1024,128]{1,0:T(8,128)(2,1)S(1)}, u32[]{:S(2)}, u32[]{:S(2)}) %collective-permute-start.9) | collective-permute-done | bytes 262176 | tf_op jit(solution)/shard_map/ppermute | solution.py:24
  48.0 2.2 %shard_map.103 = bf16[1024,128]{1,0:T(8,128)(2,1)S(1)} custom-call(s32[192]{0:T(256)S(1)} %multiply_add_fusion.pos_ref, s32[8]{0:T(128)S(1)} %convert_reduce_fusion.1.count_ref, s32[2]{0:T(128)S(1)} %copy-done.7, bf16[768,256]{1,0:T(8,128)(2,1)S(1)} %get-tuple-element.33.refs_0_, bf16[768,256]{1,0:T(8,128)(2,1)S(1)} %collective-permute-done.3.refs_1_, ...), custom_call_target="tpu_custom_call" | custom-call | flops 402653184 | bytes 2097152 | tf_op jit(solution)/shard_map/pallas_call | solution.py:275
  50.2 2.4 %collective-permute-done.7.refs_6_ = bf16[1024,128]{1,0:T(8,128)(2,1)S(1)} collective-permute-done((bf16[1024,128]{1,0:T(8,128)(2,1)}, bf16[1024,128]{1,0:T(8,128)(2,1)S(1)}, u32[]{:S(2)}, u32[]{:S(2)}) %collective-permute-start.7) | collective-permute-done | bytes 262176 | tf_op jit(solution)/shard_map/ppermute | solution.py:24
  53.4 5.1 %shard_map.102 = (bf16[512,128]{1,0:T(8,128)(2,1)S(1)}, bf16[1024,128]{1,0:T(8,128)(2,1)S(1)}, bf16[1024,128]{1,0:T(8,128)(2,1)S(1)}, bf16[512,128]{1,0:T(8,128)(2,1)S(1)}) custom-call(s32[192]{0:T(256)S(1)} %multiply_add_fusion.pos_ref, s32[8]{0:T(128)S(1)} %convert_reduce_fusion.1.count_ref, s32[6]{0:T(128)S(1)} %copy-done.10, ...), custom_call_target="tpu_custom_call" | custom-call | flops 1207959552 | bytes 3145728 | tf_op jit(solution)/shard_map/pallas_call | solution.py:275
  58.5 1.3 %collective-permute-start.12 = (bf16[1024,128]{1,0:T(8,128)(2,1)S(1)}, bf16[1024,128]{1,0:T(8,128)(2,1)S(1)}, u32[]{:S(2)}, u32[]{:S(2)}) collective-permute-start(bf16[1024,128]{1,0:T(8,128)(2,1)S(1)} %get-tuple-element.40), channel_id=1, source_target_pairs={{0,4},{4,0},{8,12},{12,8},{16,20},{20,16},{24,28},{28,24},{1,5},{5... | collective-permute-start | bytes 786440 | tf_op jit(solution)/shard_map/ppermute | solution.py:24
  60.4 2.2 %shard_map.105 = bf16[1024,128]{1,0:T(8,128)(2,1)S(1)} custom-call(s32[192]{0:T(256)S(1)} %multiply_add_fusion.pos_ref, s32[8]{0:T(128)S(1)} %convert_reduce_fusion.1.count_ref, s32[2]{0:T(128)S(1)} %copy-done.7, bf16[768,256]{1,0:T(8,128)(2,1)S(1)} %get-tuple-element.42.refs_0_, bf16[768,256]{1,0:T(8,128)(2,1)S(1)} %collective-permute-done.14.refs_1_, ...), custom_call_target="tpu_custom_call" | custom-call | flops 402653184 | bytes 2097152 | tf_op jit(solution)/shard_map/pallas_call | solution.py:275
  62.6 1.9 %collective-permute-start.20 = (bf16[1024,128]{1,0:T(8,128)(2,1)S(1)}, bf16[1024,128]{1,0:T(8,128)(2,1)S(1)}, u32[]{:S(2)}, u32[]{:S(2)}) collective-permute-start(bf16[1024,128]{1,0:T(8,128)(2,1)S(1)} %shard_map.105), channel_id=1, source_target_pairs={{0,4},{4,0},{8,12},{12,8},{16,20},{20,16},{24,28},{28,24},{1,5},{5... | collective-permute-start | bytes 786440 | tf_op jit(solution)/shard_map/ppermute | solution.py:24
  64.7 2.8 %collective-permute-start.11 = (bf16[1024,128]{1,0:T(8,128)(2,1)S(1)}, bf16[1024,128]{1,0:T(8,128)(2,1)S(1)}, u32[]{:S(2)}, u32[]{:S(2)}) collective-permute-start(bf16[1024,128]{1,0:T(8,128)(2,1)S(1)} %pad_maximum_fusion.1), channel_id=1, source_target_pairs={{0,8},{4,12},{8,0},{12,4},{16,24},{20,28},{24,16},{28,20},{1,9},{5... | collective-permute-start | bytes 786440 | tf_op jit(solution)/shard_map/ppermute | solution.py:24
  67.5 4.7 %shard_map.104 = (bf16[512,128]{1,0:T(8,128)(2,1)S(1)}, bf16[1024,128]{1,0:T(8,128)(2,1)S(1)}, bf16[1024,128]{1,0:T(8,128)(2,1)S(1)}, bf16[512,128]{1,0:T(8,128)(2,1)S(1)}) custom-call(s32[192]{0:T(256)S(1)} %multiply_add_fusion.pos_ref, s32[8]{0:T(128)S(1)} %convert_reduce_fusion.1.count_ref, s32[6]{0:T(128)S(1)} %copy-done.10, ...), custom_call_target="tpu_custom_call" | custom-call | flops 1207959552 | bytes 3145728 | tf_op jit(solution)/shard_map/pallas_call | solution.py:275
  72.6 1.5 %collective-permute-done.11 = bf16[1024,128]{1,0:T(8,128)(2,1)S(1)} collective-permute-done((bf16[1024,128]{1,0:T(8,128)(2,1)S(1)}, bf16[1024,128]{1,0:T(8,128)(2,1)S(1)}, u32[]{:S(2)}, u32[]{:S(2)}) %collective-permute-start.11) | collective-permute-done | bytes 262176 | tf_op jit(solution)/shard_map/ppermute | solution.py:24
  74.2 1.3 %collective-permute-start.13 = (bf16[512,128]{1,0:T(8,128)(2,1)S(1)}, bf16[512,128]{1,0:T(8,128)(2,1)S(1)}, u32[]{:S(2)}, u32[]{:S(2)}) collective-permute-start(bf16[512,128]{1,0:T(8,128)(2,1)S(1)} %add_convert_fusion.3), channel_id=1, source_target_pairs={{0,24},{4,28},{8,16},{12,20},{16,8},{20,12},{24,0},{28,4},{1,25},{... | collective-permute-start | bytes 393224 | tf_op jit(solution)/shard_map/ppermute | solution.py:24
  76.4 6.0 %collective-permute-done.13 = bf16[512,128]{1,0:T(8,128)(2,1)S(1)} collective-permute-done((bf16[512,128]{1,0:T(8,128)(2,1)S(1)}, bf16[512,128]{1,0:T(8,128)(2,1)S(1)}, u32[]{:S(2)}, u32[]{:S(2)}) %collective-permute-start.13) | collective-permute-done | bytes 131104 | tf_op jit(solution)/shard_map/ppermute | solution.py:24
  82.5 3.5 %collective-permute-done.21 = bf16[1024,128]{1,0:T(8,128)(2,1)S(1)} collective-permute-done((bf16[1024,128]{1,0:T(8,128)(2,1)S(1)}, bf16[1024,128]{1,0:T(8,128)(2,1)S(1)}, u32[]{:S(2)}, u32[]{:S(2)}) %collective-permute-start.21) | collective-permute-done | bytes 262176 | tf_op jit(solution)/shard_map/ppermute | solution.py:24
  86.1 2.2 %collective-permute-start.23 = (bf16[512,128]{1,0:T(8,128)(2,1)S(1)}, bf16[512,128]{1,0:T(8,128)(2,1)S(1)}, u32[]{:S(2)}, u32[]{:S(2)}) collective-permute-start(bf16[512,128]{1,0:T(8,128)(2,1)S(1)} %add_convert_fusion), channel_id=1, source_target_pairs={{0,24},{4,28},{8,16},{12,20},{16,8},{20,12},{24,0},{28,4},{1,25},{... | collective-permute-start | bytes 393224 | tf_op jit(solution)/shard_map/ppermute | solution.py:24
  88.3 1.8 %collective-permute-start.26 = (bf16[128,128]{1,0:T(8,128)(2,1)S(1)}, bf16[128,128]{1,0:T(8,128)(2,1)S(1)}, u32[]{:S(2)}, u32[]{:S(2)}) collective-permute-start(bf16[128,128]{1,0:T(8,128)(2,1)S(1)} %get-tuple-element.63), channel_id=1, source_target_pairs={{0,2},{1,3},{2,0},{3,1},{4,6},{5,7},{6,4},{7,5},{8,10},{9,11},{10,... | collective-permute-start | bytes 98312 | tf_op jit(solution)/shard_map/ppermute | solution.py:24
  90.2 2.7 %collective-permute-done.23 = bf16[512,128]{1,0:T(8,128)(2,1)S(1)} collective-permute-done((bf16[512,128]{1,0:T(8,128)(2,1)S(1)}, bf16[512,128]{1,0:T(8,128)(2,1)S(1)}, u32[]{:S(2)}, u32[]{:S(2)}) %collective-permute-start.23) | collective-permute-done | bytes 131104 | tf_op jit(solution)/shard_map/ppermute | solution.py:24
  93.1 1.8 %collective-permute-start.27 = (bf16[128,128]{1,0:T(8,128)(2,1)S(1)}, bf16[128,128]{1,0:T(8,128)(2,1)S(1)}, u32[]{:S(2)}, u32[]{:S(2)}) collective-permute-start(bf16[128,128]{1,0:T(8,128)(2,1)S(1)} %get-tuple-element.60), channel_id=1, source_target_pairs={{0,2},{1,3},{2,0},{3,1},{4,6},{5,7},{6,4},{7,5},{8,10},{9,11},{10,... | collective-permute-start | bytes 98312 | tf_op jit(solution)/shard_map/ppermute | solution.py:24
  94.9 1.3 %gate.1.gate_ref = f32[4,128,256]{2,1,0:T(8,128)S(1)} custom-call(s32[1]{0:T(128)} %bitcast._.me_ref, bf16[128,1024]{1,0:T(8,128)(2,1)S(1)} %copy-done.5, bf16[1024,2048]{1,0:T(8,128)(2,1)S(1)} %copy-done.2), custom_call_target="tpu_custom_call" | custom-call | flops 268435456 | bytes 2883584 | tf_op jit(solution)/shard_map/gate/pallas_call | solution.py:141
  98.2 1.4 %finish.1 = bf16[128,1024]{1,0:T(8,128)(2,1)} custom-call(s32[1]{0:T(128)} %bitcast._.me_ref, bf16[128,1024]{1,0:T(8,128)(2,1)S(1)} %copy-done.5, f32[4,128,256]{2,1,0:T(8,128)S(1)} %gate.1.gate_ref, bf16[1024,1024]{1,0:T(8,128)(2,1)S(1)} %copy-done.6, f32[128,128]{1,0:T(8,128)S(1)} %slice.114.refs_0_, f32[128,128]{1,0:T(8,128)S(1)} %slice.121.refs_1_, ...), custom_call_target="tpu_custom_call" | custom-call | flops 268435456 | bytes 3407872 | tf_op jit(solution)/shard_map/finish/pallas_call | solution.py:322
  (81 shorter events, 11.7 us)
Async XLA Ops:
  5.8 7.7 %collective-permute-start = (bf16[144,256]{1,0:T(8,128)(2,1)S(1)}, bf16[144,256]{1,0:T(8,128)(2,1)S(1)}, u32[]{:S(2)}, u32[]{:S(2)}) collective-permute-start(bf16[144,256]{1,0:T(8,128)(2,1)S(1)} %get-tuple-element.29), channel_id=1, source_target_pairs={{0,1},{1,0},{2,3},{3,2},{4,5},{5,4},{6,7},{7,6},{8,9},{9,8},{10,11... | collective-permute-start | bytes 221192 | tf_op jit(solution)/shard_map/ppermute | solution.py:24
  6.4 7.2 %collective-permute-start.1 = (bf16[144,256]{1,0:T(8,128)(2,1)S(1)}, bf16[144,256]{1,0:T(8,128)(2,1)S(1)}, u32[]{:S(2)}, u32[]{:S(2)}) collective-permute-start(bf16[144,256]{1,0:T(8,128)(2,1)S(1)} %get-tuple-element.30), channel_id=1, source_target_pairs={{0,2},{1,3},{2,0},{3,1},{4,6},{5,7},{6,4},{7,5},{8,10},{9,11},{10,... | collective-permute-start | bytes 221192 | tf_op jit(solution)/shard_map/ppermute | solution.py:24
  8.9 4.6 %collective-permute-start.2 = (bf16[144,256]{1,0:T(8,128)(2,1)S(1)}, bf16[144,256]{1,0:T(8,128)(2,1)S(1)}, u32[]{:S(2)}, u32[]{:S(2)}) collective-permute-start(bf16[144,256]{1,0:T(8,128)(2,1)S(1)} %get-tuple-element.31), channel_id=1, source_target_pairs={{0,3},{1,2},{2,1},{3,0},{4,7},{5,6},{6,5},{7,4},{8,11},{9,10},{10,... | collective-permute-start | bytes 221192 | tf_op jit(solution)/shard_map/ppermute | solution.py:24
  13.4 27.3 %collective-permute-start.3 = (bf16[768,256]{1,0:T(8,128)(2,1)}, bf16[768,256]{1,0:T(8,128)(2,1)S(1)}, u32[]{:S(2)}, u32[]{:S(2)}) collective-permute-start(bf16[768,256]{1,0:T(8,128)(2,1)} %get-tuple-element.34), channel_id=1, source_target_pairs={{0,1},{1,0},{2,3},{3,2},{4,5},{5,4},{6,7},{7,6},{8,9},{9,8},{10,11... | collective-permute-start | bytes 1179656 | tf_op jit(solution)/shard_map/ppermute | solution.py:24
  13.6 34.4 %copy-start.7 = (s32[2]{0:T(128)S(1)}, s32[2]{0:T(128)}, u32[]{:S(2)}) copy-start(s32[2]{0:T(128)} %constant.18.clone.code_ref) | copy-start | bytes 28
  13.6 11.6 %collective-permute-start.6 = (bf16[512,128]{1,0:T(8,128)(2,1)S(1)}, bf16[512,128]{1,0:T(8,128)(2,1)S(1)}, u32[]{:S(2)}, u32[]{:S(2)}) collective-permute-start(bf16[512,128]{1,0:T(8,128)(2,1)S(1)} %get-tuple-element.37.refs_4_), channel_id=1, source_target_pairs={{0,24},{4,28},{8,16},{12,20},{16,8},{20,12},{24,0},{28,4},{1,25},{... | collective-permute-start | bytes 393224 | tf_op jit(solution)/shard_map/ppermute | solution.py:24
  21.5 31.9 %copy-start.10 = (s32[6]{0:T(128)S(1)}, s32[6]{0:T(128)}, u32[]{:S(2)}) copy-start(s32[6]{0:T(128)} %constant.17.clone.code_ref) | copy-start | bytes 76
  21.5 20.8 %collective-permute-start.4 = (bf16[768,256]{1,0:T(8,128)(2,1)}, bf16[768,256]{1,0:T(8,128)(2,1)S(1)}, u32[]{:S(2)}, u32[]{:S(2)}) collective-permute-start(bf16[768,256]{1,0:T(8,128)(2,1)} %get-tuple-element.35), channel_id=1, source_target_pairs={{0,2},{1,3},{2,0},{3,1},{4,6},{5,7},{6,4},{7,5},{8,10},{9,11},{10,... | collective-permute-start | bytes 1179656 | tf_op jit(solution)/shard_map/ppermute | solution.py:24
  23.0 19.6 %collective-permute-start.5 = (bf16[768,256]{1,0:T(8,128)(2,1)}, bf16[768,256]{1,0:T(8,128)(2,1)S(1)}, u32[]{:S(2)}, u32[]{:S(2)}) collective-permute-start(bf16[768,256]{1,0:T(8,128)(2,1)} %get-tuple-element.36), channel_id=1, source_target_pairs={{0,3},{1,2},{2,1},{3,0},{4,7},{5,6},{6,5},{7,4},{8,11},{9,10},{10,... | collective-permute-start | bytes 1179656 | tf_op jit(solution)/shard_map/ppermute | solution.py:24
  23.0 6.0 %collective-permute-start.17 = (bf16[512,128]{1,0:T(8,128)(2,1)S(1)}, bf16[512,128]{1,0:T(8,128)(2,1)S(1)}, u32[]{:S(2)}, u32[]{:S(2)}) collective-permute-start(bf16[512,128]{1,0:T(8,128)(2,1)S(1)} %get-tuple-element.46.refs_4_), channel_id=1, source_target_pairs={{0,4},{4,0},{8,12},{12,8},{16,20},{20,16},{24,28},{28,24},{1,5},{5... | collective-permute-start | bytes 393224 | tf_op jit(solution)/shard_map/ppermute | solution.py:24
  25.9 14.5 %collective-permute-start.8 = (bf16[1024,128]{1,0:T(8,128)(2,1)}, bf16[1024,128]{1,0:T(8,128)(2,1)}, u32[]{:S(2)}, u32[]{:S(2)}) collective-permute-start(bf16[1024,128]{1,0:T(8,128)(2,1)} %constant_dynamic-update-slice_fusion), channel_id=1, source_target_pairs={{0,8},{4,12},{8,0},{12,4},{16,24},{20,28},{24,16},{28,20},{1,9},{5... | collective-permute-start | bytes 786440 | tf_op jit(solution)/shard_map/ppermute | solution.py:24
  29.8 10.8 %collective-permute-start.18 = (bf16[1024,128]{1,0:T(8,128)(2,1)}, bf16[1024,128]{1,0:T(8,128)(2,1)S(1)}, u32[]{:S(2)}, u32[]{:S(2)}) collective-permute-start(bf16[1024,128]{1,0:T(8,128)(2,1)} %pad_maximum_fusion.2), channel_id=1, source_target_pairs={{0,24},{4,28},{8,16},{12,20},{16,8},{20,12},{24,0},{28,4},{1,25},{... | collective-permute-start | bytes 786440 | tf_op jit(solution)/shard_map/ppermute | solution.py:24
  40.4 7.5 %collective-permute-start.9 = (bf16[1024,128]{1,0:T(8,128)(2,1)}, bf16[1024,128]{1,0:T(8,128)(2,1)S(1)}, u32[]{:S(2)}, u32[]{:S(2)}) collective-permute-start(bf16[1024,128]{1,0:T(8,128)(2,1)} %collective-permute-done.8.refs_7_), channel_id=1, source_target_pairs={{0,4},{4,0},{8,12},{12,8},{16,20},{20,16},{24,28},{28,24},{1,5},{5... | collective-permute-start | bytes 786440 | tf_op jit(solution)/shard_map/ppermute | solution.py:24
  40.6 17.9 %collective-permute-start.14 = (bf16[768,256]{1,0:T(8,128)(2,1)S(1)}, bf16[768,256]{1,0:T(8,128)(2,1)S(1)}, u32[]{:S(2)}, u32[]{:S(2)}) collective-permute-start(bf16[768,256]{1,0:T(8,128)(2,1)S(1)} %get-tuple-element.43), channel_id=1, source_target_pairs={{0,1},{1,0},{2,3},{3,2},{4,5},{5,4},{6,7},{7,6},{8,9},{9,8},{10,11... | collective-permute-start | bytes 1179656 | tf_op jit(solution)/shard_map/ppermute | solution.py:24
  40.7 19.1 %collective-permute-start.15 = (bf16[768,256]{1,0:T(8,128)(2,1)}, bf16[768,256]{1,0:T(8,128)(2,1)S(1)}, u32[]{:S(2)}, u32[]{:S(2)}) collective-permute-start(bf16[768,256]{1,0:T(8,128)(2,1)} %copy-done.9), channel_id=1, source_target_pairs={{0,2},{1,3},{2,0},{3,1},{4,6},{5,7},{6,4},{7,5},{8,10},{9,11},{10,... | collective-permute-start | bytes 1179656 | tf_op jit(solution)/shard_map/ppermute | solution.py:24
  42.3 18.2 %collective-permute-start.16 = (bf16[768,256]{1,0:T(8,128)(2,1)S(1)}, bf16[768,256]{1,0:T(8,128)(2,1)S(1)}, u32[]{:S(2)}, u32[]{:S(2)}) collective-permute-start(bf16[768,256]{1,0:T(8,128)(2,1)S(1)} %get-tuple-element.45), channel_id=1, source_target_pairs={{0,3},{1,2},{2,1},{3,0},{4,7},{5,6},{6,5},{7,4},{8,11},{9,10},{10,... | collective-permute-start | bytes 1179656 | tf_op jit(solution)/shard_map/ppermute | solution.py:24
  42.6 10.0 %collective-permute-start.7 = (bf16[1024,128]{1,0:T(8,128)(2,1)}, bf16[1024,128]{1,0:T(8,128)(2,1)S(1)}, u32[]{:S(2)}, u32[]{:S(2)}) collective-permute-start(bf16[1024,128]{1,0:T(8,128)(2,1)} %constant_dynamic-update-slice_fusion), channel_id=1, source_target_pairs={{0,4},{4,0},{8,12},{12,8},{16,20},{20,16},{24,28},{28,24},{1,5},{5... | collective-permute-start | bytes 786440 | tf_op jit(solution)/shard_map/ppermute | solution.py:24
  47.9 12.5 %collective-permute-start.19 = (bf16[2048,128]{1,0:T(8,128)(2,1)S(1)}, bf16[2048,128]{1,0:T(8,128)(2,1)S(1)}, u32[]{:S(2)}, u32[]{:S(2)}) collective-permute-start(bf16[2048,128]{1,0:T(8,128)(2,1)S(1)} %pad_maximum_fusion), channel_id=1, source_target_pairs={{0,8},{4,12},{8,0},{12,4},{16,24},{20,28},{24,16},{28,20},{1,9},{5... | collective-permute-start | bytes 1572872 | tf_op jit(solution)/shard_map/ppermute | solution.py:24
  52.6 12.0 %collective-permute-start.10 = (bf16[1024,128]{1,0:T(8,128)(2,1)S(1)}, bf16[1024,128]{1,0:T(8,128)(2,1)S(1)}, u32[]{:S(2)}, u32[]{:S(2)}) collective-permute-start(bf16[1024,128]{1,0:T(8,128)(2,1)S(1)} %shard_map.103), channel_id=1, source_target_pairs={{0,4},{4,0},{8,12},{12,8},{16,20},{20,16},{24,28},{28,24},{1,5},{5... | collective-permute-start | bytes 786440 | tf_op jit(solution)/shard_map/ppermute | solution.py:24
  58.5 14.1 %collective-permute-start.12 = (bf16[1024,128]{1,0:T(8,128)(2,1)S(1)}, bf16[1024,128]{1,0:T(8,128)(2,1)S(1)}, u32[]{:S(2)}, u32[]{:S(2)}) collective-permute-start(bf16[1024,128]{1,0:T(8,128)(2,1)S(1)} %get-tuple-element.40), channel_id=1, source_target_pairs={{0,4},{4,0},{8,12},{12,8},{16,20},{20,16},{24,28},{28,24},{1,5},{5... | collective-permute-start | bytes 786440 | tf_op jit(solution)/shard_map/ppermute | solution.py:24
  62.6 9.9 %collective-permute-start.20 = (bf16[1024,128]{1,0:T(8,128)(2,1)S(1)}, bf16[1024,128]{1,0:T(8,128)(2,1)S(1)}, u32[]{:S(2)}, u32[]{:S(2)}) collective-permute-start(bf16[1024,128]{1,0:T(8,128)(2,1)S(1)} %shard_map.105), channel_id=1, source_target_pairs={{0,4},{4,0},{8,12},{12,8},{16,20},{20,16},{24,28},{28,24},{1,5},{5... | collective-permute-start | bytes 786440 | tf_op jit(solution)/shard_map/ppermute | solution.py:24
  64.7 9.4 %collective-permute-start.11 = (bf16[1024,128]{1,0:T(8,128)(2,1)S(1)}, bf16[1024,128]{1,0:T(8,128)(2,1)S(1)}, u32[]{:S(2)}, u32[]{:S(2)}) collective-permute-start(bf16[1024,128]{1,0:T(8,128)(2,1)S(1)} %pad_maximum_fusion.1), channel_id=1, source_target_pairs={{0,8},{4,12},{8,0},{12,4},{16,24},{20,28},{24,16},{28,20},{1,9},{5... | collective-permute-start | bytes 786440 | tf_op jit(solution)/shard_map/ppermute | solution.py:24
  72.1 10.3 %collective-permute-start.22 = (bf16[1024,128]{1,0:T(8,128)(2,1)S(1)}, bf16[1024,128]{1,0:T(8,128)(2,1)S(1)}, u32[]{:S(2)}, u32[]{:S(2)}) collective-permute-start(bf16[1024,128]{1,0:T(8,128)(2,1)S(1)} %get-tuple-element.49), channel_id=1, source_target_pairs={{0,4},{4,0},{8,12},{12,8},{16,20},{20,16},{24,28},{28,24},{1,5},{5... | collective-permute-start | bytes 786440 | tf_op jit(solution)/shard_map/ppermute | solution.py:24
  74.2 8.2 %collective-permute-start.13 = (bf16[512,128]{1,0:T(8,128)(2,1)S(1)}, bf16[512,128]{1,0:T(8,128)(2,1)S(1)}, u32[]{:S(2)}, u32[]{:S(2)}) collective-permute-start(bf16[512,128]{1,0:T(8,128)(2,1)S(1)} %add_convert_fusion.3), channel_id=1, source_target_pairs={{0,24},{4,28},{8,16},{12,20},{16,8},{20,12},{24,0},{28,4},{1,25},{... | collective-permute-start | bytes 393224 | tf_op jit(solution)/shard_map/ppermute | solution.py:24
  75.5 10.5 %collective-permute-start.21 = (bf16[1024,128]{1,0:T(8,128)(2,1)S(1)}, bf16[1024,128]{1,0:T(8,128)(2,1)S(1)}, u32[]{:S(2)}, u32[]{:S(2)}) collective-permute-start(bf16[1024,128]{1,0:T(8,128)(2,1)S(1)} %pad_maximum_fusion.3), channel_id=1, source_target_pairs={{0,8},{4,12},{8,0},{12,4},{16,24},{20,28},{24,16},{28,20},{1,9},{5... | collective-permute-start | bytes 786440 | tf_op jit(solution)/shard_map/ppermute | solution.py:24
  86.1 6.8 %collective-permute-start.23 = (bf16[512,128]{1,0:T(8,128)(2,1)S(1)}, bf16[512,128]{1,0:T(8,128)(2,1)S(1)}, u32[]{:S(2)}, u32[]{:S(2)}) collective-permute-start(bf16[512,128]{1,0:T(8,128)(2,1)S(1)} %add_convert_fusion), channel_id=1, source_target_pairs={{0,24},{4,28},{8,16},{12,20},{16,8},{20,12},{24,0},{28,4},{1,25},{... | collective-permute-start | bytes 393224 | tf_op jit(solution)/shard_map/ppermute | solution.py:24
  88.2 6.7 %collective-permute-start.24 = (bf16[128,128]{1,0:T(8,128)(2,1)S(1)}, bf16[128,128]{1,0:T(8,128)(2,1)S(1)}, u32[]{:S(2)}, u32[]{:S(2)}) collective-permute-start(bf16[128,128]{1,0:T(8,128)(2,1)S(1)} %get-tuple-element.64), channel_id=1, source_target_pairs={{0,1},{1,0},{2,3},{3,2},{4,5},{5,4},{6,7},{7,6},{8,9},{9,8},{10,11... | collective-permute-start | bytes 98312 | tf_op jit(solution)/shard_map/ppermute | solution.py:24
  88.3 8.0 %collective-permute-start.26 = (bf16[128,128]{1,0:T(8,128)(2,1)S(1)}, bf16[128,128]{1,0:T(8,128)(2,1)S(1)}, u32[]{:S(2)}, u32[]{:S(2)}) collective-permute-start(bf16[128,128]{1,0:T(8,128)(2,1)S(1)} %get-tuple-element.63), channel_id=1, source_target_pairs={{0,2},{1,3},{2,0},{3,1},{4,6},{5,7},{6,4},{7,5},{8,10},{9,11},{10,... | collective-permute-start | bytes 98312 | tf_op jit(solution)/shard_map/ppermute | solution.py:24
  90.1 6.2 %collective-permute-start.28 = (bf16[128,128]{1,0:T(8,128)(2,1)S(1)}, bf16[128,128]{1,0:T(8,128)(2,1)S(1)}, u32[]{:S(2)}, u32[]{:S(2)}) collective-permute-start(bf16[128,128]{1,0:T(8,128)(2,1)S(1)} %get-tuple-element.62), channel_id=1, source_target_pairs={{0,3},{1,2},{2,1},{3,0},{4,7},{5,6},{6,5},{7,4},{8,11},{9,10},{10,... | collective-permute-start | bytes 98312 | tf_op jit(solution)/shard_map/ppermute | solution.py:24
  93.0 3.4 %collective-permute-start.25 = (bf16[128,128]{1,0:T(8,128)(2,1)S(1)}, bf16[128,128]{1,0:T(8,128)(2,1)S(1)}, u32[]{:S(2)}, u32[]{:S(2)}) collective-permute-start(bf16[128,128]{1,0:T(8,128)(2,1)S(1)} %get-tuple-element.61), channel_id=1, source_target_pairs={{0,1},{1,0},{2,3},{3,2},{4,5},{5,4},{6,7},{7,6},{8,9},{9,8},{10,11... | collective-permute-start | bytes 98312 | tf_op jit(solution)/shard_map/ppermute | solution.py:24
  93.1 4.0 %collective-permute-start.27 = (bf16[128,128]{1,0:T(8,128)(2,1)S(1)}, bf16[128,128]{1,0:T(8,128)(2,1)S(1)}, u32[]{:S(2)}, u32[]{:S(2)}) collective-permute-start(bf16[128,128]{1,0:T(8,128)(2,1)S(1)} %get-tuple-element.60), channel_id=1, source_target_pairs={{0,2},{1,3},{2,0},{3,1},{4,6},{5,7},{6,4},{7,5},{8,10},{9,11},{10,... | collective-permute-start | bytes 98312 | tf_op jit(solution)/shard_map/ppermute | solution.py:24
  94.9 3.4 %collective-permute-start.29 = (bf16[128,128]{1,0:T(8,128)(2,1)S(1)}, bf16[128,128]{1,0:T(8,128)(2,1)S(1)}, u32[]{:S(2)}, u32[]{:S(2)}) collective-permute-start(bf16[128,128]{1,0:T(8,128)(2,1)S(1)} %get-tuple-element.59), channel_id=1, source_target_pairs={{0,3},{1,2},{2,1},{3,0},{4,7},{5,6},{6,5},{7,4},{8,11},{9,10},{10,... | collective-permute-start | bytes 98312 | tf_op jit(solution)/shard_map/ppermute | solution.py:24
  (9 other events, 98.6 us)

commit v5 on v4

--- a/solution.py
+++ b/solution.py
@@ -10,6 +10,7 @@
 
 HEAD = 128
 TILE = 256
+VMEM = 67043328
 BF16 = jnp.bfloat16
 F32 = jnp.float32
 
@@ -96,9 +97,7 @@
             pltpu.VMEM((rows, width), BF16),
             pltpu.SemaphoreType.DMA((parts + 1,)),
         ],
-        compiler_params=room_for(
-            ((width, width), BF16), ((4, rows + extra, width), BF16), ((rows, width), F32)
-        ),
+        compiler_params=pltpu.CompilerParams(vmem_limit_bytes=VMEM - 2 * w_qu.size),
         cost_estimate=cost(2 * rows * width * width, 2 * width * width + 4 * rows * width),
         name="queries",
     )(me, candidates, w_qu, block_owner.reshape(1, blocks))

time: 99.8 us -> 104 us (1.042)
  waiting for transfers between devices: 35.6 us -> 31.3 us
  Pallas kernels: 24.6 us -> 28.2 us
  local copies, waits for them, and re-layouts: 7.75 us -> 10.1 us
  other arithmetic: 1.51 us -> 3.29 us
    ppermute x30, waiting for transfers between devices: 35.6 us -> 31.3 us  [swap(): return lax.ppermute(value, axis, [(i, i ^ mask) for i in range(count)])]
    pallas_call x1, Pallas kernels: 1.69 us -> 4.04 us  [project_queries(): pl.pallas_call(query_kernel, in_specs=[pl.BlockSpec(memory_space=pltpu.SM...]
    unnamed x23 -> x41, local copies, waits for them, and re-layouts: 6.97 us -> 9.02 us
    concatenate x4, other arithmetic: 0.79 us -> 1.9 us  [joined(): return pieces[0] if len(pieces) == 1 else jnp.concatenate(pieces, axis=0)]
  transfers between devices with their start and end apart: 30 -> 30, of which waited for: 11 -> 11; matrix products, arithmetic and copies ran while one was open for 3% -> 5% of each run, Pallas kernels for 22% -> 22%
where the time goes in v5:
time: 104 us
  waiting for transfers between devices  31.3 us (30%)
  starting transfers between devices  30.7 us (30%)
  Pallas kernels  28.2 us (27%)
  local copies, waits for them, and re-layouts  10.1 us (10%)
  other arithmetic  3.29 us (3%)
    ppermute x30, waiting for transfers between devices, swap(): return lax.ppermute(value, axis, [(i, i ^ mask) for i in range(count)])  31.3 us
    ppermute x30, starting transfers between devices, swap(): return lax.ppermute(value, axis, [(i, i ^ mask) for i in range(count)])  30.7 us
    pallas_call x4, Pallas kernels, attend(): pl.pallas_call(functools.partial(attend_kernel, source, sink, events, roo...  14.7 us
    unnamed x41, local copies, waits for them, and re-layouts  9.02 us
    pallas_call x2, Pallas kernels, project_keys_values(): pl.pallas_call(functools.partial(keys_values_kernel, count, each), grid_s...  6.08 us
    pallas_call x1, Pallas kernels, project_queries(): pl.pallas_call(query_kernel, in_specs=[pl.BlockSpec(memory_space=pltpu.SM...  4.04 us
  transfers between devices with their start and end apart: 30, of which 11 were waited for; matrix products, arithmetic and copies ran while one was open for 5% of the time, Pallas kernels for 22%

profile of v5, /device:TPU:0, one launch (start us, length us, event | category | flops | bytes accessed | tf_op | source)
XLA Modules:
  0.0 103.9 jit_solution(11067456550946238888)
XLA Ops:
  0.0 4.0 %queries.1 = (bf16[144,256]{1,0:T(8,128)(2,1)}, bf16[144,256]{1,0:T(8,128)(2,1)}, bf16[144,256]{1,0:T(8,128)(2,1)}, bf16[144,256]{1,0:T(8,128)(2,1)}) custom-call(s32[1]{0:T(128)} %bitcast._.me_ref, bf16[128,1024]{1,0:T(8,128)(2,1)} %cand_ref.3, bf16[1024,2048]{1,0:T(8,128)(2,1)} %w_hbm.1, s32[1,48]{1,0:T(1,128)} %bitcast.2), custom_call_target="tpu_custom_call" | custom-call | flops 268435456 | bytes 2621440 | tf_op jit(solution)/shard_map/queries/pallas_call | solution.py:89
  4.6 2.6 %collective-permute-start.1 = (bf16[144,256]{1,0:T(8,128)(2,1)}, bf16[144,256]{1,0:T(8,128)(2,1)S(1)}, u32[]{:S(2)}, u32[]{:S(2)}) collective-permute-start(bf16[144,256]{1,0:T(8,128)(2,1)} %get-tuple-element.30), channel_id=1, source_target_pairs={{0,2},{1,3},{2,0},{3,1},{4,6},{5,7},{6,4},{7,5},{8,10},{9,11},{10,... | collective-permute-start | bytes 221192 | tf_op jit(solution)/shard_map/ppermute | solution.py:25
  7.2 1.4 %copy-done.2 = bf16[768,1024]{1,0:T(8,128)(2,1)S(1)} copy-done((bf16[768,1024]{1,0:T(8,128)(2,1)S(1)}, bf16[768,1024]{1,0:T(8,128)(2,1)}, u32[]{:S(2)}) %copy-start.2) | copy-done | bytes 1572888
  8.6 3.0 %shard_map.100 = (bf16[768,256]{1,0:T(8,128)(2,1)S(1)}, bf16[768,256]{1,0:T(8,128)(2,1)S(1)}, bf16[768,256]{1,0:T(8,128)(2,1)}, bf16[768,256]{1,0:T(8,128)(2,1)S(1)}) custom-call(s32[1]{0:T(128)} %bitcast._.me_ref, bf16[768,1024]{1,0:T(8,128)(2,1)S(1)} %copy-done.2, bf16[1024,2048]{1,0:T(8,128)(2,1)S(1)} %copy-done, bf16[1024,2048]{1,0:T(8,128)(2,1)S(1)} %copy-done, ...), custom_call_target="tpu_custom_call" | custom-call | flops 1610612736 | bytes 5242880 | tf_op jit(solution)/shard_map/pallas_call | solution.py:180
  16.0 4.1 %collective-permute-start.6 = (bf16[512,128]{1,0:T(8,128)(2,1)}, bf16[512,128]{1,0:T(8,128)(2,1)}, u32[]{:S(2)}, u32[]{:S(2)}) collective-permute-start(bf16[512,128]{1,0:T(8,128)(2,1)} %get-tuple-element.37.refs_4_), channel_id=1, source_target_pairs={{0,24},{4,28},{8,16},{12,20},{16,8},{20,12},{24,0},{28,4},{1,25},{... | collective-permute-start | bytes 393224 | tf_op jit(solution)/shard_map/ppermute | solution.py:25
  20.1 3.0 %shard_map.101 = (bf16[768,256]{1,0:T(8,128)(2,1)}, bf16[768,256]{1,0:T(8,128)(2,1)S(1)}, bf16[768,256]{1,0:T(8,128)(2,1)}, bf16[768,256]{1,0:T(8,128)(2,1)S(1)}) custom-call(s32[1]{0:T(128)} %bitcast._.me_ref, bf16[768,1024]{1,0:T(8,128)(2,1)S(1)} %copy-done.2, bf16[1024,2048]{1,0:T(8,128)(2,1)S(1)} %copy-done, bf16[1024,2048]{1,0:T(8,128)(2,1)S(1)} %copy-done, ...), custom_call_target="tpu_custom_call" | custom-call | flops 1610612736 | bytes 5242880 | tf_op jit(solution)/shard_map/pallas_call | solution.py:180
  24.6 1.5 %collective-permute-start.4 = (bf16[768,256]{1,0:T(8,128)(2,1)}, bf16[768,256]{1,0:T(8,128)(2,1)S(1)}, u32[]{:S(2)}, u32[]{:S(2)}) collective-permute-start(bf16[768,256]{1,0:T(8,128)(2,1)} %get-tuple-element.35), channel_id=1, source_target_pairs={{0,2},{1,3},{2,0},{3,1},{4,6},{5,7},{6,4},{7,5},{8,10},{9,11},{10,... | collective-permute-start | bytes 1179656 | tf_op jit(solution)/shard_map/ppermute | solution.py:25
  26.1 1.5 %collective-permute-start.17 = (bf16[512,128]{1,0:T(8,128)(2,1)}, bf16[512,128]{1,0:T(8,128)(2,1)S(1)}, u32[]{:S(2)}, u32[]{:S(2)}) collective-permute-start(bf16[512,128]{1,0:T(8,128)(2,1)} %copy-done.5), channel_id=1, source_target_pairs={{0,4},{4,0},{8,12},{12,8},{16,20},{20,16},{24,28},{28,24},{1,5},{5... | collective-permute-start | bytes 393224 | tf_op jit(solution)/shard_map/ppermute | solution.py:25
  29.7 2.7 %collective-permute-done.17.refs_5_ = bf16[512,128]{1,0:T(8,128)(2,1)S(1)} collective-permute-done((bf16[512,128]{1,0:T(8,128)(2,1)}, bf16[512,128]{1,0:T(8,128)(2,1)S(1)}, u32[]{:S(2)}, u32[]{:S(2)}) %collective-permute-start.17) | collective-permute-done | bytes 131104 | tf_op jit(solution)/shard_map/ppermute | solution.py:25
  34.2 9.7 %collective-permute-done.8.refs_7_ = bf16[1024,128]{1,0:T(8,128)(2,1)S(1)} collective-permute-done((bf16[1024,128]{1,0:T(8,128)(2,1)S(1)}, bf16[1024,128]{1,0:T(8,128)(2,1)S(1)}, u32[]{:S(2)}, u32[]{:S(2)}) %collective-permute-start.8) | collective-permute-done | bytes 262176 | tf_op jit(solution)/shard_map/ppermute | solution.py:25
  45.1 1.6 %collective-permute-start.15 = (bf16[768,256]{1,0:T(8,128)(2,1)}, bf16[768,256]{1,0:T(8,128)(2,1)S(1)}, u32[]{:S(2)}, u32[]{:S(2)}) collective-permute-start(bf16[768,256]{1,0:T(8,128)(2,1)} %copy-done.18), channel_id=1, source_target_pairs={{0,2},{1,3},{2,0},{3,1},{4,6},{5,7},{6,4},{7,5},{8,10},{9,11},{10,... | collective-permute-start | bytes 1179656 | tf_op jit(solution)/shard_map/ppermute | solution.py:25
  47.0 2.0 %collective-permute-start.7 = (bf16[1024,128]{1,0:T(8,128)(2,1)S(1)}, bf16[1024,128]{1,0:T(8,128)(2,1)S(1)}, u32[]{:S(2)}, u32[]{:S(2)}) collective-permute-start(bf16[1024,128]{1,0:T(8,128)(2,1)S(1)} %constant_dynamic-update-slice_fusion), channel_id=1, source_target_pairs={{0,4},{4,0},{8,12},{12,8},{16,20},{20,16},{24,28},{28,24},{1,5},{5... | collective-permute-start | bytes 786440 | tf_op jit(solution)/shard_map/ppermute | solution.py:25
  49.0 1.2 %collective-permute-done.9.refs_4_ = bf16[1024,128]{1,0:T(8,128)(2,1)S(1)} collective-permute-done((bf16[1024,128]{1,0:T(8,128)(2,1)S(1)}, bf16[1024,128]{1,0:T(8,128)(2,1)S(1)}, u32[]{:S(2)}, u32[]{:S(2)}) %collective-permute-start.9) | collective-permute-done | bytes 262176 | tf_op jit(solution)/shard_map/ppermute | solution.py:25
  52.8 2.6 %shard_map.103 = bf16[1024,128]{1,0:T(8,128)(2,1)S(1)} custom-call(s32[192]{0:T(256)S(1)} %multiply_add_fusion.pos_ref, s32[8]{0:T(128)S(1)} %convert_reduce_fusion.1.count_ref, s32[2]{0:T(128)S(1)} %copy-done.14, bf16[768,256]{1,0:T(8,128)(2,1)S(1)} %copy-done.8, bf16[768,256]{1,0:T(8,128)(2,1)} %collective-permute-done.3.refs_1_, ...), custom_call_target="tpu_custom_call" | custom-call | flops 402653184 | bytes 2097152 | tf_op jit(solution)/shard_map/pallas_call | solution.py:274
  55.8 1.7 %collective-permute-start.10 = (bf16[1024,128]{1,0:T(8,128)(2,1)S(1)}, bf16[1024,128]{1,0:T(8,128)(2,1)S(1)}, u32[]{:S(2)}, u32[]{:S(2)}) collective-permute-start(bf16[1024,128]{1,0:T(8,128)(2,1)S(1)} %shard_map.103), channel_id=1, source_target_pairs={{0,4},{4,0},{8,12},{12,8},{16,20},{20,16},{24,28},{28,24},{1,5},{5... | collective-permute-start | bytes 786440 | tf_op jit(solution)/shard_map/ppermute | solution.py:25
  57.5 5.2 %shard_map.102 = (bf16[512,128]{1,0:T(8,128)(2,1)S(1)}, bf16[1024,128]{1,0:T(8,128)(2,1)S(1)}, bf16[1024,128]{1,0:T(8,128)(2,1)S(1)}, bf16[512,128]{1,0:T(8,128)(2,1)S(1)}) custom-call(s32[192]{0:T(256)S(1)} %multiply_add_fusion.pos_ref, s32[8]{0:T(128)S(1)} %convert_reduce_fusion.1.count_ref, s32[6]{0:T(128)S(1)} %copy-done.19, ...), custom_call_target="tpu_custom_call" | custom-call | flops 1207959552 | bytes 3145728 | tf_op jit(solution)/shard_map/pallas_call | solution.py:274
  63.2 1.6 %collective-permute-done.16.refs_3_ = bf16[768,256]{1,0:T(8,128)(2,1)S(1)} collective-permute-done((bf16[768,256]{1,0:T(8,128)(2,1)}, bf16[768,256]{1,0:T(8,128)(2,1)S(1)}, u32[]{:S(2)}, u32[]{:S(2)}) %collective-permute-start.16) | collective-permute-done | bytes 393248 | tf_op jit(solution)/shard_map/ppermute | solution.py:25
  64.8 2.2 %shard_map.105 = bf16[1024,128]{1,0:T(8,128)(2,1)S(1)} custom-call(s32[192]{0:T(256)S(1)} %multiply_add_fusion.pos_ref, s32[8]{0:T(128)S(1)} %convert_reduce_fusion.1.count_ref, s32[2]{0:T(128)S(1)} %copy-done.15, bf16[768,256]{1,0:T(8,128)(2,1)S(1)} %copy-done.11, bf16[768,256]{1,0:T(8,128)(2,1)S(1)} %collective-permute-done.14.refs_1_, ...), custom_call_target="tpu_custom_call" | custom-call | flops 402653184 | bytes 2097152 | tf_op jit(solution)/shard_map/pallas_call | solution.py:274
  67.0 1.9 %collective-permute-start.20 = (bf16[1024,128]{1,0:T(8,128)(2,1)S(1)}, bf16[1024,128]{1,0:T(8,128)(2,1)S(1)}, u32[]{:S(2)}, u32[]{:S(2)}) collective-permute-start(bf16[1024,128]{1,0:T(8,128)(2,1)S(1)} %shard_map.105), channel_id=1, source_target_pairs={{0,4},{4,0},{8,12},{12,8},{16,20},{20,16},{24,28},{28,24},{1,5},{5... | collective-permute-start | bytes 786440 | tf_op jit(solution)/shard_map/ppermute | solution.py:25
  69.1 2.5 %collective-permute-start.11 = (bf16[1024,128]{1,0:T(8,128)(2,1)S(1)}, bf16[1024,128]{1,0:T(8,128)(2,1)S(1)}, u32[]{:S(2)}, u32[]{:S(2)}) collective-permute-start(bf16[1024,128]{1,0:T(8,128)(2,1)S(1)} %pad_maximum_fusion.1), channel_id=1, source_target_pairs={{0,8},{4,12},{8,0},{12,4},{16,24},{20,28},{24,16},{28,20},{1,9},{5... | collective-permute-start | bytes 786440 | tf_op jit(solution)/shard_map/ppermute | solution.py:25
  71.6 4.7 %shard_map.104 = (bf16[512,128]{1,0:T(8,128)(2,1)S(1)}, bf16[1024,128]{1,0:T(8,128)(2,1)S(1)}, bf16[1024,128]{1,0:T(8,128)(2,1)S(1)}, bf16[512,128]{1,0:T(8,128)(2,1)S(1)}) custom-call(s32[192]{0:T(256)S(1)} %multiply_add_fusion.pos_ref, s32[8]{0:T(128)S(1)} %convert_reduce_fusion.1.count_ref, s32[6]{0:T(128)S(1)} %copy-done.19, ...), custom_call_target="tpu_custom_call" | custom-call | flops 1207959552 | bytes 3145728 | tf_op jit(solution)/shard_map/pallas_call | solution.py:274
  76.9 1.4 %collective-permute-done.11 = bf16[1024,128]{1,0:T(8,128)(2,1)S(1)} collective-permute-done((bf16[1024,128]{1,0:T(8,128)(2,1)S(1)}, bf16[1024,128]{1,0:T(8,128)(2,1)S(1)}, u32[]{:S(2)}, u32[]{:S(2)}) %collective-permute-start.11) | collective-permute-done | bytes 262176 | tf_op jit(solution)/shard_map/ppermute | solution.py:25
  78.4 1.4 %collective-permute-start.13 = (bf16[512,128]{1,0:T(8,128)(2,1)S(1)}, bf16[512,128]{1,0:T(8,128)(2,1)S(1)}, u32[]{:S(2)}, u32[]{:S(2)}) collective-permute-start(bf16[512,128]{1,0:T(8,128)(2,1)S(1)} %add_convert_fusion.3), channel_id=1, source_target_pairs={{0,24},{4,28},{8,16},{12,20},{16,8},{20,12},{24,0},{28,4},{1,25},{... | collective-permute-start | bytes 393224 | tf_op jit(solution)/shard_map/ppermute | solution.py:25
  80.7 5.9 %collective-permute-done.13 = bf16[512,128]{1,0:T(8,128)(2,1)S(1)} collective-permute-done((bf16[512,128]{1,0:T(8,128)(2,1)S(1)}, bf16[512,128]{1,0:T(8,128)(2,1)S(1)}, u32[]{:S(2)}, u32[]{:S(2)}) %collective-permute-start.13) | collective-permute-done | bytes 131104 | tf_op jit(solution)/shard_map/ppermute | solution.py:25
  86.7 3.6 %collective-permute-done.21 = bf16[1024,128]{1,0:T(8,128)(2,1)S(1)} collective-permute-done((bf16[1024,128]{1,0:T(8,128)(2,1)S(1)}, bf16[1024,128]{1,0:T(8,128)(2,1)S(1)}, u32[]{:S(2)}, u32[]{:S(2)}) %collective-permute-start.21) | collective-permute-done | bytes 262176 | tf_op jit(solution)/shard_map/ppermute | solution.py:25
  90.4 2.2 %collective-permute-start.23 = (bf16[512,128]{1,0:T(8,128)(2,1)S(1)}, bf16[512,128]{1,0:T(8,128)(2,1)S(1)}, u32[]{:S(2)}, u32[]{:S(2)}) collective-permute-start(bf16[512,128]{1,0:T(8,128)(2,1)S(1)} %add_convert_fusion), channel_id=1, source_target_pairs={{0,24},{4,28},{8,16},{12,20},{16,8},{20,12},{24,0},{28,4},{1,25},{... | collective-permute-start | bytes 393224 | tf_op jit(solution)/shard_map/ppermute | solution.py:25
  92.6 1.8 %collective-permute-start.26 = (bf16[128,128]{1,0:T(8,128)(2,1)S(1)}, bf16[128,128]{1,0:T(8,128)(2,1)S(1)}, u32[]{:S(2)}, u32[]{:S(2)}) collective-permute-start(bf16[128,128]{1,0:T(8,128)(2,1)S(1)} %get-tuple-element.63), channel_id=1, source_target_pairs={{0,2},{1,3},{2,0},{3,1},{4,6},{5,7},{6,4},{7,5},{8,10},{9,11},{10,... | collective-permute-start | bytes 98312 | tf_op jit(solution)/shard_map/ppermute | solution.py:25
  94.5 2.7 %collective-permute-done.23 = bf16[512,128]{1,0:T(8,128)(2,1)S(1)} collective-permute-done((bf16[512,128]{1,0:T(8,128)(2,1)S(1)}, bf16[512,128]{1,0:T(8,128)(2,1)S(1)}, u32[]{:S(2)}, u32[]{:S(2)}) %collective-permute-start.23) | collective-permute-done | bytes 131104 | tf_op jit(solution)/shard_map/ppermute | solution.py:25
  97.4 1.8 %collective-permute-start.27 = (bf16[128,128]{1,0:T(8,128)(2,1)S(1)}, bf16[128,128]{1,0:T(8,128)(2,1)S(1)}, u32[]{:S(2)}, u32[]{:S(2)}) collective-permute-start(bf16[128,128]{1,0:T(8,128)(2,1)S(1)} %get-tuple-element.60), channel_id=1, source_target_pairs={{0,2},{1,3},{2,0},{3,1},{4,6},{5,7},{6,4},{7,5},{8,10},{9,11},{10,... | collective-permute-start | bytes 98312 | tf_op jit(solution)/shard_map/ppermute | solution.py:25
  99.3 1.3 %gate.1.gate_ref = f32[4,128,256]{2,1,0:T(8,128)S(1)} custom-call(s32[1]{0:T(128)} %bitcast._.me_ref, bf16[128,1024]{1,0:T(8,128)(2,1)S(1)} %copy-done.3, bf16[1024,2048]{1,0:T(8,128)(2,1)S(1)} %copy-done.1), custom_call_target="tpu_custom_call" | custom-call | flops 268435456 | bytes 2883584 | tf_op jit(solution)/shard_map/gate/pallas_call | solution.py:140
  101.4 1.2 %collective-permute-done.29.refs_7_ = bf16[128,128]{1,0:T(8,128)(2,1)S(1)} collective-permute-done((bf16[128,128]{1,0:T(8,128)(2,1)S(1)}, bf16[128,128]{1,0:T(8,128)(2,1)S(1)}, u32[]{:S(2)}, u32[]{:S(2)}) %collective-permute-start.29) | collective-permute-done | bytes 32800 | tf_op jit(solution)/shard_map/ppermute | solution.py:25
  102.6 1.3 %finish.1 = bf16[128,1024]{1,0:T(8,128)(2,1)} custom-call(s32[1]{0:T(128)} %bitcast._.me_ref, bf16[128,1024]{1,0:T(8,128)(2,1)S(1)} %copy-done.3, f32[4,128,256]{2,1,0:T(8,128)S(1)} %gate.1.gate_ref, bf16[1024,1024]{1,0:T(8,128)(2,1)S(1)} %copy-done.4, f32[128,128]{1,0:T(8,128)S(1)} %slice.114.refs_0_, f32[128,128]{1,0:T(8,128)S(1)} %slice.121.refs_1_, ...), custom_call_target="tpu_custom_call" | custom-call | flops 268435456 | bytes 3407872 | tf_op jit(solution)/shard_map/finish/pallas_call | solution.py:321
  (99 shorter events, 18.0 us)
Async XLA Ops:
  4.0 10.0 %collective-permute-start = (bf16[144,256]{1,0:T(8,128)(2,1)}, bf16[144,256]{1,0:T(8,128)(2,1)S(1)}, u32[]{:S(2)}, u32[]{:S(2)}) collective-permute-start(bf16[144,256]{1,0:T(8,128)(2,1)} %get-tuple-element.29), channel_id=1, source_target_pairs={{0,1},{1,0},{2,3},{3,2},{4,5},{5,4},{6,7},{7,6},{8,9},{9,8},{10,11... | collective-permute-start | bytes 221192 | tf_op jit(solution)/shard_map/ppermute | solution.py:25
  4.6 9.5 %collective-permute-start.1 = (bf16[144,256]{1,0:T(8,128)(2,1)}, bf16[144,256]{1,0:T(8,128)(2,1)S(1)}, u32[]{:S(2)}, u32[]{:S(2)}) collective-permute-start(bf16[144,256]{1,0:T(8,128)(2,1)} %get-tuple-element.30), channel_id=1, source_target_pairs={{0,2},{1,3},{2,0},{3,1},{4,6},{5,7},{6,4},{7,5},{8,10},{9,11},{10,... | collective-permute-start | bytes 221192 | tf_op jit(solution)/shard_map/ppermute | solution.py:25
  7.2 6.9 %collective-permute-start.2 = (bf16[144,256]{1,0:T(8,128)(2,1)}, bf16[144,256]{1,0:T(8,128)(2,1)S(1)}, u32[]{:S(2)}, u32[]{:S(2)}) collective-permute-start(bf16[144,256]{1,0:T(8,128)(2,1)} %get-tuple-element.31), channel_id=1, source_target_pairs={{0,3},{1,2},{2,1},{3,0},{4,7},{5,6},{6,5},{7,4},{8,11},{9,10},{10,... | collective-permute-start | bytes 221192 | tf_op jit(solution)/shard_map/ppermute | solution.py:25
  13.9 31.1 %collective-permute-start.3 = (bf16[768,256]{1,0:T(8,128)(2,1)}, bf16[768,256]{1,0:T(8,128)(2,1)}, u32[]{:S(2)}, u32[]{:S(2)}) collective-permute-start(bf16[768,256]{1,0:T(8,128)(2,1)} %get-tuple-element.34), channel_id=1, source_target_pairs={{0,1},{1,0},{2,3},{3,2},{4,5},{5,4},{6,7},{7,6},{8,9},{9,8},{10,11... | collective-permute-start | bytes 1179656 | tf_op jit(solution)/shard_map/ppermute | solution.py:25
  16.0 12.6 %collective-permute-start.6 = (bf16[512,128]{1,0:T(8,128)(2,1)}, bf16[512,128]{1,0:T(8,128)(2,1)}, u32[]{:S(2)}, u32[]{:S(2)}) collective-permute-start(bf16[512,128]{1,0:T(8,128)(2,1)} %get-tuple-element.37.refs_4_), channel_id=1, source_target_pairs={{0,24},{4,28},{8,16},{12,20},{16,8},{20,12},{24,0},{28,4},{1,25},{... | collective-permute-start | bytes 393224 | tf_op jit(solution)/shard_map/ppermute | solution.py:25
  24.6 22.0 %collective-permute-start.4 = (bf16[768,256]{1,0:T(8,128)(2,1)}, bf16[768,256]{1,0:T(8,128)(2,1)S(1)}, u32[]{:S(2)}, u32[]{:S(2)}) collective-permute-start(bf16[768,256]{1,0:T(8,128)(2,1)} %get-tuple-element.35), channel_id=1, source_target_pairs={{0,2},{1,3},{2,0},{3,1},{4,6},{5,7},{6,4},{7,5},{8,10},{9,11},{10,... | collective-permute-start | bytes 1179656 | tf_op jit(solution)/shard_map/ppermute | solution.py:25
  26.1 20.9 %collective-permute-start.5 = (bf16[768,256]{1,0:T(8,128)(2,1)}, bf16[768,256]{1,0:T(8,128)(2,1)S(1)}, u32[]{:S(2)}, u32[]{:S(2)}) collective-permute-start(bf16[768,256]{1,0:T(8,128)(2,1)} %get-tuple-element.36), channel_id=1, source_target_pairs={{0,3},{1,2},{2,1},{3,0},{4,7},{5,6},{6,5},{7,4},{8,11},{9,10},{10,... | collective-permute-start | bytes 1179656 | tf_op jit(solution)/shard_map/ppermute | solution.py:25
  26.1 6.3 %collective-permute-start.17 = (bf16[512,128]{1,0:T(8,128)(2,1)}, bf16[512,128]{1,0:T(8,128)(2,1)S(1)}, u32[]{:S(2)}, u32[]{:S(2)}) collective-permute-start(bf16[512,128]{1,0:T(8,128)(2,1)} %copy-done.5), channel_id=1, source_target_pairs={{0,4},{4,0},{8,12},{12,8},{16,20},{20,16},{24,28},{28,24},{1,5},{5... | collective-permute-start | bytes 393224 | tf_op jit(solution)/shard_map/ppermute | solution.py:25
  28.6 36.2 %copy-start.11 = (bf16[768,256]{1,0:T(8,128)(2,1)S(1)}, bf16[768,256]{1,0:T(8,128)(2,1)}, u32[]{:S(2)}) copy-start(bf16[768,256]{1,0:T(8,128)(2,1)} %copy-done.10) | copy-start | bytes 1179652
  28.6 36.2 %copy-start.15 = (s32[2]{0:T(128)S(1)}, s32[2]{0:T(128)}, u32[]{:S(2)}) copy-start(s32[2]{0:T(128)} %constant.18.clone.code_ref) | copy-start | bytes 28
  29.6 14.3 %collective-permute-start.8 = (bf16[1024,128]{1,0:T(8,128)(2,1)S(1)}, bf16[1024,128]{1,0:T(8,128)(2,1)S(1)}, u32[]{:S(2)}, u32[]{:S(2)}) collective-permute-start(bf16[1024,128]{1,0:T(8,128)(2,1)S(1)} %constant_dynamic-update-slice_fusion), channel_id=1, source_target_pairs={{0,8},{4,12},{8,0},{12,4},{16,24},{20,28},{24,16},{28,20},{1,9},{5... | collective-permute-start | bytes 786440 | tf_op jit(solution)/shard_map/ppermute | solution.py:25
  33.3 10.7 %collective-permute-start.18 = (bf16[1024,128]{1,0:T(8,128)(2,1)S(1)}, bf16[1024,128]{1,0:T(8,128)(2,1)S(1)}, u32[]{:S(2)}, u32[]{:S(2)}) collective-permute-start(bf16[1024,128]{1,0:T(8,128)(2,1)S(1)} %pad_maximum_fusion.2), channel_id=1, source_target_pairs={{0,24},{4,28},{8,16},{12,20},{16,8},{20,12},{24,0},{28,4},{1,25},{... | collective-permute-start | bytes 786440 | tf_op jit(solution)/shard_map/ppermute | solution.py:25
  43.8 6.4 %collective-permute-start.9 = (bf16[1024,128]{1,0:T(8,128)(2,1)S(1)}, bf16[1024,128]{1,0:T(8,128)(2,1)S(1)}, u32[]{:S(2)}, u32[]{:S(2)}) collective-permute-start(bf16[1024,128]{1,0:T(8,128)(2,1)S(1)} %collective-permute-done.8.refs_7_), channel_id=1, source_target_pairs={{0,4},{4,0},{8,12},{12,8},{16,20},{20,16},{24,28},{28,24},{1,5},{5... | collective-permute-start | bytes 786440 | tf_op jit(solution)/shard_map/ppermute | solution.py:25
  44.0 18.7 %collective-permute-start.14 = (bf16[768,256]{1,0:T(8,128)(2,1)}, bf16[768,256]{1,0:T(8,128)(2,1)S(1)}, u32[]{:S(2)}, u32[]{:S(2)}) collective-permute-start(bf16[768,256]{1,0:T(8,128)(2,1)} %copy-done.16), channel_id=1, source_target_pairs={{0,1},{1,0},{2,3},{3,2},{4,5},{5,4},{6,7},{7,6},{8,9},{9,8},{10,11... | collective-permute-start | bytes 1179656 | tf_op jit(solution)/shard_map/ppermute | solution.py:25
  45.1 18.1 %collective-permute-start.15 = (bf16[768,256]{1,0:T(8,128)(2,1)}, bf16[768,256]{1,0:T(8,128)(2,1)S(1)}, u32[]{:S(2)}, u32[]{:S(2)}) collective-permute-start(bf16[768,256]{1,0:T(8,128)(2,1)} %copy-done.18), channel_id=1, source_target_pairs={{0,2},{1,3},{2,0},{3,1},{4,6},{5,7},{6,4},{7,5},{8,10},{9,11},{10,... | collective-permute-start | bytes 1179656 | tf_op jit(solution)/shard_map/ppermute | solution.py:25
  46.6 18.2 %collective-permute-start.16 = (bf16[768,256]{1,0:T(8,128)(2,1)}, bf16[768,256]{1,0:T(8,128)(2,1)S(1)}, u32[]{:S(2)}, u32[]{:S(2)}) collective-permute-start(bf16[768,256]{1,0:T(8,128)(2,1)} %copy-done.17), channel_id=1, source_target_pairs={{0,3},{1,2},{2,1},{3,0},{4,7},{5,6},{6,5},{7,4},{8,11},{9,10},{10,... | collective-permute-start | bytes 1179656 | tf_op jit(solution)/shard_map/ppermute | solution.py:25
  47.0 8.8 %collective-permute-start.7 = (bf16[1024,128]{1,0:T(8,128)(2,1)S(1)}, bf16[1024,128]{1,0:T(8,128)(2,1)S(1)}, u32[]{:S(2)}, u32[]{:S(2)}) collective-permute-start(bf16[1024,128]{1,0:T(8,128)(2,1)S(1)} %constant_dynamic-update-slice_fusion), channel_id=1, source_target_pairs={{0,4},{4,0},{8,12},{12,8},{16,20},{20,16},{24,28},{28,24},{1,5},{5... | collective-permute-start | bytes 786440 | tf_op jit(solution)/shard_map/ppermute | solution.py:25
  50.3 14.6 %collective-permute-start.19 = (bf16[2048,128]{1,0:T(8,128)(2,1)S(1)}, bf16[2048,128]{1,0:T(8,128)(2,1)S(1)}, u32[]{:S(2)}, u32[]{:S(2)}) collective-permute-start(bf16[2048,128]{1,0:T(8,128)(2,1)S(1)} %pad_maximum_fusion), channel_id=1, source_target_pairs={{0,8},{4,12},{8,0},{12,4},{16,24},{20,28},{24,16},{28,20},{1,9},{5... | collective-permute-start | bytes 1572872 | tf_op jit(solution)/shard_map/ppermute | solution.py:25
  55.8 13.1 %collective-permute-start.10 = (bf16[1024,128]{1,0:T(8,128)(2,1)S(1)}, bf16[1024,128]{1,0:T(8,128)(2,1)S(1)}, u32[]{:S(2)}, u32[]{:S(2)}) collective-permute-start(bf16[1024,128]{1,0:T(8,128)(2,1)S(1)} %shard_map.103), channel_id=1, source_target_pairs={{0,4},{4,0},{8,12},{12,8},{16,20},{20,16},{24,28},{28,24},{1,5},{5... | collective-permute-start | bytes 786440 | tf_op jit(solution)/shard_map/ppermute | solution.py:25
  62.8 14.1 %collective-permute-start.12 = (bf16[1024,128]{1,0:T(8,128)(2,1)S(1)}, bf16[1024,128]{1,0:T(8,128)(2,1)S(1)}, u32[]{:S(2)}, u32[]{:S(2)}) collective-permute-start(bf16[1024,128]{1,0:T(8,128)(2,1)S(1)} %get-tuple-element.40), channel_id=1, source_target_pairs={{0,4},{4,0},{8,12},{12,8},{16,20},{20,16},{24,28},{28,24},{1,5},{5... | collective-permute-start | bytes 786440 | tf_op jit(solution)/shard_map/ppermute | solution.py:25
  67.0 9.8 %collective-permute-start.20 = (bf16[1024,128]{1,0:T(8,128)(2,1)S(1)}, bf16[1024,128]{1,0:T(8,128)(2,1)S(1)}, u32[]{:S(2)}, u32[]{:S(2)}) collective-permute-start(bf16[1024,128]{1,0:T(8,128)(2,1)S(1)} %shard_map.105), channel_id=1, source_target_pairs={{0,4},{4,0},{8,12},{12,8},{16,20},{20,16},{24,28},{28,24},{1,5},{5... | collective-permute-start | bytes 786440 | tf_op jit(solution)/shard_map/ppermute | solution.py:25
  69.1 9.2 %collective-permute-start.11 = (bf16[1024,128]{1,0:T(8,128)(2,1)S(1)}, bf16[1024,128]{1,0:T(8,128)(2,1)S(1)}, u32[]{:S(2)}, u32[]{:S(2)}) collective-permute-start(bf16[1024,128]{1,0:T(8,128)(2,1)S(1)} %pad_maximum_fusion.1), channel_id=1, source_target_pairs={{0,8},{4,12},{8,0},{12,4},{16,24},{20,28},{24,16},{28,20},{1,9},{5... | collective-permute-start | bytes 786440 | tf_op jit(solution)/shard_map/ppermute | solution.py:25
  76.3 10.4 %collective-permute-start.22 = (bf16[1024,128]{1,0:T(8,128)(2,1)S(1)}, bf16[1024,128]{1,0:T(8,128)(2,1)S(1)}, u32[]{:S(2)}, u32[]{:S(2)}) collective-permute-start(bf16[1024,128]{1,0:T(8,128)(2,1)S(1)} %get-tuple-element.49), channel_id=1, source_target_pairs={{0,4},{4,0},{8,12},{12,8},{16,20},{20,16},{24,28},{28,24},{1,5},{5... | collective-permute-start | bytes 786440 | tf_op jit(solution)/shard_map/ppermute | solution.py:25
  78.4 8.2 %collective-permute-start.13 = (bf16[512,128]{1,0:T(8,128)(2,1)S(1)}, bf16[512,128]{1,0:T(8,128)(2,1)S(1)}, u32[]{:S(2)}, u32[]{:S(2)}) collective-permute-start(bf16[512,128]{1,0:T(8,128)(2,1)S(1)} %add_convert_fusion.3), channel_id=1, source_target_pairs={{0,24},{4,28},{8,16},{12,20},{16,8},{20,12},{24,0},{28,4},{1,25},{... | collective-permute-start | bytes 393224 | tf_op jit(solution)/shard_map/ppermute | solution.py:25
  79.8 10.5 %collective-permute-start.21 = (bf16[1024,128]{1,0:T(8,128)(2,1)S(1)}, bf16[1024,128]{1,0:T(8,128)(2,1)S(1)}, u32[]{:S(2)}, u32[]{:S(2)}) collective-permute-start(bf16[1024,128]{1,0:T(8,128)(2,1)S(1)} %pad_maximum_fusion.3), channel_id=1, source_target_pairs={{0,8},{4,12},{8,0},{12,4},{16,24},{20,28},{24,16},{28,20},{1,9},{5... | collective-permute-start | bytes 786440 | tf_op jit(solution)/shard_map/ppermute | solution.py:25
  90.4 6.8 %collective-permute-start.23 = (bf16[512,128]{1,0:T(8,128)(2,1)S(1)}, bf16[512,128]{1,0:T(8,128)(2,1)S(1)}, u32[]{:S(2)}, u32[]{:S(2)}) collective-permute-start(bf16[512,128]{1,0:T(8,128)(2,1)S(1)} %add_convert_fusion), channel_id=1, source_target_pairs={{0,24},{4,28},{8,16},{12,20},{16,8},{20,12},{24,0},{28,4},{1,25},{... | collective-permute-start | bytes 393224 | tf_op jit(solution)/shard_map/ppermute | solution.py:25
  92.6 6.7 %collective-permute-start.24 = (bf16[128,128]{1,0:T(8,128)(2,1)S(1)}, bf16[128,128]{1,0:T(8,128)(2,1)S(1)}, u32[]{:S(2)}, u32[]{:S(2)}) collective-permute-start(bf16[128,128]{1,0:T(8,128)(2,1)S(1)} %get-tuple-element.64), channel_id=1, source_target_pairs={{0,1},{1,0},{2,3},{3,2},{4,5},{5,4},{6,7},{7,6},{8,9},{9,8},{10,11... | collective-permute-start | bytes 98312 | tf_op jit(solution)/shard_map/ppermute | solution.py:25
  92.6 8.0 %collective-permute-start.26 = (bf16[128,128]{1,0:T(8,128)(2,1)S(1)}, bf16[128,128]{1,0:T(8,128)(2,1)S(1)}, u32[]{:S(2)}, u32[]{:S(2)}) collective-permute-start(bf16[128,128]{1,0:T(8,128)(2,1)S(1)} %get-tuple-element.63), channel_id=1, source_target_pairs={{0,2},{1,3},{2,0},{3,1},{4,6},{5,7},{6,4},{7,5},{8,10},{9,11},{10,... | collective-permute-start | bytes 98312 | tf_op jit(solution)/shard_map/ppermute | solution.py:25
  94.4 6.2 %collective-permute-start.28 = (bf16[128,128]{1,0:T(8,128)(2,1)S(1)}, bf16[128,128]{1,0:T(8,128)(2,1)S(1)}, u32[]{:S(2)}, u32[]{:S(2)}) collective-permute-start(bf16[128,128]{1,0:T(8,128)(2,1)S(1)} %get-tuple-element.62), channel_id=1, source_target_pairs={{0,3},{1,2},{2,1},{3,0},{4,7},{5,6},{6,5},{7,4},{8,11},{9,10},{10,... | collective-permute-start | bytes 98312 | tf_op jit(solution)/shard_map/ppermute | solution.py:25
  97.3 3.3 %collective-permute-start.25 = (bf16[128,128]{1,0:T(8,128)(2,1)S(1)}, bf16[128,128]{1,0:T(8,128)(2,1)S(1)}, u32[]{:S(2)}, u32[]{:S(2)}) collective-permute-start(bf16[128,128]{1,0:T(8,128)(2,1)S(1)} %get-tuple-element.61), channel_id=1, source_target_pairs={{0,1},{1,0},{2,3},{3,2},{4,5},{5,4},{6,7},{7,6},{8,9},{9,8},{10,11... | collective-permute-start | bytes 98312 | tf_op jit(solution)/shard_map/ppermute | solution.py:25
  97.4 4.0 %collective-permute-start.27 = (bf16[128,128]{1,0:T(8,128)(2,1)S(1)}, bf16[128,128]{1,0:T(8,128)(2,1)S(1)}, u32[]{:S(2)}, u32[]{:S(2)}) collective-permute-start(bf16[128,128]{1,0:T(8,128)(2,1)S(1)} %get-tuple-element.60), channel_id=1, source_target_pairs={{0,2},{1,3},{2,0},{3,1},{4,6},{5,7},{6,4},{7,5},{8,10},{9,11},{10,... | collective-permute-start | bytes 98312 | tf_op jit(solution)/shard_map/ppermute | solution.py:25
  99.2 3.4 %collective-permute-start.29 = (bf16[128,128]{1,0:T(8,128)(2,1)S(1)}, bf16[128,128]{1,0:T(8,128)(2,1)S(1)}, u32[]{:S(2)}, u32[]{:S(2)}) collective-permute-start(bf16[128,128]{1,0:T(8,128)(2,1)S(1)} %get-tuple-element.59), channel_id=1, source_target_pairs={{0,3},{1,2},{2,1},{3,0},{4,7},{5,6},{6,5},{7,4},{8,11},{9,10},{10,... | collective-permute-start | bytes 98312 | tf_op jit(solution)/shard_map/ppermute | solution.py:25
  (18 other events, 185.8 us)

commit v6 on v5

--- a/solution.py
+++ b/solution.py
@@ -58,10 +58,14 @@
     cols = outs[0].shape[1]
     blocks = owner_ref.shape[1]
     extra = outs[0].shape[0] - rows
+    width = cand.shape[1]
+    step = width // parts
     fetch = [pltpu.make_async_copy(cand_hbm, cand, sems.at[parts])]
     for k in range(parts):
-        at = pl.ds(k * cols, cols)
-        fetch.append(pltpu.make_async_copy(w_hbm.at[:, at], weight.at[:, at], sems.at[k]))
+        at = pl.ds(k * step, step)
+        fetch.append(
+            pltpu.make_async_copy(w_hbm.at[at, pl.ds(0, width)], weight.at[at, :], sems.at[k])
+        )
     for copy in fetch:
         copy.start()
     owners = jnp.broadcast_to(owner_ref[...].astype(F32), (extra, blocks)).astype(BF16)
@@ -69,11 +73,13 @@
         out[rows:, :] = jnp.zeros((extra, cols), BF16)
         out[rows:, :blocks] = owners
     fetch[0].wait()
+    projected = None
     for k in range(parts):
         fetch[k + 1].wait()
-        at = slice(k * cols, (k + 1) * cols)
-        projected = jnp.dot(cand[...], weight[:, at], preferred_element_type=F32)
-        made[:, at] = silu(projected).astype(BF16)
+        at = slice(k * step, (k + 1) * step)
+        part = jnp.dot(cand[:, at], weight[at, :], preferred_element_type=F32)
+        projected = part if projected is None else projected + part
+    made[...] = silu(projected).astype(BF16)
     for k, out in enumerate(outs):
         at = pl.multiple_of((k ^ me_ref[0]) * cols, cols)
         out[:rows, :] = made[:, pl.ds(at, cols)]

time: 104 us -> 104 us (level)
  no operation moved by 1% of the time
where the time goes in v6:
time: 104 us
  waiting for transfers between devices  31.2 us (30%)
  starting transfers between devices  30.8 us (30%)
  Pallas kernels  27.8 us (27%)
  local copies, waits for them, and re-layouts  10.1 us (10%)
  other arithmetic  3.29 us (3%)
    ppermute x30, waiting for transfers between devices, swap(): return lax.ppermute(value, axis, [(i, i ^ mask) for i in range(count)])  31.2 us
    ppermute x30, starting transfers between devices, swap(): return lax.ppermute(value, axis, [(i, i ^ mask) for i in range(count)])  30.8 us
    pallas_call x4, Pallas kernels, attend(): pl.pallas_call(functools.partial(attend_kernel, source, sink, events, roo...  14.7 us
    unnamed x41, local copies, waits for them, and re-layouts  9.02 us
    pallas_call x2, Pallas kernels, project_keys_values(): pl.pallas_call(functools.partial(keys_values_kernel, count, each), grid_s...  6.08 us
    pallas_call x1, Pallas kernels, project_queries(): pl.pallas_call(query_kernel, in_specs=[pl.BlockSpec(memory_space=pltpu.SM...  3.59 us
  transfers between devices with their start and end apart: 30, of which 11 were waited for; matrix products, arithmetic and copies ran while one was open for 5% of the time, Pallas kernels for 22%

profile of v6, /device:TPU:0, one launch (start us, length us, event | category | flops | bytes accessed | tf_op | source)
XLA Modules:
  0.0 103.5 jit_solution(13268071009496570953)
XLA Ops:
  0.0 3.6 %queries.1 = (bf16[144,256]{1,0:T(8,128)(2,1)}, bf16[144,256]{1,0:T(8,128)(2,1)}, bf16[144,256]{1,0:T(8,128)(2,1)}, bf16[144,256]{1,0:T(8,128)(2,1)}) custom-call(s32[1]{0:T(128)} %bitcast._.me_ref, bf16[128,1024]{1,0:T(8,128)(2,1)} %cand_ref.3, bf16[1024,2048]{1,0:T(8,128)(2,1)} %w_hbm.1, s32[1,48]{1,0:T(1,128)} %bitcast.2), custom_call_target="tpu_custom_call" | custom-call | flops 268435456 | bytes 2621440 | tf_op jit(solution)/shard_map/queries/pallas_call | solution.py:95
  4.2 2.6 %collective-permute-start.1 = (bf16[144,256]{1,0:T(8,128)(2,1)}, bf16[144,256]{1,0:T(8,128)(2,1)S(1)}, u32[]{:S(2)}, u32[]{:S(2)}) collective-permute-start(bf16[144,256]{1,0:T(8,128)(2,1)} %get-tuple-element.30), channel_id=1, source_target_pairs={{0,2},{1,3},{2,0},{3,1},{4,6},{5,7},{6,4},{7,5},{8,10},{9,11},{10,... | collective-permute-start | bytes 221192 | tf_op jit(solution)/shard_map/ppermute | solution.py:25
  6.8 1.4 %copy-done.2 = bf16[768,1024]{1,0:T(8,128)(2,1)S(1)} copy-done((bf16[768,1024]{1,0:T(8,128)(2,1)S(1)}, bf16[768,1024]{1,0:T(8,128)(2,1)}, u32[]{:S(2)}) %copy-start.2) | copy-done | bytes 1572888
  8.2 3.0 %shard_map.100 = (bf16[768,256]{1,0:T(8,128)(2,1)S(1)}, bf16[768,256]{1,0:T(8,128)(2,1)S(1)}, bf16[768,256]{1,0:T(8,128)(2,1)}, bf16[768,256]{1,0:T(8,128)(2,1)S(1)}) custom-call(s32[1]{0:T(128)} %bitcast._.me_ref, bf16[768,1024]{1,0:T(8,128)(2,1)S(1)} %copy-done.2, bf16[1024,2048]{1,0:T(8,128)(2,1)S(1)} %copy-done, bf16[1024,2048]{1,0:T(8,128)(2,1)S(1)} %copy-done, ...), custom_call_target="tpu_custom_call" | custom-call | flops 1610612736 | bytes 5242880 | tf_op jit(solution)/shard_map/pallas_call | solution.py:186
  15.6 4.1 %collective-permute-start.6 = (bf16[512,128]{1,0:T(8,128)(2,1)}, bf16[512,128]{1,0:T(8,128)(2,1)}, u32[]{:S(2)}, u32[]{:S(2)}) collective-permute-start(bf16[512,128]{1,0:T(8,128)(2,1)} %get-tuple-element.37.refs_4_), channel_id=1, source_target_pairs={{0,24},{4,28},{8,16},{12,20},{16,8},{20,12},{24,0},{28,4},{1,25},{... | collective-permute-start | bytes 393224 | tf_op jit(solution)/shard_map/ppermute | solution.py:25
  19.7 3.0 %shard_map.101 = (bf16[768,256]{1,0:T(8,128)(2,1)}, bf16[768,256]{1,0:T(8,128)(2,1)S(1)}, bf16[768,256]{1,0:T(8,128)(2,1)}, bf16[768,256]{1,0:T(8,128)(2,1)S(1)}) custom-call(s32[1]{0:T(128)} %bitcast._.me_ref, bf16[768,1024]{1,0:T(8,128)(2,1)S(1)} %copy-done.2, bf16[1024,2048]{1,0:T(8,128)(2,1)S(1)} %copy-done, bf16[1024,2048]{1,0:T(8,128)(2,1)S(1)} %copy-done, ...), custom_call_target="tpu_custom_call" | custom-call | flops 1610612736 | bytes 5242880 | tf_op jit(solution)/shard_map/pallas_call | solution.py:186
  24.2 1.5 %collective-permute-start.4 = (bf16[768,256]{1,0:T(8,128)(2,1)}, bf16[768,256]{1,0:T(8,128)(2,1)S(1)}, u32[]{:S(2)}, u32[]{:S(2)}) collective-permute-start(bf16[768,256]{1,0:T(8,128)(2,1)} %get-tuple-element.35), channel_id=1, source_target_pairs={{0,2},{1,3},{2,0},{3,1},{4,6},{5,7},{6,4},{7,5},{8,10},{9,11},{10,... | collective-permute-start | bytes 1179656 | tf_op jit(solution)/shard_map/ppermute | solution.py:25
  25.7 1.5 %collective-permute-start.17 = (bf16[512,128]{1,0:T(8,128)(2,1)}, bf16[512,128]{1,0:T(8,128)(2,1)S(1)}, u32[]{:S(2)}, u32[]{:S(2)}) collective-permute-start(bf16[512,128]{1,0:T(8,128)(2,1)} %copy-done.5), channel_id=1, source_target_pairs={{0,4},{4,0},{8,12},{12,8},{16,20},{20,16},{24,28},{28,24},{1,5},{5... | collective-permute-start | bytes 393224 | tf_op jit(solution)/shard_map/ppermute | solution.py:25
  29.2 2.7 %collective-permute-done.17.refs_5_ = bf16[512,128]{1,0:T(8,128)(2,1)S(1)} collective-permute-done((bf16[512,128]{1,0:T(8,128)(2,1)}, bf16[512,128]{1,0:T(8,128)(2,1)S(1)}, u32[]{:S(2)}, u32[]{:S(2)}) %collective-permute-start.17) | collective-permute-done | bytes 131104 | tf_op jit(solution)/shard_map/ppermute | solution.py:25
  33.7 9.7 %collective-permute-done.8.refs_7_ = bf16[1024,128]{1,0:T(8,128)(2,1)S(1)} collective-permute-done((bf16[1024,128]{1,0:T(8,128)(2,1)S(1)}, bf16[1024,128]{1,0:T(8,128)(2,1)S(1)}, u32[]{:S(2)}, u32[]{:S(2)}) %collective-permute-start.8) | collective-permute-done | bytes 262176 | tf_op jit(solution)/shard_map/ppermute | solution.py:25
  44.6 1.6 %collective-permute-start.15 = (bf16[768,256]{1,0:T(8,128)(2,1)}, bf16[768,256]{1,0:T(8,128)(2,1)S(1)}, u32[]{:S(2)}, u32[]{:S(2)}) collective-permute-start(bf16[768,256]{1,0:T(8,128)(2,1)} %copy-done.18), channel_id=1, source_target_pairs={{0,2},{1,3},{2,0},{3,1},{4,6},{5,7},{6,4},{7,5},{8,10},{9,11},{10,... | collective-permute-start | bytes 1179656 | tf_op jit(solution)/shard_map/ppermute | solution.py:25
  46.5 2.0 %collective-permute-start.7 = (bf16[1024,128]{1,0:T(8,128)(2,1)S(1)}, bf16[1024,128]{1,0:T(8,128)(2,1)S(1)}, u32[]{:S(2)}, u32[]{:S(2)}) collective-permute-start(bf16[1024,128]{1,0:T(8,128)(2,1)S(1)} %constant_dynamic-update-slice_fusion), channel_id=1, source_target_pairs={{0,4},{4,0},{8,12},{12,8},{16,20},{20,16},{24,28},{28,24},{1,5},{5... | collective-permute-start | bytes 786440 | tf_op jit(solution)/shard_map/ppermute | solution.py:25
  48.6 1.2 %collective-permute-done.9.refs_4_ = bf16[1024,128]{1,0:T(8,128)(2,1)S(1)} collective-permute-done((bf16[1024,128]{1,0:T(8,128)(2,1)S(1)}, bf16[1024,128]{1,0:T(8,128)(2,1)S(1)}, u32[]{:S(2)}, u32[]{:S(2)}) %collective-permute-start.9) | collective-permute-done | bytes 262176 | tf_op jit(solution)/shard_map/ppermute | solution.py:25
  52.4 2.6 %shard_map.103 = bf16[1024,128]{1,0:T(8,128)(2,1)S(1)} custom-call(s32[192]{0:T(256)S(1)} %multiply_add_fusion.pos_ref, s32[8]{0:T(128)S(1)} %convert_reduce_fusion.1.count_ref, s32[2]{0:T(128)S(1)} %copy-done.14, bf16[768,256]{1,0:T(8,128)(2,1)S(1)} %copy-done.8, bf16[768,256]{1,0:T(8,128)(2,1)} %collective-permute-done.3.refs_1_, ...), custom_call_target="tpu_custom_call" | custom-call | flops 402653184 | bytes 2097152 | tf_op jit(solution)/shard_map/pallas_call | solution.py:280
  55.4 1.7 %collective-permute-start.10 = (bf16[1024,128]{1,0:T(8,128)(2,1)S(1)}, bf16[1024,128]{1,0:T(8,128)(2,1)S(1)}, u32[]{:S(2)}, u32[]{:S(2)}) collective-permute-start(bf16[1024,128]{1,0:T(8,128)(2,1)S(1)} %shard_map.103), channel_id=1, source_target_pairs={{0,4},{4,0},{8,12},{12,8},{16,20},{20,16},{24,28},{28,24},{1,5},{5... | collective-permute-start | bytes 786440 | tf_op jit(solution)/shard_map/ppermute | solution.py:25
  57.1 5.2 %shard_map.102 = (bf16[512,128]{1,0:T(8,128)(2,1)S(1)}, bf16[1024,128]{1,0:T(8,128)(2,1)S(1)}, bf16[1024,128]{1,0:T(8,128)(2,1)S(1)}, bf16[512,128]{1,0:T(8,128)(2,1)S(1)}) custom-call(s32[192]{0:T(256)S(1)} %multiply_add_fusion.pos_ref, s32[8]{0:T(128)S(1)} %convert_reduce_fusion.1.count_ref, s32[6]{0:T(128)S(1)} %copy-done.19, ...), custom_call_target="tpu_custom_call" | custom-call | flops 1207959552 | bytes 3145728 | tf_op jit(solution)/shard_map/pallas_call | solution.py:280
  62.7 1.6 %collective-permute-done.16.refs_3_ = bf16[768,256]{1,0:T(8,128)(2,1)S(1)} collective-permute-done((bf16[768,256]{1,0:T(8,128)(2,1)}, bf16[768,256]{1,0:T(8,128)(2,1)S(1)}, u32[]{:S(2)}, u32[]{:S(2)}) %collective-permute-start.16) | collective-permute-done | bytes 393248 | tf_op jit(solution)/shard_map/ppermute | solution.py:25
  64.4 2.2 %shard_map.105 = bf16[1024,128]{1,0:T(8,128)(2,1)S(1)} custom-call(s32[192]{0:T(256)S(1)} %multiply_add_fusion.pos_ref, s32[8]{0:T(128)S(1)} %convert_reduce_fusion.1.count_ref, s32[2]{0:T(128)S(1)} %copy-done.15, bf16[768,256]{1,0:T(8,128)(2,1)S(1)} %copy-done.11, bf16[768,256]{1,0:T(8,128)(2,1)S(1)} %collective-permute-done.14.refs_1_, ...), custom_call_target="tpu_custom_call" | custom-call | flops 402653184 | bytes 2097152 | tf_op jit(solution)/shard_map/pallas_call | solution.py:280
  66.5 1.9 %collective-permute-start.20 = (bf16[1024,128]{1,0:T(8,128)(2,1)S(1)}, bf16[1024,128]{1,0:T(8,128)(2,1)S(1)}, u32[]{:S(2)}, u32[]{:S(2)}) collective-permute-start(bf16[1024,128]{1,0:T(8,128)(2,1)S(1)} %shard_map.105), channel_id=1, source_target_pairs={{0,4},{4,0},{8,12},{12,8},{16,20},{20,16},{24,28},{28,24},{1,5},{5... | collective-permute-start | bytes 786440 | tf_op jit(solution)/shard_map/ppermute | solution.py:25
  68.6 2.5 %collective-permute-start.11 = (bf16[1024,128]{1,0:T(8,128)(2,1)S(1)}, bf16[1024,128]{1,0:T(8,128)(2,1)S(1)}, u32[]{:S(2)}, u32[]{:S(2)}) collective-permute-start(bf16[1024,128]{1,0:T(8,128)(2,1)S(1)} %pad_maximum_fusion.1), channel_id=1, source_target_pairs={{0,8},{4,12},{8,0},{12,4},{16,24},{20,28},{24,16},{28,20},{1,9},{5... | collective-permute-start | bytes 786440 | tf_op jit(solution)/shard_map/ppermute | solution.py:25
  71.2 4.7 %shard_map.104 = (bf16[512,128]{1,0:T(8,128)(2,1)S(1)}, bf16[1024,128]{1,0:T(8,128)(2,1)S(1)}, bf16[1024,128]{1,0:T(8,128)(2,1)S(1)}, bf16[512,128]{1,0:T(8,128)(2,1)S(1)}) custom-call(s32[192]{0:T(256)S(1)} %multiply_add_fusion.pos_ref, s32[8]{0:T(128)S(1)} %convert_reduce_fusion.1.count_ref, s32[6]{0:T(128)S(1)} %copy-done.19, ...), custom_call_target="tpu_custom_call" | custom-call | flops 1207959552 | bytes 3145728 | tf_op jit(solution)/shard_map/pallas_call | solution.py:280
  76.5 1.4 %collective-permute-done.11 = bf16[1024,128]{1,0:T(8,128)(2,1)S(1)} collective-permute-done((bf16[1024,128]{1,0:T(8,128)(2,1)S(1)}, bf16[1024,128]{1,0:T(8,128)(2,1)S(1)}, u32[]{:S(2)}, u32[]{:S(2)}) %collective-permute-start.11) | collective-permute-done | bytes 262176 | tf_op jit(solution)/shard_map/ppermute | solution.py:25
  77.9 1.4 %collective-permute-start.13 = (bf16[512,128]{1,0:T(8,128)(2,1)S(1)}, bf16[512,128]{1,0:T(8,128)(2,1)S(1)}, u32[]{:S(2)}, u32[]{:S(2)}) collective-permute-start(bf16[512,128]{1,0:T(8,128)(2,1)S(1)} %add_convert_fusion.3), channel_id=1, source_target_pairs={{0,24},{4,28},{8,16},{12,20},{16,8},{20,12},{24,0},{28,4},{1,25},{... | collective-permute-start | bytes 393224 | tf_op jit(solution)/shard_map/ppermute | solution.py:25
  80.3 5.9 %collective-permute-done.13 = bf16[512,128]{1,0:T(8,128)(2,1)S(1)} collective-permute-done((bf16[512,128]{1,0:T(8,128)(2,1)S(1)}, bf16[512,128]{1,0:T(8,128)(2,1)S(1)}, u32[]{:S(2)}, u32[]{:S(2)}) %collective-permute-start.13) | collective-permute-done | bytes 131104 | tf_op jit(solution)/shard_map/ppermute | solution.py:25
  86.3 3.6 %collective-permute-done.21 = bf16[1024,128]{1,0:T(8,128)(2,1)S(1)} collective-permute-done((bf16[1024,128]{1,0:T(8,128)(2,1)S(1)}, bf16[1024,128]{1,0:T(8,128)(2,1)S(1)}, u32[]{:S(2)}, u32[]{:S(2)}) %collective-permute-start.21) | collective-permute-done | bytes 262176 | tf_op jit(solution)/shard_map/ppermute | solution.py:25
  89.9 2.2 %collective-permute-start.23 = (bf16[512,128]{1,0:T(8,128)(2,1)S(1)}, bf16[512,128]{1,0:T(8,128)(2,1)S(1)}, u32[]{:S(2)}, u32[]{:S(2)}) collective-permute-start(bf16[512,128]{1,0:T(8,128)(2,1)S(1)} %add_convert_fusion), channel_id=1, source_target_pairs={{0,24},{4,28},{8,16},{12,20},{16,8},{20,12},{24,0},{28,4},{1,25},{... | collective-permute-start | bytes 393224 | tf_op jit(solution)/shard_map/ppermute | solution.py:25
  92.2 1.8 %collective-permute-start.26 = (bf16[128,128]{1,0:T(8,128)(2,1)S(1)}, bf16[128,128]{1,0:T(8,128)(2,1)S(1)}, u32[]{:S(2)}, u32[]{:S(2)}) collective-permute-start(bf16[128,128]{1,0:T(8,128)(2,1)S(1)} %get-tuple-element.63), channel_id=1, source_target_pairs={{0,2},{1,3},{2,0},{3,1},{4,6},{5,7},{6,4},{7,5},{8,10},{9,11},{10,... | collective-permute-start | bytes 98312 | tf_op jit(solution)/shard_map/ppermute | solution.py:25
  94.0 2.7 %collective-permute-done.23 = bf16[512,128]{1,0:T(8,128)(2,1)S(1)} collective-permute-done((bf16[512,128]{1,0:T(8,128)(2,1)S(1)}, bf16[512,128]{1,0:T(8,128)(2,1)S(1)}, u32[]{:S(2)}, u32[]{:S(2)}) %collective-permute-start.23) | collective-permute-done | bytes 131104 | tf_op jit(solution)/shard_map/ppermute | solution.py:25
  97.0 1.8 %collective-permute-start.27 = (bf16[128,128]{1,0:T(8,128)(2,1)S(1)}, bf16[128,128]{1,0:T(8,128)(2,1)S(1)}, u32[]{:S(2)}, u32[]{:S(2)}) collective-permute-start(bf16[128,128]{1,0:T(8,128)(2,1)S(1)} %get-tuple-element.60), channel_id=1, source_target_pairs={{0,2},{1,3},{2,0},{3,1},{4,6},{5,7},{6,4},{7,5},{8,10},{9,11},{10,... | collective-permute-start | bytes 98312 | tf_op jit(solution)/shard_map/ppermute | solution.py:25
  98.8 1.3 %gate.1.gate_ref = f32[4,128,256]{2,1,0:T(8,128)S(1)} custom-call(s32[1]{0:T(128)} %bitcast._.me_ref, bf16[128,1024]{1,0:T(8,128)(2,1)S(1)} %copy-done.3, bf16[1024,2048]{1,0:T(8,128)(2,1)S(1)} %copy-done.1), custom_call_target="tpu_custom_call" | custom-call | flops 268435456 | bytes 2883584 | tf_op jit(solution)/shard_map/gate/pallas_call | solution.py:146
  100.9 1.2 %collective-permute-done.29.refs_7_ = bf16[128,128]{1,0:T(8,128)(2,1)S(1)} collective-permute-done((bf16[128,128]{1,0:T(8,128)(2,1)S(1)}, bf16[128,128]{1,0:T(8,128)(2,1)S(1)}, u32[]{:S(2)}, u32[]{:S(2)}) %collective-permute-start.29) | collective-permute-done | bytes 32800 | tf_op jit(solution)/shard_map/ppermute | solution.py:25
  102.1 1.4 %finish.1 = bf16[128,1024]{1,0:T(8,128)(2,1)} custom-call(s32[1]{0:T(128)} %bitcast._.me_ref, bf16[128,1024]{1,0:T(8,128)(2,1)S(1)} %copy-done.3, f32[4,128,256]{2,1,0:T(8,128)S(1)} %gate.1.gate_ref, bf16[1024,1024]{1,0:T(8,128)(2,1)S(1)} %copy-done.4, f32[128,128]{1,0:T(8,128)S(1)} %slice.114.refs_0_, f32[128,128]{1,0:T(8,128)S(1)} %slice.121.refs_1_, ...), custom_call_target="tpu_custom_call" | custom-call | flops 268435456 | bytes 3407872 | tf_op jit(solution)/shard_map/finish/pallas_call | solution.py:327
  (99 shorter events, 17.9 us)
Async XLA Ops:
  3.6 10.0 %collective-permute-start = (bf16[144,256]{1,0:T(8,128)(2,1)}, bf16[144,256]{1,0:T(8,128)(2,1)S(1)}, u32[]{:S(2)}, u32[]{:S(2)}) collective-permute-start(bf16[144,256]{1,0:T(8,128)(2,1)} %get-tuple-element.29), channel_id=1, source_target_pairs={{0,1},{1,0},{2,3},{3,2},{4,5},{5,4},{6,7},{7,6},{8,9},{9,8},{10,11... | collective-permute-start | bytes 221192 | tf_op jit(solution)/shard_map/ppermute | solution.py:25
  4.2 9.5 %collective-permute-start.1 = (bf16[144,256]{1,0:T(8,128)(2,1)}, bf16[144,256]{1,0:T(8,128)(2,1)S(1)}, u32[]{:S(2)}, u32[]{:S(2)}) collective-permute-start(bf16[144,256]{1,0:T(8,128)(2,1)} %get-tuple-element.30), channel_id=1, source_target_pairs={{0,2},{1,3},{2,0},{3,1},{4,6},{5,7},{6,4},{7,5},{8,10},{9,11},{10,... | collective-permute-start | bytes 221192 | tf_op jit(solution)/shard_map/ppermute | solution.py:25
  6.7 6.9 %collective-permute-start.2 = (bf16[144,256]{1,0:T(8,128)(2,1)}, bf16[144,256]{1,0:T(8,128)(2,1)S(1)}, u32[]{:S(2)}, u32[]{:S(2)}) collective-permute-start(bf16[144,256]{1,0:T(8,128)(2,1)} %get-tuple-element.31), channel_id=1, source_target_pairs={{0,3},{1,2},{2,1},{3,0},{4,7},{5,6},{6,5},{7,4},{8,11},{9,10},{10,... | collective-permute-start | bytes 221192 | tf_op jit(solution)/shard_map/ppermute | solution.py:25
  13.5 31.1 %collective-permute-start.3 = (bf16[768,256]{1,0:T(8,128)(2,1)}, bf16[768,256]{1,0:T(8,128)(2,1)}, u32[]{:S(2)}, u32[]{:S(2)}) collective-permute-start(bf16[768,256]{1,0:T(8,128)(2,1)} %get-tuple-element.34), channel_id=1, source_target_pairs={{0,1},{1,0},{2,3},{3,2},{4,5},{5,4},{6,7},{7,6},{8,9},{9,8},{10,11... | collective-permute-start | bytes 1179656 | tf_op jit(solution)/shard_map/ppermute | solution.py:25
  15.6 12.6 %collective-permute-start.6 = (bf16[512,128]{1,0:T(8,128)(2,1)}, bf16[512,128]{1,0:T(8,128)(2,1)}, u32[]{:S(2)}, u32[]{:S(2)}) collective-permute-start(bf16[512,128]{1,0:T(8,128)(2,1)} %get-tuple-element.37.refs_4_), channel_id=1, source_target_pairs={{0,24},{4,28},{8,16},{12,20},{16,8},{20,12},{24,0},{28,4},{1,25},{... | collective-permute-start | bytes 393224 | tf_op jit(solution)/shard_map/ppermute | solution.py:25
  24.2 22.0 %collective-permute-start.4 = (bf16[768,256]{1,0:T(8,128)(2,1)}, bf16[768,256]{1,0:T(8,128)(2,1)S(1)}, u32[]{:S(2)}, u32[]{:S(2)}) collective-permute-start(bf16[768,256]{1,0:T(8,128)(2,1)} %get-tuple-element.35), channel_id=1, source_target_pairs={{0,2},{1,3},{2,0},{3,1},{4,6},{5,7},{6,4},{7,5},{8,10},{9,11},{10,... | collective-permute-start | bytes 1179656 | tf_op jit(solution)/shard_map/ppermute | solution.py:25
  25.7 20.9 %collective-permute-start.5 = (bf16[768,256]{1,0:T(8,128)(2,1)}, bf16[768,256]{1,0:T(8,128)(2,1)S(1)}, u32[]{:S(2)}, u32[]{:S(2)}) collective-permute-start(bf16[768,256]{1,0:T(8,128)(2,1)} %get-tuple-element.36), channel_id=1, source_target_pairs={{0,3},{1,2},{2,1},{3,0},{4,7},{5,6},{6,5},{7,4},{8,11},{9,10},{10,... | collective-permute-start | bytes 1179656 | tf_op jit(solution)/shard_map/ppermute | solution.py:25
  25.7 6.3 %collective-permute-start.17 = (bf16[512,128]{1,0:T(8,128)(2,1)}, bf16[512,128]{1,0:T(8,128)(2,1)S(1)}, u32[]{:S(2)}, u32[]{:S(2)}) collective-permute-start(bf16[512,128]{1,0:T(8,128)(2,1)} %copy-done.5), channel_id=1, source_target_pairs={{0,4},{4,0},{8,12},{12,8},{16,20},{20,16},{24,28},{28,24},{1,5},{5... | collective-permute-start | bytes 393224 | tf_op jit(solution)/shard_map/ppermute | solution.py:25
  28.1 36.2 %copy-start.11 = (bf16[768,256]{1,0:T(8,128)(2,1)S(1)}, bf16[768,256]{1,0:T(8,128)(2,1)}, u32[]{:S(2)}) copy-start(bf16[768,256]{1,0:T(8,128)(2,1)} %copy-done.10) | copy-start | bytes 1179652
  28.1 36.2 %copy-start.15 = (s32[2]{0:T(128)S(1)}, s32[2]{0:T(128)}, u32[]{:S(2)}) copy-start(s32[2]{0:T(128)} %constant.18.clone.code_ref) | copy-start | bytes 28
  29.1 14.3 %collective-permute-start.8 = (bf16[1024,128]{1,0:T(8,128)(2,1)S(1)}, bf16[1024,128]{1,0:T(8,128)(2,1)S(1)}, u32[]{:S(2)}, u32[]{:S(2)}) collective-permute-start(bf16[1024,128]{1,0:T(8,128)(2,1)S(1)} %constant_dynamic-update-slice_fusion), channel_id=1, source_target_pairs={{0,8},{4,12},{8,0},{12,4},{16,24},{20,28},{24,16},{28,20},{1,9},{5... | collective-permute-start | bytes 786440 | tf_op jit(solution)/shard_map/ppermute | solution.py:25
  32.9 10.7 %collective-permute-start.18 = (bf16[1024,128]{1,0:T(8,128)(2,1)S(1)}, bf16[1024,128]{1,0:T(8,128)(2,1)S(1)}, u32[]{:S(2)}, u32[]{:S(2)}) collective-permute-start(bf16[1024,128]{1,0:T(8,128)(2,1)S(1)} %pad_maximum_fusion.2), channel_id=1, source_target_pairs={{0,24},{4,28},{8,16},{12,20},{16,8},{20,12},{24,0},{28,4},{1,25},{... | collective-permute-start | bytes 786440 | tf_op jit(solution)/shard_map/ppermute | solution.py:25
  43.4 6.4 %collective-permute-start.9 = (bf16[1024,128]{1,0:T(8,128)(2,1)S(1)}, bf16[1024,128]{1,0:T(8,128)(2,1)S(1)}, u32[]{:S(2)}, u32[]{:S(2)}) collective-permute-start(bf16[1024,128]{1,0:T(8,128)(2,1)S(1)} %collective-permute-done.8.refs_7_), channel_id=1, source_target_pairs={{0,4},{4,0},{8,12},{12,8},{16,20},{20,16},{24,28},{28,24},{1,5},{5... | collective-permute-start | bytes 786440 | tf_op jit(solution)/shard_map/ppermute | solution.py:25
  43.6 18.7 %collective-permute-start.14 = (bf16[768,256]{1,0:T(8,128)(2,1)}, bf16[768,256]{1,0:T(8,128)(2,1)S(1)}, u32[]{:S(2)}, u32[]{:S(2)}) collective-permute-start(bf16[768,256]{1,0:T(8,128)(2,1)} %copy-done.16), channel_id=1, source_target_pairs={{0,1},{1,0},{2,3},{3,2},{4,5},{5,4},{6,7},{7,6},{8,9},{9,8},{10,11... | collective-permute-start | bytes 1179656 | tf_op jit(solution)/shard_map/ppermute | solution.py:25
  44.6 18.1 %collective-permute-start.15 = (bf16[768,256]{1,0:T(8,128)(2,1)}, bf16[768,256]{1,0:T(8,128)(2,1)S(1)}, u32[]{:S(2)}, u32[]{:S(2)}) collective-permute-start(bf16[768,256]{1,0:T(8,128)(2,1)} %copy-done.18), channel_id=1, source_target_pairs={{0,2},{1,3},{2,0},{3,1},{4,6},{5,7},{6,4},{7,5},{8,10},{9,11},{10,... | collective-permute-start | bytes 1179656 | tf_op jit(solution)/shard_map/ppermute | solution.py:25
  46.2 18.2 %collective-permute-start.16 = (bf16[768,256]{1,0:T(8,128)(2,1)}, bf16[768,256]{1,0:T(8,128)(2,1)S(1)}, u32[]{:S(2)}, u32[]{:S(2)}) collective-permute-start(bf16[768,256]{1,0:T(8,128)(2,1)} %copy-done.17), channel_id=1, source_target_pairs={{0,3},{1,2},{2,1},{3,0},{4,7},{5,6},{6,5},{7,4},{8,11},{9,10},{10,... | collective-permute-start | bytes 1179656 | tf_op jit(solution)/shard_map/ppermute | solution.py:25
  46.5 8.8 %collective-permute-start.7 = (bf16[1024,128]{1,0:T(8,128)(2,1)S(1)}, bf16[1024,128]{1,0:T(8,128)(2,1)S(1)}, u32[]{:S(2)}, u32[]{:S(2)}) collective-permute-start(bf16[1024,128]{1,0:T(8,128)(2,1)S(1)} %constant_dynamic-update-slice_fusion), channel_id=1, source_target_pairs={{0,4},{4,0},{8,12},{12,8},{16,20},{20,16},{24,28},{28,24},{1,5},{5... | collective-permute-start | bytes 786440 | tf_op jit(solution)/shard_map/ppermute | solution.py:25
  49.8 14.6 %collective-permute-start.19 = (bf16[2048,128]{1,0:T(8,128)(2,1)S(1)}, bf16[2048,128]{1,0:T(8,128)(2,1)S(1)}, u32[]{:S(2)}, u32[]{:S(2)}) collective-permute-start(bf16[2048,128]{1,0:T(8,128)(2,1)S(1)} %pad_maximum_fusion), channel_id=1, source_target_pairs={{0,8},{4,12},{8,0},{12,4},{16,24},{20,28},{24,16},{28,20},{1,9},{5... | collective-permute-start | bytes 1572872 | tf_op jit(solution)/shard_map/ppermute | solution.py:25
  55.4 13.1 %collective-permute-start.10 = (bf16[1024,128]{1,0:T(8,128)(2,1)S(1)}, bf16[1024,128]{1,0:T(8,128)(2,1)S(1)}, u32[]{:S(2)}, u32[]{:S(2)}) collective-permute-start(bf16[1024,128]{1,0:T(8,128)(2,1)S(1)} %shard_map.103), channel_id=1, source_target_pairs={{0,4},{4,0},{8,12},{12,8},{16,20},{20,16},{24,28},{28,24},{1,5},{5... | collective-permute-start | bytes 786440 | tf_op jit(solution)/shard_map/ppermute | solution.py:25
  62.3 14.1 %collective-permute-start.12 = (bf16[1024,128]{1,0:T(8,128)(2,1)S(1)}, bf16[1024,128]{1,0:T(8,128)(2,1)S(1)}, u32[]{:S(2)}, u32[]{:S(2)}) collective-permute-start(bf16[1024,128]{1,0:T(8,128)(2,1)S(1)} %get-tuple-element.40), channel_id=1, source_target_pairs={{0,4},{4,0},{8,12},{12,8},{16,20},{20,16},{24,28},{28,24},{1,5},{5... | collective-permute-start | bytes 786440 | tf_op jit(solution)/shard_map/ppermute | solution.py:25
  66.5 9.8 %collective-permute-start.20 = (bf16[1024,128]{1,0:T(8,128)(2,1)S(1)}, bf16[1024,128]{1,0:T(8,128)(2,1)S(1)}, u32[]{:S(2)}, u32[]{:S(2)}) collective-permute-start(bf16[1024,128]{1,0:T(8,128)(2,1)S(1)} %shard_map.105), channel_id=1, source_target_pairs={{0,4},{4,0},{8,12},{12,8},{16,20},{20,16},{24,28},{28,24},{1,5},{5... | collective-permute-start | bytes 786440 | tf_op jit(solution)/shard_map/ppermute | solution.py:25
  68.6 9.3 %collective-permute-start.11 = (bf16[1024,128]{1,0:T(8,128)(2,1)S(1)}, bf16[1024,128]{1,0:T(8,128)(2,1)S(1)}, u32[]{:S(2)}, u32[]{:S(2)}) collective-permute-start(bf16[1024,128]{1,0:T(8,128)(2,1)S(1)} %pad_maximum_fusion.1), channel_id=1, source_target_pairs={{0,8},{4,12},{8,0},{12,4},{16,24},{20,28},{24,16},{28,20},{1,9},{5... | collective-permute-start | bytes 786440 | tf_op jit(solution)/shard_map/ppermute | solution.py:25
  75.9 10.4 %collective-permute-start.22 = (bf16[1024,128]{1,0:T(8,128)(2,1)S(1)}, bf16[1024,128]{1,0:T(8,128)(2,1)S(1)}, u32[]{:S(2)}, u32[]{:S(2)}) collective-permute-start(bf16[1024,128]{1,0:T(8,128)(2,1)S(1)} %get-tuple-element.49), channel_id=1, source_target_pairs={{0,4},{4,0},{8,12},{12,8},{16,20},{20,16},{24,28},{28,24},{1,5},{5... | collective-permute-start | bytes 786440 | tf_op jit(solution)/shard_map/ppermute | solution.py:25
  77.9 8.2 %collective-permute-start.13 = (bf16[512,128]{1,0:T(8,128)(2,1)S(1)}, bf16[512,128]{1,0:T(8,128)(2,1)S(1)}, u32[]{:S(2)}, u32[]{:S(2)}) collective-permute-start(bf16[512,128]{1,0:T(8,128)(2,1)S(1)} %add_convert_fusion.3), channel_id=1, source_target_pairs={{0,24},{4,28},{8,16},{12,20},{16,8},{20,12},{24,0},{28,4},{1,25},{... | collective-permute-start | bytes 393224 | tf_op jit(solution)/shard_map/ppermute | solution.py:25
  79.4 10.5 %collective-permute-start.21 = (bf16[1024,128]{1,0:T(8,128)(2,1)S(1)}, bf16[1024,128]{1,0:T(8,128)(2,1)S(1)}, u32[]{:S(2)}, u32[]{:S(2)}) collective-permute-start(bf16[1024,128]{1,0:T(8,128)(2,1)S(1)} %pad_maximum_fusion.3), channel_id=1, source_target_pairs={{0,8},{4,12},{8,0},{12,4},{16,24},{20,28},{24,16},{28,20},{1,9},{5... | collective-permute-start | bytes 786440 | tf_op jit(solution)/shard_map/ppermute | solution.py:25
  89.9 6.8 %collective-permute-start.23 = (bf16[512,128]{1,0:T(8,128)(2,1)S(1)}, bf16[512,128]{1,0:T(8,128)(2,1)S(1)}, u32[]{:S(2)}, u32[]{:S(2)}) collective-permute-start(bf16[512,128]{1,0:T(8,128)(2,1)S(1)} %add_convert_fusion), channel_id=1, source_target_pairs={{0,24},{4,28},{8,16},{12,20},{16,8},{20,12},{24,0},{28,4},{1,25},{... | collective-permute-start | bytes 393224 | tf_op jit(solution)/shard_map/ppermute | solution.py:25
  92.1 6.7 %collective-permute-start.24 = (bf16[128,128]{1,0:T(8,128)(2,1)S(1)}, bf16[128,128]{1,0:T(8,128)(2,1)S(1)}, u32[]{:S(2)}, u32[]{:S(2)}) collective-permute-start(bf16[128,128]{1,0:T(8,128)(2,1)S(1)} %get-tuple-element.64), channel_id=1, source_target_pairs={{0,1},{1,0},{2,3},{3,2},{4,5},{5,4},{6,7},{7,6},{8,9},{9,8},{10,11... | collective-permute-start | bytes 98312 | tf_op jit(solution)/shard_map/ppermute | solution.py:25
  92.2 8.0 %collective-permute-start.26 = (bf16[128,128]{1,0:T(8,128)(2,1)S(1)}, bf16[128,128]{1,0:T(8,128)(2,1)S(1)}, u32[]{:S(2)}, u32[]{:S(2)}) collective-permute-start(bf16[128,128]{1,0:T(8,128)(2,1)S(1)} %get-tuple-element.63), channel_id=1, source_target_pairs={{0,2},{1,3},{2,0},{3,1},{4,6},{5,7},{6,4},{7,5},{8,10},{9,11},{10,... | collective-permute-start | bytes 98312 | tf_op jit(solution)/shard_map/ppermute | solution.py:25
  94.0 6.2 %collective-permute-start.28 = (bf16[128,128]{1,0:T(8,128)(2,1)S(1)}, bf16[128,128]{1,0:T(8,128)(2,1)S(1)}, u32[]{:S(2)}, u32[]{:S(2)}) collective-permute-start(bf16[128,128]{1,0:T(8,128)(2,1)S(1)} %get-tuple-element.62), channel_id=1, source_target_pairs={{0,3},{1,2},{2,1},{3,0},{4,7},{5,6},{6,5},{7,4},{8,11},{9,10},{10,... | collective-permute-start | bytes 98312 | tf_op jit(solution)/shard_map/ppermute | solution.py:25
  96.9 3.4 %collective-permute-start.25 = (bf16[128,128]{1,0:T(8,128)(2,1)S(1)}, bf16[128,128]{1,0:T(8,128)(2,1)S(1)}, u32[]{:S(2)}, u32[]{:S(2)}) collective-permute-start(bf16[128,128]{1,0:T(8,128)(2,1)S(1)} %get-tuple-element.61), channel_id=1, source_target_pairs={{0,1},{1,0},{2,3},{3,2},{4,5},{5,4},{6,7},{7,6},{8,9},{9,8},{10,11... | collective-permute-start | bytes 98312 | tf_op jit(solution)/shard_map/ppermute | solution.py:25
  97.0 4.0 %collective-permute-start.27 = (bf16[128,128]{1,0:T(8,128)(2,1)S(1)}, bf16[128,128]{1,0:T(8,128)(2,1)S(1)}, u32[]{:S(2)}, u32[]{:S(2)}) collective-permute-start(bf16[128,128]{1,0:T(8,128)(2,1)S(1)} %get-tuple-element.60), channel_id=1, source_target_pairs={{0,2},{1,3},{2,0},{3,1},{4,6},{5,7},{6,4},{7,5},{8,10},{9,11},{10,... | collective-permute-start | bytes 98312 | tf_op jit(solution)/shard_map/ppermute | solution.py:25
  98.8 3.4 %collective-permute-start.29 = (bf16[128,128]{1,0:T(8,128)(2,1)S(1)}, bf16[128,128]{1,0:T(8,128)(2,1)S(1)}, u32[]{:S(2)}, u32[]{:S(2)}) collective-permute-start(bf16[128,128]{1,0:T(8,128)(2,1)S(1)} %get-tuple-element.59), channel_id=1, source_target_pairs={{0,3},{1,2},{2,1},{3,0},{4,7},{5,6},{6,5},{7,4},{8,11},{9,10},{10,... | collective-permute-start | bytes 98312 | tf_op jit(solution)/shard_map/ppermute | solution.py:25
  (18 other events, 185.4 us)

commit v7 on v6

--- a/solution.py
+++ b/solution.py
@@ -374,7 +374,19 @@
 
 
 def scatter_plan(count):
-    return stages(count, False)
+    outer = [mask for mask, codes in stages(count, True) if mask != 1]
+    plan, main, side = [], [0], [1]
+    for mask in outer[:-1]:
+        plan.append((mask, tuple(main)))
+        main += [c ^ mask for c in main]
+    plan.append((1, (0,)))
+    for mask in outer[:-1]:
+        plan.append((mask, tuple(side)))
+        side += [c ^ mask for c in side]
+    for mask in outer[-1:]:
+        plan.append((mask, tuple(main)))
+        plan.append((1, tuple(c ^ mask for c in main)))
+    return plan
 
 
 def gather_queries(own, plan):
@@ -393,16 +405,43 @@
     held = {}
     for group, array in zip(groups, arrays):
         for j, c in enumerate(group):
-            held[c] = array[j * cands : (j + 1) * cands]
+            held[c] = [(array, j * cands)]
     for number in reversed(range(len(plan))):
         mask, codes = plan[number]
         away = tuple(c ^ mask for c in codes)
-        sent = whole[away] if away in whole else joined([held[c].astype(BF16) for c in away])
+        if away in whole:
+            sent = whole[away]
+        else:
+            sums = [sum(a[at : at + cands].astype(F32) for a, at in held[c]) for c in away]
+            sent = joined([part.astype(BF16) for part in sums])
         got = swap(sent, "req", mask)
         whole = {g: a for g, a in whole.items() if not set(g) & set(codes)}
         for j, c in enumerate(codes):
-            held[c] = held[c].astype(F32) + got[j * cands : (j + 1) * cands].astype(F32)
+            held[c].append((got, j * cands))
     return held[0]
+
+
+def total_kernel(starts, *refs):
+    arrays, outs = refs[: len(starts)], refs[len(starts) :]
+    mine = outs[0].shape[0]
+    for k, out in enumerate(outs):
+        rows = [slice(at + k * mine, at + (k + 1) * mine) for at in starts]
+        total = sum(ref[r, :].astype(F32) for ref, r in zip(arrays, rows))
+        out[...] = total.astype(out.dtype)
+
+
+def add_up(terms, cands, count):
+    vmem = pl.BlockSpec(memory_space=pltpu.VMEM)
+    mine = cands // count
+    kinds = [F32] + [BF16] * (count - 1)
+    return pl.pallas_call(
+        functools.partial(total_kernel, [at for _, at in terms]),
+        in_specs=[vmem] * len(terms),
+        out_specs=[vmem] * count,
+        out_shape=[jax.ShapeDtypeStruct((mine, HEAD), kind) for kind in kinds],
+        compiler_params=room_for(*[(a.shape, a.dtype) for a, _ in terms], ((cands, HEAD), F32)),
+        cost_estimate=cost(len(terms) * cands * HEAD, 4 * len(terms) * cands * HEAD),
+    )(*[a for a, _ in terms])
 
 
 def on_device(history, block_owner, candidates, w_kv, w_qu, w_out):
@@ -459,22 +498,16 @@
                 cands, events, room,
             )
             sums.update(zip(call, made))
-        total = scatter_sums(plan, groups, [sums[i] for i in range(len(groups))], cands)
-        parts[0][h] = total[:mine]
-        for k in range(1, n_ctx):
-            piece = total[k * mine : (k + 1) * mine].astype(BF16)
-            parts[k][h] = swap(piece, "ctx", k)
+        terms = scatter_sums(plan, groups, [sums[i] for i in range(len(groups))], cands)
+        pieces = add_up(terms, cands, n_ctx)
+        for k, piece in enumerate(pieces):
+            parts[k][h] = piece if k == 0 else swap(piece, "ctx", k)
     return finish(me_ctx, candidates, gate, w_out, [p for row in parts for p in row])
 
 
 def calls_of(count, head):
-    plan = scatter_plan(count)
-    everything = list(range(len(plan) + 1))
-    inner = [i for i in range(len(plan)) if plan[i][0] == 1]
-    if len(inner) < 2:
-        return [everything]
-    last = inner[-1]
-    rest = [i for i in everything if i != last]
+    last = len(scatter_plan(count)) - 1
+    rest = [i for i in range(last + 2) if i != last]
     return [rest, [last]] if head % 2 == 0 else [[last], rest]
 
 

time: 104 us -> 108 us (1.038)
  starting transfers between devices: 30.8 us -> 49.6 us
  waiting for transfers between devices: 31.2 us -> 22.1 us
  local copies, waits for them, and re-layouts: 10.1 us -> 7.11 us
  other arithmetic: 3.29 us -> 0.69 us
    ppermute x30 -> x32, starting transfers between devices: 30.8 us -> 49.6 us  [swap(): return lax.ppermute(value, axis, [(i, i ^ mask) for i in range(count)])]
    ppermute x30 -> x32, waiting for transfers between devices: 31.2 us -> 22.1 us  [swap(): return lax.ppermute(value, axis, [(i, i ^ mask) for i in range(count)])]
    unnamed x41 -> x35, local copies, waits for them, and re-layouts: 9.02 us -> 7.01 us
    concatenate x4, other arithmetic: 1.9 us -> 0.09 us  [joined(): return pieces[0] if len(pieces) == 1 else jnp.concatenate(pieces, axis=0)]
  transfers between devices with their start and end apart: 30 -> 32, of which waited for: 11 -> 11; matrix products, arithmetic and copies ran while one was open for 5% -> 1% of each run, Pallas kernels for 22% -> 21%
where the time goes in v7:
time: 108 us; the launch traced here: 107 us
  starting transfers between devices  49.6 us (46%)
  Pallas kernels  27.7 us (26%)
  waiting for transfers between devices  22.1 us (20%)
  local copies, waits for them, and re-layouts  7.11 us (7%)
    ppermute x32, starting transfers between devices, swap(): return lax.ppermute(value, axis, [(i, i ^ mask) for i in range(count)])  49.6 us
    ppermute x32, waiting for transfers between devices, swap(): return lax.ppermute(value, axis, [(i, i ^ mask) for i in range(count)])  22.1 us
    pallas_call x4, Pallas kernels, attend(): pl.pallas_call(functools.partial(attend_kernel, source, sink, events, roo...  14.6 us
    unnamed x35, local copies, waits for them, and re-layouts  7.01 us
    pallas_call x2, Pallas kernels, project_keys_values(): pl.pallas_call(functools.partial(keys_values_kernel, count, each), grid_s...  5.71 us
    pallas_call x1, Pallas kernels, project_queries(): pl.pallas_call(query_kernel, in_specs=[pl.BlockSpec(memory_space=pltpu.SM...  3.58 us
  transfers between devices with their start and end apart: 32, of which 11 were waited for; matrix products, arithmetic and copies ran while one was open for 1% of the time, Pallas kernels for 21%

profile of v7, /device:TPU:0, one launch (start us, length us, event | category | flops | bytes accessed | tf_op | source)
XLA Modules:
  0.0 107.5 jit_solution(6483848243678295749)
XLA Ops:
  0.0 3.6 %queries.1 = (bf16[144,256]{1,0:T(8,128)(2,1)}, bf16[144,256]{1,0:T(8,128)(2,1)}, bf16[144,256]{1,0:T(8,128)(2,1)}, bf16[144,256]{1,0:T(8,128)(2,1)}) custom-call(s32[1]{0:T(128)} %bitcast._.me_ref, bf16[128,1024]{1,0:T(8,128)(2,1)} %cand_ref.3, bf16[1024,2048]{1,0:T(8,128)(2,1)} %w_hbm.1, s32[1,48]{1,0:T(1,128)} %bitcast.2), custom_call_target="tpu_custom_call" | custom-call | flops 268435456 | bytes 2621440 | tf_op jit(solution)/shard_map/queries/pallas_call | solution.py:95
  4.1 2.6 %collective-permute-start.1 = (bf16[144,256]{1,0:T(8,128)(2,1)}, bf16[144,256]{1,0:T(8,128)(2,1)}, u32[]{:S(2)}, u32[]{:S(2)}) collective-permute-start(bf16[144,256]{1,0:T(8,128)(2,1)} %get-tuple-element.40), channel_id=1, source_target_pairs={{0,2},{1,3},{2,0},{3,1},{4,6},{5,7},{6,4},{7,5},{8,10},{9,11},{10,... | collective-permute-start | bytes 221192 | tf_op jit(solution)/shard_map/ppermute | solution.py:25
  6.7 1.4 %copy-done.2 = bf16[768,1024]{1,0:T(8,128)(2,1)S(1)} copy-done((bf16[768,1024]{1,0:T(8,128)(2,1)S(1)}, bf16[768,1024]{1,0:T(8,128)(2,1)}, u32[]{:S(2)}) %copy-start.2) | copy-done | bytes 1572888
  8.1 3.0 %shard_map.100 = (bf16[768,256]{1,0:T(8,128)(2,1)S(1)}, bf16[768,256]{1,0:T(8,128)(2,1)S(1)}, bf16[768,256]{1,0:T(8,128)(2,1)}, bf16[768,256]{1,0:T(8,128)(2,1)S(1)}) custom-call(s32[1]{0:T(128)} %bitcast._.me_ref, bf16[768,1024]{1,0:T(8,128)(2,1)S(1)} %copy-done.2, bf16[1024,2048]{1,0:T(8,128)(2,1)S(1)} %copy-done, bf16[1024,2048]{1,0:T(8,128)(2,1)S(1)} %copy-done, ...), custom_call_target="tpu_custom_call" | custom-call | flops 1610612736 | bytes 5242880 | tf_op jit(solution)/shard_map/pallas_call | solution.py:186
  12.1 2.7 %shard_map.101 = (bf16[768,256]{1,0:T(8,128)(2,1)}, bf16[768,256]{1,0:T(8,128)(2,1)S(1)}, bf16[768,256]{1,0:T(8,128)(2,1)S(1)}, bf16[768,256]{1,0:T(8,128)(2,1)S(1)}) custom-call(s32[1]{0:T(128)} %bitcast._.me_ref, bf16[768,1024]{1,0:T(8,128)(2,1)S(1)} %copy-done.2, bf16[1024,2048]{1,0:T(8,128)(2,1)S(1)} %copy-done, bf16[1024,2048]{1,0:T(8,128)(2,1)S(1)} %copy-done, ...), custom_call_target="tpu_custom_call" | custom-call | flops 1610612736 | bytes 5242880 | tf_op jit(solution)/shard_map/pallas_call | solution.py:186
  17.0 2.0 %collective-permute-start.4 = (bf16[768,256]{1,0:T(8,128)(2,1)}, bf16[768,256]{1,0:T(8,128)(2,1)S(1)}, u32[]{:S(2)}, u32[]{:S(2)}) collective-permute-start(bf16[768,256]{1,0:T(8,128)(2,1)} %get-tuple-element.45), channel_id=1, source_target_pairs={{0,2},{1,3},{2,0},{3,1},{4,6},{5,7},{6,4},{7,5},{8,10},{9,11},{10,... | collective-permute-start | bytes 1179656 | tf_op jit(solution)/shard_map/ppermute | solution.py:25
  20.9 1.6 %collective-permute-start.18 = (bf16[512,128]{1,0:T(8,128)(2,1)S(1)}, bf16[512,128]{1,0:T(8,128)(2,1)S(1)}, u32[]{:S(2)}, u32[]{:S(2)}) collective-permute-start(bf16[512,128]{1,0:T(8,128)(2,1)S(1)} %get-tuple-element.58.refs_4_), channel_id=1, source_target_pairs={{0,4},{4,0},{8,12},{12,8},{16,20},{20,16},{24,28},{28,24},{1,5},{5... | collective-permute-start | bytes 393224 | tf_op jit(solution)/shard_map/ppermute | solution.py:25
  22.5 3.6 %collective-permute-start.6 = (bf16[512,128]{1,0:T(8,128)(2,1)S(1)}, bf16[512,128]{1,0:T(8,128)(2,1)S(1)}, u32[]{:S(2)}, u32[]{:S(2)}) collective-permute-start(bf16[512,128]{1,0:T(8,128)(2,1)S(1)} %get-tuple-element.47.refs_4_), channel_id=1, source_target_pairs={{0,24},{4,28},{8,16},{12,20},{16,8},{20,12},{24,0},{28,4},{1,25},{... | collective-permute-start | bytes 393224 | tf_op jit(solution)/shard_map/ppermute | solution.py:25
  26.8 3.9 %collective-permute-start.19 = (bf16[1024,128]{1,0:T(8,128)(2,1)S(1)}, bf16[1024,128]{1,0:T(8,128)(2,1)S(1)}, u32[]{:S(2)}, u32[]{:S(2)}) collective-permute-start(bf16[1024,128]{1,0:T(8,128)(2,1)S(1)} %pad_maximum_fusion.2), channel_id=1, source_target_pairs={{0,24},{4,28},{8,16},{12,20},{16,8},{20,12},{24,0},{28,4},{1,25},{... | collective-permute-start | bytes 786440 | tf_op jit(solution)/shard_map/ppermute | solution.py:25
  30.7 8.2 %collective-permute-start.8 = (bf16[1024,128]{1,0:T(8,128)(2,1)S(1)}, bf16[1024,128]{1,0:T(8,128)(2,1)S(1)}, u32[]{:S(2)}, u32[]{:S(2)}) collective-permute-start(bf16[1024,128]{1,0:T(8,128)(2,1)S(1)} %constant_dynamic-update-slice_fusion), channel_id=1, source_target_pairs={{0,8},{4,12},{8,0},{12,4},{16,24},{20,28},{24,16},{28,20},{1,9},{5... | collective-permute-start | bytes 786440 | tf_op jit(solution)/shard_map/ppermute | solution.py:25
  39.7 3.9 %collective-permute-done.8.refs_7_ = bf16[1024,128]{1,0:T(8,128)(2,1)S(1)} collective-permute-done((bf16[1024,128]{1,0:T(8,128)(2,1)S(1)}, bf16[1024,128]{1,0:T(8,128)(2,1)S(1)}, u32[]{:S(2)}, u32[]{:S(2)}) %collective-permute-start.8) | collective-permute-done | bytes 262176 | tf_op jit(solution)/shard_map/ppermute | solution.py:25
  44.3 1.8 %collective-permute-start.20 = (bf16[2048,128]{1,0:T(8,128)(2,1)S(1)}, bf16[2048,128]{1,0:T(8,128)(2,1)S(1)}, u32[]{:S(2)}, u32[]{:S(2)}) collective-permute-start(bf16[2048,128]{1,0:T(8,128)(2,1)S(1)} %pad_maximum_fusion), channel_id=1, source_target_pairs={{0,8},{4,12},{8,0},{12,4},{16,24},{20,28},{24,16},{28,20},{1,9},{5... | collective-permute-start | bytes 1572872 | tf_op jit(solution)/shard_map/ppermute | solution.py:25
  46.2 1.6 %collective-permute-start.16 = (bf16[768,256]{1,0:T(8,128)(2,1)}, bf16[768,256]{1,0:T(8,128)(2,1)S(1)}, u32[]{:S(2)}, u32[]{:S(2)}) collective-permute-start(bf16[768,256]{1,0:T(8,128)(2,1)} %copy-done.13), channel_id=1, source_target_pairs={{0,2},{1,3},{2,0},{3,1},{4,6},{5,7},{6,4},{7,5},{8,10},{9,11},{10,... | collective-permute-start | bytes 1179656 | tf_op jit(solution)/shard_map/ppermute | solution.py:25
  49.7 5.1 %shard_map.102 = (bf16[512,128]{1,0:T(8,128)(2,1)S(1)}, bf16[512,128]{1,0:T(8,128)(2,1)S(1)}, bf16[512,128]{1,0:T(8,128)(2,1)S(1)}, bf16[1024,128]{1,0:T(8,128)(2,1)S(1)}, bf16[512,128]{1,0:T(8,128)(2,1)S(1)}) custom-call(s32[192]{0:T(256)S(1)} %multiply_add_fusion.pos_ref, s32[8]{0:T(128)S(1)} %convert_reduce_fusion.1.count_ref, s32[6]{0:T(128)S(1)} %copy-done.15, ...), custom_call_target="tpu_custom_call" | custom-call | flops 1207959552 | bytes 3145728 | tf_op jit(solution)/shard_map/pallas_call | solution.py:280
  54.9 2.5 %collective-permute-start.12 = (bf16[512,128]{1,0:T(8,128)(2,1)S(1)}, bf16[512,128]{1,0:T(8,128)(2,1)S(1)}, u32[]{:S(2)}, u32[]{:S(2)}) collective-permute-start(bf16[512,128]{1,0:T(8,128)(2,1)S(1)} %get-tuple-element.51), channel_id=1, source_target_pairs={{0,24},{4,28},{8,16},{12,20},{16,8},{20,12},{24,0},{28,4},{1,25},{... | collective-permute-start | bytes 393224 | tf_op jit(solution)/shard_map/ppermute | solution.py:25
  57.5 2.6 %shard_map.103 = bf16[1024,128]{1,0:T(8,128)(2,1)S(1)} custom-call(s32[192]{0:T(256)S(1)} %multiply_add_fusion.pos_ref, s32[8]{0:T(128)S(1)} %convert_reduce_fusion.1.count_ref, s32[2]{0:T(128)S(1)} %copy-done.10, bf16[768,256]{1,0:T(8,128)(2,1)S(1)} %copy-done.6, bf16[768,256]{1,0:T(8,128)(2,1)} %collective-permute-done.3.refs_1_, ...), custom_call_target="tpu_custom_call" | custom-call | flops 402653184 | bytes 2097152 | tf_op jit(solution)/shard_map/pallas_call | solution.py:280
  60.1 3.0 %collective-permute-done.12 = bf16[512,128]{1,0:T(8,128)(2,1)S(1)} collective-permute-done((bf16[512,128]{1,0:T(8,128)(2,1)S(1)}, bf16[512,128]{1,0:T(8,128)(2,1)S(1)}, u32[]{:S(2)}, u32[]{:S(2)}) %collective-permute-start.12) | collective-permute-done | bytes 131104 | tf_op jit(solution)/shard_map/ppermute | solution.py:25
  65.8 2.2 %shard_map.106 = bf16[1024,128]{1,0:T(8,128)(2,1)S(1)} custom-call(s32[192]{0:T(256)S(1)} %multiply_add_fusion.pos_ref, s32[8]{0:T(128)S(1)} %convert_reduce_fusion.1.count_ref, s32[2]{0:T(128)S(1)} %copy-done.10, bf16[768,256]{1,0:T(8,128)(2,1)S(1)} %copy-done.8, bf16[768,256]{1,0:T(8,128)(2,1)S(1)} %collective-permute-done.15.refs_1_, ...), custom_call_target="tpu_custom_call" | custom-call | flops 402653184 | bytes 2097152 | tf_op jit(solution)/shard_map/pallas_call | solution.py:280
  68.0 1.4 %collective-permute-start.21 = (bf16[1024,128]{1,0:T(8,128)(2,1)S(1)}, bf16[1024,128]{1,0:T(8,128)(2,1)S(1)}, u32[]{:S(2)}, u32[]{:S(2)}) collective-permute-start(bf16[1024,128]{1,0:T(8,128)(2,1)S(1)} %shard_map.106), channel_id=1, source_target_pairs={{0,4},{4,0},{8,12},{12,8},{16,20},{20,16},{24,28},{28,24},{1,5},{5... | collective-permute-start | bytes 786440 | tf_op jit(solution)/shard_map/ppermute | solution.py:25
  69.4 4.7 %shard_map.105 = (bf16[512,128]{1,0:T(8,128)(2,1)S(1)}, bf16[512,128]{1,0:T(8,128)(2,1)S(1)}, bf16[512,128]{1,0:T(8,128)(2,1)S(1)}, bf16[1024,128]{1,0:T(8,128)(2,1)S(1)}, bf16[512,128]{1,0:T(8,128)(2,1)S(1)}) custom-call(s32[192]{0:T(256)S(1)} %multiply_add_fusion.pos_ref, s32[8]{0:T(128)S(1)} %convert_reduce_fusion.1.count_ref, s32[6]{0:T(128)S(1)} %copy-done.16, ...), custom_call_target="tpu_custom_call" | custom-call | flops 1207959552 | bytes 3145728 | tf_op jit(solution)/shard_map/pallas_call | solution.py:280
  74.1 2.7 %collective-permute-start.23 = (bf16[512,128]{1,0:T(8,128)(2,1)S(1)}, bf16[512,128]{1,0:T(8,128)(2,1)S(1)}, u32[]{:S(2)}, u32[]{:S(2)}) collective-permute-start(bf16[512,128]{1,0:T(8,128)(2,1)S(1)} %get-tuple-element.62), channel_id=1, source_target_pairs={{0,24},{4,28},{8,16},{12,20},{16,8},{20,12},{24,0},{28,4},{1,25},{... | collective-permute-start | bytes 393224 | tf_op jit(solution)/shard_map/ppermute | solution.py:25
  76.9 1.3 %collective-permute-start.11 = (bf16[1024,128]{1,0:T(8,128)(2,1)S(1)}, bf16[1024,128]{1,0:T(8,128)(2,1)S(1)}, u32[]{:S(2)}, u32[]{:S(2)}) collective-permute-start(bf16[1024,128]{1,0:T(8,128)(2,1)S(1)} %pad_maximum_fusion.1), channel_id=1, source_target_pairs={{0,8},{4,12},{8,0},{12,4},{16,24},{20,28},{24,16},{28,20},{1,9},{5... | collective-permute-start | bytes 786440 | tf_op jit(solution)/shard_map/ppermute | solution.py:25
  78.2 1.6 %collective-permute-done.21 = bf16[1024,128]{1,0:T(8,128)(2,1)S(1)} collective-permute-done((bf16[1024,128]{1,0:T(8,128)(2,1)S(1)}, bf16[1024,128]{1,0:T(8,128)(2,1)S(1)}, u32[]{:S(2)}, u32[]{:S(2)}) %collective-permute-start.21) | collective-permute-done | bytes 262176 | tf_op jit(solution)/shard_map/ppermute | solution.py:25
  79.9 3.3 %collective-permute-start.22 = (bf16[1024,128]{1,0:T(8,128)(2,1)S(1)}, bf16[1024,128]{1,0:T(8,128)(2,1)S(1)}, u32[]{:S(2)}, u32[]{:S(2)}) collective-permute-start(bf16[1024,128]{1,0:T(8,128)(2,1)S(1)} %pad_maximum_fusion.3), channel_id=1, source_target_pairs={{0,8},{4,12},{8,0},{12,4},{16,24},{20,28},{24,16},{28,20},{1,9},{5... | collective-permute-start | bytes 786440 | tf_op jit(solution)/shard_map/ppermute | solution.py:25
  84.4 3.2 %collective-permute-done.11.refs_1_ = bf16[1024,128]{1,0:T(8,128)(2,1)S(1)} collective-permute-done((bf16[1024,128]{1,0:T(8,128)(2,1)S(1)}, bf16[1024,128]{1,0:T(8,128)(2,1)S(1)}, u32[]{:S(2)}, u32[]{:S(2)}) %collective-permute-start.11) | collective-permute-done | bytes 262176 | tf_op jit(solution)/shard_map/ppermute | solution.py:25
  87.6 2.6 %collective-permute-start.14 = (bf16[512,128]{1,0:T(8,128)(2,1)S(1)}, bf16[512,128]{1,0:T(8,128)(2,1)S(1)}, u32[]{:S(2)}, u32[]{:S(2)}) collective-permute-start(bf16[512,128]{1,0:T(8,128)(2,1)S(1)} %add_convert_fusion.4), channel_id=1, source_target_pairs={{0,24},{4,28},{8,16},{12,20},{16,8},{20,12},{24,0},{28,4},{1,25},{... | collective-permute-start | bytes 393224 | tf_op jit(solution)/shard_map/ppermute | solution.py:25
  90.2 3.5 %collective-permute-done.22.refs_1_ = bf16[1024,128]{1,0:T(8,128)(2,1)S(1)} collective-permute-done((bf16[1024,128]{1,0:T(8,128)(2,1)S(1)}, bf16[1024,128]{1,0:T(8,128)(2,1)S(1)}, u32[]{:S(2)}, u32[]{:S(2)}) %collective-permute-start.22) | collective-permute-done | bytes 262176 | tf_op jit(solution)/shard_map/ppermute | solution.py:25
  96.1 1.6 %collective-permute-start.28 = (bf16[128,128]{1,0:T(8,128)(2,1)S(1)}, bf16[128,128]{1,0:T(8,128)(2,1)S(1)}, u32[]{:S(2)}, u32[]{:S(2)}) collective-permute-start(bf16[128,128]{1,0:T(8,128)(2,1)S(1)} %get-tuple-element.67), channel_id=1, source_target_pairs={{0,2},{1,3},{2,0},{3,1},{4,6},{5,7},{6,4},{7,5},{8,10},{9,11},{10,... | collective-permute-start | bytes 98312 | tf_op jit(solution)/shard_map/ppermute | solution.py:25
  98.0 3.1 %collective-permute-done.25.refs_3_ = bf16[512,128]{1,0:T(8,128)(2,1)S(1)} collective-permute-done((bf16[512,128]{1,0:T(8,128)(2,1)S(1)}, bf16[512,128]{1,0:T(8,128)(2,1)S(1)}, u32[]{:S(2)}, u32[]{:S(2)}) %collective-permute-start.25) | collective-permute-done | bytes 131104 | tf_op jit(solution)/shard_map/ppermute | solution.py:25
  101.2 1.6 %collective-permute-start.29 = (bf16[128,128]{1,0:T(8,128)(2,1)S(1)}, bf16[128,128]{1,0:T(8,128)(2,1)S(1)}, u32[]{:S(2)}, u32[]{:S(2)}) collective-permute-start(bf16[128,128]{1,0:T(8,128)(2,1)S(1)} %get-tuple-element.68), channel_id=1, source_target_pairs={{0,2},{1,3},{2,0},{3,1},{4,6},{5,7},{6,4},{7,5},{8,10},{9,11},{10,... | collective-permute-start | bytes 98312 | tf_op jit(solution)/shard_map/ppermute | solution.py:25
  103.1 1.3 %gate.1.gate_ref = f32[4,128,256]{2,1,0:T(8,128)S(1)} custom-call(s32[1]{0:T(128)} %bitcast._.me_ref, bf16[128,1024]{1,0:T(8,128)(2,1)S(1)} %copy-done.3, bf16[1024,2048]{1,0:T(8,128)(2,1)S(1)} %copy-done.1), custom_call_target="tpu_custom_call" | custom-call | flops 268435456 | bytes 2883584 | tf_op jit(solution)/shard_map/gate/pallas_call | solution.py:146
  106.2 1.3 %finish.1 = bf16[128,1024]{1,0:T(8,128)(2,1)} custom-call(s32[1]{0:T(128)} %bitcast._.me_ref, bf16[128,1024]{1,0:T(8,128)(2,1)S(1)} %copy-done.3, f32[4,128,256]{2,1,0:T(8,128)S(1)} %gate.1.gate_ref, bf16[1024,1024]{1,0:T(8,128)(2,1)S(1)} %copy-done.4, f32[128,128]{1,0:T(8,128)S(1)} %get-tuple-element.53.refs_0_, f32[128,128]{1,0:T(8,128)S(1)} %get-tuple-element.64.refs_1_, ...), custom_call_target="tpu_custom_call" | custom-call | flops 268435456 | bytes 3407872 | tf_op jit(solution)/shard_map/finish/pallas_call | solution.py:327
  (95 shorter events, 18.8 us)
Async XLA Ops:
  3.6 15.4 %collective-permute-start = (bf16[144,256]{1,0:T(8,128)(2,1)}, bf16[144,256]{1,0:T(8,128)(2,1)}, u32[]{:S(2)}, u32[]{:S(2)}) collective-permute-start(bf16[144,256]{1,0:T(8,128)(2,1)} %get-tuple-element.39), channel_id=1, source_target_pairs={{0,1},{1,0},{2,3},{3,2},{4,5},{5,4},{6,7},{7,6},{8,9},{9,8},{10,11... | collective-permute-start | bytes 221192 | tf_op jit(solution)/shard_map/ppermute | solution.py:25
  4.1 14.9 %collective-permute-start.1 = (bf16[144,256]{1,0:T(8,128)(2,1)}, bf16[144,256]{1,0:T(8,128)(2,1)}, u32[]{:S(2)}, u32[]{:S(2)}) collective-permute-start(bf16[144,256]{1,0:T(8,128)(2,1)} %get-tuple-element.40), channel_id=1, source_target_pairs={{0,2},{1,3},{2,0},{3,1},{4,6},{5,7},{6,4},{7,5},{8,10},{9,11},{10,... | collective-permute-start | bytes 221192 | tf_op jit(solution)/shard_map/ppermute | solution.py:25
  6.7 12.3 %collective-permute-start.2 = (bf16[144,256]{1,0:T(8,128)(2,1)}, bf16[144,256]{1,0:T(8,128)(2,1)}, u32[]{:S(2)}, u32[]{:S(2)}) collective-permute-start(bf16[144,256]{1,0:T(8,128)(2,1)} %get-tuple-element.41), channel_id=1, source_target_pairs={{0,3},{1,2},{2,1},{3,0},{4,7},{5,6},{6,5},{7,4},{8,11},{9,10},{10,... | collective-permute-start | bytes 221192 | tf_op jit(solution)/shard_map/ppermute | solution.py:25
  11.9 32.4 %collective-permute-start.3 = (bf16[768,256]{1,0:T(8,128)(2,1)}, bf16[768,256]{1,0:T(8,128)(2,1)}, u32[]{:S(2)}, u32[]{:S(2)}) collective-permute-start(bf16[768,256]{1,0:T(8,128)(2,1)} %get-tuple-element.44), channel_id=1, source_target_pairs={{0,1},{1,0},{2,3},{3,2},{4,5},{5,4},{6,7},{7,6},{8,9},{9,8},{10,11... | collective-permute-start | bytes 1179656 | tf_op jit(solution)/shard_map/ppermute | solution.py:25
  17.0 29.1 %collective-permute-start.4 = (bf16[768,256]{1,0:T(8,128)(2,1)}, bf16[768,256]{1,0:T(8,128)(2,1)S(1)}, u32[]{:S(2)}, u32[]{:S(2)}) collective-permute-start(bf16[768,256]{1,0:T(8,128)(2,1)} %get-tuple-element.45), channel_id=1, source_target_pairs={{0,2},{1,3},{2,0},{3,1},{4,6},{5,7},{6,4},{7,5},{8,10},{9,11},{10,... | collective-permute-start | bytes 1179656 | tf_op jit(solution)/shard_map/ppermute | solution.py:25
  19.0 27.2 %collective-permute-start.5 = (bf16[768,256]{1,0:T(8,128)(2,1)}, bf16[768,256]{1,0:T(8,128)(2,1)S(1)}, u32[]{:S(2)}, u32[]{:S(2)}) collective-permute-start(bf16[768,256]{1,0:T(8,128)(2,1)} %copy-done.14), channel_id=1, source_target_pairs={{0,3},{1,2},{2,1},{3,0},{4,7},{5,6},{6,5},{7,4},{8,11},{9,10},{10,... | collective-permute-start | bytes 1179656 | tf_op jit(solution)/shard_map/ppermute | solution.py:25
  20.9 5.9 %collective-permute-start.18 = (bf16[512,128]{1,0:T(8,128)(2,1)S(1)}, bf16[512,128]{1,0:T(8,128)(2,1)S(1)}, u32[]{:S(2)}, u32[]{:S(2)}) collective-permute-start(bf16[512,128]{1,0:T(8,128)(2,1)S(1)} %get-tuple-element.58.refs_4_), channel_id=1, source_target_pairs={{0,4},{4,0},{8,12},{12,8},{16,20},{20,16},{24,28},{28,24},{1,5},{5... | collective-permute-start | bytes 393224 | tf_op jit(solution)/shard_map/ppermute | solution.py:25
  22.5 8.2 %collective-permute-start.6 = (bf16[512,128]{1,0:T(8,128)(2,1)S(1)}, bf16[512,128]{1,0:T(8,128)(2,1)S(1)}, u32[]{:S(2)}, u32[]{:S(2)}) collective-permute-start(bf16[512,128]{1,0:T(8,128)(2,1)S(1)} %get-tuple-element.47.refs_4_), channel_id=1, source_target_pairs={{0,24},{4,28},{8,16},{12,20},{16,8},{20,12},{24,0},{28,4},{1,25},{... | collective-permute-start | bytes 393224 | tf_op jit(solution)/shard_map/ppermute | solution.py:25
  26.8 12.3 %collective-permute-start.19 = (bf16[1024,128]{1,0:T(8,128)(2,1)S(1)}, bf16[1024,128]{1,0:T(8,128)(2,1)S(1)}, u32[]{:S(2)}, u32[]{:S(2)}) collective-permute-start(bf16[1024,128]{1,0:T(8,128)(2,1)S(1)} %pad_maximum_fusion.2), channel_id=1, source_target_pairs={{0,24},{4,28},{8,16},{12,20},{16,8},{20,12},{24,0},{28,4},{1,25},{... | collective-permute-start | bytes 786440 | tf_op jit(solution)/shard_map/ppermute | solution.py:25
  30.7 12.8 %collective-permute-start.8 = (bf16[1024,128]{1,0:T(8,128)(2,1)S(1)}, bf16[1024,128]{1,0:T(8,128)(2,1)S(1)}, u32[]{:S(2)}, u32[]{:S(2)}) collective-permute-start(bf16[1024,128]{1,0:T(8,128)(2,1)S(1)} %constant_dynamic-update-slice_fusion), channel_id=1, source_target_pairs={{0,8},{4,12},{8,0},{12,4},{16,24},{20,28},{24,16},{28,20},{1,9},{5... | collective-permute-start | bytes 786440 | tf_op jit(solution)/shard_map/ppermute | solution.py:25
  39.2 8.6 %collective-permute-start.7 = (bf16[1024,128]{1,0:T(8,128)(2,1)S(1)}, bf16[1024,128]{1,0:T(8,128)(2,1)S(1)}, u32[]{:S(2)}, u32[]{:S(2)}) collective-permute-start(bf16[1024,128]{1,0:T(8,128)(2,1)S(1)} %constant_dynamic-update-slice_fusion), channel_id=1, source_target_pairs={{0,4},{4,0},{8,12},{12,8},{16,20},{20,16},{24,28},{28,24},{1,5},{5... | collective-permute-start | bytes 786440 | tf_op jit(solution)/shard_map/ppermute | solution.py:25
  43.5 11.4 %collective-permute-start.9 = (bf16[1024,128]{1,0:T(8,128)(2,1)S(1)}, bf16[1024,128]{1,0:T(8,128)(2,1)S(1)}, u32[]{:S(2)}, u32[]{:S(2)}) collective-permute-start(bf16[1024,128]{1,0:T(8,128)(2,1)S(1)} %collective-permute-done.8.refs_7_), channel_id=1, source_target_pairs={{0,4},{4,0},{8,12},{12,8},{16,20},{20,16},{24,28},{28,24},{1,5},{5... | collective-permute-start | bytes 786440 | tf_op jit(solution)/shard_map/ppermute | solution.py:25
  44.3 21.6 %collective-permute-start.20 = (bf16[2048,128]{1,0:T(8,128)(2,1)S(1)}, bf16[2048,128]{1,0:T(8,128)(2,1)S(1)}, u32[]{:S(2)}, u32[]{:S(2)}) collective-permute-start(bf16[2048,128]{1,0:T(8,128)(2,1)S(1)} %pad_maximum_fusion), channel_id=1, source_target_pairs={{0,8},{4,12},{8,0},{12,4},{16,24},{20,28},{24,16},{28,20},{1,9},{5... | collective-permute-start | bytes 1572872 | tf_op jit(solution)/shard_map/ppermute | solution.py:25
  46.1 18.0 %collective-permute-start.15 = (bf16[768,256]{1,0:T(8,128)(2,1)}, bf16[768,256]{1,0:T(8,128)(2,1)S(1)}, u32[]{:S(2)}, u32[]{:S(2)}) collective-permute-start(bf16[768,256]{1,0:T(8,128)(2,1)} %copy-done.12), channel_id=1, source_target_pairs={{0,1},{1,0},{2,3},{3,2},{4,5},{5,4},{6,7},{7,6},{8,9},{9,8},{10,11... | collective-permute-start | bytes 1179656 | tf_op jit(solution)/shard_map/ppermute | solution.py:25
  46.2 19.0 %collective-permute-start.16 = (bf16[768,256]{1,0:T(8,128)(2,1)}, bf16[768,256]{1,0:T(8,128)(2,1)S(1)}, u32[]{:S(2)}, u32[]{:S(2)}) collective-permute-start(bf16[768,256]{1,0:T(8,128)(2,1)} %copy-done.13), channel_id=1, source_target_pairs={{0,2},{1,3},{2,0},{3,1},{4,6},{5,7},{6,4},{7,5},{8,10},{9,11},{10,... | collective-permute-start | bytes 1179656 | tf_op jit(solution)/shard_map/ppermute | solution.py:25
  47.8 18.0 %collective-permute-start.17 = (bf16[768,256]{1,0:T(8,128)(2,1)}, bf16[768,256]{1,0:T(8,128)(2,1)S(1)}, u32[]{:S(2)}, u32[]{:S(2)}) collective-permute-start(bf16[768,256]{1,0:T(8,128)(2,1)} %copy-done.11), channel_id=1, source_target_pairs={{0,3},{1,2},{2,1},{3,0},{4,7},{5,6},{6,5},{7,4},{8,11},{9,10},{10,... | collective-permute-start | bytes 1179656 | tf_op jit(solution)/shard_map/ppermute | solution.py:25
  54.9 8.2 %collective-permute-start.12 = (bf16[512,128]{1,0:T(8,128)(2,1)S(1)}, bf16[512,128]{1,0:T(8,128)(2,1)S(1)}, u32[]{:S(2)}, u32[]{:S(2)}) collective-permute-start(bf16[512,128]{1,0:T(8,128)(2,1)S(1)} %get-tuple-element.51), channel_id=1, source_target_pairs={{0,24},{4,28},{8,16},{12,20},{16,8},{20,12},{24,0},{28,4},{1,25},{... | collective-permute-start | bytes 393224 | tf_op jit(solution)/shard_map/ppermute | solution.py:25
  63.1 13.7 %collective-permute-start.10 = (bf16[1024,128]{1,0:T(8,128)(2,1)S(1)}, bf16[1024,128]{1,0:T(8,128)(2,1)S(1)}, u32[]{:S(2)}, u32[]{:S(2)}) collective-permute-start(bf16[1024,128]{1,0:T(8,128)(2,1)S(1)} %shard_map.103), channel_id=1, source_target_pairs={{0,4},{4,0},{8,12},{12,8},{16,20},{20,16},{24,28},{28,24},{1,5},{5... | collective-permute-start | bytes 786440 | tf_op jit(solution)/shard_map/ppermute | solution.py:25
  64.1 30.9 %collective-permute-start.13 = (bf16[512,128]{1,0:T(8,128)(2,1)S(1)}, bf16[512,128]{1,0:T(8,128)(2,1)S(1)}, u32[]{:S(2)}, u32[]{:S(2)}) collective-permute-start(bf16[512,128]{1,0:T(8,128)(2,1)S(1)} %add_convert_fusion.5), channel_id=1, source_target_pairs={{0,4},{4,0},{8,12},{12,8},{16,20},{20,16},{24,28},{28,24},{1,5},{5... | collective-permute-start | bytes 393224 | tf_op jit(solution)/shard_map/ppermute | solution.py:25
  68.0 11.8 %collective-permute-start.21 = (bf16[1024,128]{1,0:T(8,128)(2,1)S(1)}, bf16[1024,128]{1,0:T(8,128)(2,1)S(1)}, u32[]{:S(2)}, u32[]{:S(2)}) collective-permute-start(bf16[1024,128]{1,0:T(8,128)(2,1)S(1)} %shard_map.106), channel_id=1, source_target_pairs={{0,4},{4,0},{8,12},{12,8},{16,20},{20,16},{24,28},{28,24},{1,5},{5... | collective-permute-start | bytes 786440 | tf_op jit(solution)/shard_map/ppermute | solution.py:25
  74.1 9.2 %collective-permute-start.23 = (bf16[512,128]{1,0:T(8,128)(2,1)S(1)}, bf16[512,128]{1,0:T(8,128)(2,1)S(1)}, u32[]{:S(2)}, u32[]{:S(2)}) collective-permute-start(bf16[512,128]{1,0:T(8,128)(2,1)S(1)} %get-tuple-element.62), channel_id=1, source_target_pairs={{0,24},{4,28},{8,16},{12,20},{16,8},{20,12},{24,0},{28,4},{1,25},{... | collective-permute-start | bytes 393224 | tf_op jit(solution)/shard_map/ppermute | solution.py:25
  76.9 10.7 %collective-permute-start.11 = (bf16[1024,128]{1,0:T(8,128)(2,1)S(1)}, bf16[1024,128]{1,0:T(8,128)(2,1)S(1)}, u32[]{:S(2)}, u32[]{:S(2)}) collective-permute-start(bf16[1024,128]{1,0:T(8,128)(2,1)S(1)} %pad_maximum_fusion.1), channel_id=1, source_target_pairs={{0,8},{4,12},{8,0},{12,4},{16,24},{20,28},{24,16},{28,20},{1,9},{5... | collective-permute-start | bytes 786440 | tf_op jit(solution)/shard_map/ppermute | solution.py:25
  79.9 13.7 %collective-permute-start.22 = (bf16[1024,128]{1,0:T(8,128)(2,1)S(1)}, bf16[1024,128]{1,0:T(8,128)(2,1)S(1)}, u32[]{:S(2)}, u32[]{:S(2)}) collective-permute-start(bf16[1024,128]{1,0:T(8,128)(2,1)S(1)} %pad_maximum_fusion.3), channel_id=1, source_target_pairs={{0,8},{4,12},{8,0},{12,4},{16,24},{20,28},{24,16},{28,20},{1,9},{5... | collective-permute-start | bytes 786440 | tf_op jit(solution)/shard_map/ppermute | solution.py:25
  83.3 14.6 %collective-permute-start.24 = (bf16[512,128]{1,0:T(8,128)(2,1)S(1)}, bf16[512,128]{1,0:T(8,128)(2,1)S(1)}, u32[]{:S(2)}, u32[]{:S(2)}) collective-permute-start(bf16[512,128]{1,0:T(8,128)(2,1)S(1)} %add_convert_fusion.1), channel_id=1, source_target_pairs={{0,4},{4,0},{8,12},{12,8},{16,20},{20,16},{24,28},{28,24},{1,5},{5... | collective-permute-start | bytes 393224 | tf_op jit(solution)/shard_map/ppermute | solution.py:25
  87.6 8.4 %collective-permute-start.14 = (bf16[512,128]{1,0:T(8,128)(2,1)S(1)}, bf16[512,128]{1,0:T(8,128)(2,1)S(1)}, u32[]{:S(2)}, u32[]{:S(2)}) collective-permute-start(bf16[512,128]{1,0:T(8,128)(2,1)S(1)} %add_convert_fusion.4), channel_id=1, source_target_pairs={{0,24},{4,28},{8,16},{12,20},{16,8},{20,12},{24,0},{28,4},{1,25},{... | collective-permute-start | bytes 393224 | tf_op jit(solution)/shard_map/ppermute | solution.py:25
  93.7 7.4 %collective-permute-start.25 = (bf16[512,128]{1,0:T(8,128)(2,1)S(1)}, bf16[512,128]{1,0:T(8,128)(2,1)S(1)}, u32[]{:S(2)}, u32[]{:S(2)}) collective-permute-start(bf16[512,128]{1,0:T(8,128)(2,1)S(1)} %add_convert_fusion), channel_id=1, source_target_pairs={{0,24},{4,28},{8,16},{12,20},{16,8},{20,12},{24,0},{28,4},{1,25},{... | collective-permute-start | bytes 393224 | tf_op jit(solution)/shard_map/ppermute | solution.py:25
  96.0 6.8 %collective-permute-start.26 = (bf16[128,128]{1,0:T(8,128)(2,1)S(1)}, bf16[128,128]{1,0:T(8,128)(2,1)S(1)}, u32[]{:S(2)}, u32[]{:S(2)}) collective-permute-start(bf16[128,128]{1,0:T(8,128)(2,1)S(1)} %get-tuple-element.65), channel_id=1, source_target_pairs={{0,1},{1,0},{2,3},{3,2},{4,5},{5,4},{6,7},{7,6},{8,9},{9,8},{10,11... | collective-permute-start | bytes 98312 | tf_op jit(solution)/shard_map/ppermute | solution.py:25
  96.1 8.3 %collective-permute-start.28 = (bf16[128,128]{1,0:T(8,128)(2,1)S(1)}, bf16[128,128]{1,0:T(8,128)(2,1)S(1)}, u32[]{:S(2)}, u32[]{:S(2)}) collective-permute-start(bf16[128,128]{1,0:T(8,128)(2,1)S(1)} %get-tuple-element.67), channel_id=1, source_target_pairs={{0,2},{1,3},{2,0},{3,1},{4,6},{5,7},{6,4},{7,5},{8,10},{9,11},{10,... | collective-permute-start | bytes 98312 | tf_op jit(solution)/shard_map/ppermute | solution.py:25
  97.7 6.8 %collective-permute-start.30 = (bf16[128,128]{1,0:T(8,128)(2,1)S(1)}, bf16[128,128]{1,0:T(8,128)(2,1)S(1)}, u32[]{:S(2)}, u32[]{:S(2)}) collective-permute-start(bf16[128,128]{1,0:T(8,128)(2,1)S(1)} %get-tuple-element.69), channel_id=1, source_target_pairs={{0,3},{1,2},{2,1},{3,0},{4,7},{5,6},{6,5},{7,4},{8,11},{9,10},{10,... | collective-permute-start | bytes 98312 | tf_op jit(solution)/shard_map/ppermute | solution.py:25
  101.2 3.3 %collective-permute-start.27 = (bf16[128,128]{1,0:T(8,128)(2,1)S(1)}, bf16[128,128]{1,0:T(8,128)(2,1)S(1)}, u32[]{:S(2)}, u32[]{:S(2)}) collective-permute-start(bf16[128,128]{1,0:T(8,128)(2,1)S(1)} %get-tuple-element.66), channel_id=1, source_target_pairs={{0,1},{1,0},{2,3},{3,2},{4,5},{5,4},{6,7},{7,6},{8,9},{9,8},{10,11... | collective-permute-start | bytes 98312 | tf_op jit(solution)/shard_map/ppermute | solution.py:25
  101.2 4.0 %collective-permute-start.29 = (bf16[128,128]{1,0:T(8,128)(2,1)S(1)}, bf16[128,128]{1,0:T(8,128)(2,1)S(1)}, u32[]{:S(2)}, u32[]{:S(2)}) collective-permute-start(bf16[128,128]{1,0:T(8,128)(2,1)S(1)} %get-tuple-element.68), channel_id=1, source_target_pairs={{0,2},{1,3},{2,0},{3,1},{4,6},{5,7},{6,4},{7,5},{8,10},{9,11},{10,... | collective-permute-start | bytes 98312 | tf_op jit(solution)/shard_map/ppermute | solution.py:25
  102.8 3.4 %collective-permute-start.31 = (bf16[128,128]{1,0:T(8,128)(2,1)S(1)}, bf16[128,128]{1,0:T(8,128)(2,1)S(1)}, u32[]{:S(2)}, u32[]{:S(2)}) collective-permute-start(bf16[128,128]{1,0:T(8,128)(2,1)S(1)} %get-tuple-element.70), channel_id=1, source_target_pairs={{0,3},{1,2},{2,1},{3,0},{4,7},{5,6},{6,5},{7,4},{8,11},{9,10},{10,... | collective-permute-start | bytes 98312 | tf_op jit(solution)/shard_map/ppermute | solution.py:25
  (17 other events, 215.0 us)

commit v8 on v7

--- a/solution.py
+++ b/solution.py
@@ -370,10 +370,17 @@
 
 
 def gather_plan(count, head):
-    return stages(count, head % 2 == 1)
-
-
-def scatter_plan(count):
+    plan = stages(count, head % 2 == 1)
+    if head % 2 == 1:
+        mask, codes = plan.pop()
+        cut = len(codes) // 2
+        plan += [(mask, half) for half in (codes[:cut], codes[cut:]) if half]
+    return plan
+
+
+def scatter_plan(count, head):
+    if head % 2 == 1:
+        return stages(count, False)
     outer = [mask for mask, codes in stages(count, True) if mask != 1]
     plan, main, side = [], [0], [1]
     for mask in outer[:-1]:
@@ -489,7 +496,7 @@
     parts = [[None] * each for _ in range(n_ctx)]
     for h in range(each):
         arrays, where = gather_queries(asked[h], gather_plan(n_req, h))
-        plan = scatter_plan(n_req)
+        plan = scatter_plan(n_req, h)
         groups = [[c ^ mask for c in codes] for mask, codes in plan] + [[0]]
         sums = {}
         for call in calls_of(n_req, h):
@@ -506,7 +513,7 @@
 
 
 def calls_of(count, head):
-    last = len(scatter_plan(count)) - 1
+    last = len(scatter_plan(count, head)) - 1
     rest = [i for i in range(last + 2) if i != last]
     return [rest, [last]] if head % 2 == 0 else [[last], rest]
 

time: 108 us -> 112 us (1.037)
  waiting for transfers between devices: 22.1 us -> 35.2 us
  starting transfers between devices: 49.6 us -> 39.6 us
    ppermute x32, waiting for transfers between devices: 22.1 us -> 35.2 us  [swap(): return lax.ppermute(value, axis, [(i, i ^ mask) for i in range(count)])]
    ppermute x32, starting transfers between devices: 49.6 us -> 39.6 us  [swap(): return lax.ppermute(value, axis, [(i, i ^ mask) for i in range(count)])]
    unnamed x35 -> x40, local copies, waits for them, and re-layouts: 7.01 us -> 7.88 us
  transfers between devices with their start and end apart: 32 -> 32, of which waited for: 11 -> 9; matrix products, arithmetic and copies ran while one was open for 1% -> 1% of each run, Pallas kernels for 21% -> 20%
where the time goes in v8:
time: 112 us; the launch traced here: 111 us
  starting transfers between devices  39.6 us (35%)
  waiting for transfers between devices  35.2 us (31%)
  Pallas kernels  27.7 us (25%)
  local copies, waits for them, and re-layouts  7.99 us (7%)
    ppermute x32, starting transfers between devices, swap(): return lax.ppermute(value, axis, [(i, i ^ mask) for i in range(count)])  39.6 us
    ppermute x32, waiting for transfers between devices, swap(): return lax.ppermute(value, axis, [(i, i ^ mask) for i in range(count)])  35.2 us
    pallas_call x4, Pallas kernels, attend(): pl.pallas_call(functools.partial(attend_kernel, source, sink, events, roo...  14.6 us
    unnamed x40, local copies, waits for them, and re-layouts  7.88 us
    pallas_call x2, Pallas kernels, project_keys_values(): pl.pallas_call(functools.partial(keys_values_kernel, count, each), grid_s...  5.72 us
    pallas_call x1, Pallas kernels, project_queries(): pl.pallas_call(query_kernel, in_specs=[pl.BlockSpec(memory_space=pltpu.SM...  3.59 us
  transfers between devices with their start and end apart: 32, of which 9 were waited for; matrix products, arithmetic and copies ran while one was open for 1% of the time, Pallas kernels for 20%

profile of v8, /device:TPU:0, one launch (start us, length us, event | category | flops | bytes accessed | tf_op | source)
XLA Modules:
  0.0 111.5 jit_solution(18390889357215629237)
XLA Ops:
  0.0 3.6 %queries.1 = (bf16[144,256]{1,0:T(8,128)(2,1)}, bf16[144,256]{1,0:T(8,128)(2,1)}, bf16[144,256]{1,0:T(8,128)(2,1)}, bf16[144,256]{1,0:T(8,128)(2,1)}) custom-call(s32[1]{0:T(128)} %bitcast._.me_ref, bf16[128,1024]{1,0:T(8,128)(2,1)} %cand_ref.3, bf16[1024,2048]{1,0:T(8,128)(2,1)} %w_hbm.1, s32[1,48]{1,0:T(1,128)} %bitcast.2), custom_call_target="tpu_custom_call" | custom-call | flops 268435456 | bytes 2621440 | tf_op jit(solution)/shard_map/queries/pallas_call | solution.py:95
  4.2 2.6 %collective-permute-start.1 = (bf16[144,256]{1,0:T(8,128)(2,1)}, bf16[144,256]{1,0:T(8,128)(2,1)}, u32[]{:S(2)}, u32[]{:S(2)}) collective-permute-start(bf16[144,256]{1,0:T(8,128)(2,1)} %get-tuple-element.39), channel_id=1, source_target_pairs={{0,2},{1,3},{2,0},{3,1},{4,6},{5,7},{6,4},{7,5},{8,10},{9,11},{10,... | collective-permute-start | bytes 221192 | tf_op jit(solution)/shard_map/ppermute | solution.py:25
  6.7 1.4 %copy-done.2 = bf16[768,1024]{1,0:T(8,128)(2,1)S(1)} copy-done((bf16[768,1024]{1,0:T(8,128)(2,1)S(1)}, bf16[768,1024]{1,0:T(8,128)(2,1)}, u32[]{:S(2)}) %copy-start.2) | copy-done | bytes 1572888
  8.2 3.0 %shard_map.100 = (bf16[768,256]{1,0:T(8,128)(2,1)S(1)}, bf16[768,256]{1,0:T(8,128)(2,1)S(1)}, bf16[768,256]{1,0:T(8,128)(2,1)S(1)}, bf16[768,256]{1,0:T(8,128)(2,1)}) custom-call(s32[1]{0:T(128)} %bitcast._.me_ref, bf16[768,1024]{1,0:T(8,128)(2,1)S(1)} %copy-done.2, bf16[1024,2048]{1,0:T(8,128)(2,1)S(1)} %copy-done, bf16[1024,2048]{1,0:T(8,128)(2,1)S(1)} %copy-done, ...), custom_call_target="tpu_custom_call" | custom-call | flops 1610612736 | bytes 5242880 | tf_op jit(solution)/shard_map/pallas_call | solution.py:186
  11.3 2.7 %shard_map.101 = (bf16[768,256]{1,0:T(8,128)(2,1)S(1)}, bf16[768,256]{1,0:T(8,128)(2,1)}, bf16[768,256]{1,0:T(8,128)(2,1)S(1)}, bf16[768,256]{1,0:T(8,128)(2,1)S(1)}) custom-call(s32[1]{0:T(128)} %bitcast._.me_ref, bf16[768,1024]{1,0:T(8,128)(2,1)S(1)} %copy-done.2, bf16[1024,2048]{1,0:T(8,128)(2,1)S(1)} %copy-done, bf16[1024,2048]{1,0:T(8,128)(2,1)S(1)} %copy-done, ...), custom_call_target="tpu_custom_call" | custom-call | flops 1610612736 | bytes 5242880 | tf_op jit(solution)/shard_map/pallas_call | solution.py:186
  16.3 2.0 %collective-permute-start.16 = (bf16[768,256]{1,0:T(8,128)(2,1)}, bf16[768,256]{1,0:T(8,128)(2,1)S(1)}, u32[]{:S(2)}, u32[]{:S(2)}) collective-permute-start(bf16[768,256]{1,0:T(8,128)(2,1)} %get-tuple-element.55), channel_id=1, source_target_pairs={{0,2},{1,3},{2,0},{3,1},{4,6},{5,7},{6,4},{7,5},{8,10},{9,11},{10,... | collective-permute-start | bytes 1179656 | tf_op jit(solution)/shard_map/ppermute | solution.py:25
  19.2 1.0 assemble.1
  20.2 1.6 %collective-permute-start.18 = (bf16[512,128]{1,0:T(8,128)(2,1)S(1)}, bf16[512,128]{1,0:T(8,128)(2,1)S(1)}, u32[]{:S(2)}, u32[]{:S(2)}) collective-permute-start(bf16[512,128]{1,0:T(8,128)(2,1)S(1)} %get-tuple-element.57.refs_4_), channel_id=1, source_target_pairs={{0,4},{4,0},{8,12},{12,8},{16,20},{20,16},{24,28},{28,24},{1,5},{5... | collective-permute-start | bytes 393224 | tf_op jit(solution)/shard_map/ppermute | solution.py:25
  21.8 3.7 %collective-permute-start.6 = (bf16[512,128]{1,0:T(8,128)(2,1)S(1)}, bf16[512,128]{1,0:T(8,128)(2,1)S(1)}, u32[]{:S(2)}, u32[]{:S(2)}) collective-permute-start(bf16[512,128]{1,0:T(8,128)(2,1)S(1)} %get-tuple-element.46.refs_4_), channel_id=1, source_target_pairs={{0,24},{4,28},{8,16},{12,20},{16,8},{20,12},{24,0},{28,4},{1,25},{... | collective-permute-start | bytes 393224 | tf_op jit(solution)/shard_map/ppermute | solution.py:25
  26.1 3.9 %collective-permute-start.19 = (bf16[1024,128]{1,0:T(8,128)(2,1)S(1)}, bf16[1024,128]{1,0:T(8,128)(2,1)S(1)}, u32[]{:S(2)}, u32[]{:S(2)}) collective-permute-start(bf16[1024,128]{1,0:T(8,128)(2,1)S(1)} %constant_dynamic-update-slice_fusion.2), channel_id=1, source_target_pairs={{0,24},{4,28},{8,16},{12,20},{16,8},{20,12},{24,0},{28,4},{1,25},{... | collective-permute-start | bytes 786440 | tf_op jit(solution)/shard_map/ppermute | solution.py:25
  30.0 8.2 %collective-permute-start.20 = (bf16[1024,128]{1,0:T(8,128)(2,1)S(1)}, bf16[1024,128]{1,0:T(8,128)(2,1)S(1)}, u32[]{:S(2)}, u32[]{:S(2)}) collective-permute-start(bf16[1024,128]{1,0:T(8,128)(2,1)S(1)} %constant_dynamic-update-slice_fusion.2), channel_id=1, source_target_pairs={{0,8},{4,12},{8,0},{12,4},{16,24},{20,28},{24,16},{28,20},{1,9},{5... | collective-permute-start | bytes 786440 | tf_op jit(solution)/shard_map/ppermute | solution.py:25
  38.4 1.5 %collective-permute-start.4 = (bf16[768,256]{1,0:T(8,128)(2,1)}, bf16[768,256]{1,0:T(8,128)(2,1)S(1)}, u32[]{:S(2)}, u32[]{:S(2)}) collective-permute-start(bf16[768,256]{1,0:T(8,128)(2,1)} %copy-done.16), channel_id=1, source_target_pairs={{0,2},{1,3},{2,0},{3,1},{4,6},{5,7},{6,4},{7,5},{8,10},{9,11},{10,... | collective-permute-start | bytes 1179656 | tf_op jit(solution)/shard_map/ppermute | solution.py:25
  40.5 4.9 %collective-permute-done.20.refs_7_.refs_4_ = bf16[1024,128]{1,0:T(8,128)(2,1)S(1)} collective-permute-done((bf16[1024,128]{1,0:T(8,128)(2,1)S(1)}, bf16[1024,128]{1,0:T(8,128)(2,1)S(1)}, u32[]{:S(2)}, u32[]{:S(2)}) %collective-permute-start.20) | collective-permute-done | bytes 262176 | tf_op jit(solution)/shard_map/ppermute | solution.py:25
  45.4 2.0 %collective-permute-start.21 = (bf16[1024,128]{1,0:T(8,128)(2,1)S(1)}, bf16[1024,128]{1,0:T(8,128)(2,1)S(1)}, u32[]{:S(2)}, u32[]{:S(2)}) collective-permute-start(bf16[1024,128]{1,0:T(8,128)(2,1)S(1)} %collective-permute-done.19.refs_6_), channel_id=1, source_target_pairs={{0,8},{4,12},{8,0},{12,4},{16,24},{20,28},{24,16},{28,20},{1,9},{5... | collective-permute-start | bytes 786440 | tf_op jit(solution)/shard_map/ppermute | solution.py:25
  47.5 3.4 %collective-permute-done.8.refs_7_ = bf16[1024,128]{1,0:T(8,128)(2,1)S(1)} collective-permute-done((bf16[1024,128]{1,0:T(8,128)(2,1)S(1)}, bf16[1024,128]{1,0:T(8,128)(2,1)S(1)}, u32[]{:S(2)}, u32[]{:S(2)}) %collective-permute-start.8) | collective-permute-done | bytes 262176 | tf_op jit(solution)/shard_map/ppermute | solution.py:25
  50.9 3.1 %collective-permute-done.21.refs_8_.refs_5_ = bf16[1024,128]{1,0:T(8,128)(2,1)S(1)} collective-permute-done((bf16[1024,128]{1,0:T(8,128)(2,1)S(1)}, bf16[1024,128]{1,0:T(8,128)(2,1)S(1)}, u32[]{:S(2)}, u32[]{:S(2)}) %collective-permute-start.21) | collective-permute-done | bytes 262176 | tf_op jit(solution)/shard_map/ppermute | solution.py:25
  54.7 1.0 copy-done.9
  56.3 2.6 %shard_map.106 = bf16[1024,128]{1,0:T(8,128)(2,1)S(1)} custom-call(s32[192]{0:T(256)S(1)} %multiply_add_fusion.pos_ref, s32[8]{0:T(128)S(1)} %convert_reduce_fusion.1.count_ref, s32[2]{0:T(128)S(1)} %copy-done.12, bf16[768,256]{1,0:T(8,128)(2,1)S(1)} %copy-done.9, bf16[768,256]{1,0:T(8,128)(2,1)} %collective-permute-done.15.refs_1_, ...), custom_call_target="tpu_custom_call" | custom-call | flops 402653184 | bytes 2097152 | tf_op jit(solution)/shard_map/pallas_call | solution.py:280
  59.0 1.3 %collective-permute-start.22 = (bf16[1024,128]{1,0:T(8,128)(2,1)S(1)}, bf16[1024,128]{1,0:T(8,128)(2,1)S(1)}, u32[]{:S(2)}, u32[]{:S(2)}) collective-permute-start(bf16[1024,128]{1,0:T(8,128)(2,1)S(1)} %shard_map.106), channel_id=1, source_target_pairs={{0,4},{4,0},{8,12},{12,8},{16,20},{20,16},{24,28},{28,24},{1,5},{5... | collective-permute-start | bytes 786440 | tf_op jit(solution)/shard_map/ppermute | solution.py:25
  61.9 4.7 %shard_map.102 = (bf16[512,128]{1,0:T(8,128)(2,1)S(1)}, bf16[512,128]{1,0:T(8,128)(2,1)S(1)}, bf16[512,128]{1,0:T(8,128)(2,1)S(1)}, bf16[1024,128]{1,0:T(8,128)(2,1)S(1)}, bf16[512,128]{1,0:T(8,128)(2,1)S(1)}) custom-call(s32[192]{0:T(256)S(1)} %multiply_add_fusion.pos_ref, s32[8]{0:T(128)S(1)} %convert_reduce_fusion.1.count_ref, s32[6]{0:T(128)S(1)} %copy-done.18, ...), custom_call_target="tpu_custom_call" | custom-call | flops 1207959552 | bytes 3145728 | tf_op jit(solution)/shard_map/pallas_call | solution.py:280
  66.6 2.9 %collective-permute-start.12 = (bf16[512,128]{1,0:T(8,128)(2,1)S(1)}, bf16[512,128]{1,0:T(8,128)(2,1)S(1)}, u32[]{:S(2)}, u32[]{:S(2)}) collective-permute-start(bf16[512,128]{1,0:T(8,128)(2,1)S(1)} %get-tuple-element.50), channel_id=1, source_target_pairs={{0,24},{4,28},{8,16},{12,20},{16,8},{20,12},{24,0},{28,4},{1,25},{... | collective-permute-start | bytes 393224 | tf_op jit(solution)/shard_map/ppermute | solution.py:25
  69.5 5.1 %shard_map.105 = (bf16[512,128]{1,0:T(8,128)(2,1)S(1)}, bf16[1024,128]{1,0:T(8,128)(2,1)S(1)}, bf16[1024,128]{1,0:T(8,128)(2,1)S(1)}, bf16[512,128]{1,0:T(8,128)(2,1)S(1)}) custom-call(s32[192]{0:T(256)S(1)} %multiply_add_fusion.pos_ref, s32[8]{0:T(128)S(1)} %convert_reduce_fusion.1.count_ref, s32[6]{0:T(128)S(1)} %copy-done.18, ...), custom_call_target="tpu_custom_call" | custom-call | flops 1207959552 | bytes 3145728 | tf_op jit(solution)/shard_map/pallas_call | solution.py:280
  74.7 1.5 %collective-permute-start.24 = (bf16[1024,128]{1,0:T(8,128)(2,1)S(1)}, bf16[1024,128]{1,0:T(8,128)(2,1)S(1)}, u32[]{:S(2)}, u32[]{:S(2)}) collective-permute-start(bf16[1024,128]{1,0:T(8,128)(2,1)S(1)} %get-tuple-element.60), channel_id=1, source_target_pairs={{0,4},{4,0},{8,12},{12,8},{16,20},{20,16},{24,28},{28,24},{1,5},{5... | collective-permute-start | bytes 786440 | tf_op jit(solution)/shard_map/ppermute | solution.py:25
  76.2 2.2 %shard_map.103 = bf16[1024,128]{1,0:T(8,128)(2,1)S(1)} custom-call(s32[192]{0:T(256)S(1)} %multiply_add_fusion.pos_ref, s32[8]{0:T(128)S(1)} %convert_reduce_fusion.1.count_ref, s32[2]{0:T(128)S(1)} %copy-done.13, bf16[768,256]{1,0:T(8,128)(2,1)S(1)} %copy-done.7, bf16[768,256]{1,0:T(8,128)(2,1)S(1)} %collective-permute-done.3.refs_1_, ...), custom_call_target="tpu_custom_call" | custom-call | flops 402653184 | bytes 2097152 | tf_op jit(solution)/shard_map/pallas_call | solution.py:280
  79.1 8.4 %collective-permute-done.10 = bf16[1024,128]{1,0:T(8,128)(2,1)S(1)} collective-permute-done((bf16[1024,128]{1,0:T(8,128)(2,1)S(1)}, bf16[1024,128]{1,0:T(8,128)(2,1)S(1)}, u32[]{:S(2)}, u32[]{:S(2)}) %collective-permute-start.10) | collective-permute-done | bytes 262176 | tf_op jit(solution)/shard_map/ppermute | solution.py:25
  87.7 1.8 %collective-permute-start.13 = (bf16[512,128]{1,0:T(8,128)(2,1)S(1)}, bf16[512,128]{1,0:T(8,128)(2,1)S(1)}, u32[]{:S(2)}, u32[]{:S(2)}) collective-permute-start(bf16[512,128]{1,0:T(8,128)(2,1)S(1)} %add_convert_fusion.4), channel_id=1, source_target_pairs={{0,4},{4,0},{8,12},{12,8},{16,20},{20,16},{24,28},{28,24},{1,5},{5... | collective-permute-start | bytes 393224 | tf_op jit(solution)/shard_map/ppermute | solution.py:25
  89.9 8.3 %collective-permute-done.11.refs_1_ = bf16[1024,128]{1,0:T(8,128)(2,1)S(1)} collective-permute-done((bf16[1024,128]{1,0:T(8,128)(2,1)S(1)}, bf16[1024,128]{1,0:T(8,128)(2,1)S(1)}, u32[]{:S(2)}, u32[]{:S(2)}) %collective-permute-start.11) | collective-permute-done | bytes 262176 | tf_op jit(solution)/shard_map/ppermute | solution.py:25
  98.5 1.5 %collective-permute-start.29 = (bf16[128,128]{1,0:T(8,128)(2,1)S(1)}, bf16[128,128]{1,0:T(8,128)(2,1)S(1)}, u32[]{:S(2)}, u32[]{:S(2)}) collective-permute-start(bf16[128,128]{1,0:T(8,128)(2,1)S(1)} %get-tuple-element.66), channel_id=1, source_target_pairs={{0,2},{1,3},{2,0},{3,1},{4,6},{5,7},{6,4},{7,5},{8,10},{9,11},{10,... | collective-permute-start | bytes 98312 | tf_op jit(solution)/shard_map/ppermute | solution.py:25
  100.3 4.7 %collective-permute-done.14.refs_3_ = bf16[512,128]{1,0:T(8,128)(2,1)S(1)} collective-permute-done((bf16[512,128]{1,0:T(8,128)(2,1)S(1)}, bf16[512,128]{1,0:T(8,128)(2,1)S(1)}, u32[]{:S(2)}, u32[]{:S(2)}) %collective-permute-start.14) | collective-permute-done | bytes 131104 | tf_op jit(solution)/shard_map/ppermute | solution.py:25
  105.2 1.5 %collective-permute-start.28 = (bf16[128,128]{1,0:T(8,128)(2,1)S(1)}, bf16[128,128]{1,0:T(8,128)(2,1)S(1)}, u32[]{:S(2)}, u32[]{:S(2)}) collective-permute-start(bf16[128,128]{1,0:T(8,128)(2,1)S(1)} %get-tuple-element.65), channel_id=1, source_target_pairs={{0,2},{1,3},{2,0},{3,1},{4,6},{5,7},{6,4},{7,5},{8,10},{9,11},{10,... | collective-permute-start | bytes 98312 | tf_op jit(solution)/shard_map/ppermute | solution.py:25
  107.1 1.3 %gate.1.gate_ref = f32[4,128,256]{2,1,0:T(8,128)S(1)} custom-call(s32[1]{0:T(128)} %bitcast._.me_ref, bf16[128,1024]{1,0:T(8,128)(2,1)S(1)} %copy-done.3, bf16[1024,2048]{1,0:T(8,128)(2,1)S(1)} %copy-done.1), custom_call_target="tpu_custom_call" | custom-call | flops 268435456 | bytes 2883584 | tf_op jit(solution)/shard_map/gate/pallas_call | solution.py:146
  110.1 1.3 %finish.1 = bf16[128,1024]{1,0:T(8,128)(2,1)} custom-call(s32[1]{0:T(128)} %bitcast._.me_ref, bf16[128,1024]{1,0:T(8,128)(2,1)S(1)} %copy-done.3, f32[4,128,256]{2,1,0:T(8,128)S(1)} %gate.1.gate_ref, bf16[1024,1024]{1,0:T(8,128)(2,1)S(1)} %copy-done.4, f32[128,128]{1,0:T(8,128)S(1)} %get-tuple-element.52.refs_0_, f32[128,128]{1,0:T(8,128)S(1)} %get-tuple-element.62.refs_1_, ...), custom_call_target="tpu_custom_call" | custom-call | flops 268435456 | bytes 3407872 | tf_op jit(solution)/shard_map/finish/pallas_call | solution.py:327
  (98 shorter events, 12.3 us)
Async XLA Ops:
  3.6 14.7 %collective-permute-start = (bf16[144,256]{1,0:T(8,128)(2,1)}, bf16[144,256]{1,0:T(8,128)(2,1)}, u32[]{:S(2)}, u32[]{:S(2)}) collective-permute-start(bf16[144,256]{1,0:T(8,128)(2,1)} %get-tuple-element.38), channel_id=1, source_target_pairs={{0,1},{1,0},{2,3},{3,2},{4,5},{5,4},{6,7},{7,6},{8,9},{9,8},{10,11... | collective-permute-start | bytes 221192 | tf_op jit(solution)/shard_map/ppermute | solution.py:25
  4.2 14.1 %collective-permute-start.1 = (bf16[144,256]{1,0:T(8,128)(2,1)}, bf16[144,256]{1,0:T(8,128)(2,1)}, u32[]{:S(2)}, u32[]{:S(2)}) collective-permute-start(bf16[144,256]{1,0:T(8,128)(2,1)} %get-tuple-element.39), channel_id=1, source_target_pairs={{0,2},{1,3},{2,0},{3,1},{4,6},{5,7},{6,4},{7,5},{8,10},{9,11},{10,... | collective-permute-start | bytes 221192 | tf_op jit(solution)/shard_map/ppermute | solution.py:25
  6.7 11.6 %collective-permute-start.2 = (bf16[144,256]{1,0:T(8,128)(2,1)}, bf16[144,256]{1,0:T(8,128)(2,1)}, u32[]{:S(2)}, u32[]{:S(2)}) collective-permute-start(bf16[144,256]{1,0:T(8,128)(2,1)} %get-tuple-element.40), channel_id=1, source_target_pairs={{0,3},{1,2},{2,1},{3,0},{4,7},{5,6},{6,5},{7,4},{8,11},{9,10},{10,... | collective-permute-start | bytes 221192 | tf_op jit(solution)/shard_map/ppermute | solution.py:25
  11.1 27.1 %collective-permute-start.15 = (bf16[768,256]{1,0:T(8,128)(2,1)}, bf16[768,256]{1,0:T(8,128)(2,1)}, u32[]{:S(2)}, u32[]{:S(2)}) collective-permute-start(bf16[768,256]{1,0:T(8,128)(2,1)} %get-tuple-element.54), channel_id=1, source_target_pairs={{0,1},{1,0},{2,3},{3,2},{4,5},{5,4},{6,7},{7,6},{8,9},{9,8},{10,11... | collective-permute-start | bytes 1179656 | tf_op jit(solution)/shard_map/ppermute | solution.py:25
  16.3 22.1 %collective-permute-start.16 = (bf16[768,256]{1,0:T(8,128)(2,1)}, bf16[768,256]{1,0:T(8,128)(2,1)S(1)}, u32[]{:S(2)}, u32[]{:S(2)}) collective-permute-start(bf16[768,256]{1,0:T(8,128)(2,1)} %get-tuple-element.55), channel_id=1, source_target_pairs={{0,2},{1,3},{2,0},{3,1},{4,6},{5,7},{6,4},{7,5},{8,10},{9,11},{10,... | collective-permute-start | bytes 1179656 | tf_op jit(solution)/shard_map/ppermute | solution.py:25
  18.3 20.2 %collective-permute-start.17 = (bf16[768,256]{1,0:T(8,128)(2,1)}, bf16[768,256]{1,0:T(8,128)(2,1)S(1)}, u32[]{:S(2)}, u32[]{:S(2)}) collective-permute-start(bf16[768,256]{1,0:T(8,128)(2,1)} %copy-done.17), channel_id=1, source_target_pairs={{0,3},{1,2},{2,1},{3,0},{4,7},{5,6},{6,5},{7,4},{8,11},{9,10},{10,... | collective-permute-start | bytes 1179656 | tf_op jit(solution)/shard_map/ppermute | solution.py:25
  20.2 5.9 %collective-permute-start.18 = (bf16[512,128]{1,0:T(8,128)(2,1)S(1)}, bf16[512,128]{1,0:T(8,128)(2,1)S(1)}, u32[]{:S(2)}, u32[]{:S(2)}) collective-permute-start(bf16[512,128]{1,0:T(8,128)(2,1)S(1)} %get-tuple-element.57.refs_4_), channel_id=1, source_target_pairs={{0,4},{4,0},{8,12},{12,8},{16,20},{20,16},{24,28},{28,24},{1,5},{5... | collective-permute-start | bytes 393224 | tf_op jit(solution)/shard_map/ppermute | solution.py:25
  21.8 8.2 %collective-permute-start.6 = (bf16[512,128]{1,0:T(8,128)(2,1)S(1)}, bf16[512,128]{1,0:T(8,128)(2,1)S(1)}, u32[]{:S(2)}, u32[]{:S(2)}) collective-permute-start(bf16[512,128]{1,0:T(8,128)(2,1)S(1)} %get-tuple-element.46.refs_4_), channel_id=1, source_target_pairs={{0,24},{4,28},{8,16},{12,20},{16,8},{20,12},{24,0},{28,4},{1,25},{... | collective-permute-start | bytes 393224 | tf_op jit(solution)/shard_map/ppermute | solution.py:25
  26.1 13.9 %collective-permute-start.19 = (bf16[1024,128]{1,0:T(8,128)(2,1)S(1)}, bf16[1024,128]{1,0:T(8,128)(2,1)S(1)}, u32[]{:S(2)}, u32[]{:S(2)}) collective-permute-start(bf16[1024,128]{1,0:T(8,128)(2,1)S(1)} %constant_dynamic-update-slice_fusion.2), channel_id=1, source_target_pairs={{0,24},{4,28},{8,16},{12,20},{16,8},{20,12},{24,0},{28,4},{1,25},{... | collective-permute-start | bytes 786440 | tf_op jit(solution)/shard_map/ppermute | solution.py:25
  30.0 15.4 %collective-permute-start.20 = (bf16[1024,128]{1,0:T(8,128)(2,1)S(1)}, bf16[1024,128]{1,0:T(8,128)(2,1)S(1)}, u32[]{:S(2)}, u32[]{:S(2)}) collective-permute-start(bf16[1024,128]{1,0:T(8,128)(2,1)S(1)} %constant_dynamic-update-slice_fusion.2), channel_id=1, source_target_pairs={{0,8},{4,12},{8,0},{12,4},{16,24},{20,28},{24,16},{28,20},{1,9},{5... | collective-permute-start | bytes 786440 | tf_op jit(solution)/shard_map/ppermute | solution.py:25
  38.2 12.6 %collective-permute-start.8 = (bf16[1024,128]{1,0:T(8,128)(2,1)S(1)}, bf16[1024,128]{1,0:T(8,128)(2,1)S(1)}, u32[]{:S(2)}, u32[]{:S(2)}) collective-permute-start(bf16[1024,128]{1,0:T(8,128)(2,1)S(1)} %constant_dynamic-update-slice_fusion), channel_id=1, source_target_pairs={{0,8},{4,12},{8,0},{12,4},{16,24},{20,28},{24,16},{28,20},{1,9},{5... | collective-permute-start | bytes 786440 | tf_op jit(solution)/shard_map/ppermute | solution.py:25
  38.4 20.5 %collective-permute-start.3 = (bf16[768,256]{1,0:T(8,128)(2,1)}, bf16[768,256]{1,0:T(8,128)(2,1)S(1)}, u32[]{:S(2)}, u32[]{:S(2)}) collective-permute-start(bf16[768,256]{1,0:T(8,128)(2,1)} %copy-done.14), channel_id=1, source_target_pairs={{0,1},{1,0},{2,3},{3,2},{4,5},{5,4},{6,7},{7,6},{8,9},{9,8},{10,11... | collective-permute-start | bytes 1179656 | tf_op jit(solution)/shard_map/ppermute | solution.py:25
  38.4 21.8 %collective-permute-start.4 = (bf16[768,256]{1,0:T(8,128)(2,1)}, bf16[768,256]{1,0:T(8,128)(2,1)S(1)}, u32[]{:S(2)}, u32[]{:S(2)}) collective-permute-start(bf16[768,256]{1,0:T(8,128)(2,1)} %copy-done.16), channel_id=1, source_target_pairs={{0,2},{1,3},{2,0},{3,1},{4,6},{5,7},{6,4},{7,5},{8,10},{9,11},{10,... | collective-permute-start | bytes 1179656 | tf_op jit(solution)/shard_map/ppermute | solution.py:25
  40.0 20.3 %collective-permute-start.5 = (bf16[768,256]{1,0:T(8,128)(2,1)}, bf16[768,256]{1,0:T(8,128)(2,1)S(1)}, u32[]{:S(2)}, u32[]{:S(2)}) collective-permute-start(bf16[768,256]{1,0:T(8,128)(2,1)} %copy-done.15), channel_id=1, source_target_pairs={{0,3},{1,2},{2,1},{3,0},{4,7},{5,6},{6,5},{7,4},{8,11},{9,10},{10,... | collective-permute-start | bytes 1179656 | tf_op jit(solution)/shard_map/ppermute | solution.py:25
  45.4 8.7 %collective-permute-start.21 = (bf16[1024,128]{1,0:T(8,128)(2,1)S(1)}, bf16[1024,128]{1,0:T(8,128)(2,1)S(1)}, u32[]{:S(2)}, u32[]{:S(2)}) collective-permute-start(bf16[1024,128]{1,0:T(8,128)(2,1)S(1)} %collective-permute-done.19.refs_6_), channel_id=1, source_target_pairs={{0,8},{4,12},{8,0},{12,4},{16,24},{20,28},{24,16},{28,20},{1,9},{5... | collective-permute-start | bytes 786440 | tf_op jit(solution)/shard_map/ppermute | solution.py:25
  50.9 9.4 %collective-permute-start.7 = (bf16[1024,128]{1,0:T(8,128)(2,1)S(1)}, bf16[1024,128]{1,0:T(8,128)(2,1)S(1)}, u32[]{:S(2)}, u32[]{:S(2)}) collective-permute-start(bf16[1024,128]{1,0:T(8,128)(2,1)S(1)} %constant_dynamic-update-slice_fusion), channel_id=1, source_target_pairs={{0,4},{4,0},{8,12},{12,8},{16,20},{20,16},{24,28},{28,24},{1,5},{5... | collective-permute-start | bytes 786440 | tf_op jit(solution)/shard_map/ppermute | solution.py:25
  54.0 22.1 %collective-permute-start.9 = (bf16[1024,128]{1,0:T(8,128)(2,1)S(1)}, bf16[1024,128]{1,0:T(8,128)(2,1)S(1)}, u32[]{:S(2)}, u32[]{:S(2)}) collective-permute-start(bf16[1024,128]{1,0:T(8,128)(2,1)S(1)} %collective-permute-done.8.refs_7_), channel_id=1, source_target_pairs={{0,4},{4,0},{8,12},{12,8},{16,20},{20,16},{24,28},{28,24},{1,5},{5... | collective-permute-start | bytes 786440 | tf_op jit(solution)/shard_map/ppermute | solution.py:25
  59.0 19.9 %collective-permute-start.22 = (bf16[1024,128]{1,0:T(8,128)(2,1)S(1)}, bf16[1024,128]{1,0:T(8,128)(2,1)S(1)}, u32[]{:S(2)}, u32[]{:S(2)}) collective-permute-start(bf16[1024,128]{1,0:T(8,128)(2,1)S(1)} %shard_map.106), channel_id=1, source_target_pairs={{0,4},{4,0},{8,12},{12,8},{16,20},{20,16},{24,28},{28,24},{1,5},{5... | collective-permute-start | bytes 786440 | tf_op jit(solution)/shard_map/ppermute | solution.py:25
  66.6 21.0 %collective-permute-start.12 = (bf16[512,128]{1,0:T(8,128)(2,1)S(1)}, bf16[512,128]{1,0:T(8,128)(2,1)S(1)}, u32[]{:S(2)}, u32[]{:S(2)}) collective-permute-start(bf16[512,128]{1,0:T(8,128)(2,1)S(1)} %get-tuple-element.50), channel_id=1, source_target_pairs={{0,24},{4,28},{8,16},{12,20},{16,8},{20,12},{24,0},{28,4},{1,25},{... | collective-permute-start | bytes 393224 | tf_op jit(solution)/shard_map/ppermute | solution.py:25
  74.7 14.8 %collective-permute-start.24 = (bf16[1024,128]{1,0:T(8,128)(2,1)S(1)}, bf16[1024,128]{1,0:T(8,128)(2,1)S(1)}, u32[]{:S(2)}, u32[]{:S(2)}) collective-permute-start(bf16[1024,128]{1,0:T(8,128)(2,1)S(1)} %get-tuple-element.60), channel_id=1, source_target_pairs={{0,4},{4,0},{8,12},{12,8},{16,20},{20,16},{24,28},{28,24},{1,5},{5... | collective-permute-start | bytes 786440 | tf_op jit(solution)/shard_map/ppermute | solution.py:25
  78.3 9.1 %collective-permute-start.10 = (bf16[1024,128]{1,0:T(8,128)(2,1)S(1)}, bf16[1024,128]{1,0:T(8,128)(2,1)S(1)}, u32[]{:S(2)}, u32[]{:S(2)}) collective-permute-start(bf16[1024,128]{1,0:T(8,128)(2,1)S(1)} %shard_map.103), channel_id=1, source_target_pairs={{0,4},{4,0},{8,12},{12,8},{16,20},{20,16},{24,28},{28,24},{1,5},{5... | collective-permute-start | bytes 786440 | tf_op jit(solution)/shard_map/ppermute | solution.py:25
  79.0 10.5 %collective-permute-start.23 = (bf16[1024,128]{1,0:T(8,128)(2,1)S(1)}, bf16[1024,128]{1,0:T(8,128)(2,1)S(1)}, u32[]{:S(2)}, u32[]{:S(2)}) collective-permute-start(bf16[1024,128]{1,0:T(8,128)(2,1)S(1)} %pad_maximum_fusion.1), channel_id=1, source_target_pairs={{0,8},{4,12},{8,0},{12,4},{16,24},{20,28},{24,16},{28,20},{1,9},{5... | collective-permute-start | bytes 786440 | tf_op jit(solution)/shard_map/ppermute | solution.py:25
  87.5 10.7 %collective-permute-start.11 = (bf16[1024,128]{1,0:T(8,128)(2,1)S(1)}, bf16[1024,128]{1,0:T(8,128)(2,1)S(1)}, u32[]{:S(2)}, u32[]{:S(2)}) collective-permute-start(bf16[1024,128]{1,0:T(8,128)(2,1)S(1)} %pad_maximum_fusion), channel_id=1, source_target_pairs={{0,8},{4,12},{8,0},{12,4},{16,24},{20,28},{24,16},{28,20},{1,9},{5... | collective-permute-start | bytes 786440 | tf_op jit(solution)/shard_map/ppermute | solution.py:25
  87.7 12.7 %collective-permute-start.13 = (bf16[512,128]{1,0:T(8,128)(2,1)S(1)}, bf16[512,128]{1,0:T(8,128)(2,1)S(1)}, u32[]{:S(2)}, u32[]{:S(2)}) collective-permute-start(bf16[512,128]{1,0:T(8,128)(2,1)S(1)} %add_convert_fusion.4), channel_id=1, source_target_pairs={{0,4},{4,0},{8,12},{12,8},{16,20},{20,16},{24,28},{28,24},{1,5},{5... | collective-permute-start | bytes 393224 | tf_op jit(solution)/shard_map/ppermute | solution.py:25
  89.5 8.8 %collective-permute-start.25 = (bf16[512,128]{1,0:T(8,128)(2,1)S(1)}, bf16[512,128]{1,0:T(8,128)(2,1)S(1)}, u32[]{:S(2)}, u32[]{:S(2)}) collective-permute-start(bf16[512,128]{1,0:T(8,128)(2,1)S(1)} %add_convert_fusion), channel_id=1, source_target_pairs={{0,24},{4,28},{8,16},{12,20},{16,8},{20,12},{24,0},{28,4},{1,25},{... | collective-permute-start | bytes 393224 | tf_op jit(solution)/shard_map/ppermute | solution.py:25
  98.2 6.8 %collective-permute-start.14 = (bf16[512,128]{1,0:T(8,128)(2,1)S(1)}, bf16[512,128]{1,0:T(8,128)(2,1)S(1)}, u32[]{:S(2)}, u32[]{:S(2)}) collective-permute-start(bf16[512,128]{1,0:T(8,128)(2,1)S(1)} %add_convert_fusion.3), channel_id=1, source_target_pairs={{0,24},{4,28},{8,16},{12,20},{16,8},{20,12},{24,0},{28,4},{1,25},{... | collective-permute-start | bytes 393224 | tf_op jit(solution)/shard_map/ppermute | solution.py:25
  98.4 8.4 %collective-permute-start.27 = (bf16[128,128]{1,0:T(8,128)(2,1)S(1)}, bf16[128,128]{1,0:T(8,128)(2,1)S(1)}, u32[]{:S(2)}, u32[]{:S(2)}) collective-permute-start(bf16[128,128]{1,0:T(8,128)(2,1)S(1)} %get-tuple-element.64), channel_id=1, source_target_pairs={{0,1},{1,0},{2,3},{3,2},{4,5},{5,4},{6,7},{7,6},{8,9},{9,8},{10,11... | collective-permute-start | bytes 98312 | tf_op jit(solution)/shard_map/ppermute | solution.py:25
  98.5 9.9 %collective-permute-start.29 = (bf16[128,128]{1,0:T(8,128)(2,1)S(1)}, bf16[128,128]{1,0:T(8,128)(2,1)S(1)}, u32[]{:S(2)}, u32[]{:S(2)}) collective-permute-start(bf16[128,128]{1,0:T(8,128)(2,1)S(1)} %get-tuple-element.66), channel_id=1, source_target_pairs={{0,2},{1,3},{2,0},{3,1},{4,6},{5,7},{6,4},{7,5},{8,10},{9,11},{10,... | collective-permute-start | bytes 98312 | tf_op jit(solution)/shard_map/ppermute | solution.py:25
  100.0 8.4 %collective-permute-start.31 = (bf16[128,128]{1,0:T(8,128)(2,1)S(1)}, bf16[128,128]{1,0:T(8,128)(2,1)S(1)}, u32[]{:S(2)}, u32[]{:S(2)}) collective-permute-start(bf16[128,128]{1,0:T(8,128)(2,1)S(1)} %get-tuple-element.68), channel_id=1, source_target_pairs={{0,3},{1,2},{2,1},{3,0},{4,7},{5,6},{6,5},{7,4},{8,11},{9,10},{10,... | collective-permute-start | bytes 98312 | tf_op jit(solution)/shard_map/ppermute | solution.py:25
  105.2 3.3 %collective-permute-start.26 = (bf16[128,128]{1,0:T(8,128)(2,1)S(1)}, bf16[128,128]{1,0:T(8,128)(2,1)S(1)}, u32[]{:S(2)}, u32[]{:S(2)}) collective-permute-start(bf16[128,128]{1,0:T(8,128)(2,1)S(1)} %get-tuple-element.63), channel_id=1, source_target_pairs={{0,1},{1,0},{2,3},{3,2},{4,5},{5,4},{6,7},{7,6},{8,9},{9,8},{10,11... | collective-permute-start | bytes 98312 | tf_op jit(solution)/shard_map/ppermute | solution.py:25
  105.2 4.0 %collective-permute-start.28 = (bf16[128,128]{1,0:T(8,128)(2,1)S(1)}, bf16[128,128]{1,0:T(8,128)(2,1)S(1)}, u32[]{:S(2)}, u32[]{:S(2)}) collective-permute-start(bf16[128,128]{1,0:T(8,128)(2,1)S(1)} %get-tuple-element.65), channel_id=1, source_target_pairs={{0,2},{1,3},{2,0},{3,1},{4,6},{5,7},{6,4},{7,5},{8,10},{9,11},{10,... | collective-permute-start | bytes 98312 | tf_op jit(solution)/shard_map/ppermute | solution.py:25
  106.8 3.4 %collective-permute-start.30 = (bf16[128,128]{1,0:T(8,128)(2,1)S(1)}, bf16[128,128]{1,0:T(8,128)(2,1)S(1)}, u32[]{:S(2)}, u32[]{:S(2)}) collective-permute-start(bf16[128,128]{1,0:T(8,128)(2,1)S(1)} %get-tuple-element.67), channel_id=1, source_target_pairs={{0,3},{1,2},{2,1},{3,0},{4,7},{5,6},{6,5},{7,4},{8,11},{9,10},{10,... | collective-permute-start | bytes 98312 | tf_op jit(solution)/shard_map/ppermute | solution.py:25
  (19 other events, 192.5 us)

commit v9 on v7

--- a/solution.py
+++ b/solution.py
@@ -374,19 +374,7 @@
 
 
 def scatter_plan(count):
-    outer = [mask for mask, codes in stages(count, True) if mask != 1]
-    plan, main, side = [], [0], [1]
-    for mask in outer[:-1]:
-        plan.append((mask, tuple(main)))
-        main += [c ^ mask for c in main]
-    plan.append((1, (0,)))
-    for mask in outer[:-1]:
-        plan.append((mask, tuple(side)))
-        side += [c ^ mask for c in side]
-    for mask in outer[-1:]:
-        plan.append((mask, tuple(main)))
-        plan.append((1, tuple(c ^ mask for c in main)))
-    return plan
+    return stages(count, False)
 
 
 def gather_queries(own, plan):

time: 108 us -> 117 us (1.083)
  waiting for transfers between devices: 22.1 us -> 32.8 us
  starting transfers between devices: 49.6 us -> 41.1 us
  local copies, waits for them, and re-layouts: 7.11 us -> 11.7 us
  other arithmetic: 0.69 us -> 3.1 us
    ppermute x32 -> x30, waiting for transfers between devices: 22.1 us -> 32.8 us  [swap(): return lax.ppermute(value, axis, [(i, i ^ mask) for i in range(count)])]
    ppermute x32 -> x30, starting transfers between devices: 49.6 us -> 41.1 us  [swap(): return lax.ppermute(value, axis, [(i, i ^ mask) for i in range(count)])]
    unnamed x35 -> x57, local copies, waits for them, and re-layouts: 7.01 us -> 11 us
    concatenate x4, other arithmetic: 0.09 us -> 1.87 us  [joined(): return pieces[0] if len(pieces) == 1 else jnp.concatenate(pieces, axis=0)]
  transfers between devices with their start and end apart: 32 -> 30, of which waited for: 11 -> 11; matrix products, arithmetic and copies ran while one was open for 1% -> 4% of each run, Pallas kernels for 21% -> 20%
where the time goes in v9:
time: 117 us
  starting transfers between devices  41.1 us (35%)
  waiting for transfers between devices  32.8 us (28%)
  Pallas kernels  27.8 us (24%)
  local copies, waits for them, and re-layouts  11.7 us (10%)
  other arithmetic  3.1 us (3%)
    ppermute x30, starting transfers between devices, swap(): return lax.ppermute(value, axis, [(i, i ^ mask) for i in range(count)])  41.1 us
    ppermute x30, waiting for transfers between devices, swap(): return lax.ppermute(value, axis, [(i, i ^ mask) for i in range(count)])  32.8 us
    pallas_call x4, Pallas kernels, attend(): pl.pallas_call(functools.partial(attend_kernel, source, sink, events, roo...  15.3 us
    unnamed x57, local copies, waits for them, and re-layouts  11 us
    pallas_call x2, Pallas kernels, project_keys_values(): pl.pallas_call(functools.partial(keys_values_kernel, count, each), grid_s...  6.06 us
    pallas_call x1, Pallas kernels, project_queries(): pl.pallas_call(query_kernel, in_specs=[pl.BlockSpec(memory_space=pltpu.SM...  3.58 us
  transfers between devices with their start and end apart: 30, of which 11 were waited for; matrix products, arithmetic and copies ran while one was open for 4% of the time, Pallas kernels for 20%

profile of v9, /device:TPU:0, one launch (start us, length us, event | category | flops | bytes accessed | tf_op | source)
XLA Modules:
  0.0 116.9 jit_solution(16244521891651699501)
XLA Ops:
  0.0 3.6 %queries.1 = (bf16[144,256]{1,0:T(8,128)(2,1)}, bf16[144,256]{1,0:T(8,128)(2,1)}, bf16[144,256]{1,0:T(8,128)(2,1)}, bf16[144,256]{1,0:T(8,128)(2,1)}) custom-call(s32[1]{0:T(128)} %bitcast._.me_ref, bf16[128,1024]{1,0:T(8,128)(2,1)} %cand_ref.3, bf16[1024,2048]{1,0:T(8,128)(2,1)} %w_hbm.1, s32[1,48]{1,0:T(1,128)} %bitcast.2), custom_call_target="tpu_custom_call" | custom-call | flops 268435456 | bytes 2621440 | tf_op jit(solution)/shard_map/queries/pallas_call | solution.py:95
  4.1 2.6 %collective-permute-start.1 = (bf16[144,256]{1,0:T(8,128)(2,1)}, bf16[144,256]{1,0:T(8,128)(2,1)S(1)}, u32[]{:S(2)}, u32[]{:S(2)}) collective-permute-start(bf16[144,256]{1,0:T(8,128)(2,1)} %get-tuple-element.38), channel_id=1, source_target_pairs={{0,2},{1,3},{2,0},{3,1},{4,6},{5,7},{6,4},{7,5},{8,10},{9,11},{10,... | collective-permute-start | bytes 221192 | tf_op jit(solution)/shard_map/ppermute | solution.py:25
  6.7 3.0 %collective-permute-done.1.refs_2_ = bf16[144,256]{1,0:T(8,128)(2,1)S(1)} collective-permute-done((bf16[144,256]{1,0:T(8,128)(2,1)}, bf16[144,256]{1,0:T(8,128)(2,1)S(1)}, u32[]{:S(2)}, u32[]{:S(2)}) %collective-permute-start.1) | collective-permute-done | bytes 73760 | tf_op jit(solution)/shard_map/ppermute | solution.py:25
  9.8 1.4 %collective-permute-done.2.refs_3_ = bf16[144,256]{1,0:T(8,128)(2,1)S(1)} collective-permute-done((bf16[144,256]{1,0:T(8,128)(2,1)}, bf16[144,256]{1,0:T(8,128)(2,1)S(1)}, u32[]{:S(2)}, u32[]{:S(2)}) %collective-permute-start.2) | collective-permute-done | bytes 73760 | tf_op jit(solution)/shard_map/ppermute | solution.py:25
  12.7 1.8 %collective-permute-start.17 = (bf16[512,128]{1,0:T(8,128)(2,1)S(1)}, bf16[512,128]{1,0:T(8,128)(2,1)S(1)}, u32[]{:S(2)}, u32[]{:S(2)}) collective-permute-start(bf16[512,128]{1,0:T(8,128)(2,1)S(1)} %get-tuple-element.55.refs_4_), channel_id=1, source_target_pairs={{0,4},{4,0},{8,12},{12,8},{16,20},{20,16},{24,28},{28,24},{1,5},{5... | collective-permute-start | bytes 393224 | tf_op jit(solution)/shard_map/ppermute | solution.py:25
  14.5 1.4 %copy-done.2 = bf16[768,1024]{1,0:T(8,128)(2,1)S(1)} copy-done((bf16[768,1024]{1,0:T(8,128)(2,1)S(1)}, bf16[768,1024]{1,0:T(8,128)(2,1)}, u32[]{:S(2)}) %copy-start.2) | copy-done | bytes 1572888
  15.9 3.0 %shard_map.100 = (bf16[768,256]{1,0:T(8,128)(2,1)S(1)}, bf16[768,256]{1,0:T(8,128)(2,1)S(1)}, bf16[768,256]{1,0:T(8,128)(2,1)}, bf16[768,256]{1,0:T(8,128)(2,1)S(1)}) custom-call(s32[1]{0:T(128)} %bitcast._.me_ref, bf16[768,1024]{1,0:T(8,128)(2,1)S(1)} %copy-done.2, bf16[1024,2048]{1,0:T(8,128)(2,1)S(1)} %copy-done, bf16[1024,2048]{1,0:T(8,128)(2,1)S(1)} %copy-done, ...), custom_call_target="tpu_custom_call" | custom-call | flops 1610612736 | bytes 5242880 | tf_op jit(solution)/shard_map/pallas_call | solution.py:186
  19.6 3.6 %collective-permute-start.6 = (bf16[512,128]{1,0:T(8,128)(2,1)S(1)}, bf16[512,128]{1,0:T(8,128)(2,1)S(1)}, u32[]{:S(2)}, u32[]{:S(2)}) collective-permute-start(bf16[512,128]{1,0:T(8,128)(2,1)S(1)} %get-tuple-element.45.refs_4_), channel_id=1, source_target_pairs={{0,24},{4,28},{8,16},{12,20},{16,8},{20,12},{24,0},{28,4},{1,25},{... | collective-permute-start | bytes 393224 | tf_op jit(solution)/shard_map/ppermute | solution.py:25
  24.9 2.6 %collective-permute-done.6.refs_5_ = bf16[512,128]{1,0:T(8,128)(2,1)S(1)} collective-permute-done((bf16[512,128]{1,0:T(8,128)(2,1)S(1)}, bf16[512,128]{1,0:T(8,128)(2,1)S(1)}, u32[]{:S(2)}, u32[]{:S(2)}) %collective-permute-start.6) | collective-permute-done | bytes 131104 | tf_op jit(solution)/shard_map/ppermute | solution.py:25
  28.2 8.5 %collective-permute-start.8 = (bf16[1024,128]{1,0:T(8,128)(2,1)}, bf16[1024,128]{1,0:T(8,128)(2,1)}, u32[]{:S(2)}, u32[]{:S(2)}) collective-permute-start(bf16[1024,128]{1,0:T(8,128)(2,1)} %constant_dynamic-update-slice_fusion), channel_id=1, source_target_pairs={{0,8},{4,12},{8,0},{12,4},{16,24},{20,28},{24,16},{28,20},{1,9},{5... | collective-permute-start | bytes 786440 | tf_op jit(solution)/shard_map/ppermute | solution.py:25
  36.7 3.0 %shard_map.101 = (bf16[768,256]{1,0:T(8,128)(2,1)}, bf16[768,256]{1,0:T(8,128)(2,1)S(1)}, bf16[768,256]{1,0:T(8,128)(2,1)}, bf16[768,256]{1,0:T(8,128)(2,1)S(1)}) custom-call(s32[1]{0:T(128)} %bitcast._.me_ref, bf16[768,1024]{1,0:T(8,128)(2,1)S(1)} %copy-done.3, bf16[1024,2048]{1,0:T(8,128)(2,1)S(1)} %copy-done, bf16[1024,2048]{1,0:T(8,128)(2,1)S(1)} %copy-done, ...), custom_call_target="tpu_custom_call" | custom-call | flops 1610612736 | bytes 5242880 | tf_op jit(solution)/shard_map/pallas_call | solution.py:186
  41.3 1.2 %collective-permute-start.4 = (bf16[768,256]{1,0:T(8,128)(2,1)}, bf16[768,256]{1,0:T(8,128)(2,1)S(1)}, u32[]{:S(2)}, u32[]{:S(2)}) collective-permute-start(bf16[768,256]{1,0:T(8,128)(2,1)} %get-tuple-element.43), channel_id=1, source_target_pairs={{0,2},{1,3},{2,0},{3,1},{4,6},{5,7},{6,4},{7,5},{8,10},{9,11},{10,... | collective-permute-start | bytes 1179656 | tf_op jit(solution)/shard_map/ppermute | solution.py:25
  45.9 7.0 %collective-permute-done.4.refs_2_ = bf16[768,256]{1,0:T(8,128)(2,1)S(1)} collective-permute-done((bf16[768,256]{1,0:T(8,128)(2,1)}, bf16[768,256]{1,0:T(8,128)(2,1)S(1)}, u32[]{:S(2)}, u32[]{:S(2)}) %collective-permute-start.4) | collective-permute-done | bytes 393248 | tf_op jit(solution)/shard_map/ppermute | solution.py:25
  52.8 1.7 %collective-permute-start.15 = (bf16[768,256]{1,0:T(8,128)(2,1)}, bf16[768,256]{1,0:T(8,128)(2,1)S(1)}, u32[]{:S(2)}, u32[]{:S(2)}) collective-permute-start(bf16[768,256]{1,0:T(8,128)(2,1)} %copy-done.25), channel_id=1, source_target_pairs={{0,2},{1,3},{2,0},{3,1},{4,6},{5,7},{6,4},{7,5},{8,10},{9,11},{10,... | collective-permute-start | bytes 1179656 | tf_op jit(solution)/shard_map/ppermute | solution.py:25
  54.5 6.0 %collective-permute-done.5.refs_3_ = bf16[768,256]{1,0:T(8,128)(2,1)S(1)} collective-permute-done((bf16[768,256]{1,0:T(8,128)(2,1)}, bf16[768,256]{1,0:T(8,128)(2,1)S(1)}, u32[]{:S(2)}, u32[]{:S(2)}) %collective-permute-start.5) | collective-permute-done | bytes 393248 | tf_op jit(solution)/shard_map/ppermute | solution.py:25
  60.6 1.8 %collective-permute-start.16 = (bf16[768,256]{1,0:T(8,128)(2,1)}, bf16[768,256]{1,0:T(8,128)(2,1)S(1)}, u32[]{:S(2)}, u32[]{:S(2)}) collective-permute-start(bf16[768,256]{1,0:T(8,128)(2,1)} %copy-done.24), channel_id=1, source_target_pairs={{0,3},{1,2},{2,1},{3,0},{4,7},{5,6},{6,5},{7,4},{8,11},{9,10},{10,... | collective-permute-start | bytes 1179656 | tf_op jit(solution)/shard_map/ppermute | solution.py:25
  64.7 2.7 %shard_map.103 = bf16[1024,128]{1,0:T(8,128)(2,1)S(1)} custom-call(s32[192]{0:T(256)S(1)} %multiply_add_fusion.pos_ref, s32[8]{0:T(128)S(1)} %convert_reduce_fusion.1.count_ref, s32[2]{0:T(128)S(1)} %copy-done.21, bf16[768,256]{1,0:T(8,128)(2,1)S(1)} %copy-done.11, bf16[768,256]{1,0:T(8,128)(2,1)} %collective-permute-done.3.refs_1_, ...), custom_call_target="tpu_custom_call" | custom-call | flops 402653184 | bytes 2097152 | tf_op jit(solution)/shard_map/pallas_call | solution.py:280
  67.3 2.2 %collective-permute-done.7.refs_6_ = bf16[1024,128]{1,0:T(8,128)(2,1)S(1)} collective-permute-done((bf16[1024,128]{1,0:T(8,128)(2,1)}, bf16[1024,128]{1,0:T(8,128)(2,1)S(1)}, u32[]{:S(2)}, u32[]{:S(2)}) %collective-permute-start.7) | collective-permute-done | bytes 262176 | tf_op jit(solution)/shard_map/ppermute | solution.py:25
  73.5 5.2 %shard_map.102 = (bf16[512,128]{1,0:T(8,128)(2,1)S(1)}, bf16[1024,128]{1,0:T(8,128)(2,1)S(1)}, bf16[1024,128]{1,0:T(8,128)(2,1)S(1)}, bf16[512,128]{1,0:T(8,128)(2,1)S(1)}) custom-call(s32[192]{0:T(256)S(1)} %multiply_add_fusion.pos_ref, s32[8]{0:T(128)S(1)} %convert_reduce_fusion.1.count_ref, s32[6]{0:T(128)S(1)} %copy-done.26, ...), custom_call_target="tpu_custom_call" | custom-call | flops 1207959552 | bytes 3145728 | tf_op jit(solution)/shard_map/pallas_call | solution.py:280
  78.7 1.6 %collective-permute-start.12 = (bf16[1024,128]{1,0:T(8,128)(2,1)S(1)}, bf16[1024,128]{1,0:T(8,128)(2,1)S(1)}, u32[]{:S(2)}, u32[]{:S(2)}) collective-permute-start(bf16[1024,128]{1,0:T(8,128)(2,1)S(1)} %get-tuple-element.48), channel_id=1, source_target_pairs={{0,4},{4,0},{8,12},{12,8},{16,20},{20,16},{24,28},{28,24},{1,5},{5... | collective-permute-start | bytes 786440 | tf_op jit(solution)/shard_map/ppermute | solution.py:25
  80.3 2.2 %shard_map.106 = bf16[1024,128]{1,0:T(8,128)(2,1)S(1)} custom-call(s32[192]{0:T(256)S(1)} %multiply_add_fusion.pos_ref, s32[8]{0:T(128)S(1)} %convert_reduce_fusion.1.count_ref, s32[2]{0:T(128)S(1)} %copy-done.22, bf16[768,256]{1,0:T(8,128)(2,1)S(1)} %copy-done.14, bf16[768,256]{1,0:T(8,128)(2,1)S(1)} %collective-permute-done.14.refs_1_, ...), custom_call_target="tpu_custom_call" | custom-call | flops 402653184 | bytes 2097152 | tf_op jit(solution)/shard_map/pallas_call | solution.py:280
  82.9 5.3 %shard_map.105 = (bf16[512,128]{1,0:T(8,128)(2,1)S(1)}, bf16[1024,128]{1,0:T(8,128)(2,1)S(1)}, bf16[1024,128]{1,0:T(8,128)(2,1)S(1)}, bf16[512,128]{1,0:T(8,128)(2,1)S(1)}) custom-call(s32[192]{0:T(256)S(1)} %multiply_add_fusion.pos_ref, s32[8]{0:T(128)S(1)} %convert_reduce_fusion.1.count_ref, s32[6]{0:T(128)S(1)} %copy-done.27, ...), custom_call_target="tpu_custom_call" | custom-call | flops 1207959552 | bytes 3145728 | tf_op jit(solution)/shard_map/pallas_call | solution.py:280
  88.3 1.5 %collective-permute-start.22 = (bf16[1024,128]{1,0:T(8,128)(2,1)S(1)}, bf16[1024,128]{1,0:T(8,128)(2,1)S(1)}, u32[]{:S(2)}, u32[]{:S(2)}) collective-permute-start(bf16[1024,128]{1,0:T(8,128)(2,1)S(1)} %get-tuple-element.58), channel_id=1, source_target_pairs={{0,4},{4,0},{8,12},{12,8},{16,20},{20,16},{24,28},{28,24},{1,5},{5... | collective-permute-start | bytes 786440 | tf_op jit(solution)/shard_map/ppermute | solution.py:25
  90.0 3.4 %collective-permute-done.20 = bf16[1024,128]{1,0:T(8,128)(2,1)S(1)} collective-permute-done((bf16[1024,128]{1,0:T(8,128)(2,1)S(1)}, bf16[1024,128]{1,0:T(8,128)(2,1)S(1)}, u32[]{:S(2)}, u32[]{:S(2)}) %collective-permute-start.20) | collective-permute-done | bytes 262176 | tf_op jit(solution)/shard_map/ppermute | solution.py:25
  93.6 4.1 %collective-permute-done.11.refs_1_ = bf16[1024,128]{1,0:T(8,128)(2,1)S(1)} collective-permute-done((bf16[1024,128]{1,0:T(8,128)(2,1)S(1)}, bf16[1024,128]{1,0:T(8,128)(2,1)S(1)}, u32[]{:S(2)}, u32[]{:S(2)}) %collective-permute-start.11) | collective-permute-done | bytes 262176 | tf_op jit(solution)/shard_map/ppermute | solution.py:25
  97.8 4.6 %collective-permute-start.13 = (bf16[512,128]{1,0:T(8,128)(2,1)S(1)}, bf16[512,128]{1,0:T(8,128)(2,1)S(1)}, u32[]{:S(2)}, u32[]{:S(2)}) collective-permute-start(bf16[512,128]{1,0:T(8,128)(2,1)S(1)} %add_convert_fusion.3), channel_id=1, source_target_pairs={{0,24},{4,28},{8,16},{12,20},{16,8},{20,12},{24,0},{28,4},{1,25},{... | collective-permute-start | bytes 393224 | tf_op jit(solution)/shard_map/ppermute | solution.py:25
  102.5 4.6 %collective-permute-start.23 = (bf16[512,128]{1,0:T(8,128)(2,1)S(1)}, bf16[512,128]{1,0:T(8,128)(2,1)S(1)}, u32[]{:S(2)}, u32[]{:S(2)}) collective-permute-start(bf16[512,128]{1,0:T(8,128)(2,1)S(1)} %add_convert_fusion), channel_id=1, source_target_pairs={{0,24},{4,28},{8,16},{12,20},{16,8},{20,12},{24,0},{28,4},{1,25},{... | collective-permute-start | bytes 393224 | tf_op jit(solution)/shard_map/ppermute | solution.py:25
  107.2 1.4 %collective-permute-start.26 = (bf16[128,128]{1,0:T(8,128)(2,1)S(1)}, bf16[128,128]{1,0:T(8,128)(2,1)S(1)}, u32[]{:S(2)}, u32[]{:S(2)}) collective-permute-start(bf16[128,128]{1,0:T(8,128)(2,1)S(1)} %get-tuple-element.63), channel_id=1, source_target_pairs={{0,2},{1,3},{2,0},{3,1},{4,6},{5,7},{6,4},{7,5},{8,10},{9,11},{10,... | collective-permute-start | bytes 98312 | tf_op jit(solution)/shard_map/ppermute | solution.py:25
  110.3 1.9 %collective-permute-start.27 = (bf16[128,128]{1,0:T(8,128)(2,1)S(1)}, bf16[128,128]{1,0:T(8,128)(2,1)S(1)}, u32[]{:S(2)}, u32[]{:S(2)}) collective-permute-start(bf16[128,128]{1,0:T(8,128)(2,1)S(1)} %get-tuple-element.64), channel_id=1, source_target_pairs={{0,2},{1,3},{2,0},{3,1},{4,6},{5,7},{6,4},{7,5},{8,10},{9,11},{10,... | collective-permute-start | bytes 98312 | tf_op jit(solution)/shard_map/ppermute | solution.py:25
  112.2 1.3 %gate.1.gate_ref = f32[4,128,256]{2,1,0:T(8,128)S(1)} custom-call(s32[1]{0:T(128)} %bitcast._.me_ref, bf16[128,1024]{1,0:T(8,128)(2,1)S(1)} %copy-done.4, bf16[1024,2048]{1,0:T(8,128)(2,1)S(1)} %copy-done.1), custom_call_target="tpu_custom_call" | custom-call | flops 268435456 | bytes 2883584 | tf_op jit(solution)/shard_map/gate/pallas_call | solution.py:146
  114.2 1.3 %collective-permute-done.29.refs_7_ = bf16[128,128]{1,0:T(8,128)(2,1)S(1)} collective-permute-done((bf16[128,128]{1,0:T(8,128)(2,1)S(1)}, bf16[128,128]{1,0:T(8,128)(2,1)S(1)}, u32[]{:S(2)}, u32[]{:S(2)}) %collective-permute-start.29) | collective-permute-done | bytes 32800 | tf_op jit(solution)/shard_map/ppermute | solution.py:25
  115.5 1.3 %finish.1 = bf16[128,1024]{1,0:T(8,128)(2,1)} custom-call(s32[1]{0:T(128)} %bitcast._.me_ref, bf16[128,1024]{1,0:T(8,128)(2,1)S(1)} %copy-done.4, f32[4,128,256]{2,1,0:T(8,128)S(1)} %gate.1.gate_ref, bf16[1024,1024]{1,0:T(8,128)(2,1)S(1)} %copy-done.5, f32[128,128]{1,0:T(8,128)S(1)} %get-tuple-element.50.refs_0_, f32[128,128]{1,0:T(8,128)S(1)} %get-tuple-element.60.refs_1_, ...), custom_call_target="tpu_custom_call" | custom-call | flops 268435456 | bytes 3407872 | tf_op jit(solution)/shard_map/finish/pallas_call | solution.py:327
  (111 shorter events, 19.7 us)
Async XLA Ops:
  3.6 3.1 %collective-permute-start = (bf16[144,256]{1,0:T(8,128)(2,1)}, bf16[144,256]{1,0:T(8,128)(2,1)S(1)}, u32[]{:S(2)}, u32[]{:S(2)}) collective-permute-start(bf16[144,256]{1,0:T(8,128)(2,1)} %get-tuple-element.37), channel_id=1, source_target_pairs={{0,1},{1,0},{2,3},{3,2},{4,5},{5,4},{6,7},{7,6},{8,9},{9,8},{10,11... | collective-permute-start | bytes 221192 | tf_op jit(solution)/shard_map/ppermute | solution.py:25
  4.1 5.6 %collective-permute-start.1 = (bf16[144,256]{1,0:T(8,128)(2,1)}, bf16[144,256]{1,0:T(8,128)(2,1)S(1)}, u32[]{:S(2)}, u32[]{:S(2)}) collective-permute-start(bf16[144,256]{1,0:T(8,128)(2,1)} %get-tuple-element.38), channel_id=1, source_target_pairs={{0,2},{1,3},{2,0},{3,1},{4,6},{5,7},{6,4},{7,5},{8,10},{9,11},{10,... | collective-permute-start | bytes 221192 | tf_op jit(solution)/shard_map/ppermute | solution.py:25
  6.7 4.4 %collective-permute-start.2 = (bf16[144,256]{1,0:T(8,128)(2,1)}, bf16[144,256]{1,0:T(8,128)(2,1)S(1)}, u32[]{:S(2)}, u32[]{:S(2)}) collective-permute-start(bf16[144,256]{1,0:T(8,128)(2,1)} %get-tuple-element.39), channel_id=1, source_target_pairs={{0,3},{1,2},{2,1},{3,0},{4,7},{5,6},{6,5},{7,4},{8,11},{9,10},{10,... | collective-permute-start | bytes 221192 | tf_op jit(solution)/shard_map/ppermute | solution.py:25
  12.7 11.2 %collective-permute-start.17 = (bf16[512,128]{1,0:T(8,128)(2,1)S(1)}, bf16[512,128]{1,0:T(8,128)(2,1)S(1)}, u32[]{:S(2)}, u32[]{:S(2)}) collective-permute-start(bf16[512,128]{1,0:T(8,128)(2,1)S(1)} %get-tuple-element.55.refs_4_), channel_id=1, source_target_pairs={{0,4},{4,0},{8,12},{12,8},{16,20},{20,16},{24,28},{28,24},{1,5},{5... | collective-permute-start | bytes 393224 | tf_op jit(solution)/shard_map/ppermute | solution.py:25
  19.6 25.6 %collective-permute-start.3 = (bf16[768,256]{1,0:T(8,128)(2,1)}, bf16[768,256]{1,0:T(8,128)(2,1)}, u32[]{:S(2)}, u32[]{:S(2)}) collective-permute-start(bf16[768,256]{1,0:T(8,128)(2,1)} %get-tuple-element.42), channel_id=1, source_target_pairs={{0,1},{1,0},{2,3},{3,2},{4,5},{5,4},{6,7},{7,6},{8,9},{9,8},{10,11... | collective-permute-start | bytes 1179656 | tf_op jit(solution)/shard_map/ppermute | solution.py:25
  19.6 7.9 %collective-permute-start.6 = (bf16[512,128]{1,0:T(8,128)(2,1)S(1)}, bf16[512,128]{1,0:T(8,128)(2,1)S(1)}, u32[]{:S(2)}, u32[]{:S(2)}) collective-permute-start(bf16[512,128]{1,0:T(8,128)(2,1)S(1)} %get-tuple-element.45.refs_4_), channel_id=1, source_target_pairs={{0,24},{4,28},{8,16},{12,20},{16,8},{20,12},{24,0},{28,4},{1,25},{... | collective-permute-start | bytes 393224 | tf_op jit(solution)/shard_map/ppermute | solution.py:25
  24.7 19.1 %collective-permute-start.18 = (bf16[1024,128]{1,0:T(8,128)(2,1)}, bf16[1024,128]{1,0:T(8,128)(2,1)}, u32[]{:S(2)}, u32[]{:S(2)}) collective-permute-start(bf16[1024,128]{1,0:T(8,128)(2,1)} %pad_maximum_fusion.2), channel_id=1, source_target_pairs={{0,24},{4,28},{8,16},{12,20},{16,8},{20,12},{24,0},{28,4},{1,25},{... | collective-permute-start | bytes 786440 | tf_op jit(solution)/shard_map/ppermute | solution.py:25
  28.2 15.1 %collective-permute-start.8 = (bf16[1024,128]{1,0:T(8,128)(2,1)}, bf16[1024,128]{1,0:T(8,128)(2,1)}, u32[]{:S(2)}, u32[]{:S(2)}) collective-permute-start(bf16[1024,128]{1,0:T(8,128)(2,1)} %constant_dynamic-update-slice_fusion), channel_id=1, source_target_pairs={{0,8},{4,12},{8,0},{12,4},{16,24},{20,28},{24,16},{28,20},{1,9},{5... | collective-permute-start | bytes 786440 | tf_op jit(solution)/shard_map/ppermute | solution.py:25
  41.3 39.0 %copy-start.22 = (s32[2]{0:T(128)S(1)}, s32[2]{0:T(128)}, u32[]{:S(2)}) copy-start(s32[2]{0:T(128)} %constant.18.clone.code_ref) | copy-start | bytes 28
  41.3 39.0 %copy-start.14 = (bf16[768,256]{1,0:T(8,128)(2,1)S(1)}, bf16[768,256]{1,0:T(8,128)(2,1)}, u32[]{:S(2)}) copy-start(bf16[768,256]{1,0:T(8,128)(2,1)} %copy-done.13) | copy-start | bytes 1179652
  41.3 11.5 %collective-permute-start.4 = (bf16[768,256]{1,0:T(8,128)(2,1)}, bf16[768,256]{1,0:T(8,128)(2,1)S(1)}, u32[]{:S(2)}, u32[]{:S(2)}) collective-permute-start(bf16[768,256]{1,0:T(8,128)(2,1)} %get-tuple-element.43), channel_id=1, source_target_pairs={{0,2},{1,3},{2,0},{3,1},{4,6},{5,7},{6,4},{7,5},{8,10},{9,11},{10,... | collective-permute-start | bytes 1179656 | tf_op jit(solution)/shard_map/ppermute | solution.py:25
  42.5 18.0 %collective-permute-start.5 = (bf16[768,256]{1,0:T(8,128)(2,1)}, bf16[768,256]{1,0:T(8,128)(2,1)S(1)}, u32[]{:S(2)}, u32[]{:S(2)}) collective-permute-start(bf16[768,256]{1,0:T(8,128)(2,1)} %get-tuple-element.44), channel_id=1, source_target_pairs={{0,3},{1,2},{2,1},{3,0},{4,7},{5,6},{6,5},{7,4},{8,11},{9,10},{10,... | collective-permute-start | bytes 1179656 | tf_op jit(solution)/shard_map/ppermute | solution.py:25
  43.3 19.1 %collective-permute-start.9 = (bf16[1024,128]{1,0:T(8,128)(2,1)}, bf16[1024,128]{1,0:T(8,128)(2,1)S(1)}, u32[]{:S(2)}, u32[]{:S(2)}) collective-permute-start(bf16[1024,128]{1,0:T(8,128)(2,1)} %collective-permute-done.8.refs_7_), channel_id=1, source_target_pairs={{0,4},{4,0},{8,12},{12,8},{16,20},{20,16},{24,28},{28,24},{1,5},{5... | collective-permute-start | bytes 786440 | tf_op jit(solution)/shard_map/ppermute | solution.py:25
  44.9 35.4 %collective-permute-start.19 = (bf16[2048,128]{1,0:T(8,128)(2,1)S(1)}, bf16[2048,128]{1,0:T(8,128)(2,1)S(1)}, u32[]{:S(2)}, u32[]{:S(2)}) collective-permute-start(bf16[2048,128]{1,0:T(8,128)(2,1)S(1)} %pad_maximum_fusion), channel_id=1, source_target_pairs={{0,8},{4,12},{8,0},{12,4},{16,24},{20,28},{24,16},{28,20},{1,9},{5... | collective-permute-start | bytes 1572872 | tf_op jit(solution)/shard_map/ppermute | solution.py:25
  45.3 33.4 %collective-permute-start.14 = (bf16[768,256]{1,0:T(8,128)(2,1)}, bf16[768,256]{1,0:T(8,128)(2,1)S(1)}, u32[]{:S(2)}, u32[]{:S(2)}) collective-permute-start(bf16[768,256]{1,0:T(8,128)(2,1)} %copy-done.23), channel_id=1, source_target_pairs={{0,1},{1,0},{2,3},{3,2},{4,5},{5,4},{6,7},{7,6},{8,9},{9,8},{10,11... | collective-permute-start | bytes 1179656 | tf_op jit(solution)/shard_map/ppermute | solution.py:25
  52.8 27.5 %collective-permute-start.15 = (bf16[768,256]{1,0:T(8,128)(2,1)}, bf16[768,256]{1,0:T(8,128)(2,1)S(1)}, u32[]{:S(2)}, u32[]{:S(2)}) collective-permute-start(bf16[768,256]{1,0:T(8,128)(2,1)} %copy-done.25), channel_id=1, source_target_pairs={{0,2},{1,3},{2,0},{3,1},{4,6},{5,7},{6,4},{7,5},{8,10},{9,11},{10,... | collective-permute-start | bytes 1179656 | tf_op jit(solution)/shard_map/ppermute | solution.py:25
  60.6 19.7 %collective-permute-start.16 = (bf16[768,256]{1,0:T(8,128)(2,1)}, bf16[768,256]{1,0:T(8,128)(2,1)S(1)}, u32[]{:S(2)}, u32[]{:S(2)}) collective-permute-start(bf16[768,256]{1,0:T(8,128)(2,1)} %copy-done.24), channel_id=1, source_target_pairs={{0,3},{1,2},{2,1},{3,0},{4,7},{5,6},{6,5},{7,4},{8,11},{9,10},{10,... | collective-permute-start | bytes 1179656 | tf_op jit(solution)/shard_map/ppermute | solution.py:25
  62.4 7.1 %collective-permute-start.7 = (bf16[1024,128]{1,0:T(8,128)(2,1)}, bf16[1024,128]{1,0:T(8,128)(2,1)S(1)}, u32[]{:S(2)}, u32[]{:S(2)}) collective-permute-start(bf16[1024,128]{1,0:T(8,128)(2,1)} %constant_dynamic-update-slice_fusion), channel_id=1, source_target_pairs={{0,4},{4,0},{8,12},{12,8},{16,20},{20,16},{24,28},{28,24},{1,5},{5... | collective-permute-start | bytes 786440 | tf_op jit(solution)/shard_map/ppermute | solution.py:25
  69.5 20.3 %collective-permute-start.10 = (bf16[1024,128]{1,0:T(8,128)(2,1)S(1)}, bf16[1024,128]{1,0:T(8,128)(2,1)S(1)}, u32[]{:S(2)}, u32[]{:S(2)}) collective-permute-start(bf16[1024,128]{1,0:T(8,128)(2,1)S(1)} %shard_map.103), channel_id=1, source_target_pairs={{0,4},{4,0},{8,12},{12,8},{16,20},{20,16},{24,28},{28,24},{1,5},{5... | collective-permute-start | bytes 786440 | tf_op jit(solution)/shard_map/ppermute | solution.py:25
  78.7 14.9 %collective-permute-start.12 = (bf16[1024,128]{1,0:T(8,128)(2,1)S(1)}, bf16[1024,128]{1,0:T(8,128)(2,1)S(1)}, u32[]{:S(2)}, u32[]{:S(2)}) collective-permute-start(bf16[1024,128]{1,0:T(8,128)(2,1)S(1)} %get-tuple-element.48), channel_id=1, source_target_pairs={{0,4},{4,0},{8,12},{12,8},{16,20},{20,16},{24,28},{28,24},{1,5},{5... | collective-permute-start | bytes 786440 | tf_op jit(solution)/shard_map/ppermute | solution.py:25
  82.5 10.9 %collective-permute-start.20 = (bf16[1024,128]{1,0:T(8,128)(2,1)S(1)}, bf16[1024,128]{1,0:T(8,128)(2,1)S(1)}, u32[]{:S(2)}, u32[]{:S(2)}) collective-permute-start(bf16[1024,128]{1,0:T(8,128)(2,1)S(1)} %shard_map.106), channel_id=1, source_target_pairs={{0,4},{4,0},{8,12},{12,8},{16,20},{20,16},{24,28},{28,24},{1,5},{5... | collective-permute-start | bytes 786440 | tf_op jit(solution)/shard_map/ppermute | solution.py:25
  88.3 14.2 %collective-permute-start.22 = (bf16[1024,128]{1,0:T(8,128)(2,1)S(1)}, bf16[1024,128]{1,0:T(8,128)(2,1)S(1)}, u32[]{:S(2)}, u32[]{:S(2)}) collective-permute-start(bf16[1024,128]{1,0:T(8,128)(2,1)S(1)} %get-tuple-element.58), channel_id=1, source_target_pairs={{0,4},{4,0},{8,12},{12,8},{16,20},{20,16},{24,28},{28,24},{1,5},{5... | collective-permute-start | bytes 786440 | tf_op jit(solution)/shard_map/ppermute | solution.py:25
  89.9 7.8 %collective-permute-start.11 = (bf16[1024,128]{1,0:T(8,128)(2,1)S(1)}, bf16[1024,128]{1,0:T(8,128)(2,1)S(1)}, u32[]{:S(2)}, u32[]{:S(2)}) collective-permute-start(bf16[1024,128]{1,0:T(8,128)(2,1)S(1)} %pad_maximum_fusion.1), channel_id=1, source_target_pairs={{0,8},{4,12},{8,0},{12,4},{16,24},{20,28},{24,16},{28,20},{1,9},{5... | collective-permute-start | bytes 786440 | tf_op jit(solution)/shard_map/ppermute | solution.py:25
  93.5 8.9 %collective-permute-start.21 = (bf16[1024,128]{1,0:T(8,128)(2,1)S(1)}, bf16[1024,128]{1,0:T(8,128)(2,1)S(1)}, u32[]{:S(2)}, u32[]{:S(2)}) collective-permute-start(bf16[1024,128]{1,0:T(8,128)(2,1)S(1)} %pad_maximum_fusion.3), channel_id=1, source_target_pairs={{0,8},{4,12},{8,0},{12,4},{16,24},{20,28},{24,16},{28,20},{1,9},{5... | collective-permute-start | bytes 786440 | tf_op jit(solution)/shard_map/ppermute | solution.py:25
  97.8 9.3 %collective-permute-start.13 = (bf16[512,128]{1,0:T(8,128)(2,1)S(1)}, bf16[512,128]{1,0:T(8,128)(2,1)S(1)}, u32[]{:S(2)}, u32[]{:S(2)}) collective-permute-start(bf16[512,128]{1,0:T(8,128)(2,1)S(1)} %add_convert_fusion.3), channel_id=1, source_target_pairs={{0,24},{4,28},{8,16},{12,20},{16,8},{20,12},{24,0},{28,4},{1,25},{... | collective-permute-start | bytes 393224 | tf_op jit(solution)/shard_map/ppermute | solution.py:25
  102.5 7.6 %collective-permute-start.23 = (bf16[512,128]{1,0:T(8,128)(2,1)S(1)}, bf16[512,128]{1,0:T(8,128)(2,1)S(1)}, u32[]{:S(2)}, u32[]{:S(2)}) collective-permute-start(bf16[512,128]{1,0:T(8,128)(2,1)S(1)} %add_convert_fusion), channel_id=1, source_target_pairs={{0,24},{4,28},{8,16},{12,20},{16,8},{20,12},{24,0},{28,4},{1,25},{... | collective-permute-start | bytes 393224 | tf_op jit(solution)/shard_map/ppermute | solution.py:25
  107.1 5.0 %collective-permute-start.24 = (bf16[128,128]{1,0:T(8,128)(2,1)S(1)}, bf16[128,128]{1,0:T(8,128)(2,1)S(1)}, u32[]{:S(2)}, u32[]{:S(2)}) collective-permute-start(bf16[128,128]{1,0:T(8,128)(2,1)S(1)} %get-tuple-element.61), channel_id=1, source_target_pairs={{0,1},{1,0},{2,3},{3,2},{4,5},{5,4},{6,7},{7,6},{8,9},{9,8},{10,11... | collective-permute-start | bytes 98312 | tf_op jit(solution)/shard_map/ppermute | solution.py:25
  107.2 6.4 %collective-permute-start.26 = (bf16[128,128]{1,0:T(8,128)(2,1)S(1)}, bf16[128,128]{1,0:T(8,128)(2,1)S(1)}, u32[]{:S(2)}, u32[]{:S(2)}) collective-permute-start(bf16[128,128]{1,0:T(8,128)(2,1)S(1)} %get-tuple-element.63), channel_id=1, source_target_pairs={{0,2},{1,3},{2,0},{3,1},{4,6},{5,7},{6,4},{7,5},{8,10},{9,11},{10,... | collective-permute-start | bytes 98312 | tf_op jit(solution)/shard_map/ppermute | solution.py:25
  108.6 5.0 %collective-permute-start.28 = (bf16[128,128]{1,0:T(8,128)(2,1)S(1)}, bf16[128,128]{1,0:T(8,128)(2,1)S(1)}, u32[]{:S(2)}, u32[]{:S(2)}) collective-permute-start(bf16[128,128]{1,0:T(8,128)(2,1)S(1)} %get-tuple-element.65), channel_id=1, source_target_pairs={{0,3},{1,2},{2,1},{3,0},{4,7},{5,6},{6,5},{7,4},{8,11},{9,10},{10,... | collective-permute-start | bytes 98312 | tf_op jit(solution)/shard_map/ppermute | solution.py:25
  110.2 3.4 %collective-permute-start.25 = (bf16[128,128]{1,0:T(8,128)(2,1)S(1)}, bf16[128,128]{1,0:T(8,128)(2,1)S(1)}, u32[]{:S(2)}, u32[]{:S(2)}) collective-permute-start(bf16[128,128]{1,0:T(8,128)(2,1)S(1)} %get-tuple-element.62), channel_id=1, source_target_pairs={{0,1},{1,0},{2,3},{3,2},{4,5},{5,4},{6,7},{7,6},{8,9},{9,8},{10,11... | collective-permute-start | bytes 98312 | tf_op jit(solution)/shard_map/ppermute | solution.py:25
  110.3 4.0 %collective-permute-start.27 = (bf16[128,128]{1,0:T(8,128)(2,1)S(1)}, bf16[128,128]{1,0:T(8,128)(2,1)S(1)}, u32[]{:S(2)}, u32[]{:S(2)}) collective-permute-start(bf16[128,128]{1,0:T(8,128)(2,1)S(1)} %get-tuple-element.64), channel_id=1, source_target_pairs={{0,2},{1,3},{2,0},{3,1},{4,6},{5,7},{6,4},{7,5},{8,10},{9,11},{10,... | collective-permute-start | bytes 98312 | tf_op jit(solution)/shard_map/ppermute | solution.py:25
  112.2 3.4 %collective-permute-start.29 = (bf16[128,128]{1,0:T(8,128)(2,1)S(1)}, bf16[128,128]{1,0:T(8,128)(2,1)S(1)}, u32[]{:S(2)}, u32[]{:S(2)}) collective-permute-start(bf16[128,128]{1,0:T(8,128)(2,1)S(1)} %get-tuple-element.66), channel_id=1, source_target_pairs={{0,3},{1,2},{2,1},{3,0},{4,7},{5,6},{6,5},{7,4},{8,11},{9,10},{10,... | collective-permute-start | bytes 98312 | tf_op jit(solution)/shard_map/ppermute | solution.py:25
  (26 other events, 272.0 us)

commit v10 on v8

--- a/solution.py
+++ b/solution.py
@@ -370,12 +370,7 @@
 
 
 def gather_plan(count, head):
-    plan = stages(count, head % 2 == 1)
-    if head % 2 == 1:
-        mask, codes = plan.pop()
-        cut = len(codes) // 2
-        plan += [(mask, half) for half in (codes[:cut], codes[cut:]) if half]
-    return plan
+    return stages(count, head % 2 == 1)
 
 
 def scatter_plan(count, head):

time: 112 us -> 120 us (1.071)
  waiting for transfers between devices: 35.2 us -> 39.1 us
  local copies, waits for them, and re-layouts: 7.99 us -> 11.7 us
  other arithmetic: 0.62 us -> 3.11 us
  starting transfers between devices: 39.6 us -> 37.2 us
    ppermute x32 -> x31, waiting for transfers between devices: 35.2 us -> 39.1 us  [swap(): return lax.ppermute(value, axis, [(i, i ^ mask) for i in range(count)])]
    unnamed x40 -> x57, local copies, waits for them, and re-layouts: 7.88 us -> 11 us
    ppermute x32 -> x31, starting transfers between devices: 39.6 us -> 37.2 us  [swap(): return lax.ppermute(value, axis, [(i, i ^ mask) for i in range(count)])]
    concatenate x2 -> x4, other arithmetic: 0.04 us -> 1.86 us  [joined(): return pieces[0] if len(pieces) == 1 else jnp.concatenate(pieces, axis=0)]
  transfers between devices with their start and end apart: 32 -> 31, of which waited for: 9 -> 12; matrix products, arithmetic and copies ran while one was open for 1% -> 4% of each run, Pallas kernels for 20% -> 19%
where the time goes in v10:
time: 120 us; the launch traced here: 119 us
  waiting for transfers between devices  39.1 us (33%)
  starting transfers between devices  37.2 us (31%)
  Pallas kernels  27.6 us (23%)
  local copies, waits for them, and re-layouts  11.7 us (10%)
  other arithmetic  3.11 us (3%)
    ppermute x31, waiting for transfers between devices, swap(): return lax.ppermute(value, axis, [(i, i ^ mask) for i in range(count)])  39.1 us
    ppermute x31, starting transfers between devices, swap(): return lax.ppermute(value, axis, [(i, i ^ mask) for i in range(count)])  37.2 us
    pallas_call x4, Pallas kernels, attend(): pl.pallas_call(functools.partial(attend_kernel, source, sink, events, roo...  15.1 us
    unnamed x57, local copies, waits for them, and re-layouts  11 us
    pallas_call x2, Pallas kernels, project_keys_values(): pl.pallas_call(functools.partial(keys_values_kernel, count, each), grid_s...  6.05 us
    pallas_call x1, Pallas kernels, project_queries(): pl.pallas_call(query_kernel, in_specs=[pl.BlockSpec(memory_space=pltpu.SM...  3.59 us
  transfers between devices with their start and end apart: 31, of which 12 were waited for; matrix products, arithmetic and copies ran while one was open for 4% of the time, Pallas kernels for 19%

profile of v10, /device:TPU:0, one launch (start us, length us, event | category | flops | bytes accessed | tf_op | source)
XLA Modules:
  0.0 119.1 jit_solution(7337120756405366287)
XLA Ops:
  0.0 3.6 %queries.1 = (bf16[144,256]{1,0:T(8,128)(2,1)}, bf16[144,256]{1,0:T(8,128)(2,1)}, bf16[144,256]{1,0:T(8,128)(2,1)}, bf16[144,256]{1,0:T(8,128)(2,1)}) custom-call(s32[1]{0:T(128)} %bitcast._.me_ref, bf16[128,1024]{1,0:T(8,128)(2,1)} %cand_ref.3, bf16[1024,2048]{1,0:T(8,128)(2,1)} %w_hbm.1, s32[1,48]{1,0:T(1,128)} %bitcast.2), custom_call_target="tpu_custom_call" | custom-call | flops 268435456 | bytes 2621440 | tf_op jit(solution)/shard_map/queries/pallas_call | solution.py:95
  4.2 2.6 %collective-permute-start.1 = (bf16[144,256]{1,0:T(8,128)(2,1)}, bf16[144,256]{1,0:T(8,128)(2,1)S(1)}, u32[]{:S(2)}, u32[]{:S(2)}) collective-permute-start(bf16[144,256]{1,0:T(8,128)(2,1)} %get-tuple-element.39), channel_id=1, source_target_pairs={{0,2},{1,3},{2,0},{3,1},{4,6},{5,7},{6,4},{7,5},{8,10},{9,11},{10,... | collective-permute-start | bytes 221192 | tf_op jit(solution)/shard_map/ppermute | solution.py:25
  6.7 3.0 %collective-permute-done.1.refs_2_ = bf16[144,256]{1,0:T(8,128)(2,1)S(1)} collective-permute-done((bf16[144,256]{1,0:T(8,128)(2,1)}, bf16[144,256]{1,0:T(8,128)(2,1)S(1)}, u32[]{:S(2)}, u32[]{:S(2)}) %collective-permute-start.1) | collective-permute-done | bytes 73760 | tf_op jit(solution)/shard_map/ppermute | solution.py:25
  9.8 1.4 %collective-permute-done.2.refs_3_ = bf16[144,256]{1,0:T(8,128)(2,1)S(1)} collective-permute-done((bf16[144,256]{1,0:T(8,128)(2,1)}, bf16[144,256]{1,0:T(8,128)(2,1)S(1)}, u32[]{:S(2)}, u32[]{:S(2)}) %collective-permute-start.2) | collective-permute-done | bytes 73760 | tf_op jit(solution)/shard_map/ppermute | solution.py:25
  12.7 1.8 %collective-permute-start.18 = (bf16[512,128]{1,0:T(8,128)(2,1)S(1)}, bf16[512,128]{1,0:T(8,128)(2,1)S(1)}, u32[]{:S(2)}, u32[]{:S(2)}) collective-permute-start(bf16[512,128]{1,0:T(8,128)(2,1)S(1)} %get-tuple-element.57.refs_4_), channel_id=1, source_target_pairs={{0,4},{4,0},{8,12},{12,8},{16,20},{20,16},{24,28},{28,24},{1,5},{5... | collective-permute-start | bytes 393224 | tf_op jit(solution)/shard_map/ppermute | solution.py:25
  14.5 1.4 %copy-done.2 = bf16[768,1024]{1,0:T(8,128)(2,1)S(1)} copy-done((bf16[768,1024]{1,0:T(8,128)(2,1)S(1)}, bf16[768,1024]{1,0:T(8,128)(2,1)}, u32[]{:S(2)}) %copy-start.2) | copy-done | bytes 1572888
  15.9 3.0 %shard_map.100 = (bf16[768,256]{1,0:T(8,128)(2,1)S(1)}, bf16[768,256]{1,0:T(8,128)(2,1)S(1)}, bf16[768,256]{1,0:T(8,128)(2,1)}, bf16[768,256]{1,0:T(8,128)(2,1)S(1)}) custom-call(s32[1]{0:T(128)} %bitcast._.me_ref, bf16[768,1024]{1,0:T(8,128)(2,1)S(1)} %copy-done.2, bf16[1024,2048]{1,0:T(8,128)(2,1)S(1)} %copy-done, bf16[1024,2048]{1,0:T(8,128)(2,1)S(1)} %copy-done, ...), custom_call_target="tpu_custom_call" | custom-call | flops 1610612736 | bytes 5242880 | tf_op jit(solution)/shard_map/pallas_call | solution.py:186
  19.6 3.6 %collective-permute-start.6 = (bf16[512,128]{1,0:T(8,128)(2,1)S(1)}, bf16[512,128]{1,0:T(8,128)(2,1)S(1)}, u32[]{:S(2)}, u32[]{:S(2)}) collective-permute-start(bf16[512,128]{1,0:T(8,128)(2,1)S(1)} %get-tuple-element.46.refs_4_), channel_id=1, source_target_pairs={{0,24},{4,28},{8,16},{12,20},{16,8},{20,12},{24,0},{28,4},{1,25},{... | collective-permute-start | bytes 393224 | tf_op jit(solution)/shard_map/ppermute | solution.py:25
  24.9 2.6 %collective-permute-done.6.refs_5_ = bf16[512,128]{1,0:T(8,128)(2,1)S(1)} collective-permute-done((bf16[512,128]{1,0:T(8,128)(2,1)S(1)}, bf16[512,128]{1,0:T(8,128)(2,1)S(1)}, u32[]{:S(2)}, u32[]{:S(2)}) %collective-permute-start.6) | collective-permute-done | bytes 131104 | tf_op jit(solution)/shard_map/ppermute | solution.py:25
  28.2 8.5 %collective-permute-start.8 = (bf16[1024,128]{1,0:T(8,128)(2,1)}, bf16[1024,128]{1,0:T(8,128)(2,1)}, u32[]{:S(2)}, u32[]{:S(2)}) collective-permute-start(bf16[1024,128]{1,0:T(8,128)(2,1)} %constant_dynamic-update-slice_fusion), channel_id=1, source_target_pairs={{0,8},{4,12},{8,0},{12,4},{16,24},{20,28},{24,16},{28,20},{1,9},{5... | collective-permute-start | bytes 786440 | tf_op jit(solution)/shard_map/ppermute | solution.py:25
  36.7 3.0 %shard_map.101 = (bf16[768,256]{1,0:T(8,128)(2,1)}, bf16[768,256]{1,0:T(8,128)(2,1)S(1)}, bf16[768,256]{1,0:T(8,128)(2,1)}, bf16[768,256]{1,0:T(8,128)(2,1)S(1)}) custom-call(s32[1]{0:T(128)} %bitcast._.me_ref, bf16[768,1024]{1,0:T(8,128)(2,1)S(1)} %copy-done.3, bf16[1024,2048]{1,0:T(8,128)(2,1)S(1)} %copy-done, bf16[1024,2048]{1,0:T(8,128)(2,1)S(1)} %copy-done, ...), custom_call_target="tpu_custom_call" | custom-call | flops 1610612736 | bytes 5242880 | tf_op jit(solution)/shard_map/pallas_call | solution.py:186
  41.3 1.2 %collective-permute-start.4 = (bf16[768,256]{1,0:T(8,128)(2,1)}, bf16[768,256]{1,0:T(8,128)(2,1)S(1)}, u32[]{:S(2)}, u32[]{:S(2)}) collective-permute-start(bf16[768,256]{1,0:T(8,128)(2,1)} %get-tuple-element.44), channel_id=1, source_target_pairs={{0,2},{1,3},{2,0},{3,1},{4,6},{5,7},{6,4},{7,5},{8,10},{9,11},{10,... | collective-permute-start | bytes 1179656 | tf_op jit(solution)/shard_map/ppermute | solution.py:25
  45.9 7.0 %collective-permute-done.4.refs_2_ = bf16[768,256]{1,0:T(8,128)(2,1)S(1)} collective-permute-done((bf16[768,256]{1,0:T(8,128)(2,1)}, bf16[768,256]{1,0:T(8,128)(2,1)S(1)}, u32[]{:S(2)}, u32[]{:S(2)}) %collective-permute-start.4) | collective-permute-done | bytes 393248 | tf_op jit(solution)/shard_map/ppermute | solution.py:25
  52.8 1.7 %collective-permute-start.16 = (bf16[768,256]{1,0:T(8,128)(2,1)}, bf16[768,256]{1,0:T(8,128)(2,1)S(1)}, u32[]{:S(2)}, u32[]{:S(2)}) collective-permute-start(bf16[768,256]{1,0:T(8,128)(2,1)} %copy-done.25), channel_id=1, source_target_pairs={{0,2},{1,3},{2,0},{3,1},{4,6},{5,7},{6,4},{7,5},{8,10},{9,11},{10,... | collective-permute-start | bytes 1179656 | tf_op jit(solution)/shard_map/ppermute | solution.py:25
  54.5 6.0 %collective-permute-done.5.refs_3_ = bf16[768,256]{1,0:T(8,128)(2,1)S(1)} collective-permute-done((bf16[768,256]{1,0:T(8,128)(2,1)}, bf16[768,256]{1,0:T(8,128)(2,1)S(1)}, u32[]{:S(2)}, u32[]{:S(2)}) %collective-permute-start.5) | collective-permute-done | bytes 393248 | tf_op jit(solution)/shard_map/ppermute | solution.py:25
  60.6 1.8 %collective-permute-start.17 = (bf16[768,256]{1,0:T(8,128)(2,1)}, bf16[768,256]{1,0:T(8,128)(2,1)S(1)}, u32[]{:S(2)}, u32[]{:S(2)}) collective-permute-start(bf16[768,256]{1,0:T(8,128)(2,1)} %copy-done.24), channel_id=1, source_target_pairs={{0,3},{1,2},{2,1},{3,0},{4,7},{5,6},{6,5},{7,4},{8,11},{9,10},{10,... | collective-permute-start | bytes 1179656 | tf_op jit(solution)/shard_map/ppermute | solution.py:25
  64.6 2.7 %shard_map.103 = bf16[1024,128]{1,0:T(8,128)(2,1)S(1)} custom-call(s32[192]{0:T(256)S(1)} %multiply_add_fusion.pos_ref, s32[8]{0:T(128)S(1)} %convert_reduce_fusion.1.count_ref, s32[2]{0:T(128)S(1)} %copy-done.21, bf16[768,256]{1,0:T(8,128)(2,1)S(1)} %copy-done.11, bf16[768,256]{1,0:T(8,128)(2,1)} %collective-permute-done.3.refs_1_, ...), custom_call_target="tpu_custom_call" | custom-call | flops 402653184 | bytes 2097152 | tf_op jit(solution)/shard_map/pallas_call | solution.py:280
  67.3 2.2 %collective-permute-done.7.refs_6_ = bf16[1024,128]{1,0:T(8,128)(2,1)S(1)} collective-permute-done((bf16[1024,128]{1,0:T(8,128)(2,1)}, bf16[1024,128]{1,0:T(8,128)(2,1)S(1)}, u32[]{:S(2)}, u32[]{:S(2)}) %collective-permute-start.7) | collective-permute-done | bytes 262176 | tf_op jit(solution)/shard_map/ppermute | solution.py:25
  73.5 5.2 %shard_map.102 = (bf16[512,128]{1,0:T(8,128)(2,1)S(1)}, bf16[512,128]{1,0:T(8,128)(2,1)S(1)}, bf16[512,128]{1,0:T(8,128)(2,1)S(1)}, bf16[1024,128]{1,0:T(8,128)(2,1)S(1)}, bf16[512,128]{1,0:T(8,128)(2,1)S(1)}) custom-call(s32[192]{0:T(256)S(1)} %multiply_add_fusion.pos_ref, s32[8]{0:T(128)S(1)} %convert_reduce_fusion.1.count_ref, s32[6]{0:T(128)S(1)} %copy-done.26, ...), custom_call_target="tpu_custom_call" | custom-call | flops 1207959552 | bytes 3145728 | tf_op jit(solution)/shard_map/pallas_call | solution.py:280
  78.7 3.2 %collective-permute-start.12 = (bf16[512,128]{1,0:T(8,128)(2,1)S(1)}, bf16[512,128]{1,0:T(8,128)(2,1)S(1)}, u32[]{:S(2)}, u32[]{:S(2)}) collective-permute-start(bf16[512,128]{1,0:T(8,128)(2,1)S(1)} %get-tuple-element.50), channel_id=1, source_target_pairs={{0,24},{4,28},{8,16},{12,20},{16,8},{20,12},{24,0},{28,4},{1,25},{... | collective-permute-start | bytes 393224 | tf_op jit(solution)/shard_map/ppermute | solution.py:25
  81.9 2.2 %shard_map.106 = bf16[1024,128]{1,0:T(8,128)(2,1)S(1)} custom-call(s32[192]{0:T(256)S(1)} %multiply_add_fusion.pos_ref, s32[8]{0:T(128)S(1)} %convert_reduce_fusion.1.count_ref, s32[2]{0:T(128)S(1)} %copy-done.22, bf16[768,256]{1,0:T(8,128)(2,1)S(1)} %copy-done.14, bf16[768,256]{1,0:T(8,128)(2,1)S(1)} %collective-permute-done.15.refs_1_, ...), custom_call_target="tpu_custom_call" | custom-call | flops 402653184 | bytes 2097152 | tf_op jit(solution)/shard_map/pallas_call | solution.py:280
  84.1 1.4 %collective-permute-start.21 = (bf16[1024,128]{1,0:T(8,128)(2,1)S(1)}, bf16[1024,128]{1,0:T(8,128)(2,1)S(1)}, u32[]{:S(2)}, u32[]{:S(2)}) collective-permute-start(bf16[1024,128]{1,0:T(8,128)(2,1)S(1)} %shard_map.106), channel_id=1, source_target_pairs={{0,4},{4,0},{8,12},{12,8},{16,20},{20,16},{24,28},{28,24},{1,5},{5... | collective-permute-start | bytes 786440 | tf_op jit(solution)/shard_map/ppermute | solution.py:25
  85.6 5.1 %shard_map.105 = (bf16[512,128]{1,0:T(8,128)(2,1)S(1)}, bf16[1024,128]{1,0:T(8,128)(2,1)S(1)}, bf16[1024,128]{1,0:T(8,128)(2,1)S(1)}, bf16[512,128]{1,0:T(8,128)(2,1)S(1)}) custom-call(s32[192]{0:T(256)S(1)} %multiply_add_fusion.pos_ref, s32[8]{0:T(128)S(1)} %convert_reduce_fusion.1.count_ref, s32[6]{0:T(128)S(1)} %copy-done.27, ...), custom_call_target="tpu_custom_call" | custom-call | flops 1207959552 | bytes 3145728 | tf_op jit(solution)/shard_map/pallas_call | solution.py:280
  92.1 2.1 %collective-permute-start.22 = (bf16[1024,128]{1,0:T(8,128)(2,1)S(1)}, bf16[1024,128]{1,0:T(8,128)(2,1)S(1)}, u32[]{:S(2)}, u32[]{:S(2)}) collective-permute-start(bf16[1024,128]{1,0:T(8,128)(2,1)S(1)} %pad_maximum_fusion.3), channel_id=1, source_target_pairs={{0,8},{4,12},{8,0},{12,4},{16,24},{20,28},{24,16},{28,20},{1,9},{5... | collective-permute-start | bytes 786440 | tf_op jit(solution)/shard_map/ppermute | solution.py:25
  95.3 5.8 %collective-permute-done.11.refs_1_ = bf16[1024,128]{1,0:T(8,128)(2,1)S(1)} collective-permute-done((bf16[1024,128]{1,0:T(8,128)(2,1)S(1)}, bf16[1024,128]{1,0:T(8,128)(2,1)S(1)}, u32[]{:S(2)}, u32[]{:S(2)}) %collective-permute-start.11) | collective-permute-done | bytes 262176 | tf_op jit(solution)/shard_map/ppermute | solution.py:25
  101.2 4.5 %collective-permute-done.22.refs_1_ = bf16[1024,128]{1,0:T(8,128)(2,1)S(1)} collective-permute-done((bf16[1024,128]{1,0:T(8,128)(2,1)S(1)}, bf16[1024,128]{1,0:T(8,128)(2,1)S(1)}, u32[]{:S(2)}, u32[]{:S(2)}) %collective-permute-start.22) | collective-permute-done | bytes 262176 | tf_op jit(solution)/shard_map/ppermute | solution.py:25
  105.8 2.1 %collective-permute-done.14.refs_3_ = bf16[512,128]{1,0:T(8,128)(2,1)S(1)} collective-permute-done((bf16[512,128]{1,0:T(8,128)(2,1)S(1)}, bf16[512,128]{1,0:T(8,128)(2,1)S(1)}, u32[]{:S(2)}, u32[]{:S(2)}) %collective-permute-start.14) | collective-permute-done | bytes 131104 | tf_op jit(solution)/shard_map/ppermute | solution.py:25
  109.9 2.6 %collective-permute-done.24.refs_3_ = bf16[512,128]{1,0:T(8,128)(2,1)S(1)} collective-permute-done((bf16[512,128]{1,0:T(8,128)(2,1)S(1)}, bf16[512,128]{1,0:T(8,128)(2,1)S(1)}, u32[]{:S(2)}, u32[]{:S(2)}) %collective-permute-start.24) | collective-permute-done | bytes 131104 | tf_op jit(solution)/shard_map/ppermute | solution.py:25
  112.7 1.7 %collective-permute-start.28 = (bf16[128,128]{1,0:T(8,128)(2,1)S(1)}, bf16[128,128]{1,0:T(8,128)(2,1)S(1)}, u32[]{:S(2)}, u32[]{:S(2)}) collective-permute-start(bf16[128,128]{1,0:T(8,128)(2,1)S(1)} %get-tuple-element.66), channel_id=1, source_target_pairs={{0,2},{1,3},{2,0},{3,1},{4,6},{5,7},{6,4},{7,5},{8,10},{9,11},{10,... | collective-permute-start | bytes 98312 | tf_op jit(solution)/shard_map/ppermute | solution.py:25
  114.5 1.3 %gate.1.gate_ref = f32[4,128,256]{2,1,0:T(8,128)S(1)} custom-call(s32[1]{0:T(128)} %bitcast._.me_ref, bf16[128,1024]{1,0:T(8,128)(2,1)S(1)} %copy-done.4, bf16[1024,2048]{1,0:T(8,128)(2,1)S(1)} %copy-done.1), custom_call_target="tpu_custom_call" | custom-call | flops 268435456 | bytes 2883584 | tf_op jit(solution)/shard_map/gate/pallas_call | solution.py:146
  116.7 1.1 collective-permute-done.30.refs_7_
  117.8 1.3 %finish.1 = bf16[128,1024]{1,0:T(8,128)(2,1)} custom-call(s32[1]{0:T(128)} %bitcast._.me_ref, bf16[128,1024]{1,0:T(8,128)(2,1)S(1)} %copy-done.4, f32[4,128,256]{2,1,0:T(8,128)S(1)} %gate.1.gate_ref, bf16[1024,1024]{1,0:T(8,128)(2,1)S(1)} %copy-done.5, f32[128,128]{1,0:T(8,128)S(1)} %get-tuple-element.52.refs_0_, f32[128,128]{1,0:T(8,128)S(1)} %get-tuple-element.62.refs_1_, ...), custom_call_target="tpu_custom_call" | custom-call | flops 268435456 | bytes 3407872 | tf_op jit(solution)/shard_map/finish/pallas_call | solution.py:327
  (114 shorter events, 22.0 us)
Async XLA Ops:
  3.6 3.1 %collective-permute-start = (bf16[144,256]{1,0:T(8,128)(2,1)}, bf16[144,256]{1,0:T(8,128)(2,1)S(1)}, u32[]{:S(2)}, u32[]{:S(2)}) collective-permute-start(bf16[144,256]{1,0:T(8,128)(2,1)} %get-tuple-element.38), channel_id=1, source_target_pairs={{0,1},{1,0},{2,3},{3,2},{4,5},{5,4},{6,7},{7,6},{8,9},{9,8},{10,11... | collective-permute-start | bytes 221192 | tf_op jit(solution)/shard_map/ppermute | solution.py:25
  4.2 5.6 %collective-permute-start.1 = (bf16[144,256]{1,0:T(8,128)(2,1)}, bf16[144,256]{1,0:T(8,128)(2,1)S(1)}, u32[]{:S(2)}, u32[]{:S(2)}) collective-permute-start(bf16[144,256]{1,0:T(8,128)(2,1)} %get-tuple-element.39), channel_id=1, source_target_pairs={{0,2},{1,3},{2,0},{3,1},{4,6},{5,7},{6,4},{7,5},{8,10},{9,11},{10,... | collective-permute-start | bytes 221192 | tf_op jit(solution)/shard_map/ppermute | solution.py:25
  6.7 4.4 %collective-permute-start.2 = (bf16[144,256]{1,0:T(8,128)(2,1)}, bf16[144,256]{1,0:T(8,128)(2,1)S(1)}, u32[]{:S(2)}, u32[]{:S(2)}) collective-permute-start(bf16[144,256]{1,0:T(8,128)(2,1)} %get-tuple-element.40), channel_id=1, source_target_pairs={{0,3},{1,2},{2,1},{3,0},{4,7},{5,6},{6,5},{7,4},{8,11},{9,10},{10,... | collective-permute-start | bytes 221192 | tf_op jit(solution)/shard_map/ppermute | solution.py:25
  12.7 11.2 %collective-permute-start.18 = (bf16[512,128]{1,0:T(8,128)(2,1)S(1)}, bf16[512,128]{1,0:T(8,128)(2,1)S(1)}, u32[]{:S(2)}, u32[]{:S(2)}) collective-permute-start(bf16[512,128]{1,0:T(8,128)(2,1)S(1)} %get-tuple-element.57.refs_4_), channel_id=1, source_target_pairs={{0,4},{4,0},{8,12},{12,8},{16,20},{20,16},{24,28},{28,24},{1,5},{5... | collective-permute-start | bytes 393224 | tf_op jit(solution)/shard_map/ppermute | solution.py:25
  19.6 25.6 %collective-permute-start.3 = (bf16[768,256]{1,0:T(8,128)(2,1)}, bf16[768,256]{1,0:T(8,128)(2,1)}, u32[]{:S(2)}, u32[]{:S(2)}) collective-permute-start(bf16[768,256]{1,0:T(8,128)(2,1)} %get-tuple-element.43), channel_id=1, source_target_pairs={{0,1},{1,0},{2,3},{3,2},{4,5},{5,4},{6,7},{7,6},{8,9},{9,8},{10,11... | collective-permute-start | bytes 1179656 | tf_op jit(solution)/shard_map/ppermute | solution.py:25
  19.6 7.9 %collective-permute-start.6 = (bf16[512,128]{1,0:T(8,128)(2,1)S(1)}, bf16[512,128]{1,0:T(8,128)(2,1)S(1)}, u32[]{:S(2)}, u32[]{:S(2)}) collective-permute-start(bf16[512,128]{1,0:T(8,128)(2,1)S(1)} %get-tuple-element.46.refs_4_), channel_id=1, source_target_pairs={{0,24},{4,28},{8,16},{12,20},{16,8},{20,12},{24,0},{28,4},{1,25},{... | collective-permute-start | bytes 393224 | tf_op jit(solution)/shard_map/ppermute | solution.py:25
  24.7 19.1 %collective-permute-start.19 = (bf16[1024,128]{1,0:T(8,128)(2,1)}, bf16[1024,128]{1,0:T(8,128)(2,1)}, u32[]{:S(2)}, u32[]{:S(2)}) collective-permute-start(bf16[1024,128]{1,0:T(8,128)(2,1)} %pad_maximum_fusion.2), channel_id=1, source_target_pairs={{0,24},{4,28},{8,16},{12,20},{16,8},{20,12},{24,0},{28,4},{1,25},{... | collective-permute-start | bytes 786440 | tf_op jit(solution)/shard_map/ppermute | solution.py:25
  28.2 15.1 %collective-permute-start.8 = (bf16[1024,128]{1,0:T(8,128)(2,1)}, bf16[1024,128]{1,0:T(8,128)(2,1)}, u32[]{:S(2)}, u32[]{:S(2)}) collective-permute-start(bf16[1024,128]{1,0:T(8,128)(2,1)} %constant_dynamic-update-slice_fusion), channel_id=1, source_target_pairs={{0,8},{4,12},{8,0},{12,4},{16,24},{20,28},{24,16},{28,20},{1,9},{5... | collective-permute-start | bytes 786440 | tf_op jit(solution)/shard_map/ppermute | solution.py:25
  41.3 40.6 %copy-start.14 = (bf16[768,256]{1,0:T(8,128)(2,1)S(1)}, bf16[768,256]{1,0:T(8,128)(2,1)}, u32[]{:S(2)}) copy-start(bf16[768,256]{1,0:T(8,128)(2,1)} %copy-done.13) | copy-start | bytes 1179652
  41.3 11.5 %collective-permute-start.4 = (bf16[768,256]{1,0:T(8,128)(2,1)}, bf16[768,256]{1,0:T(8,128)(2,1)S(1)}, u32[]{:S(2)}, u32[]{:S(2)}) collective-permute-start(bf16[768,256]{1,0:T(8,128)(2,1)} %get-tuple-element.44), channel_id=1, source_target_pairs={{0,2},{1,3},{2,0},{3,1},{4,6},{5,7},{6,4},{7,5},{8,10},{9,11},{10,... | collective-permute-start | bytes 1179656 | tf_op jit(solution)/shard_map/ppermute | solution.py:25
  42.5 18.0 %collective-permute-start.5 = (bf16[768,256]{1,0:T(8,128)(2,1)}, bf16[768,256]{1,0:T(8,128)(2,1)S(1)}, u32[]{:S(2)}, u32[]{:S(2)}) collective-permute-start(bf16[768,256]{1,0:T(8,128)(2,1)} %get-tuple-element.45), channel_id=1, source_target_pairs={{0,3},{1,2},{2,1},{3,0},{4,7},{5,6},{6,5},{7,4},{8,11},{9,10},{10,... | collective-permute-start | bytes 1179656 | tf_op jit(solution)/shard_map/ppermute | solution.py:25
  43.3 19.1 %collective-permute-start.9 = (bf16[1024,128]{1,0:T(8,128)(2,1)}, bf16[1024,128]{1,0:T(8,128)(2,1)S(1)}, u32[]{:S(2)}, u32[]{:S(2)}) collective-permute-start(bf16[1024,128]{1,0:T(8,128)(2,1)} %collective-permute-done.8.refs_7_), channel_id=1, source_target_pairs={{0,4},{4,0},{8,12},{12,8},{16,20},{20,16},{24,28},{28,24},{1,5},{5... | collective-permute-start | bytes 786440 | tf_op jit(solution)/shard_map/ppermute | solution.py:25
  44.9 37.0 %collective-permute-start.20 = (bf16[2048,128]{1,0:T(8,128)(2,1)S(1)}, bf16[2048,128]{1,0:T(8,128)(2,1)S(1)}, u32[]{:S(2)}, u32[]{:S(2)}) collective-permute-start(bf16[2048,128]{1,0:T(8,128)(2,1)S(1)} %pad_maximum_fusion), channel_id=1, source_target_pairs={{0,8},{4,12},{8,0},{12,4},{16,24},{20,28},{24,16},{28,20},{1,9},{5... | collective-permute-start | bytes 1572872 | tf_op jit(solution)/shard_map/ppermute | solution.py:25
  45.3 33.4 %collective-permute-start.15 = (bf16[768,256]{1,0:T(8,128)(2,1)}, bf16[768,256]{1,0:T(8,128)(2,1)S(1)}, u32[]{:S(2)}, u32[]{:S(2)}) collective-permute-start(bf16[768,256]{1,0:T(8,128)(2,1)} %copy-done.23), channel_id=1, source_target_pairs={{0,1},{1,0},{2,3},{3,2},{4,5},{5,4},{6,7},{7,6},{8,9},{9,8},{10,11... | collective-permute-start | bytes 1179656 | tf_op jit(solution)/shard_map/ppermute | solution.py:25
  52.8 29.1 %collective-permute-start.16 = (bf16[768,256]{1,0:T(8,128)(2,1)}, bf16[768,256]{1,0:T(8,128)(2,1)S(1)}, u32[]{:S(2)}, u32[]{:S(2)}) collective-permute-start(bf16[768,256]{1,0:T(8,128)(2,1)} %copy-done.25), channel_id=1, source_target_pairs={{0,2},{1,3},{2,0},{3,1},{4,6},{5,7},{6,4},{7,5},{8,10},{9,11},{10,... | collective-permute-start | bytes 1179656 | tf_op jit(solution)/shard_map/ppermute | solution.py:25
  60.6 21.4 %collective-permute-start.17 = (bf16[768,256]{1,0:T(8,128)(2,1)}, bf16[768,256]{1,0:T(8,128)(2,1)S(1)}, u32[]{:S(2)}, u32[]{:S(2)}) collective-permute-start(bf16[768,256]{1,0:T(8,128)(2,1)} %copy-done.24), channel_id=1, source_target_pairs={{0,3},{1,2},{2,1},{3,0},{4,7},{5,6},{6,5},{7,4},{8,11},{9,10},{10,... | collective-permute-start | bytes 1179656 | tf_op jit(solution)/shard_map/ppermute | solution.py:25
  62.4 7.1 %collective-permute-start.7 = (bf16[1024,128]{1,0:T(8,128)(2,1)}, bf16[1024,128]{1,0:T(8,128)(2,1)S(1)}, u32[]{:S(2)}, u32[]{:S(2)}) collective-permute-start(bf16[1024,128]{1,0:T(8,128)(2,1)} %constant_dynamic-update-slice_fusion), channel_id=1, source_target_pairs={{0,4},{4,0},{8,12},{12,8},{16,20},{20,16},{24,28},{28,24},{1,5},{5... | collective-permute-start | bytes 786440 | tf_op jit(solution)/shard_map/ppermute | solution.py:25
  69.5 22.3 %collective-permute-start.10 = (bf16[1024,128]{1,0:T(8,128)(2,1)S(1)}, bf16[1024,128]{1,0:T(8,128)(2,1)S(1)}, u32[]{:S(2)}, u32[]{:S(2)}) collective-permute-start(bf16[1024,128]{1,0:T(8,128)(2,1)S(1)} %shard_map.103), channel_id=1, source_target_pairs={{0,4},{4,0},{8,12},{12,8},{16,20},{20,16},{24,28},{28,24},{1,5},{5... | collective-permute-start | bytes 786440 | tf_op jit(solution)/shard_map/ppermute | solution.py:25
  78.7 15.4 %collective-permute-start.12 = (bf16[512,128]{1,0:T(8,128)(2,1)S(1)}, bf16[512,128]{1,0:T(8,128)(2,1)S(1)}, u32[]{:S(2)}, u32[]{:S(2)}) collective-permute-start(bf16[512,128]{1,0:T(8,128)(2,1)S(1)} %get-tuple-element.50), channel_id=1, source_target_pairs={{0,24},{4,28},{8,16},{12,20},{16,8},{20,12},{24,0},{28,4},{1,25},{... | collective-permute-start | bytes 393224 | tf_op jit(solution)/shard_map/ppermute | solution.py:25
  84.1 7.8 %collective-permute-start.21 = (bf16[1024,128]{1,0:T(8,128)(2,1)S(1)}, bf16[1024,128]{1,0:T(8,128)(2,1)S(1)}, u32[]{:S(2)}, u32[]{:S(2)}) collective-permute-start(bf16[1024,128]{1,0:T(8,128)(2,1)S(1)} %shard_map.106), channel_id=1, source_target_pairs={{0,4},{4,0},{8,12},{12,8},{16,20},{20,16},{24,28},{28,24},{1,5},{5... | collective-permute-start | bytes 786440 | tf_op jit(solution)/shard_map/ppermute | solution.py:25
  90.7 10.5 %collective-permute-start.23 = (bf16[1024,128]{1,0:T(8,128)(2,1)S(1)}, bf16[1024,128]{1,0:T(8,128)(2,1)S(1)}, u32[]{:S(2)}, u32[]{:S(2)}) collective-permute-start(bf16[1024,128]{1,0:T(8,128)(2,1)S(1)} %get-tuple-element.60), channel_id=1, source_target_pairs={{0,4},{4,0},{8,12},{12,8},{16,20},{20,16},{24,28},{28,24},{1,5},{5... | collective-permute-start | bytes 786440 | tf_op jit(solution)/shard_map/ppermute | solution.py:25
  91.9 9.1 %collective-permute-start.11 = (bf16[1024,128]{1,0:T(8,128)(2,1)S(1)}, bf16[1024,128]{1,0:T(8,128)(2,1)S(1)}, u32[]{:S(2)}, u32[]{:S(2)}) collective-permute-start(bf16[1024,128]{1,0:T(8,128)(2,1)S(1)} %pad_maximum_fusion.1), channel_id=1, source_target_pairs={{0,8},{4,12},{8,0},{12,4},{16,24},{20,28},{24,16},{28,20},{1,9},{5... | collective-permute-start | bytes 786440 | tf_op jit(solution)/shard_map/ppermute | solution.py:25
  92.1 13.6 %collective-permute-start.22 = (bf16[1024,128]{1,0:T(8,128)(2,1)S(1)}, bf16[1024,128]{1,0:T(8,128)(2,1)S(1)}, u32[]{:S(2)}, u32[]{:S(2)}) collective-permute-start(bf16[1024,128]{1,0:T(8,128)(2,1)S(1)} %pad_maximum_fusion.3), channel_id=1, source_target_pairs={{0,8},{4,12},{8,0},{12,4},{16,24},{20,28},{24,16},{28,20},{1,9},{5... | collective-permute-start | bytes 786440 | tf_op jit(solution)/shard_map/ppermute | solution.py:25
  94.2 11.6 %collective-permute-start.13 = (bf16[512,128]{1,0:T(8,128)(2,1)S(1)}, bf16[512,128]{1,0:T(8,128)(2,1)S(1)}, u32[]{:S(2)}, u32[]{:S(2)}) collective-permute-start(bf16[512,128]{1,0:T(8,128)(2,1)S(1)} %add_convert_fusion.4), channel_id=1, source_target_pairs={{0,4},{4,0},{8,12},{12,8},{16,20},{20,16},{24,28},{28,24},{1,5},{5... | collective-permute-start | bytes 393224 | tf_op jit(solution)/shard_map/ppermute | solution.py:25
  101.1 6.8 %collective-permute-start.14 = (bf16[512,128]{1,0:T(8,128)(2,1)S(1)}, bf16[512,128]{1,0:T(8,128)(2,1)S(1)}, u32[]{:S(2)}, u32[]{:S(2)}) collective-permute-start(bf16[512,128]{1,0:T(8,128)(2,1)S(1)} %add_convert_fusion.3), channel_id=1, source_target_pairs={{0,24},{4,28},{8,16},{12,20},{16,8},{20,12},{24,0},{28,4},{1,25},{... | collective-permute-start | bytes 393224 | tf_op jit(solution)/shard_map/ppermute | solution.py:25
  105.7 6.8 %collective-permute-start.24 = (bf16[512,128]{1,0:T(8,128)(2,1)S(1)}, bf16[512,128]{1,0:T(8,128)(2,1)S(1)}, u32[]{:S(2)}, u32[]{:S(2)}) collective-permute-start(bf16[512,128]{1,0:T(8,128)(2,1)S(1)} %add_convert_fusion), channel_id=1, source_target_pairs={{0,24},{4,28},{8,16},{12,20},{16,8},{20,12},{24,0},{28,4},{1,25},{... | collective-permute-start | bytes 393224 | tf_op jit(solution)/shard_map/ppermute | solution.py:25
  108.0 6.4 %collective-permute-start.25 = (bf16[128,128]{1,0:T(8,128)(2,1)S(1)}, bf16[128,128]{1,0:T(8,128)(2,1)S(1)}, u32[]{:S(2)}, u32[]{:S(2)}) collective-permute-start(bf16[128,128]{1,0:T(8,128)(2,1)S(1)} %get-tuple-element.63), channel_id=1, source_target_pairs={{0,1},{1,0},{2,3},{3,2},{4,5},{5,4},{6,7},{7,6},{8,9},{9,8},{10,11... | collective-permute-start | bytes 98312 | tf_op jit(solution)/shard_map/ppermute | solution.py:25
  108.0 7.9 %collective-permute-start.27 = (bf16[128,128]{1,0:T(8,128)(2,1)S(1)}, bf16[128,128]{1,0:T(8,128)(2,1)S(1)}, u32[]{:S(2)}, u32[]{:S(2)}) collective-permute-start(bf16[128,128]{1,0:T(8,128)(2,1)S(1)} %get-tuple-element.65), channel_id=1, source_target_pairs={{0,2},{1,3},{2,0},{3,1},{4,6},{5,7},{6,4},{7,5},{8,10},{9,11},{10,... | collective-permute-start | bytes 98312 | tf_op jit(solution)/shard_map/ppermute | solution.py:25
  109.0 6.9 %collective-permute-start.29 = (bf16[128,128]{1,0:T(8,128)(2,1)S(1)}, bf16[128,128]{1,0:T(8,128)(2,1)S(1)}, u32[]{:S(2)}, u32[]{:S(2)}) collective-permute-start(bf16[128,128]{1,0:T(8,128)(2,1)S(1)} %get-tuple-element.67), channel_id=1, source_target_pairs={{0,3},{1,2},{2,1},{3,0},{4,7},{5,6},{6,5},{7,4},{8,11},{9,10},{10,... | collective-permute-start | bytes 98312 | tf_op jit(solution)/shard_map/ppermute | solution.py:25
  112.6 3.3 %collective-permute-start.26 = (bf16[128,128]{1,0:T(8,128)(2,1)S(1)}, bf16[128,128]{1,0:T(8,128)(2,1)S(1)}, u32[]{:S(2)}, u32[]{:S(2)}) collective-permute-start(bf16[128,128]{1,0:T(8,128)(2,1)S(1)} %get-tuple-element.64), channel_id=1, source_target_pairs={{0,1},{1,0},{2,3},{3,2},{4,5},{5,4},{6,7},{7,6},{8,9},{9,8},{10,11... | collective-permute-start | bytes 98312 | tf_op jit(solution)/shard_map/ppermute | solution.py:25
  112.7 4.0 %collective-permute-start.28 = (bf16[128,128]{1,0:T(8,128)(2,1)S(1)}, bf16[128,128]{1,0:T(8,128)(2,1)S(1)}, u32[]{:S(2)}, u32[]{:S(2)}) collective-permute-start(bf16[128,128]{1,0:T(8,128)(2,1)S(1)} %get-tuple-element.66), channel_id=1, source_target_pairs={{0,2},{1,3},{2,0},{3,1},{4,6},{5,7},{6,4},{7,5},{8,10},{9,11},{10,... | collective-permute-start | bytes 98312 | tf_op jit(solution)/shard_map/ppermute | solution.py:25
  114.4 3.4 %collective-permute-start.30 = (bf16[128,128]{1,0:T(8,128)(2,1)S(1)}, bf16[128,128]{1,0:T(8,128)(2,1)S(1)}, u32[]{:S(2)}, u32[]{:S(2)}) collective-permute-start(bf16[128,128]{1,0:T(8,128)(2,1)S(1)} %get-tuple-element.68), channel_id=1, source_target_pairs={{0,3},{1,2},{2,1},{3,0},{4,7},{5,6},{6,5},{7,4},{8,11},{9,10},{10,... | collective-permute-start | bytes 98312 | tf_op jit(solution)/shard_map/ppermute | solution.py:25
  (27 other events, 325.7 us)
